TPU v7x, 32 devices: a whole 2x2x4 slice. The times are simulated.
32 devices in a mesh: dp: 4 (over z), fsdp: 2 (over x), tensor: 4 (over y, core).
Axes of the slice: x: 2, y: 2, z: 4, core: 2. Of those that a mesh axis runs over, the one named last changes fastest.
Arguments:
- tokens: bfloat16 [32, 256, 768], P(('dp', 'fsdp')), may hold values from -6 to 6
- keep_mask: int32 [32, 256], P(('dp', 'fsdp')), may hold values 0 or 1
- crop_len: int32 [32], P(('dp', 'fsdp')), may hold values from 128 to 256
- pos_index: int32 [32], replicated, may hold values from 0 to 31, each once
- pos_keys: bfloat16 [32, 768], P(('dp', 'fsdp')), may hold values from -0.08984375 to 0.08984375
- key_queue: bfloat16 [16384, 768], P(('dp', 'fsdp')), may hold values from -0.08984375 to 0.08984375
- query_weight: bfloat16 [768, 768], P(None, 'tensor'), may hold values from -0.21875 to 0.21875
- query_bias: float32 [768], P('tensor'), may hold values from -1.25 to 1.25
- key_weight: bfloat16 [768, 768], P(None, 'tensor'), may hold values from -0.21875 to 0.21875
- value_weight: bfloat16 [768, 768], P(None, 'tensor'), may hold values from -0.21875 to 0.21875
- value_bias: float32 [768], P('tensor'), may hold values from -1.25 to 1.25
- out_weight: bfloat16 [768, 768], P('tensor'), may hold values from -0.875 to 0.875
- out_bias: float32 [768], replicated, may hold values from -1.25 to 1.25
- norm_gain: float32 [768], replicated, may hold values from 0.5 to 1.5
- norm_shift: float32 [768], replicated, may hold values from -1.25 to 1.25
- up_weight: bfloat16 [768, 3072], P(None, 'tensor'), may hold values from -0.21875 to 0.21875
- up_bias: float32 [3072], P('tensor'), may hold values from -1.25 to 1.25
- down_weight: bfloat16 [3072, 768], P('tensor'), may hold values from -0.109375 to 0.109375
- down_bias: float32 [768], replicated, may hold values from -1.25 to 1.25
- final_gain: float32 [768], replicated, may hold values from 0.5 to 1.5
- final_shift: float32 [768], replicated, may hold values from -0.625 to 0.625
Outputs:
- output: bfloat16 [32, 256, 768], P(('dp', 'fsdp', 'tensor'))
- input_grad: bfloat16 [32, 256, 768], P(('dp', 'fsdp', 'tensor'))
- query_weight_grad: float32 [768, 768], P(None, 'tensor')
- query_bias_grad: float32 [768], P('tensor')
- key_weight_grad: float32 [768, 768], P(None, 'tensor')
- value_weight_grad: float32 [768, 768], P(None, 'tensor')
- value_bias_grad: float32 [768], P('tensor')
- out_weight_grad: float32 [768, 768], P('tensor')
- out_bias_grad: float32 [768], replicated
- norm_gain_grad: float32 [768], replicated
- norm_shift_grad: float32 [768], replicated
- up_weight_grad: float32 [768, 3072], P(None, 'tensor')
- up_bias_grad: float32 [3072], P('tensor')
- down_weight_grad: float32 [3072, 768], P('tensor')
- down_bias_grad: float32 [768], replicated
- final_gain_grad: float32 [768], replicated
- final_shift_grad: float32 [768], replicated
- loss: float32 [], replicated
Inputs may be any that keep to these rules, and one draw needn't show every extreme that they name: pos_index is a permutation of the crops.
All inputs are finite; a program needn't handle non-finite values. No bound on the sum of `keep_mask` on one device may be relied on, other than what follows from the above.
Results may differ from a plain program's by a relative error of at most 0.028.
Values may be sent and summed in bfloat16 or wider, within the bound.
No kernel may reach another device: no remote copies, remote signals or barrier semaphores. Data moves between devices by JAX's collectives and lax.ppermute only.
A program may use at most 128 MiB of HBM per device.

v0:
```python
import math

import jax
import jax.numpy as jnp
from jax import lax
from jax.sharding import PartitionSpec as P

HEAD = 64


eps = 1e-12
inv_temp = 20.0
loss_scale = 256.0
highest_precision = lax.Precision.HIGHEST


def combined_all(array, axis, combine):
    everything = jax.tree.map(lambda part: lax.all_gather(part, axis), array)
    leading = jax.tree.map(lambda part: part[0], everything)

    def turn(k, so_far):
        return combine(so_far, jax.tree.map(lambda part: part[k], everything))

    return lax.fori_loop(1, lax.axis_size(axis), turn, leading)


def compact_table(keep_mask, crop_len):
    length = keep_mask.shape[1]
    places = jnp.arange(length, dtype=jnp.int32)
    kept = ((keep_mask == 1) | (places == 0)[None, :]) & (places[None, :] < crop_len[:, None])
    rank = jnp.cumsum(kept.astype(jnp.int32), axis=1) - 1
    table = kept[:, None, :] & (rank[:, None, :] == places[None, :, None])
    count = jnp.sum(kept.astype(jnp.int32), axis=1)
    return (table.astype(jnp.bfloat16), count)


def norm_parts(resid):
    center = resid - jnp.mean(resid, axis=-1, keepdims=True)
    rstd = lax.rsqrt(jnp.mean(center * center, axis=-1, keepdims=True) + eps)
    return (center * rstd, rstd)


def norm_backward(upstream, normed, rstd, gain):
    scaled = upstream * gain
    inner = jnp.mean(scaled, axis=-1, keepdims=True)
    along = jnp.mean(scaled * normed, axis=-1, keepdims=True)
    return rstd * (scaled - inner - normed * along)


def gain_parts(upstream, normed):
    return (jnp.sum(upstream * normed, axis=(0, 1)), jnp.sum(upstream, axis=(0, 1)))


def small_stack(vectors, parts):
    joined = jnp.concatenate(vectors)
    return jnp.broadcast_to(joined[None, :], (parts, joined.shape[0]))


def project(token_rows, weight_matrix):
    return jnp.einsum("ixw,wk->ixk", token_rows, weight_matrix, preferred_element_type=jnp.float32)


def project_back(gradient_list, weight_matrix):
    return jnp.einsum(
        "vmk,ak->vma", gradient_list, weight_matrix, preferred_element_type=jnp.float32
    )


def weight_grad(token_rows, gradient_list):
    return jnp.einsum("zfh,zfw->hw", token_rows, gradient_list, preferred_element_type=jnp.float32)


def masked_scores(query, keys, live, scale):
    scores = jnp.einsum("bqhd,bkhd->bhqk", query, keys, preferred_element_type=jnp.float32) * scale
    return jnp.where(live[:, None, None, :], scores, -1e30)


def attend(query, keys, values, live, scale):
    scores = masked_scores(query, keys, live, scale)
    top = jnp.max(scores, axis=-1, keepdims=True)
    expo = jnp.exp(scores - top)
    total = jnp.sum(expo, axis=-1, keepdims=True)
    probs = expo / total
    context_rows = jnp.einsum(
        "bhqk,bkhd->bqhd", probs.astype(jnp.bfloat16), values, preferred_element_type=jnp.float32
    )
    return (context_rows.astype(jnp.bfloat16), top + jnp.log(total))


def attend_back(query, keys, values, live, lse, context_grad, scale):
    probs = jnp.exp(masked_scores(query, keys, live, scale) - lse)
    probs_grad = jnp.einsum(
        "bqhd,bkhd->bhqk", context_grad, values, preferred_element_type=jnp.float32
    )
    inner = jnp.sum(probs * probs_grad, axis=-1, keepdims=True)
    score_grad = probs * (probs_grad - inner)
    query_grad = (
        jnp.einsum(
            "bhqk,bkhd->bqhd", score_grad, keys.astype(jnp.float32), precision=highest_precision
        )
        * scale
    ).astype(jnp.bfloat16)
    keys_grad = (
        jnp.einsum(
            "bhqk,bqhd->bkhd", score_grad, query.astype(jnp.float32), precision=highest_precision
        )
        * scale
    ).astype(jnp.bfloat16)
    values_grad = jnp.einsum(
        "bhqk,bqhd->bkhd",
        probs.astype(jnp.bfloat16),
        context_grad,
        preferred_element_type=jnp.float32,
    ).astype(jnp.bfloat16)
    return (query_grad, keys_grad, values_grad)


def join_totals(first, second):
    top = jnp.maximum(first[0], second[0])
    return (top, first[1] * jnp.exp(first[0] - top) + second[1] * jnp.exp(second[0] - top))


def per_device(
    tokens,
    keep_mask,
    crop_len,
    pos_index,
    pos_keys,
    key_queue,
    query_weight,
    query_bias,
    key_weight,
    value_weight,
    value_bias,
    out_weight,
    out_bias,
    norm_gain,
    norm_shift,
    up_weight,
    up_bias,
    down_weight,
    down_bias,
    final_gain,
    final_shift,
):
    seqs, length, width = tokens.shape
    heads_here = query_weight.shape[1] // HEAD
    parts = lax.axis_size("tensor")
    member = lax.axis_index("tensor")
    share = seqs // parts
    scale = 1.0 / math.sqrt(HEAD)
    block = math.gcd(seqs, max(1, 512 // length))
    blocks = seqs // block

    def mine(arr):
        return lax.dynamic_slice_in_dim(arr, member * share, share, 0)

    table, count = compact_table(keep_mask, crop_len)
    places = jnp.arange(length, dtype=jnp.int32)
    live = places[None, :] < count[:, None]
    live_rows = live.astype(jnp.float32)
    counts = count.astype(jnp.float32)
    compact = jnp.einsum("sjp,spd->sjd", table, tokens, preferred_element_type=jnp.float32).astype(
        jnp.bfloat16
    )
    query = (project(compact, query_weight) + query_bias).astype(jnp.bfloat16)
    keys = project(compact, key_weight).astype(jnp.bfloat16)
    values = (project(compact, value_weight) + value_bias).astype(jnp.bfloat16)

    def by_heads(arr):
        return arr.reshape(blocks, block, length, heads_here, HEAD)

    live_blocks = live.reshape(blocks, block, length)
    head_query, head_keys, head_values = (by_heads(query), by_heads(keys), by_heads(values))
    context_rows, lse_rows = lax.map(
        lambda item: attend(item[0], item[1], item[2], item[3], scale),
        (head_query, head_keys, head_values, live_blocks),
    )
    context_rows = context_rows.reshape(seqs, length, heads_here * HEAD)
    partial_out = project(context_rows, out_weight)
    own_attn = lax.psum_scatter(partial_out, "tensor", scatter_dimension=0, tiled=True) + out_bias
    normed_one, rstd_one = norm_parts(mine(compact).astype(jnp.float32) + own_attn)
    middle = normed_one * norm_gain + norm_shift
    middle_low = lax.all_gather(middle.astype(jnp.bfloat16), "tensor", axis=0, tiled=True)
    pre = project(middle_low, up_weight) + up_bias
    hidden_full, gelu_pull = jax.vjp(lambda arr: jax.nn.gelu(arr, approximate=False), pre)
    hidden_state = hidden_full.astype(jnp.bfloat16)
    partial_ffn = project(hidden_state, down_weight)
    ffn_out = lax.psum_scatter(partial_ffn, "tensor", scatter_dimension=0, tiled=True) + down_bias
    normed_two, rstd_two = norm_parts(middle + ffn_out)
    result = normed_two * final_gain + final_shift
    own_live = mine(live_rows)
    own_counts = mine(counts)
    output = result.astype(jnp.bfloat16)
    pooled = jnp.sum(result * own_live[:, :, None], axis=1) / own_counts[:, None]
    all_query, all_pos = (
        lax.all_gather(pooled.astype(jnp.bfloat16), ("dp", "fsdp", "tensor"), axis=0, tiled=True),
        lax.all_gather(mine(pos_keys), ("dp", "fsdp", "tensor"), axis=0, tiled=True),
    )
    positive = jnp.take(all_pos, pos_index, axis=0).astype(jnp.float32)
    pos_logit = jnp.sum(all_query.astype(jnp.float32) * positive, axis=-1) * inv_temp
    logits = (
        jnp.einsum("qd,kd->qk", all_query, key_queue, preferred_element_type=jnp.float32) * inv_temp
    )
    local_top = jnp.max(logits, axis=1)
    local_sum = jnp.sum(jnp.exp(logits - local_top[:, None]), axis=1)
    top_all, sum_all = combined_all((local_top, local_sum), ("dp", "fsdp"), join_totals)
    top_final = jnp.maximum(top_all, pos_logit)
    lse = top_final + jnp.log(
        sum_all * jnp.exp(top_all - top_final) + jnp.exp(pos_logit - top_final)
    )
    loss = jnp.sum(lse - pos_logit) / all_query.shape[0]
    coeff = (jnp.exp(logits - lse[:, None]) * (loss_scale * inv_temp)).astype(jnp.bfloat16)
    partial_grad = jnp.dot(coeff, key_queue, preferred_element_type=jnp.float32)
    group_grad = lax.psum_scatter(partial_grad, ("dp", "fsdp"), scatter_dimension=0, tiled=True)
    group = lax.axis_index(("dp", "fsdp"))
    group_lse = lax.dynamic_slice_in_dim(lse, group * seqs, seqs, 0)
    group_pos = lax.dynamic_slice_in_dim(pos_logit, group * seqs, seqs, 0)
    group_positive = lax.dynamic_slice_in_dim(positive, group * seqs, seqs, 0)
    group_grad = (
        group_grad
        + loss_scale * inv_temp * (jnp.exp(group_pos - group_lse) - 1.0)[:, None] * group_positive
    )
    result_grad = mine(group_grad)[:, None, :] / own_counts[:, None, None] * own_live[:, :, None]
    two_grad = norm_backward(result_grad, normed_two, rstd_two, final_gain)
    final_gain_part, final_shift_part = gain_parts(result_grad, normed_two)
    feedforward_gradient = lax.all_gather(
        two_grad.astype(jnp.bfloat16), "tensor", axis=0, tiled=True
    )
    down_weight_grad = jnp.einsum(
        "kaf,kaj->fj", hidden_state, feedforward_gradient, preferred_element_type=jnp.float32
    )
    down_bias_grad = jnp.sum(feedforward_gradient, axis=(0, 1), dtype=jnp.float32)
    pre_grad = gelu_pull(project_back(feedforward_gradient, down_weight))[0].astype(jnp.bfloat16)
    up_weight_grad = weight_grad(middle_low, pre_grad)
    up_bias_grad = jnp.sum(pre_grad, axis=(0, 1), dtype=jnp.float32)
    back_part = project_back(pre_grad, up_weight)
    back_sum, final_sums = (
        lax.psum_scatter(back_part, "tensor", scatter_dimension=0, tiled=True),
        lax.psum_scatter(
            small_stack((final_gain_part, final_shift_part), parts),
            "tensor",
            scatter_dimension=0,
            tiled=True,
        ),
    )
    final_gain_grad = final_sums[0, :width]
    final_shift_grad = final_sums[0, width:]
    middle_grad = two_grad + back_sum
    one_grad = norm_backward(middle_grad, normed_one, rstd_one, norm_gain)
    attention_gradient = lax.all_gather(one_grad.astype(jnp.bfloat16), "tensor", axis=0, tiled=True)
    norm_gain_part, norm_shift_part = gain_parts(middle_grad, normed_one)
    out_weight_grad = jnp.einsum(
        "kaf,kaj->fj", context_rows, attention_gradient, preferred_element_type=jnp.float32
    )
    out_bias_grad = jnp.sum(attention_gradient, axis=(0, 1), dtype=jnp.float32)
    context_grad = project_back(attention_gradient, out_weight).astype(jnp.bfloat16)
    query_grad, keys_grad, values_grad = lax.map(
        lambda item: attend_back(item[0], item[1], item[2], item[3], item[4], item[5], scale),
        (head_query, head_keys, head_values, live_blocks, lse_rows, by_heads(context_grad)),
    )
    query_grad = query_grad.reshape(seqs, length, heads_here * HEAD)
    keys_grad = keys_grad.reshape(seqs, length, heads_here * HEAD)
    values_grad = values_grad.reshape(seqs, length, heads_here * HEAD)
    query_weight_grad = weight_grad(compact, query_grad)
    query_bias_grad = jnp.sum(query_grad, axis=(0, 1), dtype=jnp.float32)
    key_weight_grad = weight_grad(compact, keys_grad)
    value_weight_grad = weight_grad(compact, values_grad)
    value_bias_grad = jnp.sum(values_grad, axis=(0, 1), dtype=jnp.float32)
    partial_in = (
        project_back(query_grad, query_weight)
        + project_back(keys_grad, key_weight)
        + project_back(values_grad, value_weight)
    )
    summed_in, norm_sums = (
        lax.psum_scatter(partial_in, "tensor", scatter_dimension=0, tiled=True),
        lax.psum_scatter(
            small_stack((norm_gain_part, norm_shift_part), parts),
            "tensor",
            scatter_dimension=0,
            tiled=True,
        ),
    )
    norm_gain_grad = norm_sums[0, :width]
    norm_shift_grad = norm_sums[0, width:]
    compact_grad = one_grad + summed_in
    input_grad = jnp.einsum(
        "sjp,sjd->spd",
        mine(table),
        compact_grad.astype(jnp.bfloat16),
        preferred_element_type=jnp.float32,
    ).astype(jnp.bfloat16)
    summed = lax.psum(
        (
            query_weight_grad,
            query_bias_grad,
            key_weight_grad,
            value_weight_grad,
            value_bias_grad,
            out_weight_grad,
            out_bias_grad,
            norm_gain_grad,
            norm_shift_grad,
            up_weight_grad,
            up_bias_grad,
            down_weight_grad,
            down_bias_grad,
            final_gain_grad,
            final_shift_grad,
        ),
        ("dp", "fsdp"),
    )
    return (
        output,
        input_grad,
        summed[0],
        summed[1],
        summed[2],
        summed[3],
        summed[4],
        summed[5],
        summed[6],
        summed[7],
        summed[8],
        summed[9],
        summed[10],
        summed[11],
        summed[12],
        summed[13],
        summed[14],
        loss,
    )


def solution(mesh):
    placed = (
        P(("dp", "fsdp"), None, None),
        P(("dp", "fsdp"), None),
        P(("dp", "fsdp")),
        P(),
        P(("dp", "fsdp"), None),
        P(("dp", "fsdp"), None),
        P(None, "tensor"),
        P("tensor"),
        P(None, "tensor"),
        P(None, "tensor"),
        P("tensor"),
        P("tensor", None),
        P(),
        P(),
        P(),
        P(None, "tensor"),
        P("tensor"),
        P("tensor", None),
        P(),
        P(),
        P(),
    )
    return jax.shard_map(
        per_device,
        mesh=mesh,
        in_specs=placed,
        out_specs=(
            P(("dp", "fsdp", "tensor"), None, None),
            P(("dp", "fsdp", "tensor"), None, None),
            P(None, "tensor"),
            P("tensor"),
            P(None, "tensor"),
            P(None, "tensor"),
            P("tensor"),
            P("tensor", None),
            P(),
            P(),
            P(),
            P(None, "tensor"),
            P("tensor"),
            P("tensor", None),
            P(),
            P(),
            P(),
            P(),
        ),
        check_vma=False,
    )
```

profile of v0, /device:TPU:0, one launch (start us, length us, event | category | flops | bytes accessed | tf_op | source)
XLA Modules:
  0.0 745.6 jit_solution(1232867740413659354)
XLA Ops:
  10.7 2.0 convolution_convert_fusion.2
  13.5 1.4 fusion.51
  14.9 1.4 fusion.52
  17.1 8.6 %while.43 = (s32[]{:T(128)}, bf16[2,2,256,3,64]{2,4,3,1,0:T(8,128)(2,1)}, f32[2,2,3,256,1]{3,2,1,4,0:T(4,128)S(1)}, bf16[2,2,256,3,64]{2,4,3,1,0:T(8,128)(2,1)},...) while((s32[]{:T(128)}, ...), condition=%wide.region_6.7_spmd, body=%wide.region_3.6_spmd.sunk | while | flops 103905792 | bytes 5564509 | solution.py:175
  17.8 1.4 fusion.150
  19.4 2.0 fusion.152
  22.1 1.4 fusion.150
  23.7 2.0 fusion.152
  25.7 3.4 fusion.75
  29.1 40.7 %reduce-scatter.5.cloned.1.call-done = f32[1,256,768]{2,1,0:T(8,128)} async-done(((f32[4,256,768]{2,1,0:T(8,128)}), f32[1,256,768]{2,1,0:T(8,128)}) %reduce-scatter.5.cloned.1.call-update) | async-done | bytes 786448 | tf_op jit(solution)/shard_map/reduce_scatter | solution.py:181
  69.8 1.4 fusion.102
  72.8 1.6 fusion.68
  74.5 19.7 %all-gather.9.cloned.1.call-done = bf16[4,256,768]{2,1,0:T(8,128)(2,1)} async-done(((bf16[1,256,768]{2,1,0:T(8,128)(2,1)}), bf16[4,256,768]{2,1,0:T(8,128)(2,1)}) %all-gather.9.cloned.1.call-update) | async-done | bytes 1572880 | tf_op jit(solution)/shard_map/all_gather | solution.py:184
  94.2 3.9 fusion.67
  98.1 8.2 %multiply_convert_fusion = (bf16[4,256,768]{2,1,0:T(8,128)(2,1)S(1)}, f32[4,256,768]{2,1,0:T(8,128)}) fusion(f32[4,256,768]{2,1,0:T(8,128)S(1)} %get-tuple-element.351, f32[768]{0:T(1024)S(1)} %copy-done.51, u8[256,768]{1,0:T(8,128)(4,1)S(1)} %get-tuple-element.251, u8[256,768]{1,0:T(8,128)(4,1)S(1)} %get-tuple-element.250), kind=kLoop, calls=%fused_computation.73 | loop fusion | flops 55836672 | bytes 8260608 | tf_op jit(solution)/shard_map/convert_element_type | solution.py:187
  107.5 3.1 fusion.55
  115.0 41.2 %all-gather.4 = bf16[32,1,768]{2,1,0:T(2,128)(2,1)S(1)} all-gather(bf16[1,1,768]{2,1,0:T(2,128)(2,1)S(1)} %dynamic-slice_bitcast_fusion.3), channel_id=1, replica_groups=mesh['dp'=4,'fsdp'=2,'tensor'=4] {'dp','fsdp','tensor'}, dimensions={0}, use_global_device_ids=true | all-gather | bytes 50688 | tf_op jit(solution)/shard_map/all_gather | solution.py:198
  160.0 2.2 gather_fusion
  165.3 1.5 select_convert_fusion
  166.8 1.8 fusion.100
  171.2 36.9 %all-gather.3 = bf16[32,1,768]{2,1,0:T(2,128)(2,1)S(1)} all-gather(bf16[1,1,768]{2,1,0:T(2,128)(2,1)S(1)} %reshape.524), channel_id=2, replica_groups=mesh['dp'=4,'fsdp'=2,'tensor'=4] {'dp','fsdp','tensor'}, dimensions={0}, use_global_device_ids=true | all-gather | bytes 50688 | tf_op jit(solution)/shard_map/all_gather | solution.py:197
  214.5 18.0 %all-reduce.6 = (f32[256]{0:T(256)}, f32[256]{0:T(256)}) all-reduce(f32[256]{0:T(256)} %dynamic-update-slice, f32[256]{0:T(256)} %dynamic-update-slice.1), channel_id=3, replica_groups=mesh['dp'=4,'fsdp'=2,'tensor'=4] {'dp','fsdp'}, use_global_device_ids=true, to_apply=%add | all-reduce | flops 512 | bytes 4096
  237.6 1.6 multiply_reduce_fusion.8
  239.2 9.1 %while.44 = (s32[]{:T(128)}, f32[32]{0:T(128)}, f32[32]{0:T(128)}, f32[8,32]{1,0:T(8,128)}, f32[8,32]{1,0:T(8,128)}, /*index=5*/s32[]{:T(128)}, s32[]{:T(128)}, s32[]{:T(128)}) while((s32[]{:T(128)}, f32[32]{0:T(128)}, f32[32]{0:T(128)}, f32[8,32]{1,0:T(8,128)}, f32[8,32]{1,0:T(8,128)}, /*index=5*/s32[]{:T(128)}, s32[]{:T(128)}, ...), condition=%wide.region_17.18_spmd, body=%wide.region_16.17_spmd.sunk | while | flops 197 | bytes 899 | solution.py:24
  248.3 1.8 subtract_reduce_fusion
  250.7 2.3 fusion.87
  254.4 67.8 %all-reduce.12.cloned.1.call-done = f32[32,768]{1,0:T(8,128)} async-done(((f32[32,768]{1,0:T(8,128)}), f32[32,768]{1,0:T(8,128)}) %all-reduce.12.cloned.1.call-update) | async-done | bytes 98320
  322.2 2.1 divide_reduce_fusion
  324.3 2.2 fusion.65
  326.5 2.2 fusion.71
  328.8 18.8 %all-gather.11.cloned.1.call-done = bf16[4,256,768]{2,1,0:T(8,128)(2,1)} async-done(((bf16[1,256,768]{2,1,0:T(8,128)(2,1)}), bf16[4,256,768]{2,1,0:T(8,128)(2,1)}) %all-gather.11.cloned.1.call-update) | async-done | bytes 1572880 | tf_op jit(solution)/shard_map/all_gather | solution.py:227
  347.6 6.5 convert_reduce_fusion.1
  355.2 3.1 fusion.57
  358.5 38.0 %reduce-scatter.9.cloned.1.call-done = f32[1,256,768]{2,1,0:T(8,128)} async-done(((f32[4,256,768]{2,1,0:T(8,128)}), f32[1,256,768]{2,1,0:T(8,128)}) %reduce-scatter.9.cloned.1.call-update) | async-done | bytes 786448 | tf_op jit(solution)/shard_map/reduce_scatter | solution.py:239
  396.5 2.4 multiply_reduce_fusion.2
  400.3 19.7 %all-gather.13.cloned.1.call-done = bf16[4,256,768]{2,1,0:T(8,128)(2,1)} async-done(((bf16[1,256,768]{2,1,0:T(8,128)(2,1)}), bf16[4,256,768]{2,1,0:T(8,128)(2,1)}) %all-gather.13.cloned.1.call-update) | async-done | bytes 1572880 | tf_op jit(solution)/shard_map/all_gather | solution.py:251
  420.0 2.8 convolution_convert_fusion.4
  425.2 18.1 %while.45 = (s32[]{:T(128)}, bf16[2,2,256,3,64]{2,4,3,1,0:T(8,128)(2,1)}, bf16[2,2,256,3,64]{2,4,3,1,0:T(8,128)(2,1)}, bf16[2,2,256,3,64]{2,4,3,1,0:T(8,128)(2,1...) while((s32[]{:T(128)}, ...), condition=%wide.region_27.28_spmd, body=%wide.region_25.27_spmd.sunk | while | flops 759396864 | bytes 19317960 | solution.py:258
  425.2 1.5 fusion.160
  427.4 1.6 multiply_reduce_fusion.10
  430.8 2.0 fusion.163
  432.7 1.5 fusion.161
  434.2 1.5 fusion.160
  436.5 1.6 multiply_reduce_fusion.10
  439.8 2.0 fusion.163
  441.8 1.5 fusion.161
  443.3 1.8 fusion.77
  445.1 1.6 fusion.80
  446.7 3.4 add_add_fusion
  452.0 2.8 convolution_bitcast_fusion
  454.8 2.8 convolution_bitcast_fusion.1
  457.7 2.4 convolution_bitcast_fusion.2
  461.3 2.3 convolution_bitcast_fusion.4
  463.6 2.3 convolution_bitcast_fusion.5
  468.0 1.8 convert_reduce_fusion
  469.8 12.9 %all-reduce.8 = (f32[4,1536]{1,0:T(4,128)S(1)}, f32[4,1536]{1,0:T(4,128)S(1)}) all-reduce(f32[4,1536]{1,0:T(4,128)S(1)} %broadcast_in_dim.64, f32[4,1536]{1,0:T(4,128)S(1)} %broadcast_in_dim.65), channel_id=10, replica_groups=mesh['dp'=4,'fsdp'=2,'tensor'=4] {'tensor'}, use_global_device_ids=true, to_apply=%region_41.42.clone | all-reduce | flops 12288 | bytes 98304
  486.9 39.6 %all-reduce.5 = (f32[192]{0:T(256)}, f32[192]{0:T(256)}, f32[768]{0:T(1024)}, f32[768]{0:T(1024)}, f32[768]{0:T(1024)}, /*index=5*/f32[768]{0:T(1024)}, f32[768]{0:T(1024)}, f32[768]{0:T(1024)}, f32[768]{0:T(1024)}) all-reduce(f32[192]{0:T(256)S(1)} %reduce_sum.233, ...), channel_id=1, replica_groups=mesh['dp'=4,'fsdp'=2,'tensor'=4] {'dp','fsdp'}, use_global_device_ids=true, to_apply=%region_31.32 | all-reduce | flops 5760 | bytes 46080 | tf_op jit(solution)/shard_map/psum | solution.py:293
  526.5 2.2 fusion.53
  528.8 198.7 %all-reduce.14.cloned.1.call-done = (f32[768,192]{0,1:T(8,128)}, f32[768,192]{0,1:T(8,128)}, f32[768,192]{0,1:T(8,128)}, f32[192,768]{1,0:T(8,128)}, f32[768,768]{1,0:T(8,128)}, /*index=5*/f32[768,768]{1,0:T(8,128)}) async-done(((f32[768,192]{0,1:T(8,128)}, f32[768,192]{0,1:T(8,128)}, f32[768,192]{0,1:T(8,128)}, f32[192,768]{1,0:T(8,128)}, f32[768,768]{1,0:T(8,128)}, /*index=5*/f32[768,768]{1,0:T(8,128)}), ...) | async-done | bytes 7077904 | tf_op jit(solution)/shard_map/psum | solution.py:293
  727.4 2.1 copy.131
  729.5 1.9 copy.132
  731.4 1.9 copy.133
  734.1 1.4 copy.135
  735.5 1.4 copy.136
  (245 shorter events, 65.3 us)
Async XLA Ops:
  7.2 200.9 %copy-start = (bf16[2048,768]{1,0:T(8,128)(2,1)S(1)}, bf16[2048,768]{1,0:T(8,128)(2,1)}, u32[]{:S(2)}) copy-start(bf16[2048,768]{1,0:T(8,128)(2,1)} %param.32) | copy-start | bytes 9437188
  7.2 62.6 %reduce-scatter.5.cloned.1.call-start = ((), (), s32[]{:S(2)}) async-start(), calls=%async_computation.4 | async-start | bytes 3932160 | tf_op jit(solution)/shard_map/reduce_scatter | solution.py:181
  8.3 2.4 copy-start.42
  8.3 2.4 copy-start.56
  10.1 2.7 copy-start.26
  10.1 3.4 copy-start.23
  10.1 3.4 copy-start.60
  12.7 3.6 copy-start.2
  12.7 2.1 copy-start.27
  12.8 2.1 copy-start.61
  29.1 65.1 %all-gather.9.cloned.1.call-start = ((), (), s32[]{:S(2)}) async-start(), calls=%async_computation.5 | async-start | bytes 1966080 | tf_op jit(solution)/shard_map/all_gather | solution.py:184
  74.4 92.4 %reduce-scatter.7.cloned.1.call-start = ((), (), s32[]{:S(2)}) async-start(), calls=%async_computation.6 | async-start | bytes 3932160 | tf_op jit(solution)/shard_map/reduce_scatter | solution.py:189
  94.2 3.9 copy-start.51
  98.1 8.2 %copy-start.13 = (f32[4,256,768]{2,1,0:T(8,128)}, f32[4,256,768]{2,1,0:T(8,128)S(1)}, u32[]{:S(2)}) copy-start(f32[4,256,768]{2,1,0:T(8,128)S(1)} %get-tuple-element.351) | copy-start | bytes 9437188
  98.1 9.3 %copy-start.58 = (bf16[768,768]{1,0:T(8,128)(2,1)S(1)}, bf16[768,768]{1,0:T(8,128)(2,1)}, u32[]{:S(2)}) copy-start(bf16[768,768]{1,0:T(8,128)(2,1)} %param.44) | copy-start | bytes 3538948
  110.6 211.6 %all-reduce.12.cloned.1.call-start = ((), (), s32[]{:S(2)}) async-start(), calls=%async_computation.11 | async-start | bytes 196608
  166.8 2.7 copy-start.29
  166.8 2.7 copy-start.48
  166.8 2.7 copy-start.52
  168.6 2.5 copy-start.36
  168.9 2.3 copy-start.40
  208.1 2.6 copy-start.21
  209.2 1.4 copy-start.55
  253.0 94.6 %all-gather.11.cloned.1.call-start = ((), (), s32[]{:S(2)}) async-start(), calls=%async_computation.7 | async-start | bytes 1966080 | tf_op jit(solution)/shard_map/all_gather | solution.py:227
  328.7 67.7 %reduce-scatter.9.cloned.1.call-start = ((), (), s32[]{:S(2)}) async-start(), calls=%async_computation.8 | async-start | bytes 3932160 | tf_op jit(solution)/shard_map/reduce_scatter | solution.py:239
  347.6 7.7 %copy-start.59 = (bf16[768,768]{1,0:T(8,128)(2,1)S(1)}, bf16[768,768]{1,0:T(8,128)(2,1)}, u32[]{:S(2)}) copy-start(bf16[768,768]{1,0:T(8,128)(2,1)} %param.42) | copy-start | bytes 3538948
  358.3 38.1 %copy-start.5 = (f32[1,256,768]{2,1,0:T(8,128)S(1)}, f32[1,256,768]{2,1,0:T(8,128)}, u32[]{:S(2)}) copy-start(f32[1,256,768]{2,1,0:T(8,128)} %copy-done.4) | copy-start | bytes 2359300
  358.3 38.1 %copy-start.7 = (f32[1,256,768]{2,1,0:T(8,128)S(1)}, f32[1,256,768]{2,1,0:T(8,128)}, u32[]{:S(2)}) copy-start(f32[1,256,768]{2,1,0:T(8,128)} %copy-done.6) | copy-start | bytes 2359300
  358.3 38.1 %copy-start.30 = (f32[768]{0:T(1024)S(1)}, f32[768]{0:T(1024)}, u32[]{:S(2)}) copy-start(f32[768]{0:T(1024)} %param.46) | copy-start | bytes 9220
  358.3 38.1 %copy-start.31 = (f32[768]{0:T(1024)S(1)}, f32[768]{0:T(1024)}, u32[]{:S(2)}) copy-start(f32[768]{0:T(1024)} %param.40) | copy-start | bytes 9220
  358.3 38.1 %copy-start.33 = (f32[256]{0:T(256)S(1)}, f32[256]{0:T(256)}, u32[]{:S(2)}) copy-start(f32[256]{0:T(256)} %copy-done.32) | copy-start | bytes 3076
  358.3 38.1 %copy-start.37 = (f32[256]{0:T(256)S(1)}, f32[256]{0:T(256)}, u32[]{:S(2)}) copy-start(f32[256]{0:T(256)} %copy-done.36) | copy-start | bytes 3076
  358.3 38.1 %copy-start.39 = (f32[256]{0:T(256)S(1)}, f32[256]{0:T(256)}, u32[]{:S(2)}) copy-start(f32[256]{0:T(256)} %copy-done.38) | copy-start | bytes 3076
  358.4 38.1 %copy-start.41 = (f32[256]{0:T(256)S(1)}, f32[256]{0:T(256)}, u32[]{:S(2)}) copy-start(f32[256]{0:T(256)} %copy-done.40) | copy-start | bytes 3076
  358.4 38.1 %copy-start.49 = (f32[1,256]{1,0:T(1,128)S(1)}, f32[1,256]{1,0:T(1,128)}, u32[]{:S(2)}) copy-start(f32[1,256]{1,0:T(1,128)} %compare_convert_fusion) | copy-start | bytes 3076
  358.4 61.6 %copy-start.25 = (bf16[192,768]{1,0:T(8,128)(2,1)S(1)}, bf16[192,768]{1,0:T(8,128)(2,1)}, u32[]{:S(2)}) copy-start(bf16[192,768]{1,0:T(8,128)(2,1)} %param.38) | copy-start | bytes 884740
  358.4 61.6 %all-gather.13.cloned.1.call-start = ((), (), s32[]{:S(2)}) async-start(), calls=%async_computation.9 | async-start | bytes 1966080 | tf_op jit(solution)/shard_map/all_gather | solution.py:251
  400.2 126.3 %reduce-scatter.11.cloned.1.call-start = ((), (), s32[]{:S(2)}) async-start(), calls=%async_computation.10 | async-start | bytes 3932160 | tf_op jit(solution)/shard_map/reduce_scatter | solution.py:276
  425.2 3.8 copy-start.8
  425.2 3.8 copy-start.10
  434.2 3.8 copy-start.8
  434.2 3.8 copy-start.10
  443.3 1.8 copy-start.28
  443.3 3.4 copy-start.24
  450.1 1.4 copy-start.19
  450.1 1.9 copy-start.20
  450.1 277.3 %all-reduce.14.cloned.1.call-start = ((), (), s32[]{:S(2)}) async-start(), calls=%async_computation.12 | async-start | bytes 14155776 | tf_op jit(solution)/shard_map/psum | solution.py:293
  451.9 2.9 copy-start.57
  452.0 2.9 copy-start.64
  454.8 2.9 copy-start.3
  454.8 5.2 copy-start.12
  460.0 3.6 copy-start.9
  465.9 1.2 copy-start.35
  465.9 1.2 copy-start.43
  465.9 2.1 copy-start.44
  465.9 2.1 copy-start.45
  465.9 3.8 copy-start.46
  465.9 3.8 copy-start.47
  466.6 20.4 %copy-start.53 = (f32[768]{0:T(1024)S(1)}, f32[768]{0:T(1024)}, u32[]{:S(2)}) copy-start(f32[768]{0:T(1024)} %get-tuple-element.354) | copy-start | bytes 9220
  466.6 60.0 %copy-start.14 = (f32[1,256,768]{2,1,0:T(8,128)S(1)}, f32[1,256,768]{2,1,0:T(8,128)}, u32[]{:S(2)}) copy-start(f32[1,256,768]{2,1,0:T(8,128)} %get-tuple-element.332) | copy-start | bytes 2359300
  727.4 5.9 copy-start.22
  727.4 6.7 copy-start.17
  733.3 2.2 copy-start.16
  734.1 3.8 copy-start.1
  (13 other events, 10.3 us)
Sparse Core Ops, SparseCore 0:
  29.2 40.5 reduce-scatter.4
  74.6 19.6 all-gather.8
  110.7 38.4 reduce-scatter.6
  253.1 69.0 all-reduce.11
  328.8 18.6 all-gather.10
  358.5 37.8 reduce-scatter.8
  400.4 19.6 all-gather.12
  450.2 38.6 reduce-scatter.10
  495.2 232.2 all-reduce.13
where the time goes:
time: 748 us; the launch traced here: 746 us
  waiting for transfers between devices  404 us (54%)
  blocking collectives  149 us (20%)
  matrix products  76.4 us (10%)
  other arithmetic  53.2 us (7%)
  local copies, waits for them, and re-layouts  45.7 us (6%)
  between operations  17.5 us (2%)
    psum x1, waiting for transfers between devices, per_device(): lax.psum((query_weight_grad, query_bias_grad, key_weight_grad, value_weig...  199 us
    unnamed x10, waiting for transfers between devices  68 us
    all_gather x1, blocking collectives, per_device(): lax.all_gather(mine(pos_keys), ('dp', 'fsdp', 'tensor'), axis=0, tiled=True)  41.2 us
    reduce_scatter x1, waiting for transfers between devices, per_device(): lax.psum_scatter(partial_out, 'tensor', scatter_dimension=0, tiled=True)  40.7 us
    psum x1, blocking collectives, per_device(): lax.psum((query_weight_grad, query_bias_grad, key_weight_grad, value_weig...  39.6 us
    reduce_scatter x1, waiting for transfers between devices, per_device(): lax.psum_scatter(back_part, 'tensor', scatter_dimension=0, tiled=True)  38 us
    all_gather x1, blocking collectives, per_device(): lax.all_gather(pooled.astype(jnp.bfloat16), ('dp', 'fsdp', 'tensor'), axi...  36.9 us
    unnamed x2, blocking collectives  30.9 us
  transfers between devices with their start and end apart: 9, of which 7 were waited for; matrix products, arithmetic and copies ran while one was open for 5% of the time, Pallas kernels for 0%

commit v1 on v0

v1 whole, which is shorter than its diff:
```python
import math

import jax
import jax.numpy as jnp
from jax import lax
from jax.experimental import pallas as pl
from jax.experimental.pallas import tpu as pltpu
from jax.sharding import PartitionSpec as P

HEAD = 64
eps = 1e-12
inv_temp = 20.0
loss_scale = 256.0
low = jnp.bfloat16
full = jnp.float32
LANES = 128

RELATIVE = (0, 2, 1, 3)


def dot(a, b, dims=((1,), (0,))):
    return lax.dot_general(a, b, (dims, ((), ())), preferred_element_type=full)


def swap(array, axis, stride):
    size = lax.axis_size(axis)
    return lax.ppermute(array, axis, [(i, i ^ stride) for i in range(size)])


def strides(axis):
    size = lax.axis_size(axis)
    assert size & (size - 1) == 0
    return [1 << k for k in range(size.bit_length() - 1)]


def tensor_gather(block):
    pair = jnp.stack([block, swap(block, "tensor", 2)])
    return jnp.concatenate([pair, swap(pair, "tensor", 1)])


def tensor_sum(parts):
    other = swap(parts[2:], "tensor", 1)
    far = swap((parts[1].astype(full) + other[1].astype(full)).astype(low), "tensor", 2)
    return parts[0].astype(full) + other[0].astype(full) + far.astype(full)


def group_sum(grad):
    rows = grad.shape[0] // 2
    f = lax.axis_index("fsdp")
    kept = lax.dynamic_slice_in_dim(grad, f * rows, rows, 0)
    sent = lax.dynamic_slice_in_dim(grad, (1 - f) * rows, rows, 0)
    part = kept.astype(full) + swap(sent, "fsdp", 1).astype(full)
    if lax.axis_size("dp") == 4:
        z = lax.axis_index("dp")
        part = part + lax.ppermute(part.astype(low), "dp", [(0, 1), (3, 2)]).astype(full)
        part = part.astype(low)
        total = part.astype(full) + lax.ppermute(part, "dp", [(1, 2), (2, 1)]).astype(full)
        total = total.astype(low)
        outer = lax.ppermute(total, "dp", [(1, 0), (2, 3)])
        total = jnp.where((z == 0) | (z == 3), outer, total)
    else:
        total = lax.psum(part, "dp").astype(low)
    other = swap(total, "fsdp", 1)
    first = jnp.where(f == 0, total, other)
    second = jnp.where(f == 0, other, total)
    return jnp.concatenate([first, second])


def norm_parts(resid):
    center = resid - jnp.mean(resid, axis=-1, keepdims=True)
    rstd = lax.rsqrt(jnp.mean(center * center, axis=-1, keepdims=True) + eps)
    return (center * rstd, rstd)


def norm_backward(scaled, normed, rstd):
    inner = jnp.mean(scaled, axis=-1, keepdims=True)
    along = jnp.mean(scaled * normed, axis=-1, keepdims=True)
    return rstd * (scaled - inner - normed * along)


def gelu_parts(pre):
    cdf = 0.5 * (1.0 + lax.erf(pre * math.sqrt(0.5)))
    slope = cdf + pre * (jnp.exp(-0.5 * pre * pre) * (1.0 / math.sqrt(2.0 * math.pi)))
    return (pre * cdf, slope)


def attend_kernel(
    order, lens, mask, tokens, wq, wk, wv, wo, bq, bv, compact_out, q_out, k_out, v_out, p_out, ctx_out, part_out, table_out, count_out
):
    b = pl.program_id(0)
    length = mask.shape[-1]
    crop_len = lens[order[b]]
    lane = lax.broadcasted_iota(jnp.int32, (1, length), 1)
    kept = jnp.where(((mask[0] == 1) | (lane == 0)) & (lane < crop_len), 1.0, 0.0)
    rows = lax.broadcasted_iota(jnp.int32, (length, length), 0)
    cols = lax.broadcasted_iota(jnp.int32, (length, length), 1)
    upto = jnp.where(rows <= cols, 1.0, 0.0).astype(low)
    rank = dot(jnp.broadcast_to(kept, (8, length)).astype(low), upto)[0:1]
    place = jnp.where(kept > 0.0, rank - 1.0, -1.0)
    table = jnp.where(place == rows.astype(full), 1.0, 0.0).astype(low)
    count = jnp.sum(kept)

    @pl.when(b == 0)
    def _():
        table_out[...] = table
        count_out[...] = jnp.full(count_out.shape, count, full)

    compact = dot(table, tokens[0]).astype(low)
    compact_out[0] = compact
    query = (dot(compact, wq[...]) + bq[...]).astype(low)
    keys = dot(compact, wk[...]).astype(low)
    values = (dot(compact, wv[...]) + bv[...]).astype(low)
    q_out[0], k_out[0], v_out[0] = query, keys, values
    live = lane.astype(full) < count
    contexts = []
    for h in range(query.shape[1] // HEAD):
        span = slice(h * HEAD, (h + 1) * HEAD)
        scores = dot(query[:, span], keys[:, span], ((1,), (1,))) * (1.0 / math.sqrt(HEAD))
        scores = jnp.where(live, scores, -1e30)
        expo = jnp.exp(scores - jnp.max(scores, axis=1, keepdims=True))
        probs = (expo / jnp.sum(expo, axis=1, keepdims=True)).astype(low)
        p_out[0, h] = probs
        contexts.append(dot(probs, values[:, span]).astype(low))
    context = jnp.concatenate(contexts, axis=1)
    ctx_out[0] = context
    part_out[0] = dot(context, wo[...]).astype(low)


def attend(tokens, keep_mask, crop_len, order, wq, wk, wv, wo, bq, bv):
    seqs, length, width = tokens.shape
    mine = wq.shape[1]
    heads = mine // HEAD

    def const(shape):
        return pl.BlockSpec(shape, lambda b, *_: (0,) * len(shape))

    def per(*shape):
        return pl.BlockSpec((1, *shape), lambda b, *_: (b,) + (0,) * len(shape))

    def picked(*shape):
        return pl.BlockSpec((1, *shape), lambda b, order, lens: (order[b],) + (0,) * len(shape))

    S = jax.ShapeDtypeStruct
    return pl.pallas_call(
        attend_kernel,
        grid_spec=pltpu.PrefetchScalarGridSpec(
            num_scalar_prefetch=2,
            grid=(seqs,),
            in_specs=[
                picked(1, length),
                picked(length, width),
                const((width, mine)),
                const((width, mine)),
                const((width, mine)),
                const((mine, width)),
                const((1, mine)),
                const((1, mine)),
            ],
            out_specs=[
                per(length, width),
                per(length, mine),
                per(length, mine),
                per(length, mine),
                per(heads, length, length),
                per(length, mine),
                per(length, width),
                const((length, length)),
                const((8, LANES)),
            ],
        ),
        out_shape=[
            S((seqs, length, width), low),
            S((seqs, length, mine), low),
            S((seqs, length, mine), low),
            S((seqs, length, mine), low),
            S((seqs, heads, length, length), low),
            S((seqs, length, mine), low),
            S((seqs, length, width), low),
            S((length, length), low),
            S((8, LANES), full),
        ],
        name="attend",
    )(order, crop_len, keep_mask[:, None, :], tokens, wq, wk, wv, wo, bq[None], bv[None])


def attend_back_kernel(
    grads, compact, q_in, k_in, v_in, p_in, ctx_in, wq, wk, wv, wo, part_out, weight_out, qb_out, vb_out, weights, qb, vb
):
    b = pl.program_id(0)

    @pl.when(b == 0)
    def _():
        weights[...] = jnp.zeros_like(weights)
        qb[...] = jnp.zeros_like(qb)
        vb[...] = jnp.zeros_like(vb)

    scale = 1.0 / math.sqrt(HEAD)
    grad = grads[0]
    mine = wq.shape[1]
    query, keys, values = q_in[0], k_in[0], v_in[0]
    context_grad = dot(grad, wo[...], ((1,), (1,))).astype(low)
    query_grads, keys_grads, values_grads = [], [], []
    for h in range(mine // HEAD):
        span = slice(h * HEAD, (h + 1) * HEAD)
        probs = p_in[0, h]
        wide = probs.astype(full)
        probs_grad = dot(context_grad[:, span], values[:, span], ((1,), (1,)))
        inner = jnp.sum(wide * probs_grad, axis=1, keepdims=True)
        score_grad = (wide * (probs_grad - inner)).astype(low)
        query_grads.append((dot(score_grad, keys[:, span]) * scale).astype(low))
        keys_grads.append((dot(score_grad, query[:, span], ((0,), (0,))) * scale).astype(low))
        values_grads.append(dot(probs, context_grad[:, span], ((0,), (0,))).astype(low))
    query_grad = jnp.concatenate(query_grads, axis=1)
    keys_grad = jnp.concatenate(keys_grads, axis=1)
    values_grad = jnp.concatenate(values_grads, axis=1)
    every = jnp.concatenate([query_grad, keys_grad, values_grad], axis=1)
    weights[:, : 3 * mine] += dot(compact[0], every, ((0,), (0,)))
    weights[:, 3 * mine :] += dot(grad, ctx_in[0], ((0,), (0,)))
    qb[...] += jnp.sum(query_grad.astype(full), axis=0, keepdims=True)
    vb[...] += jnp.sum(values_grad.astype(full), axis=0, keepdims=True)
    back = dot(query_grad, wq[...], ((1,), (1,)))
    back += dot(keys_grad, wk[...], ((1,), (1,)))
    back += dot(values_grad, wv[...], ((1,), (1,)))
    part_out[0] = back.astype(low)

    @pl.when(b == pl.num_programs(0) - 1)
    def _():
        weight_out[...] = weights[...].astype(low)
        qb_out[...] = qb[...]
        vb_out[...] = vb[...]


def attend_back(grads, compact, query, keys, values, probs, context, wq, wk, wv, wo):
    seqs, length, width = grads.shape
    mine = wq.shape[1]
    heads = mine // HEAD

    def const(shape):
        return pl.BlockSpec(shape, lambda b: (0,) * len(shape))

    def per(*shape):
        return pl.BlockSpec((1, *shape), lambda b: (b,) + (0,) * len(shape))

    S = jax.ShapeDtypeStruct
    return pl.pallas_call(
        attend_back_kernel,
        grid=(seqs,),
        in_specs=[
            per(length, width),
            per(length, width),
            per(length, mine),
            per(length, mine),
            per(length, mine),
            per(heads, length, length),
            per(length, mine),
            const((width, mine)),
            const((width, mine)),
            const((width, mine)),
            const((mine, width)),
        ],
        out_specs=[
            per(length, width),
            const((width, 4 * mine)),
            const((1, mine)),
            const((1, mine)),
        ],
        out_shape=[
            S((seqs, length, width), low),
            S((width, 4 * mine), low),
            S((1, mine), full),
            S((1, mine), full),
        ],
        scratch_shapes=[
            pltpu.VMEM((width, 4 * mine), full),
            pltpu.VMEM((1, mine), full),
            pltpu.VMEM((1, mine), full),
        ],
        name="attend_back",
    )(grads, compact, query, keys, values, probs, context, wq, wk, wv, wo)


def contrast(pooled, key_queue):
    width = pooled.shape[1]
    queries = jnp.concatenate([pooled, swap(pooled, "fsdp", 1)])
    for stride in strides("dp"):
        queries = jnp.concatenate([queries, swap(queries, "dp", stride)])
    logits = dot(queries, key_queue, ((1,), (1,))) * inv_temp
    top = jnp.max(logits, axis=1, keepdims=True)
    expo = jnp.exp(logits - top)
    total = jnp.sum(expo, axis=1, keepdims=True)
    rows = dot(expo.astype(low), key_queue)
    state = jnp.concatenate([rows, jnp.broadcast_to(top, (top.shape[0], LANES)), jnp.broadcast_to(total, (top.shape[0], LANES))], axis=1)
    for axis, stride in [("dp", s) for s in reversed(strides("dp"))] + [("fsdp", 1)]:
        half = state.shape[0] // 2
        kept, other = state[:half], swap(state[half:], axis, stride)
        top = jnp.maximum(kept[:, width : width + 1], other[:, width : width + 1])
        summed = kept * jnp.exp(kept[:, width : width + 1] - top) + other * jnp.exp(other[:, width : width + 1] - top)
        state = jnp.concatenate([summed[:, :width], jnp.broadcast_to(top, (half, LANES)), summed[:, width + LANES :]], axis=1)
    return (state[:, width : width + 1], state[:, width + LANES : width + LANES + 1], state[:, :width])


def own_positive(pos_keys, pos_index, group, member):
    share = pos_keys.shape[0]
    everything = jnp.concatenate([pos_keys, swap(pos_keys, "fsdp", 1)])
    for stride in strides("dp"):
        everything = jnp.concatenate([everything, swap(everything, "dp", stride)])
    place = lax.dynamic_index_in_dim(pos_index, group * share + member, 0, keepdims=False)
    row = ((place // share) ^ group) * share + place % share
    return lax.dynamic_slice_in_dim(everything, row, 1, 0).astype(full)


def per_device(
    tokens,
    keep_mask,
    crop_len,
    pos_index,
    pos_keys,
    key_queue,
    query_weight,
    query_bias,
    key_weight,
    value_weight,
    value_bias,
    out_weight,
    out_bias,
    norm_gain,
    norm_shift,
    up_weight,
    up_bias,
    down_weight,
    down_bias,
    final_gain,
    final_shift,
):
    seqs, length, width = tokens.shape
    assert seqs == 4 and lax.axis_size("tensor") == 4 and lax.axis_size("fsdp") == 2
    member = lax.axis_index("tensor")
    group = lax.axis_index(("dp", "fsdp"))
    devices = seqs * lax.axis_size("dp") * lax.axis_size("fsdp")
    mine = query_weight.shape[1]
    hidden = up_weight.shape[1]
    order = (member ^ jnp.array(RELATIVE, jnp.int32)).astype(jnp.int32)

    positive = own_positive(pos_keys, pos_index, group, member)
    compact, query, keys, values, probs, context, partial_out, table, counts = attend(
        tokens, keep_mask, crop_len, order, query_weight, key_weight, value_weight, out_weight, query_bias, value_bias
    )
    count = counts[0:1, 0:1]
    live = (jnp.arange(length, dtype=jnp.int32)[:, None].astype(full) < count).astype(full)
    normed_one, rstd_one = norm_parts(compact[0].astype(full) + tensor_sum(partial_out) + out_bias)
    middle = normed_one * norm_gain + norm_shift
    middle_all = tensor_gather(middle.astype(low)).reshape(seqs * length, width)
    pre = dot(middle_all, up_weight) + up_bias
    hidden_state, slope = gelu_parts(pre)
    hidden_state = hidden_state.astype(low)
    partial_ffn = dot(hidden_state, down_weight).astype(low).reshape(seqs, length, width)
    normed_two, rstd_two = norm_parts(middle + tensor_sum(partial_ffn) + down_bias)
    output = (normed_two * final_gain + final_shift).astype(low)
    live_sum = jnp.sum(normed_two * live, axis=0, keepdims=True)
    pooled = (live_sum / count * final_gain + final_shift).astype(low)

    pos_logit = jnp.sum(pooled.astype(full) * positive, axis=1, keepdims=True) * inv_temp
    top, total, key_sum = contrast(pooled, key_queue)
    top_final = jnp.maximum(top, pos_logit)
    lse = top_final + jnp.log(total * jnp.exp(top - top_final) + jnp.exp(pos_logit - top_final))
    loss_part = lse - pos_logit
    step = loss_scale * inv_temp
    pooled_grad = key_sum * (step * jnp.exp(top - lse)) + step * (jnp.exp(pos_logit - lse) - 1.0) * positive

    result_row = pooled_grad / count
    two_grad = norm_backward(result_row * final_gain * live, normed_two, rstd_two)
    final_gain_part = result_row * live_sum
    ffn_grad = two_grad.astype(low)
    down_bias_part = jnp.sum(ffn_grad.astype(full), axis=0, keepdims=True)
    ffn_grads = tensor_gather(ffn_grad).reshape(seqs * length, width)
    pre_grad = (slope * dot(ffn_grads, down_weight, ((1,), (1,)))).astype(low)
    back_part = dot(pre_grad, up_weight, ((1,), (1,))).astype(low).reshape(seqs, length, width)
    middle_grad = two_grad + tensor_sum(back_part)
    one_grad = norm_backward(middle_grad * norm_gain, normed_one, rstd_one)
    attn_grad = one_grad.astype(low)
    attn_grads = tensor_gather(attn_grad)
    down_weight_grad = group_sum(dot(hidden_state, ffn_grads, ((0,), (0,))).astype(low))
    up_weight_grad = group_sum(dot(middle_all, pre_grad, ((0,), (0,))).astype(low))
    up_bias_part = jnp.sum(pre_grad.astype(full), axis=0, keepdims=True)
    norm_gain_part = jnp.sum(middle_grad * normed_one, axis=0, keepdims=True)
    norm_shift_part = jnp.sum(middle_grad, axis=0, keepdims=True)
    out_bias_part = jnp.sum(attn_grad.astype(full), axis=0, keepdims=True)

    partial_in, attn_weight_grad, query_bias_part, value_bias_part = attend_back(
        attn_grads, compact, query, keys, values, probs, context, query_weight, key_weight, value_weight, out_weight
    )
    attn_weight_grad = group_sum(attn_weight_grad).astype(full)
    compact_grad = (one_grad + tensor_sum(partial_in)).astype(low)
    input_grad = dot(table, compact_grad, ((0,), (0,))).astype(low)

    vectors = jnp.concatenate(
        [
            final_gain_part,
            pooled_grad,
            norm_gain_part,
            norm_shift_part,
            down_bias_part,
            out_bias_part,
            jnp.broadcast_to(loss_part / devices, (1, width)),
        ]
    )
    vectors = lax.optimization_barrier(vectors)
    for stride in (1, 2):
        vectors = vectors + swap(vectors, "tensor", stride)
    pad = jnp.zeros((1, width - 2 * mine), full)
    narrow = jnp.concatenate([query_bias_part, value_bias_part, pad], axis=1)
    vectors = jnp.concatenate([vectors, narrow, up_bias_part.reshape(-1, width)])
    vectors = vectors + swap(vectors, "fsdp", 1)
    for stride in strides("dp"):
        vectors = vectors + swap(vectors, "dp", stride)
    return (
        output[None],
        input_grad[None],
        attn_weight_grad[:, :mine],
        vectors[7, :mine],
        attn_weight_grad[:, mine : 2 * mine],
        attn_weight_grad[:, 2 * mine : 3 * mine],
        vectors[7, mine : 2 * mine],
        attn_weight_grad[:, 3 * mine :].T,
        vectors[5],
        vectors[2],
        vectors[3],
        up_weight_grad.astype(full),
        vectors[8:].reshape(-1),
        down_weight_grad.astype(full),
        vectors[4],
        vectors[0],
        vectors[1],
        vectors[6, 0],
    )


def solution(mesh):
    placed = (
        P(("dp", "fsdp"), None, None),
        P(("dp", "fsdp"), None),
        P(("dp", "fsdp")),
        P(),
        P(("dp", "fsdp"), None),
        P(("dp", "fsdp"), None),
        P(None, "tensor"),
        P("tensor"),
        P(None, "tensor"),
        P(None, "tensor"),
        P("tensor"),
        P("tensor", None),
        P(),
        P(),
        P(),
        P(None, "tensor"),
        P("tensor"),
        P("tensor", None),
        P(),
        P(),
        P(),
    )
    return jax.shard_map(
        per_device,
        mesh=mesh,
        in_specs=placed,
        out_specs=(
            P(("dp", "fsdp", "tensor"), None, None),
            P(("dp", "fsdp", "tensor"), None, None),
            P(None, "tensor"),
            P("tensor"),
            P(None, "tensor"),
            P(None, "tensor"),
            P("tensor"),
            P("tensor", None),
            P(),
            P(),
            P(),
            P(None, "tensor"),
            P("tensor"),
            P("tensor", None),
            P(),
            P(),
            P(),
            P(),
        ),
        check_vma=False,
    )
```

time: 748 us -> 265 us (0.35)
  waiting for transfers between devices: 404 us -> 111 us
  blocking collectives: 149 us -> 0 us
  matrix products: 76.4 us -> 16.7 us
  starting transfers between devices: 0.59 us -> 51.3 us
  other arithmetic: 53.2 us -> 25.5 us
  Pallas kernels: 0 us -> 24.7 us
  local copies, waits for them, and re-layouts: 45.7 us -> 26.7 us
  between operations: 17.5 us -> 8.38 us
    psum x1 -> x0, waiting for transfers between devices: 199 us -> none  [per_device(): lax.psum((query_weight_grad, query_bias_grad, key_weight_grad, value_weig...]
    ppermute x0 -> x43, waiting for transfers between devices: none -> 111 us  [the longest x34 97.7 us: swap(): return lax.ppermute(array, axis, [(i, i ^ stride) for i in range(size)])]
    reduce_scatter x4 -> x0, waiting for transfers between devices: 78.7 us -> none  [the longest x1 40.7 us: per_device(): lax.psum_scatter(partial_out, 'tensor', scatter_dimension=0, tiled=True)]
    all_gather x2 -> x0, blocking collectives: 78.1 us -> none  [the longest x1 41.2 us: per_device(): lax.all_gather(mine(pos_keys), ('dp', 'fsdp', 'tensor'), axis=0, tiled=True)]
    unnamed x10 -> x0, waiting for transfers between devices: 68 us -> none
    dot_general x36 -> x9, matrix products: 76.4 us -> 16.7 us  [dot(): return lax.dot_general(a, b, (dims, ((), ())), preferred_element_type=full)]
    all_gather x3 -> x0, waiting for transfers between devices: 58.3 us -> none  [the longest x1 19.7 us: per_device(): lax.all_gather(middle.astype(jnp.bfloat16), 'tensor', axis=0, tiled=True)]
    ppermute x0 -> x43, starting transfers between devices: none -> 51.3 us  [the longest x34 34.6 us: swap(): return lax.ppermute(array, axis, [(i, i ^ stride) for i in range(size)])]
  transfers between devices with their start and end apart: 9 -> 43, of which waited for: 7 -> 28; matrix products, arithmetic and copies ran while one was open for 5% -> 12% of each run, Pallas kernels for 0% -> 5%
where the time goes in v1:
time: 265 us
  waiting for transfers between devices  111 us (42%)
  starting transfers between devices  51.3 us (19%)
  local copies, waits for them, and re-layouts  26.7 us (10%)
  other arithmetic  25.5 us (10%)
  Pallas kernels  24.7 us (9%)
  matrix products  16.7 us (6%)
  between operations  8.38 us (3%)
    ppermute x34, waiting for transfers between devices, swap(): return lax.ppermute(array, axis, [(i, i ^ stride) for i in range(size)])  97.7 us
    ppermute x34, starting transfers between devices, swap(): return lax.ppermute(array, axis, [(i, i ^ stride) for i in range(size)])  34.6 us
    dot_general x9, matrix products, dot(): return lax.dot_general(a, b, (dims, ((), ())), preferred_element_type=full)  16.7 us
    pallas_call x1, Pallas kernels, attend_back(): pl.pallas_call(attend_back_kernel, grid=(seqs,), in_specs=[per(length, wi...  13.4 us
    unnamed x81, local copies, waits for them, and re-layouts  13.3 us
    pallas_call x1, Pallas kernels, attend(): pl.pallas_call(attend_kernel, grid_spec=pltpu.PrefetchScalarGridSpec(num_...  11.3 us
    ppermute x3, waiting for transfers between devices, group_sum(): outer = lax.ppermute(total, 'dp', [(1, 0), (2, 3)])  10.2 us
    ppermute x3, starting transfers between devices, group_sum(): lax.ppermute(part.astype(low), 'dp', [(0, 1), (3, 2)]).astype(full)  9.51 us
  transfers between devices with their start and end apart: 43, of which 28 were waited for; matrix products, arithmetic and copies ran while one was open for 12% of the time, Pallas kernels for 5%

profile of v1, /device:TPU:0, one launch (start us, length us, event | category | flops | bytes accessed | tf_op | source)
XLA Modules:
  0.0 264.6 jit_solution(17504820057976350994)
XLA Ops:
  0.7 1.5 broadcast_in_dim.44.mask
  2.2 1.9 copy.52.wq
  4.0 1.9 copy.53.wk
  7.3 11.3 %attend.1 = (bf16[4,256,768]{2,1,0:T(8,128)(2,1)}, bf16[4,256,192]{2,1,0:T(8,128)(2,1)}, bf16[4,256,192]{2,1,0:T(8,128)(2,1)}, bf16[4,256,192]{2,1,0:T(8,128)(2,...) custom-call(s32[4]{0:T(128)} %broadcast_xor_fusion.order, ...), custom_call_target="tpu_custom_call" | custom-call | tf_op jit(solution)/shard_map/attend/pallas_call | solution.py:144
  18.7 1.3 slice.194
  20.5 1.9 collective-permute-done
  22.6 2.9 %collective-permute-start.1 = (bf16[256,768]{1,0:T(8,128)(2,1)S(1)}, bf16[256,768]{1,0:T(8,128)(2,1)S(1)}, u32[]{:S(2)}, u32[]{:S(2)}) collective-permute-start(bf16[256,768]{1,0:T(8,128)(2,1)S(1)} %fusion.25), channel_id=1, source_target_pairs={{0,2},{1,3},{2,0},{3,1},{4,6},{5,7},{6,4},{7,5},{8,10},{9,11},{10,... | collective-permute-start | bytes 1179656 | tf_op jit(solution)/shard_map/ppermute | solution.py:27
  25.5 9.4 %collective-permute-done.1 = bf16[256,768]{1,0:T(8,128)(2,1)S(1)} collective-permute-done((bf16[256,768]{1,0:T(8,128)(2,1)S(1)}, bf16[256,768]{1,0:T(8,128)(2,1)S(1)}, u32[]{:S(2)}, u32[]{:S(2)}) %collective-permute-start.1) | collective-permute-done | bytes 393248 | tf_op jit(solution)/shard_map/ppermute | solution.py:27
  34.9 1.3 fusion.60
  36.7 1.8 collective-permute-start.2
  38.7 8.6 %collective-permute-done.2 = bf16[256,768]{1,0:T(8,128)(2,1)S(1)} collective-permute-done((bf16[256,768]{1,0:T(8,128)(2,1)S(1)}, bf16[256,768]{1,0:T(8,128)(2,1)S(1)}, u32[]{:S(2)}, u32[]{:S(2)}) %collective-permute-start.2) | collective-permute-done | bytes 393248 | tf_op jit(solution)/shard_map/ppermute | solution.py:27
  47.6 2.3 collective-permute-done.3
  50.0 3.3 %multiply_convert_fusion = (bf16[1024,768]{1,0:T(8,128)(2,1)S(1)}, f32[1024,768]{1,0:T(8,128)}) fusion(f32[768]{0:T(1024)S(1)} %copy-done.30, bf16[1024,768]{1,0:T(8,128)(2,1)S(1)} %bitcast.93, bf16[768,768]{1,0:T(8,128)(2,1)S(1)} %copy-done.28), kind=kOutput, calls=%fused_computation.8 | convolution fusion | flops 1212678144 | bytes 7474176 | tf_op jit(solution)/shard_map/dot_general | solution.py:22
  53.4 1.4 convolution_convert_fusion.1
  55.0 2.1 collective-permute-done.4
  57.3 1.5 collective-permute-start.5
  60.7 7.8 %collective-permute-done.5 = bf16[256,768]{1,0:T(8,128)(2,1)S(1)} collective-permute-done((bf16[256,768]{1,0:T(8,128)(2,1)S(1)}, bf16[256,768]{1,0:T(8,128)(2,1)S(1)}, u32[]{:S(2)}, u32[]{:S(2)}) %collective-permute-start.5) | collective-permute-done | bytes 393248 | tf_op jit(solution)/shard_map/ppermute | solution.py:27
  70.7 1.5 collective-permute-start.6
  72.2 2.2 collective-permute-done.6
  74.4 1.6 collective-permute-start.7
  76.0 1.5 collective-permute-start.12
  80.7 2.7 %collective-permute-start.8 = (bf16[4,768]{1,0:T(4,128)(2,1)S(1)}, bf16[4,768]{1,0:T(4,128)(2,1)S(1)}, u32[]{:S(2)}, u32[]{:S(2)}) collective-permute-start(bf16[4,768]{1,0:T(4,128)(2,1)S(1)} %pad_maximum_fusion.12), channel_id=1, source_target_pairs={{0,16},{8,24},{16,0},{24,8},{1,17},{9,25},{17,1},{25,9},{2,18},{10... | collective-permute-start | bytes 18440 | tf_op jit(solution)/shard_map/ppermute | solution.py:27
  83.9 1.4 collective-permute-done.8
  87.3 2.7 %collective-permute-start.9 = (f32[4,1024]{1,0:T(4,128)S(1)}, f32[4,1024]{1,0:T(4,128)S(1)}, u32[]{:S(2)}, u32[]{:S(2)}) collective-permute-start(f32[4,1024]{1,0:T(4,128)S(1)} %slice.256), channel_id=1, source_target_pairs={{0,16},{8,24},{16,0},{24,8},{1,17},{9,25},{17,1},{25,9},{2,18},{10... | collective-permute-start | bytes 49160 | tf_op jit(solution)/shard_map/ppermute | solution.py:27
  90.1 2.2 collective-permute-done.9
  92.9 2.6 collective-permute-start.14
  105.6 1.5 multiply_reduce_fusion
  107.4 1.6 collective-permute-start.15
  109.0 6.3 %collective-permute-done.15 = bf16[256,768]{1,0:T(8,128)(2,1)S(1)} collective-permute-done((bf16[256,768]{1,0:T(8,128)(2,1)S(1)}, bf16[256,768]{1,0:T(8,128)(2,1)S(1)}, u32[]{:S(2)}, u32[]{:S(2)}) %collective-permute-start.15) | collective-permute-done | bytes 393248 | tf_op jit(solution)/shard_map/ppermute | solution.py:27
  115.4 2.3 collective-permute-done.16
  117.9 3.0 %convert_reduce_fusion = (f32[768]{0:T(1024)S(1)}, bf16[1024,768]{1,0:T(8,128)(2,1)S(1)}) fusion(bf16[1024,768]{1,0:T(8,128)(2,1)S(1)} %bitcast.95, bf16[768,768]{1,0:T(8,128)(2,1)S(1)} %copy-done.27, f32[1024,768]{1,0:T(8,128)S(1)} %copy-done.36, f32[768]{0:T(1024)S(1)} %copy-done.30), kind=kOutput, calls=%fused_computation.7 | convolution fusion | flops 1218182400 | bytes 7477248 | tf_op jit(solution)/shard_map/dot_general | solution.py:22
  120.9 1.4 convolution_convert_fusion
  123.6 2.4 collective-permute-done.17
  126.0 1.6 collective-permute-start.18
  127.6 3.3 %convolution_convert_fusion.2 = bf16[768,768]{1,0:T(8,128)(2,1)S(1)} fusion(bf16[1024,768]{1,0:T(8,128)(2,1)} %copy-done.33, bf16[1024,768]{1,0:T(8,128)(2,1)} %bitcast.96), kind=kOutput, calls=%fused_computation.16 | convolution fusion | flops 1208549376 | bytes 4325376 | tf_op jit(solution)/shard_map/dot_general | solution.py:22
  131.6 5.6 %collective-permute-done.18 = bf16[256,768]{1,0:T(8,128)(2,1)S(1)} collective-permute-done((bf16[256,768]{1,0:T(8,128)(2,1)S(1)}, bf16[256,768]{1,0:T(8,128)(2,1)S(1)}, u32[]{:S(2)}, u32[]{:S(2)}) %collective-permute-start.18) | collective-permute-done | bytes 393248 | tf_op jit(solution)/shard_map/ppermute | solution.py:27
  137.3 2.7 %multiply_reduce_fusion.1 = (f32[768]{0:T(1024)S(1)}, f32[256]{0:T(256)S(1)}, f32[256]{0:T(256)S(1)}, f32[768]{0:T(1024)S(1)}, f32[256,768]{1,0:T(8,128)S(1)}, /*index=5*/bf16[1,256,768]{2,1,0:T(8,128)(2,1)}) fusion(f32[256,768]{1,0:T(8,128)S(1)} %copy-done.3, f32[256]{0:T(256)S(1)} %add_rsqrt_fusion.1, f32[256]{0:T(256)S(1)} %broadcast_multiply_fusion.5, ...), kind=kLoop, calls=%fused_computation.64 | loop fusion | flops 4913152 | bytes 3959808 | tf_op jit(solution)/shard_map/reduce_sum | solution.py:385
  140.3 1.6 collective-permute-start.19
  141.9 1.5 convolution_convert_fusion.3
  144.0 3.2 %collective-permute-done.38 = bf16[384,768]{1,0:T(8,128)(2,1)S(1)} collective-permute-done((bf16[384,768]{1,0:T(8,128)(2,1)S(1)}, bf16[384,768]{1,0:T(8,128)(2,1)S(1)}, u32[]{:S(2)}, u32[]{:S(2)}) %collective-permute-start.38) | collective-permute-done | bytes 589856 | tf_op jit(solution)/shard_map/ppermute | solution.py:27
  147.4 2.9 %collective-permute-start.39 = (bf16[384,768]{1,0:T(8,128)(2,1)S(1)}, bf16[384,768]{1,0:T(8,128)(2,1)S(1)}, u32[]{:S(2)}, u32[]{:S(2)}) collective-permute-start(bf16[384,768]{1,0:T(8,128)(2,1)S(1)} %fusion.9), channel_id=1, source_target_pairs={{0,8},{24,16},{1,9},{25,17},{2,10},{26,18},{3,11},{27,19},{4,12},{... | collective-permute-start | bytes 1769480 | tf_op jit(solution)/shard_map/ppermute | solution.py:55
  150.8 8.0 %collective-permute-done.33 = bf16[384,768]{1,0:T(8,128)(2,1)S(1)} collective-permute-done((bf16[384,768]{1,0:T(8,128)(2,1)S(1)}, bf16[384,768]{1,0:T(8,128)(2,1)S(1)}, u32[]{:S(2)}, u32[]{:S(2)}) %collective-permute-start.33) | collective-permute-done | bytes 589856 | tf_op jit(solution)/shard_map/ppermute | solution.py:27
  159.8 3.7 %collective-permute-start.34 = (bf16[384,768]{1,0:T(8,128)(2,1)}, bf16[384,768]{1,0:T(8,128)(2,1)}, u32[]{:S(2)}, u32[]{:S(2)}) collective-permute-start(bf16[384,768]{1,0:T(8,128)(2,1)} %fusion.8), channel_id=1, source_target_pairs={{0,8},{24,16},{1,9},{25,17},{2,10},{26,18},{3,11},{27,19},{4,12},{... | collective-permute-start | bytes 1769480 | tf_op jit(solution)/shard_map/ppermute | solution.py:55
  164.6 1.5 collective-permute-start.40
  167.4 13.4 %attend_back.1 = (bf16[4,256,768]{2,1,0:T(8,128)(2,1)}, bf16[768,768]{1,0:T(8,128)(2,1)}, f32[1,192]{1,0:T(1,128)}, f32[1,192]{1,0:T(1,128)}) custom-call(bf16[4,256,768]{2,1,0:T(8,128)(2,1)} %pad_maximum_fusion.2.grads, bf16[4,256,768]{2,1,0:T(8,128)(2,1)} %get-tuple-element.31.compact, bf16[4,256,192]{2,1,0:T(8,128)(2,1)} %get-tuple-element.35.q_in, ...), custom_call_target="tpu_custom_call" | custom-call | tf_op jit(solution)/shard_map/attend_back/pallas_call | solution.py:245
  180.8 1.9 constant_dynamic-slice_fusion.2
  185.3 1.5 add_convert_fusion.3
  188.5 1.4 add_convert_fusion
  191.2 5.8 %collective-permute-done.23 = bf16[384,768]{1,0:T(8,128)(2,1)} collective-permute-done((bf16[384,768]{1,0:T(8,128)(2,1)}, bf16[384,768]{1,0:T(8,128)(2,1)}, u32[]{:S(2)}, u32[]{:S(2)}) %collective-permute-start.23) | collective-permute-done | bytes 589856 | tf_op jit(solution)/shard_map/ppermute | solution.py:27
  198.2 2.9 %collective-permute-start.24 = (bf16[384,768]{1,0:T(8,128)(2,1)S(1)}, bf16[384,768]{1,0:T(8,128)(2,1)S(1)}, u32[]{:S(2)}, u32[]{:S(2)}) collective-permute-start(bf16[384,768]{1,0:T(8,128)(2,1)S(1)} %fusion.7), channel_id=1, source_target_pairs={{0,8},{24,16},{1,9},{25,17},{2,10},{26,18},{3,11},{27,19},{4,12},{... | collective-permute-start | bytes 1769480 | tf_op jit(solution)/shard_map/ppermute | solution.py:55
  203.2 2.1 collective-permute-done.30
  205.4 2.2 collective-permute-start.31
  207.6 3.4 %collective-permute-done.24 = bf16[384,768]{1,0:T(8,128)(2,1)S(1)} collective-permute-done((bf16[384,768]{1,0:T(8,128)(2,1)S(1)}, bf16[384,768]{1,0:T(8,128)(2,1)S(1)}, u32[]{:S(2)}, u32[]{:S(2)}) %collective-permute-start.24) | collective-permute-done | bytes 589856 | tf_op jit(solution)/shard_map/ppermute | solution.py:55
  214.0 7.0 %collective-permute-done.31 = f32[9,768]{1,0:T(8,128)S(1)} collective-permute-done((f32[9,768]{1,0:T(8,128)S(1)}, f32[9,768]{1,0:T(8,128)S(1)}, u32[]{:S(2)}, u32[]{:S(2)}) %collective-permute-start.31) | collective-permute-done | bytes 27680 | tf_op jit(solution)/shard_map/ppermute | solution.py:27
  221.5 1.6 collective-permute-start.37
  223.2 7.3 %collective-permute-done.32 = f32[9,768]{1,0:T(8,128)S(1)} collective-permute-done((f32[9,768]{1,0:T(8,128)S(1)}, f32[9,768]{1,0:T(8,128)S(1)}, u32[]{:S(2)}, u32[]{:S(2)}) %collective-permute-start.32) | collective-permute-done | bytes 27680 | tf_op jit(solution)/shard_map/ppermute | solution.py:27
  234.1 10.2 %collective-permute-done.26 = bf16[384,768]{1,0:T(8,128)(2,1)S(1)} collective-permute-done((bf16[384,768]{1,0:T(8,128)(2,1)S(1)}, bf16[384,768]{1,0:T(8,128)(2,1)S(1)}, u32[]{:S(2)}, u32[]{:S(2)}) %collective-permute-start.26) | collective-permute-done | bytes 589856 | tf_op jit(solution)/shard_map/ppermute | solution.py:59
  245.0 1.6 maximum_convert_fusion.1
  246.6 1.6 maximum_convert_fusion.2
  249.4 5.3 %collective-permute-done.27 = bf16[384,768]{1,0:T(8,128)(2,1)S(1)} collective-permute-done((bf16[384,768]{1,0:T(8,128)(2,1)S(1)}, bf16[384,768]{1,0:T(8,128)(2,1)S(1)}, u32[]{:S(2)}, u32[]{:S(2)}) %collective-permute-start.27) | collective-permute-done | bytes 589856 | tf_op jit(solution)/shard_map/ppermute | solution.py:27
  254.9 1.9 slice_bitcast_fusion
  257.8 2.3 copy.62
  260.2 2.2 copy.61
  262.4 2.2 copy.60
  (224 shorter events, 43.9 us)
Async XLA Ops:
  0.7 84.7 %copy-start = (bf16[2048,768]{1,0:T(8,128)(2,1)S(1)}, bf16[2048,768]{1,0:T(8,128)(2,1)}, u32[]{:S(2)}) copy-start(bf16[2048,768]{1,0:T(8,128)(2,1)} %param.27) | copy-start | bytes 9437188
  0.7 6.2 %copy-start.32 = (s32[4]{0:T(128)S(1)}, s32[4]{0:T(128)}, u32[]{:S(2)}) copy-start(s32[4]{0:T(128)} %constant.93.clone) | copy-start | bytes 52
  0.7 5.2 %copy-start.15 = (bf16[768,192]{0,1:T(8,128)(2,1)S(1)}, bf16[768,192]{0,1:T(8,128)(2,1)}, u32[]{:S(2)}) copy-start(bf16[768,192]{0,1:T(8,128)(2,1)} %param.31) | copy-start | bytes 884740
  18.7 16.3 %copy-start.22 = (f32[768]{0:T(1024)S(1)}, f32[768]{0:T(1024)}, u32[]{:S(2)}) copy-start(f32[768]{0:T(1024)} %param.34) | copy-start | bytes 9220
  20.0 2.5 collective-permute-start
  22.6 12.4 %collective-permute-start.1 = (bf16[256,768]{1,0:T(8,128)(2,1)S(1)}, bf16[256,768]{1,0:T(8,128)(2,1)S(1)}, u32[]{:S(2)}, u32[]{:S(2)}) collective-permute-start(bf16[256,768]{1,0:T(8,128)(2,1)S(1)} %fusion.25), channel_id=1, source_target_pairs={{0,2},{1,3},{2,0},{3,1},{4,6},{5,7},{6,4},{7,5},{8,10},{9,11},{10,... | collective-permute-start | bytes 1179656 | tf_op jit(solution)/shard_map/ppermute | solution.py:27
  36.3 32.3 %copy-start.2 = (f32[256,768]{1,0:T(8,128)}, f32[256,768]{1,0:T(8,128)S(1)}, u32[]{:S(2)}) copy-start(f32[256,768]{1,0:T(8,128)S(1)} %get-tuple-element.115) | copy-start | bytes 2359300
  36.7 10.6 %collective-permute-start.2 = (bf16[256,768]{1,0:T(8,128)(2,1)S(1)}, bf16[256,768]{1,0:T(8,128)(2,1)S(1)}, u32[]{:S(2)}, u32[]{:S(2)}) collective-permute-start(bf16[256,768]{1,0:T(8,128)(2,1)S(1)} %fusion.23), channel_id=1, source_target_pairs={{0,2},{1,3},{2,0},{3,1},{4,6},{5,7},{6,4},{7,5},{8,10},{9,11},{10,... | collective-permute-start | bytes 1179656 | tf_op jit(solution)/shard_map/ppermute | solution.py:27
  47.5 2.4 collective-permute-start.3
  54.8 13.8 %copy-start.23 = (f32[768]{0:T(1024)S(1)}, f32[768]{0:T(1024)}, u32[]{:S(2)}) copy-start(f32[768]{0:T(1024)} %param.40) | copy-start | bytes 9220
  54.8 2.4 collective-permute-start.4
  57.3 11.2 %collective-permute-start.5 = (bf16[256,768]{1,0:T(8,128)(2,1)S(1)}, bf16[256,768]{1,0:T(8,128)(2,1)S(1)}, u32[]{:S(2)}, u32[]{:S(2)}) collective-permute-start(bf16[256,768]{1,0:T(8,128)(2,1)S(1)} %fusion.16), channel_id=1, source_target_pairs={{0,2},{1,3},{2,0},{3,1},{4,6},{5,7},{6,4},{7,5},{8,10},{9,11},{10,... | collective-permute-start | bytes 1179656 | tf_op jit(solution)/shard_map/ppermute | solution.py:27
  60.7 9.4 %copy-start.20 = (f32[768]{0:T(1024)S(1)}, f32[768]{0:T(1024)}, u32[]{:S(2)}) copy-start(f32[768]{0:T(1024)} %param.41) | copy-start | bytes 9220
  60.7 9.4 %copy-start.21 = (f32[768]{0:T(1024)S(1)}, f32[768]{0:T(1024)}, u32[]{:S(2)}) copy-start(f32[768]{0:T(1024)} %param.42) | copy-start | bytes 9220
  60.7 15.3 %copy-start.18 = (bf16[4,768]{1,0:T(4,128)(2,1)S(1)}, bf16[4,768]{1,0:T(4,128)(2,1)}, u32[]{:S(2)}) copy-start(bf16[4,768]{1,0:T(4,128)(2,1)} %param.26) | copy-start | bytes 18436
  60.7 16.8 %copy-start.31 = (s32[32]{0:T(128)S(1)}, s32[32]{0:T(128)}, u32[]{:S(2)}) copy-start(s32[32]{0:T(128)} %param.25) | copy-start | bytes 388
  70.7 3.7 %collective-permute-start.6 = (bf16[1,768]{1,0:T(2,128)(2,1)S(1)}, bf16[1,768]{1,0:T(2,128)(2,1)S(1)}, u32[]{:S(2)}, u32[]{:S(2)}) collective-permute-start(bf16[1,768]{1,0:T(2,128)(2,1)S(1)} %convert_element_type.286), channel_id=1, source_target_pairs={{0,4},{4,0},{1,5},{5,1},{2,6},{6,2},{3,7},{7,3},{8,12},{12,8},{9,1... | collective-permute-start | bytes 4616 | tf_op jit(solution)/shard_map/ppermute | solution.py:27
  74.4 6.3 %collective-permute-start.7 = (bf16[2,768]{1,0:T(2,128)(2,1)S(1)}, bf16[2,768]{1,0:T(2,128)(2,1)S(1)}, u32[]{:S(2)}, u32[]{:S(2)}) collective-permute-start(bf16[2,768]{1,0:T(2,128)(2,1)S(1)} %pad_maximum_fusion.13), channel_id=1, source_target_pairs={{0,8},{8,0},{16,24},{24,16},{1,9},{9,1},{17,25},{25,17},{2,10},{10... | collective-permute-start | bytes 9224 | tf_op jit(solution)/shard_map/ppermute | solution.py:27
  76.0 7.4 %collective-permute-start.12 = (bf16[4,768]{1,0:T(4,128)(2,1)S(1)}, bf16[4,768]{1,0:T(4,128)(2,1)S(1)}, u32[]{:S(2)}, u32[]{:S(2)}) collective-permute-start(bf16[4,768]{1,0:T(4,128)(2,1)S(1)} %copy-done.18), channel_id=1, source_target_pairs={{0,4},{4,0},{1,5},{5,1},{2,6},{6,2},{3,7},{7,3},{8,12},{12,8},{9,1... | collective-permute-start | bytes 18440 | tf_op jit(solution)/shard_map/ppermute | solution.py:27
  80.7 4.6 %collective-permute-start.8 = (bf16[4,768]{1,0:T(4,128)(2,1)S(1)}, bf16[4,768]{1,0:T(4,128)(2,1)S(1)}, u32[]{:S(2)}, u32[]{:S(2)}) collective-permute-start(bf16[4,768]{1,0:T(4,128)(2,1)S(1)} %pad_maximum_fusion.12), channel_id=1, source_target_pairs={{0,16},{8,24},{16,0},{24,8},{1,17},{9,25},{17,1},{25,9},{2,18},{10... | collective-permute-start | bytes 18440 | tf_op jit(solution)/shard_map/ppermute | solution.py:27
  83.4 9.5 %collective-permute-start.13 = (bf16[8,768]{1,0:T(8,128)(2,1)S(1)}, bf16[8,768]{1,0:T(8,128)(2,1)S(1)}, u32[]{:S(2)}, u32[]{:S(2)}) collective-permute-start(bf16[8,768]{1,0:T(8,128)(2,1)S(1)} %pad_maximum_fusion.10), channel_id=1, source_target_pairs={{0,8},{8,0},{16,24},{24,16},{1,9},{9,1},{17,25},{25,17},{2,10},{10... | collective-permute-start | bytes 36872 | tf_op jit(solution)/shard_map/ppermute | solution.py:27
  87.2 19.9 %copy-start.5 = (f32[256,768]{1,0:T(8,128)S(1)}, f32[256,768]{1,0:T(8,128)}, u32[]{:S(2)}) copy-start(f32[256,768]{1,0:T(8,128)} %copy-done.4) | copy-start | bytes 2359300
  87.3 4.9 %collective-permute-start.9 = (f32[4,1024]{1,0:T(4,128)S(1)}, f32[4,1024]{1,0:T(4,128)S(1)}, u32[]{:S(2)}, u32[]{:S(2)}) collective-permute-start(f32[4,1024]{1,0:T(4,128)S(1)} %slice.256), channel_id=1, source_target_pairs={{0,16},{8,24},{16,0},{24,8},{1,17},{9,25},{17,1},{25,9},{2,18},{10... | collective-permute-start | bytes 49160 | tf_op jit(solution)/shard_map/ppermute | solution.py:27
  92.6 3.7 %collective-permute-start.10 = (f32[2,1024]{1,0:T(2,128)S(1)}, f32[2,1024]{1,0:T(2,128)S(1)}, u32[]{:S(2)}, u32[]{:S(2)}) collective-permute-start(f32[2,1024]{1,0:T(2,128)S(1)} %slice.261), channel_id=1, source_target_pairs={{0,8},{8,0},{16,24},{24,16},{1,9},{9,1},{17,25},{25,17},{2,10},{10... | collective-permute-start | bytes 24584 | tf_op jit(solution)/shard_map/ppermute | solution.py:27
  92.9 4.8 %collective-permute-start.14 = (bf16[16,768]{1,0:T(8,128)(2,1)S(1)}, bf16[16,768]{1,0:T(8,128)(2,1)S(1)}, u32[]{:S(2)}, u32[]{:S(2)}) collective-permute-start(bf16[16,768]{1,0:T(8,128)(2,1)S(1)} %pad_maximum_fusion.8), channel_id=1, source_target_pairs={{0,16},{8,24},{16,0},{24,8},{1,17},{9,25},{17,1},{25,9},{2,18},{10... | collective-permute-start | bytes 73736 | tf_op jit(solution)/shard_map/ppermute | solution.py:27
  96.6 3.7 %collective-permute-start.11 = (f32[1,1024]{1,0:T(1,128)S(1)}, f32[1,1024]{1,0:T(1,128)S(1)}, u32[]{:S(2)}, u32[]{:S(2)}) collective-permute-start(f32[1,1024]{1,0:T(1,128)S(1)} %slice.266), channel_id=1, source_target_pairs={{0,4},{4,0},{1,5},{5,1},{2,6},{6,2},{3,7},{7,3},{8,12},{12,8},{9,1... | collective-permute-start | bytes 12296 | tf_op jit(solution)/shard_map/ppermute | solution.py:27
  107.4 7.8 %collective-permute-start.15 = (bf16[256,768]{1,0:T(8,128)(2,1)S(1)}, bf16[256,768]{1,0:T(8,128)(2,1)S(1)}, u32[]{:S(2)}, u32[]{:S(2)}) collective-permute-start(bf16[256,768]{1,0:T(8,128)(2,1)S(1)} %get-tuple-element.103), channel_id=1, source_target_pairs={{0,2},{1,3},{2,0},{3,1},{4,6},{5,7},{6,4},{7,5},{8,10},{9,11},{10,... | collective-permute-start | bytes 1179656 | tf_op jit(solution)/shard_map/ppermute | solution.py:27
  115.3 2.4 collective-permute-start.16
  122.3 5.3 %copy-start.11 = (bf16[1024,768]{1,0:T(8,128)(2,1)}, bf16[1024,768]{1,0:T(8,128)(2,1)S(1)}, u32[]{:S(2)}) copy-start(bf16[1024,768]{1,0:T(8,128)(2,1)S(1)} %convolution_convert_fusion) | copy-start | bytes 4718596
  123.4 2.5 collective-permute-start.17
  125.9 5.0 %copy-start.14 = (bf16[2,256,768]{2,1,0:T(8,128)(2,1)}, bf16[2,256,768]{2,1,0:T(8,128)(2,1)S(1)}, u32[]{:S(2)}) copy-start(bf16[2,256,768]{2,1,0:T(8,128)(2,1)S(1)} %collective-permute-done.17) | copy-start | bytes 2359300
  126.0 11.2 %collective-permute-start.18 = (bf16[256,768]{1,0:T(8,128)(2,1)S(1)}, bf16[256,768]{1,0:T(8,128)(2,1)S(1)}, u32[]{:S(2)}, u32[]{:S(2)}) collective-permute-start(bf16[256,768]{1,0:T(8,128)(2,1)S(1)} %fusion.13), channel_id=1, source_target_pairs={{0,2},{1,3},{2,0},{3,1},{4,6},{5,7},{6,4},{7,5},{8,10},{9,11},{10,... | collective-permute-start | bytes 1179656 | tf_op jit(solution)/shard_map/ppermute | solution.py:27
  130.9 6.3 %copy-start.3 = (f32[256,768]{1,0:T(8,128)S(1)}, f32[256,768]{1,0:T(8,128)}, u32[]{:S(2)}) copy-start(f32[256,768]{1,0:T(8,128)} %copy-done.2) | copy-start | bytes 2359300
  131.0 16.2 %collective-permute-start.38 = (bf16[384,768]{1,0:T(8,128)(2,1)S(1)}, bf16[384,768]{1,0:T(8,128)(2,1)S(1)}, u32[]{:S(2)}, u32[]{:S(2)}) collective-permute-start(bf16[384,768]{1,0:T(8,128)(2,1)S(1)} %constant_dynamic-slice_fusion), channel_id=1, source_target_pairs={{0,4},{4,0},{1,5},{5,1},{2,6},{6,2},{3,7},{7,3},{8,12},{12,8},{9,1... | collective-permute-start | bytes 1769480 | tf_op jit(solution)/shard_map/ppermute | solution.py:27
  137.3 4.6 %copy-start.35 = (bf16[1024,768]{1,0:T(8,128)(2,1)S(1)}, bf16[1024,768]{1,0:T(8,128)(2,1)}, u32[]{:S(2)}) copy-start(bf16[1024,768]{1,0:T(8,128)(2,1)} %copy-done.34) | copy-start | bytes 4718596
  140.3 10.4 %collective-permute-start.19 = (bf16[256,768]{1,0:T(8,128)(2,1)S(1)}, bf16[256,768]{1,0:T(8,128)(2,1)S(1)}, u32[]{:S(2)}, u32[]{:S(2)}) collective-permute-start(bf16[256,768]{1,0:T(8,128)(2,1)S(1)} %get-tuple-element.100), channel_id=1, source_target_pairs={{0,2},{1,3},{2,0},{3,1},{4,6},{5,7},{6,4},{7,5},{8,10},{9,11},{10,... | collective-permute-start | bytes 1179656 | tf_op jit(solution)/shard_map/ppermute | solution.py:27
  143.4 15.4 %collective-permute-start.33 = (bf16[384,768]{1,0:T(8,128)(2,1)S(1)}, bf16[384,768]{1,0:T(8,128)(2,1)S(1)}, u32[]{:S(2)}, u32[]{:S(2)}) collective-permute-start(bf16[384,768]{1,0:T(8,128)(2,1)S(1)} %constant_dynamic-slice_fusion.1), channel_id=1, source_target_pairs={{0,4},{4,0},{1,5},{5,1},{2,6},{6,2},{3,7},{7,3},{8,12},{12,8},{9,1... | collective-permute-start | bytes 1769480 | tf_op jit(solution)/shard_map/ppermute | solution.py:27
  147.4 16.1 %collective-permute-start.39 = (bf16[384,768]{1,0:T(8,128)(2,1)S(1)}, bf16[384,768]{1,0:T(8,128)(2,1)S(1)}, u32[]{:S(2)}, u32[]{:S(2)}) collective-permute-start(bf16[384,768]{1,0:T(8,128)(2,1)S(1)} %fusion.9), channel_id=1, source_target_pairs={{0,8},{24,16},{1,9},{25,17},{2,10},{26,18},{3,11},{27,19},{4,12},{... | collective-permute-start | bytes 1769480 | tf_op jit(solution)/shard_map/ppermute | solution.py:55
  150.8 15.3 %collective-permute-start.20 = (bf16[2,256,768]{2,1,0:T(8,128)(2,1)S(1)}, bf16[2,256,768]{2,1,0:T(8,128)(2,1)S(1)}, u32[]{:S(2)}, u32[]{:S(2)}) collective-permute-start(bf16[2,256,768]{2,1,0:T(8,128)(2,1)S(1)} %pad_maximum_fusion.5), channel_id=1, source_target_pairs={{0,1},{1,0},{2,3},{3,2},{4,5},{5,4},{6,7},{7,6},{8,9},{9,8},{10,11... | collective-permute-start | bytes 2359304 | tf_op jit(solution)/shard_map/ppermute | solution.py:27
  158.8 5.8 %copy-start.7 = (bf16[384,768]{1,0:T(8,128)(2,1)}, bf16[384,768]{1,0:T(8,128)(2,1)S(1)}, u32[]{:S(2)}) copy-start(bf16[384,768]{1,0:T(8,128)(2,1)S(1)} %collective-permute-done.33) | copy-start | bytes 1769476
  159.8 25.5 %collective-permute-start.34 = (bf16[384,768]{1,0:T(8,128)(2,1)}, bf16[384,768]{1,0:T(8,128)(2,1)}, u32[]{:S(2)}, u32[]{:S(2)}) collective-permute-start(bf16[384,768]{1,0:T(8,128)(2,1)} %fusion.8), channel_id=1, source_target_pairs={{0,8},{24,16},{1,9},{25,17},{2,10},{26,18},{3,11},{27,19},{4,12},{... | collective-permute-start | bytes 1769480 | tf_op jit(solution)/shard_map/ppermute | solution.py:55
  164.6 23.9 %collective-permute-start.40 = (bf16[384,768]{1,0:T(8,128)(2,1)}, bf16[384,768]{1,0:T(8,128)(2,1)}, u32[]{:S(2)}, u32[]{:S(2)}) collective-permute-start(bf16[384,768]{1,0:T(8,128)(2,1)} %add_convert_fusion.1), channel_id=1, source_target_pairs={{8,16},{16,8},{9,17},{17,9},{10,18},{18,10},{11,19},{19,11},{12,20... | collective-permute-start | bytes 1769480 | tf_op jit(solution)/shard_map/ppermute | solution.py:57
  182.7 14.3 %collective-permute-start.23 = (bf16[384,768]{1,0:T(8,128)(2,1)}, bf16[384,768]{1,0:T(8,128)(2,1)}, u32[]{:S(2)}, u32[]{:S(2)}) collective-permute-start(bf16[384,768]{1,0:T(8,128)(2,1)} %constant_dynamic-slice_fusion.2), channel_id=1, source_target_pairs={{0,4},{4,0},{1,5},{5,1},{2,6},{6,2},{3,7},{7,3},{8,12},{12,8},{9,1... | collective-permute-start | bytes 1769480 | tf_op jit(solution)/shard_map/ppermute | solution.py:27
  183.4 1.3 collective-permute-start.28
  184.6 12.4 %copy-start.6 = (bf16[768,768]{1,0:T(8,128)(2,1)S(1)}, bf16[768,768]{1,0:T(8,128)(2,1)}, u32[]{:S(2)}) copy-start(bf16[768,768]{1,0:T(8,128)(2,1)} %get-tuple-element.41) | copy-start | bytes 3538948
  184.6 3.9 %collective-permute-start.29 = (f32[7,768]{1,0:T(8,128)S(1)}, f32[7,768]{1,0:T(8,128)S(1)}, u32[]{:S(2)}, u32[]{:S(2)}) collective-permute-start(f32[7,768]{1,0:T(8,128)S(1)} %add.268), channel_id=1, source_target_pairs={{0,2},{1,3},{2,0},{3,1},{4,6},{5,7},{6,4},{7,5},{8,10},{9,11},{10,... | collective-permute-start | bytes 64520 | tf_op jit(solution)/shard_map/ppermute | solution.py:27
  186.8 15.0 %collective-permute-start.35 = (bf16[384,768]{1,0:T(8,128)(2,1)S(1)}, bf16[384,768]{1,0:T(8,128)(2,1)S(1)}, u32[]{:S(2)}, u32[]{:S(2)}) collective-permute-start(bf16[384,768]{1,0:T(8,128)(2,1)S(1)} %add_convert_fusion.3), channel_id=1, source_target_pairs={{8,16},{16,8},{9,17},{17,9},{10,18},{18,10},{11,19},{19,11},{12,20... | collective-permute-start | bytes 1769480 | tf_op jit(solution)/shard_map/ppermute | solution.py:57
  188.5 12.6 %copy-start.24 = (f32[1,192]{1,0:T(1,128)S(1)}, f32[1,192]{1,0:T(1,128)}, u32[]{:S(2)}) copy-start(f32[1,192]{1,0:T(1,128)} %get-tuple-element.42) | copy-start | bytes 2308
  188.5 12.6 %copy-start.25 = (f32[1,192]{1,0:T(1,128)S(1)}, f32[1,192]{1,0:T(1,128)}, u32[]{:S(2)}) copy-start(f32[1,192]{1,0:T(1,128)} %get-tuple-element.43) | copy-start | bytes 2308
  189.9 23.4 %collective-permute-start.41 = (bf16[384,768]{1,0:T(8,128)(2,1)S(1)}, bf16[384,768]{1,0:T(8,128)(2,1)S(1)}, u32[]{:S(2)}, u32[]{:S(2)}) collective-permute-start(bf16[384,768]{1,0:T(8,128)(2,1)S(1)} %add_convert_fusion), channel_id=1, source_target_pairs={{8,0},{16,24},{9,1},{17,25},{10,2},{18,26},{11,3},{19,27},{12,4},{... | collective-permute-start | bytes 1769480 | tf_op jit(solution)/shard_map/ppermute | solution.py:59
  198.2 12.7 %collective-permute-start.24 = (bf16[384,768]{1,0:T(8,128)(2,1)S(1)}, bf16[384,768]{1,0:T(8,128)(2,1)S(1)}, u32[]{:S(2)}, u32[]{:S(2)}) collective-permute-start(bf16[384,768]{1,0:T(8,128)(2,1)S(1)} %fusion.7), channel_id=1, source_target_pairs={{0,8},{24,16},{1,9},{25,17},{2,10},{26,18},{3,11},{27,19},{4,12},{... | collective-permute-start | bytes 1769480 | tf_op jit(solution)/shard_map/ppermute | solution.py:55
  201.2 4.1 %collective-permute-start.30 = (f32[9,768]{1,0:T(8,128)S(1)}, f32[9,768]{1,0:T(8,128)S(1)}, u32[]{:S(2)}, u32[]{:S(2)}) collective-permute-start(f32[9,768]{1,0:T(8,128)S(1)} %pad_maximum_fusion.6), channel_id=1, source_target_pairs={{0,4},{4,0},{1,5},{5,1},{2,6},{6,2},{3,7},{7,3},{8,12},{12,8},{9,1... | collective-permute-start | bytes 82952 | tf_op jit(solution)/shard_map/ppermute | solution.py:27
  201.9 19.5 %collective-permute-start.36 = (bf16[384,768]{1,0:T(8,128)(2,1)S(1)}, bf16[384,768]{1,0:T(8,128)(2,1)S(1)}, u32[]{:S(2)}, u32[]{:S(2)}) collective-permute-start(bf16[384,768]{1,0:T(8,128)(2,1)S(1)} %add_convert_fusion.2), channel_id=1, source_target_pairs={{8,0},{16,24},{9,1},{17,25},{10,2},{18,26},{11,3},{19,27},{12,4},{... | collective-permute-start | bytes 1769480 | tf_op jit(solution)/shard_map/ppermute | solution.py:59
  205.4 15.6 %collective-permute-start.31 = (f32[9,768]{1,0:T(8,128)S(1)}, f32[9,768]{1,0:T(8,128)S(1)}, u32[]{:S(2)}, u32[]{:S(2)}) collective-permute-start(f32[9,768]{1,0:T(8,128)S(1)} %fusion.51), channel_id=1, source_target_pairs={{0,8},{8,0},{16,24},{24,16},{1,9},{9,1},{17,25},{25,17},{2,10},{10... | collective-permute-start | bytes 82952 | tf_op jit(solution)/shard_map/ppermute | solution.py:27
  212.2 10.8 %copy-start.10 = (bf16[4,256,768]{2,1,0:T(8,128)(2,1)S(1)}, bf16[4,256,768]{2,1,0:T(8,128)(2,1)}, u32[]{:S(2)}) copy-start(bf16[4,256,768]{2,1,0:T(8,128)(2,1)} %get-tuple-element.40) | copy-start | bytes 4718596
  212.2 18.9 %collective-permute-start.25 = (bf16[384,768]{1,0:T(8,128)(2,1)S(1)}, bf16[384,768]{1,0:T(8,128)(2,1)S(1)}, u32[]{:S(2)}, u32[]{:S(2)}) collective-permute-start(bf16[384,768]{1,0:T(8,128)(2,1)S(1)} %add_convert_fusion.5), channel_id=1, source_target_pairs={{8,16},{16,8},{9,17},{17,9},{10,18},{18,10},{11,19},{19,11},{12,20... | collective-permute-start | bytes 1769480 | tf_op jit(solution)/shard_map/ppermute | solution.py:57
  213.4 20.4 %collective-permute-start.42 = (bf16[384,768]{1,0:T(8,128)(2,1)S(1)}, bf16[384,768]{1,0:T(8,128)(2,1)S(1)}, u32[]{:S(2)}, u32[]{:S(2)}) collective-permute-start(bf16[384,768]{1,0:T(8,128)(2,1)S(1)} %broadcast_select_fusion), channel_id=1, source_target_pairs={{0,4},{4,0},{1,5},{5,1},{2,6},{6,2},{3,7},{7,3},{8,12},{12,8},{9,1... | collective-permute-start | bytes 1769480 | tf_op jit(solution)/shard_map/ppermute | solution.py:27
  221.0 9.5 %collective-permute-start.32 = (f32[9,768]{1,0:T(8,128)S(1)}, f32[9,768]{1,0:T(8,128)S(1)}, u32[]{:S(2)}, u32[]{:S(2)}) collective-permute-start(f32[9,768]{1,0:T(8,128)S(1)} %add.271), channel_id=1, source_target_pairs={{0,16},{8,24},{16,0},{24,8},{1,17},{9,25},{17,1},{25,9},{2,18},{10... | collective-permute-start | bytes 82952 | tf_op jit(solution)/shard_map/ppermute | solution.py:27
  221.5 23.5 %collective-permute-start.37 = (bf16[384,768]{1,0:T(8,128)(2,1)S(1)}, bf16[384,768]{1,0:T(8,128)(2,1)S(1)}, u32[]{:S(2)}, u32[]{:S(2)}) collective-permute-start(bf16[384,768]{1,0:T(8,128)(2,1)S(1)} %broadcast_select_fusion.1), channel_id=1, source_target_pairs={{0,4},{4,0},{1,5},{5,1},{2,6},{6,2},{3,7},{7,3},{8,12},{12,8},{9,1... | collective-permute-start | bytes 1769480 | tf_op jit(solution)/shard_map/ppermute | solution.py:27
  223.1 10.8 %collective-permute-start.21 = (bf16[2,256,768]{2,1,0:T(8,128)(2,1)S(1)}, bf16[2,256,768]{2,1,0:T(8,128)(2,1)S(1)}, u32[]{:S(2)}, u32[]{:S(2)}) collective-permute-start(bf16[2,256,768]{2,1,0:T(8,128)(2,1)S(1)} %slice.230), channel_id=1, source_target_pairs={{0,1},{1,0},{2,3},{3,2},{4,5},{5,4},{6,7},{7,6},{8,9},{9,8},{10,11... | collective-permute-start | bytes 2359304 | tf_op jit(solution)/shard_map/ppermute | solution.py:27
  231.3 13.0 %collective-permute-start.26 = (bf16[384,768]{1,0:T(8,128)(2,1)S(1)}, bf16[384,768]{1,0:T(8,128)(2,1)S(1)}, u32[]{:S(2)}, u32[]{:S(2)}) collective-permute-start(bf16[384,768]{1,0:T(8,128)(2,1)S(1)} %add_convert_fusion.4), channel_id=1, source_target_pairs={{8,0},{16,24},{9,1},{17,25},{10,2},{18,26},{11,3},{19,27},{12,4},{... | collective-permute-start | bytes 1769480 | tf_op jit(solution)/shard_map/ppermute | solution.py:59
  234.0 14.2 %collective-permute-start.22 = (bf16[256,768]{1,0:T(8,128)(2,1)S(1)}, bf16[256,768]{1,0:T(8,128)(2,1)S(1)}, u32[]{:S(2)}, u32[]{:S(2)}) collective-permute-start(bf16[256,768]{1,0:T(8,128)(2,1)S(1)} %fusion.27), channel_id=1, source_target_pairs={{0,2},{1,3},{2,0},{3,1},{4,6},{5,7},{6,4},{7,5},{8,10},{9,11},{10,... | collective-permute-start | bytes 1179656 | tf_op jit(solution)/shard_map/ppermute | solution.py:27
  244.3 10.3 %collective-permute-start.27 = (bf16[384,768]{1,0:T(8,128)(2,1)S(1)}, bf16[384,768]{1,0:T(8,128)(2,1)S(1)}, u32[]{:S(2)}, u32[]{:S(2)}) collective-permute-start(bf16[384,768]{1,0:T(8,128)(2,1)S(1)} %broadcast_select_fusion.2), channel_id=1, source_target_pairs={{0,4},{4,0},{1,5},{5,1},{2,6},{6,2},{3,7},{7,3},{8,12},{12,8},{9,1... | collective-permute-start | bytes 1769480 | tf_op jit(solution)/shard_map/ppermute | solution.py:27
  257.8 6.8 %copy-start.1 = (bf16[2048,768]{1,0:T(8,128)(2,1)S(1)}, bf16[2048,768]{1,0:T(8,128)(2,1)}, u32[]{:S(2)}) copy-start(bf16[2048,768]{1,0:T(8,128)(2,1)} %param.27) | copy-start | bytes 9437188
  (16 other events, 37.3 us)

commit v2 on v1

--- a/solution.py
+++ b/solution.py
@@ -107,9 +107,9 @@
 
     compact = dot(table, tokens[0]).astype(low)
     compact_out[0] = compact
-    query = (dot(compact, wq[...]) + bq[...]).astype(low)
-    keys = dot(compact, wk[...]).astype(low)
-    values = (dot(compact, wv[...]) + bv[...]).astype(low)
+    query = (dot(compact, wq[...], ((1,), (1,))) + bq[...]).astype(low)
+    keys = dot(compact, wk[...], ((1,), (1,))).astype(low)
+    values = (dot(compact, wv[...], ((1,), (1,))) + bv[...]).astype(low)
     q_out[0], k_out[0], v_out[0] = query, keys, values
     live = lane.astype(full) < count
     contexts = []
@@ -128,7 +128,7 @@
 
 def attend(tokens, keep_mask, crop_len, order, wq, wk, wv, wo, bq, bv):
     seqs, length, width = tokens.shape
-    mine = wq.shape[1]
+    mine = wq.shape[0]
     heads = mine // HEAD
 
     def const(shape):
@@ -149,9 +149,9 @@
             in_specs=[
                 picked(1, length),
                 picked(length, width),
-                const((width, mine)),
-                const((width, mine)),
-                const((width, mine)),
+                const((mine, width)),
+                const((mine, width)),
+                const((mine, width)),
                 const((mine, width)),
                 const((1, mine)),
                 const((1, mine)),
@@ -196,7 +196,7 @@
 
     scale = 1.0 / math.sqrt(HEAD)
     grad = grads[0]
-    mine = wq.shape[1]
+    mine = wq.shape[0]
     query, keys, values = q_in[0], k_in[0], v_in[0]
     context_grad = dot(grad, wo[...], ((1,), (1,))).astype(low)
     query_grads, keys_grads, values_grads = [], [], []
@@ -214,13 +214,13 @@
     keys_grad = jnp.concatenate(keys_grads, axis=1)
     values_grad = jnp.concatenate(values_grads, axis=1)
     every = jnp.concatenate([query_grad, keys_grad, values_grad], axis=1)
-    weights[:, : 3 * mine] += dot(compact[0], every, ((0,), (0,)))
-    weights[:, 3 * mine :] += dot(grad, ctx_in[0], ((0,), (0,)))
+    weights[: 3 * mine] += dot(every, compact[0], ((0,), (0,)))
+    weights[3 * mine :] += dot(ctx_in[0], grad, ((0,), (0,)))
     qb[...] += jnp.sum(query_grad.astype(full), axis=0, keepdims=True)
     vb[...] += jnp.sum(values_grad.astype(full), axis=0, keepdims=True)
-    back = dot(query_grad, wq[...], ((1,), (1,)))
-    back += dot(keys_grad, wk[...], ((1,), (1,)))
-    back += dot(values_grad, wv[...], ((1,), (1,)))
+    back = dot(query_grad, wq[...])
+    back += dot(keys_grad, wk[...])
+    back += dot(values_grad, wv[...])
     part_out[0] = back.astype(low)
 
     @pl.when(b == pl.num_programs(0) - 1)
@@ -232,7 +232,7 @@
 
 def attend_back(grads, compact, query, keys, values, probs, context, wq, wk, wv, wo):
     seqs, length, width = grads.shape
-    mine = wq.shape[1]
+    mine = wq.shape[0]
     heads = mine // HEAD
 
     def const(shape):
@@ -253,30 +253,52 @@
             per(length, mine),
             per(heads, length, length),
             per(length, mine),
-            const((width, mine)),
-            const((width, mine)),
-            const((width, mine)),
+            const((mine, width)),
+            const((mine, width)),
+            const((mine, width)),
             const((mine, width)),
         ],
         out_specs=[
             per(length, width),
-            const((width, 4 * mine)),
+            const((4 * mine, width)),
             const((1, mine)),
             const((1, mine)),
         ],
         out_shape=[
             S((seqs, length, width), low),
-            S((width, 4 * mine), low),
+            S((4 * mine, width), low),
             S((1, mine), full),
             S((1, mine), full),
         ],
         scratch_shapes=[
-            pltpu.VMEM((width, 4 * mine), full),
+            pltpu.VMEM((4 * mine, width), full),
             pltpu.VMEM((1, mine), full),
             pltpu.VMEM((1, mine), full),
         ],
         name="attend_back",
     )(grads, compact, query, keys, values, probs, context, wq, wk, wv, wo)
+
+
+def gather_feedforward(up_weight, up_bias, down_weight):
+    f = lax.axis_index("fsdp")
+    half = up_weight.shape[1] // 2
+    up_y = swap(lax.dynamic_slice_in_dim(up_weight, f * half, half, 1), "tensor", 2)
+    down_y = swap(lax.dynamic_slice_in_dim(down_weight, f * half, half, 0), "tensor", 2)
+    up_x = swap(up_y, "fsdp", 1)
+    down_x = swap(down_y, "fsdp", 1)
+    bias = up_bias[None]
+    bias = jnp.concatenate([bias, swap(bias, "tensor", 2)])
+    bias = jnp.concatenate([bias, swap(bias, "tensor", 1)])
+    blocks = []
+    for base, other in ((0, False), (2, True)):
+        across = (lambda a: swap(a, "tensor", 1)) if other else (lambda a: a)
+        far = bias[base + 1 : base + 2]
+        bias_y = lax.dynamic_slice_in_dim(far, f * half, half, 1)
+        bias_x = lax.dynamic_slice_in_dim(far, (1 - f) * half, half, 1)
+        blocks.append((across(up_weight), bias[base : base + 1], across(down_weight)))
+        blocks.append((across(up_y), bias_y, across(down_y)))
+        blocks.append((across(up_x), bias_x, across(down_x)))
+    return [blocks[i] for i in (0, 3, 1, 4, 2, 5)]
 
 
 def contrast(pooled, key_queue):
@@ -338,26 +360,33 @@
     group = lax.axis_index(("dp", "fsdp"))
     devices = seqs * lax.axis_size("dp") * lax.axis_size("fsdp")
     mine = query_weight.shape[1]
-    hidden = up_weight.shape[1]
     order = (member ^ jnp.array(RELATIVE, jnp.int32)).astype(jnp.int32)
 
     positive = own_positive(pos_keys, pos_index, group, member)
+    blocks = gather_feedforward(up_weight, up_bias, down_weight)
     compact, query, keys, values, probs, context, partial_out, table, counts = attend(
-        tokens, keep_mask, crop_len, order, query_weight, key_weight, value_weight, out_weight, query_bias, value_bias
+        tokens, keep_mask, crop_len, order, query_weight.T, key_weight.T, value_weight.T, out_weight, query_bias, value_bias
     )
     count = counts[0:1, 0:1]
     live = (jnp.arange(length, dtype=jnp.int32)[:, None].astype(full) < count).astype(full)
-    normed_one, rstd_one = norm_parts(compact[0].astype(full) + tensor_sum(partial_out) + out_bias)
+    attn_out, positive = lax.optimization_barrier((tensor_sum(partial_out), positive))
+    normed_one, rstd_one = norm_parts(compact[0].astype(full) + attn_out + out_bias)
     middle = normed_one * norm_gain + norm_shift
-    middle_all = tensor_gather(middle.astype(low)).reshape(seqs * length, width)
-    pre = dot(middle_all, up_weight) + up_bias
-    hidden_state, slope = gelu_parts(pre)
-    hidden_state = hidden_state.astype(low)
-    partial_ffn = dot(hidden_state, down_weight).astype(low).reshape(seqs, length, width)
-    normed_two, rstd_two = norm_parts(middle + tensor_sum(partial_ffn) + down_bias)
+    middle_low = middle.astype(low)
+    ffn_out = middle + down_bias
+    slopes = []
+    for up, bias, down in blocks:
+        hidden_part, slope_part = gelu_parts(dot(middle_low, up) + bias)
+        slopes.append(slope_part.astype(low))
+        ffn_out = ffn_out + dot(hidden_part.astype(low), down)
+    normed_two, rstd_two = norm_parts(ffn_out)
     output = (normed_two * final_gain + final_shift).astype(low)
     live_sum = jnp.sum(normed_two * live, axis=0, keepdims=True)
     pooled = (live_sum / count * final_gain + final_shift).astype(low)
+
+    middle_all = tensor_gather(middle_low).reshape(seqs * length, width)
+    hidden_state, slope = gelu_parts(dot(middle_all, up_weight) + up_bias)
+    hidden_state = hidden_state.astype(low)
 
     pos_logit = jnp.sum(pooled.astype(full) * positive, axis=1, keepdims=True) * inv_temp
     top, total, key_sum = contrast(pooled, key_queue)
@@ -372,13 +401,15 @@
     final_gain_part = result_row * live_sum
     ffn_grad = two_grad.astype(low)
     down_bias_part = jnp.sum(ffn_grad.astype(full), axis=0, keepdims=True)
-    ffn_grads = tensor_gather(ffn_grad).reshape(seqs * length, width)
-    pre_grad = (slope * dot(ffn_grads, down_weight, ((1,), (1,)))).astype(low)
-    back_part = dot(pre_grad, up_weight, ((1,), (1,))).astype(low).reshape(seqs, length, width)
-    middle_grad = two_grad + tensor_sum(back_part)
+    middle_grad = two_grad
+    for (up, _, down), slope_part in zip(blocks, slopes):
+        grad_part = (slope_part.astype(full) * dot(ffn_grad, down, ((1,), (1,)))).astype(low)
+        middle_grad = middle_grad + dot(grad_part, up, ((1,), (1,)))
     one_grad = norm_backward(middle_grad * norm_gain, normed_one, rstd_one)
     attn_grad = one_grad.astype(low)
     attn_grads = tensor_gather(attn_grad)
+    ffn_grads = tensor_gather(ffn_grad).reshape(seqs * length, width)
+    pre_grad = (slope * dot(ffn_grads, down_weight, ((1,), (1,)))).astype(low)
     down_weight_grad = group_sum(dot(hidden_state, ffn_grads, ((0,), (0,))).astype(low))
     up_weight_grad = group_sum(dot(middle_all, pre_grad, ((0,), (0,))).astype(low))
     up_bias_part = jnp.sum(pre_grad.astype(full), axis=0, keepdims=True)
@@ -387,7 +418,7 @@
     out_bias_part = jnp.sum(attn_grad.astype(full), axis=0, keepdims=True)
 
     partial_in, attn_weight_grad, query_bias_part, value_bias_part = attend_back(
-        attn_grads, compact, query, keys, values, probs, context, query_weight, key_weight, value_weight, out_weight
+        attn_grads, compact, query, keys, values, probs, context, query_weight.T, key_weight.T, value_weight.T, out_weight
     )
     attn_weight_grad = group_sum(attn_weight_grad).astype(full)
     compact_grad = (one_grad + tensor_sum(partial_in)).astype(low)
@@ -416,12 +447,12 @@
     return (
         output[None],
         input_grad[None],
-        attn_weight_grad[:, :mine],
+        attn_weight_grad[:mine].T,
         vectors[7, :mine],
-        attn_weight_grad[:, mine : 2 * mine],
-        attn_weight_grad[:, 2 * mine : 3 * mine],
+        attn_weight_grad[mine : 2 * mine].T,
+        attn_weight_grad[2 * mine : 3 * mine].T,
         vectors[7, mine : 2 * mine],
-        attn_weight_grad[:, 3 * mine :].T,
+        attn_weight_grad[3 * mine :],
         vectors[5],
         vectors[2],
         vectors[3],

time: 265 us -> 309 us (1.17)
  matrix products: 16.7 us -> 40.2 us
  starting transfers between devices: 51.3 us -> 64.8 us
  waiting for transfers between devices: 111 us -> 124 us
  local copies, waits for them, and re-layouts: 26.7 us -> 18.3 us
    ppermute x34 -> x42, waiting for transfers between devices: 97.7 us -> 73.7 us  [swap(): return lax.ppermute(array, axis, [(i, i ^ stride) for i in range(size)])]
    dot_general x9 -> x25, matrix products: 16.7 us -> 40.2 us  [dot(): return lax.dot_general(a, b, (dims, ((), ())), preferred_element_type=full)]
    ppermute x3, waiting for transfers between devices: 10.2 us -> 32.6 us  [group_sum(): outer = lax.ppermute(total, 'dp', [(1, 0), (2, 3)])]
    ppermute x34 -> x42, starting transfers between devices: 34.6 us -> 49.3 us  [swap(): return lax.ppermute(array, axis, [(i, i ^ stride) for i in range(size)])]
    ppermute x3, waiting for transfers between devices: 3.39 us -> 17.7 us  [group_sum(): lax.ppermute(part.astype(low), 'dp', [(0, 1), (3, 2)]).astype(full)]
    unnamed x81 -> x138, local copies, waits for them, and re-layouts: 13.3 us -> 3.34 us
    another operation x4, other arithmetic: 0.42 us -> 4.98 us  [tensor_gather(): pair = jnp.stack([block, swap(block, 'tensor', 2)])]
    concatenate x3, other arithmetic: 1.61 us -> 5.21 us  [tensor_gather(): return jnp.concatenate([pair, swap(pair, 'tensor', 1)])]
  transfers between devices with their start and end apart: 43 -> 51, of which waited for: 28 -> 25; matrix products, arithmetic and copies ran while one was open for 12% -> 25% of each run, Pallas kernels for 5% -> 4%
where the time goes in v2:
time: 309 us; the launch traced here: 308 us
  waiting for transfers between devices  124 us (40%)
  starting transfers between devices  64.8 us (21%)
  matrix products  40.2 us (13%)
  other arithmetic  28.4 us (9%)
  Pallas kernels  23.5 us (8%)
  local copies, waits for them, and re-layouts  18.3 us (6%)
  between operations  8.82 us (3%)
    ppermute x42, waiting for transfers between devices, swap(): return lax.ppermute(array, axis, [(i, i ^ stride) for i in range(size)])  73.7 us
    ppermute x42, starting transfers between devices, swap(): return lax.ppermute(array, axis, [(i, i ^ stride) for i in range(size)])  49.3 us
    dot_general x25, matrix products, dot(): return lax.dot_general(a, b, (dims, ((), ())), preferred_element_type=full)  40.2 us
    ppermute x3, waiting for transfers between devices, group_sum(): outer = lax.ppermute(total, 'dp', [(1, 0), (2, 3)])  32.6 us
    ppermute x3, waiting for transfers between devices, group_sum(): lax.ppermute(part.astype(low), 'dp', [(0, 1), (3, 2)]).astype(full)  17.7 us
    pallas_call x1, Pallas kernels, attend_back(): pl.pallas_call(attend_back_kernel, grid=(seqs,), in_specs=[per(length, wi...  12.3 us
    pallas_call x1, Pallas kernels, attend(): pl.pallas_call(attend_kernel, grid_spec=pltpu.PrefetchScalarGridSpec(num_...  11.2 us
    ppermute x3, starting transfers between devices, group_sum(): lax.ppermute(part.astype(low), 'dp', [(0, 1), (3, 2)]).astype(full)  9.34 us
  transfers between devices with their start and end apart: 51, of which 25 were waited for; matrix products, arithmetic and copies ran while one was open for 25% of the time, Pallas kernels for 4%

profile of v2, /device:TPU:0, one launch (start us, length us, event | category | flops | bytes accessed | tf_op | source)
XLA Modules:
  0.0 308.0 jit_solution(2573253770740740339)
XLA Ops:
  3.3 11.2 %attend.1 = (bf16[4,256,768]{2,1,0:T(8,128)(2,1)}, bf16[4,256,192]{2,1,0:T(8,128)(2,1)}, bf16[4,256,192]{2,1,0:T(8,128)(2,1)}, bf16[4,256,192]{2,1,0:T(8,128)(2,...) custom-call(s32[4]{0:T(128)} %broadcast_xor_fusion.order, ...), custom_call_target="tpu_custom_call" | custom-call | tf_op jit(solution)/shard_map/attend/pallas_call | solution.py:144
  14.5 2.1 slice.160
  17.1 2.0 constant_dynamic-slice_fusion.6
  19.1 3.0 collective-permute-start.10
  22.1 1.5 collective-permute-start.2
  30.6 5.4 %collective-permute-done.6 = f32[1,768]{1,0:T(1,128)S(1)} collective-permute-done((f32[1,768]{1,0:T(1,128)S(1)}, f32[1,768]{1,0:T(1,128)S(1)}, u32[]{:S(2)}, u32[]{:S(2)}) %collective-permute-start.6) | collective-permute-done | bytes 3104 | tf_op jit(solution)/shard_map/ppermute | solution.py:27
  36.0 1.7 collective-permute-start.9
  37.9 1.6 collective-permute-start.3
  42.0 2.8 collective-permute-start.4
  44.9 1.9 collective-permute-done.4
  46.8 1.8 collective-permute-start.14
  48.6 3.8 %collective-permute-done.9 = bf16[768,384]{1,0:T(8,128)(2,1)S(1)} collective-permute-done((bf16[768,384]{1,0:T(8,128)(2,1)}, bf16[768,384]{1,0:T(8,128)(2,1)S(1)}, u32[]{:S(2)}, u32[]{:S(2)}) %collective-permute-start.9) | collective-permute-done | bytes 589856 | tf_op jit(solution)/shard_map/ppermute | solution.py:27
  52.4 6.9 %collective-permute-done.1 = bf16[256,768]{1,0:T(8,128)(2,1)S(1)} collective-permute-done((bf16[256,768]{1,0:T(8,128)(2,1)S(1)}, bf16[256,768]{1,0:T(8,128)(2,1)S(1)}, u32[]{:S(2)}, u32[]{:S(2)}) %collective-permute-start.1) | collective-permute-done | bytes 393248 | tf_op jit(solution)/shard_map/ppermute | solution.py:27
  64.1 1.6 fusion.81
  66.3 9.2 %collective-permute-done.13 = bf16[768,384]{1,0:T(8,128)(2,1)S(1)} collective-permute-done((bf16[768,384]{1,0:T(8,128)(2,1)S(1)}, bf16[768,384]{1,0:T(8,128)(2,1)S(1)}, u32[]{:S(2)}, u32[]{:S(2)}) %collective-permute-start.13) | collective-permute-done | bytes 589856 | tf_op jit(solution)/shard_map/ppermute | solution.py:27
  76.5 2.1 convolution_add_fusion.8
  78.6 1.8 fusion.12
  85.8 1.8 collective-permute-start.17
  87.5 1.9 collective-permute-done.17
  89.5 1.8 collective-permute-start.18
  91.3 1.6 collective-permute-start.34
  93.1 2.9 collective-permute-start.19
  99.8 2.9 collective-permute-start.20
  102.7 1.7 collective-permute-done.20
  104.8 1.9 collective-permute-start.21
  106.7 2.1 pad_maximum_fusion.4
  109.1 1.6 collective-permute-start.22
  120.1 3.4 %convolution_add_fusion.5 = f32[256,768]{1,0:T(8,128)} fusion(bf16[768,768]{1,0:T(8,128)(2,1)S(1)} %copy-done.19, bf16[256,768]{1,0:T(8,128)(2,1)S(1)} %get-tuple-element.75, bf16[768,768]{1,0:T(8,128)(2,1)} %param.39, f32[256,768]{1,0:T(8,128)S(1)} %copy-done.5, f32[256,768]{1,0:T(8,128)} %copy-done.34, f32[256]{0:T(256)S(1)} %get-tuple-element.105, ...), kind=kOutput, calls=%fused_computation.30 | convolution fusion | flops 607911936 | bytes 5120000 | tf_op jit(solution)/shard_map/dot_general | solution.py:22
  123.5 2.9 fusion.20
  126.4 3.2 %fusion.21 = f32[256,768]{1,0:T(8,128)} fusion(bf16[768,384]{1,0:T(8,128)(2,1)} %copy-done.24, bf16[256,768]{1,0:T(8,128)(2,1)S(1)} %get-tuple-element.75, bf16[384,768]{1,0:T(8,128)(2,1)} %collective-permute-done.10, f32[256,384]{1,0:T(8,128)S(1)} %copy-done.14), kind=kOutput, calls=%fused_computation.68 | convolution fusion | flops 303169536 | bytes 2752512 | tf_op jit(solution)/shard_map/dot_general | solution.py:22
  129.6 3.7 %fusion.11 = f32[256,768]{1,0:T(8,128)} fusion(f32[256,768]{1,0:T(8,128)} %fusion.21, f32[256,768]{1,0:T(8,128)} %convolution_add_fusion.5, bf16[768,768]{1,0:T(8,128)(2,1)S(1)} %copy-done.9, bf16[256,768]{1,0:T(8,128)(2,1)S(1)} %get-tuple-element.75, bf16[768,768]{1,0:T(8,128)(2,1)} %collective-permute-done.8, f32[256,768]{1,0:T(8,128)S(1)} %copy-done.7), kind=kOutput, calls=%fused_computation.28 | convolution fusion | flops 606732288 | bytes 5898240 | tf_op jit(solution)/shard_map/dot_general | solution.py:22
  133.3 2.5 fusion.10
  135.9 2.8 multiply_reduce_fusion.1
  139.0 1.5 collective-permute-start.23
  141.1 10.0 %collective-permute-done.23 = bf16[256,768]{1,0:T(8,128)(2,1)S(1)} collective-permute-done((bf16[256,768]{1,0:T(8,128)(2,1)S(1)}, bf16[256,768]{1,0:T(8,128)(2,1)S(1)}, u32[]{:S(2)}, u32[]{:S(2)}) %collective-permute-start.23) | collective-permute-done | bytes 393248 | tf_op jit(solution)/shard_map/ppermute | solution.py:27
  152.7 1.9 collective-permute-done.32
  154.7 1.5 collective-permute-start.33
  156.1 2.8 collective-permute-done.33
  160.5 1.5 pad_maximum_fusion.1
  162.1 3.0 fusion.144
  165.2 2.4 pad_maximum_fusion.grads
  167.6 12.3 %attend_back.1 = (bf16[4,256,768]{2,1,0:T(8,128)(2,1)}, bf16[768,768]{1,0:T(8,128)(2,1)}, f32[1,192]{1,0:T(1,128)}, f32[1,192]{1,0:T(1,128)}) custom-call(bf16[4,256,768]{2,1,0:T(8,128)(2,1)} %pad_maximum_fusion.grads, bf16[4,256,768]{2,1,0:T(8,128)(2,1)} %get-tuple-element.33.compact, bf16[4,256,192]{2,1,0:T(8,128)(2,1)} %get-tuple-element.39.q_in, ...), custom_call_target="tpu_custom_call" | custom-call | tf_op jit(solution)/shard_map/attend_back/pallas_call | solution.py:245
  183.8 3.7 %convert_reduce_fusion = (f32[768]{0:T(1024)S(1)}, bf16[1024,768]{1,0:T(8,128)(2,1)S(1)}) fusion(bf16[1024,768]{1,0:T(8,128)(2,1)S(1)} %bitcast.106, bf16[768,768]{1,0:T(8,128)(2,1)} %param.39, f32[1024,768]{1,0:T(8,128)S(1)} %copy-done.68, f32[768]{0:T(1024)S(1)} %copy-done.52), kind=kOutput, calls=%fused_computation.8 | convolution fusion | flops 1218182400 | bytes 7477248 | tf_op jit(solution)/shard_map/dot_general | solution.py:22
  188.6 1.5 convolution_convert_fusion
  191.2 7.4 %collective-permute-done.38 = f32[9,768]{1,0:T(8,128)S(1)} collective-permute-done((f32[9,768]{1,0:T(8,128)S(1)}, f32[9,768]{1,0:T(8,128)S(1)}, u32[]{:S(2)}, u32[]{:S(2)}) %collective-permute-start.38) | collective-permute-done | bytes 27680 | tf_op jit(solution)/shard_map/ppermute | solution.py:27
  199.8 1.8 fusion.8
  202.8 2.7 collective-permute-start.40
  208.1 3.0 collective-permute-start.28
  211.4 3.0 collective-permute-start.42
  215.1 8.1 %collective-permute-done.46 = bf16[384,768]{1,0:T(8,128)(2,1)S(1)} collective-permute-done((bf16[384,768]{1,0:T(8,128)(2,1)S(1)}, bf16[384,768]{1,0:T(8,128)(2,1)S(1)}, u32[]{:S(2)}, u32[]{:S(2)}) %collective-permute-start.46) | collective-permute-done | bytes 589856 | tf_op jit(solution)/shard_map/ppermute | solution.py:27
  223.4 3.3 %collective-permute-start.47 = (bf16[384,768]{1,0:T(8,128)(2,1)S(1)}, bf16[384,768]{1,0:T(8,128)(2,1)S(1)}, u32[]{:S(2)}, u32[]{:S(2)}) collective-permute-start(bf16[384,768]{1,0:T(8,128)(2,1)S(1)} %fusion.24), channel_id=1, source_target_pairs={{0,8},{24,16},{1,9},{25,17},{2,10},{26,18},{3,11},{27,19},{4,12},{... | collective-permute-start | bytes 1769480 | tf_op jit(solution)/shard_map/ppermute | solution.py:55
  227.6 9.8 %collective-permute-done.42 = bf16[384,768]{1,0:T(8,128)(2,1)S(1)} collective-permute-done((bf16[384,768]{1,0:T(8,128)(2,1)S(1)}, bf16[384,768]{1,0:T(8,128)(2,1)S(1)}, u32[]{:S(2)}, u32[]{:S(2)}) %collective-permute-start.42) | collective-permute-done | bytes 589856 | tf_op jit(solution)/shard_map/ppermute | solution.py:55
  239.5 7.8 %collective-permute-done.47 = bf16[384,768]{1,0:T(8,128)(2,1)S(1)} collective-permute-done((bf16[384,768]{1,0:T(8,128)(2,1)S(1)}, bf16[384,768]{1,0:T(8,128)(2,1)S(1)}, u32[]{:S(2)}, u32[]{:S(2)}) %collective-permute-start.47) | collective-permute-done | bytes 589856 | tf_op jit(solution)/shard_map/ppermute | solution.py:55
  251.4 1.6 collective-permute-start.26
  254.6 15.3 %collective-permute-done.30 = bf16[384,768]{1,0:T(8,128)(2,1)S(1)} collective-permute-done((bf16[384,768]{1,0:T(8,128)(2,1)S(1)}, bf16[384,768]{1,0:T(8,128)(2,1)S(1)}, u32[]{:S(2)}, u32[]{:S(2)}) %collective-permute-start.30) | collective-permute-done | bytes 589856 | tf_op jit(solution)/shard_map/ppermute | solution.py:59
  269.9 1.5 collective-permute-start.31
  271.5 11.0 %collective-permute-done.44 = bf16[384,768]{1,0:T(8,128)(2,1)S(1)} collective-permute-done((bf16[384,768]{1,0:T(8,128)(2,1)S(1)}, bf16[384,768]{1,0:T(8,128)(2,1)S(1)}, u32[]{:S(2)}, u32[]{:S(2)}) %collective-permute-start.44) | collective-permute-done | bytes 589856 | tf_op jit(solution)/shard_map/ppermute | solution.py:59
  282.6 1.5 collective-permute-start.45
  285.3 6.3 %collective-permute-done.49 = bf16[384,768]{1,0:T(8,128)(2,1)S(1)} collective-permute-done((bf16[384,768]{1,0:T(8,128)(2,1)S(1)}, bf16[384,768]{1,0:T(8,128)(2,1)S(1)}, u32[]{:S(2)}, u32[]{:S(2)}) %collective-permute-start.49) | collective-permute-done | bytes 589856 | tf_op jit(solution)/shard_map/ppermute | solution.py:59
  291.7 2.0 collective-permute-start.50
  294.0 1.6 maximum_convert_fusion.1
  295.6 1.4 fusion.139
  297.1 8.1 %collective-permute-done.50 = bf16[384,768]{1,0:T(8,128)(2,1)S(1)} collective-permute-done((bf16[384,768]{1,0:T(8,128)(2,1)S(1)}, bf16[384,768]{1,0:T(8,128)(2,1)S(1)}, u32[]{:S(2)}, u32[]{:S(2)}) %collective-permute-start.50) | collective-permute-done | bytes 589856 | tf_op jit(solution)/shard_map/ppermute | solution.py:27
  305.3 1.6 maximum_convert_fusion.2
  (316 shorter events, 59.1 us)
Async XLA Ops:
  0.7 97.1 %copy-start = (bf16[2048,768]{1,0:T(8,128)(2,1)S(1)}, bf16[2048,768]{1,0:T(8,128)(2,1)}, u32[]{:S(2)}) copy-start(bf16[2048,768]{1,0:T(8,128)(2,1)} %param.27) | copy-start | bytes 9437188
  16.6 21.3 %collective-permute-start = (bf16[2,256,768]{2,1,0:T(8,128)(2,1)}, bf16[2,256,768]{2,1,0:T(8,128)(2,1)}, u32[]{:S(2)}, u32[]{:S(2)}) collective-permute-start(bf16[2,256,768]{2,1,0:T(8,128)(2,1)} %slice.160), channel_id=1, source_target_pairs={{0,1},{1,0},{2,3},{3,2},{4,5},{5,4},{6,7},{7,6},{8,9},{9,8},{10,11... | collective-permute-start | bytes 2359304 | tf_op jit(solution)/shard_map/ppermute | solution.py:27
  17.1 61.5 %collective-permute-start.8 = (bf16[768,768]{1,0:T(8,128)(2,1)}, bf16[768,768]{1,0:T(8,128)(2,1)}, u32[]{:S(2)}, u32[]{:S(2)}) collective-permute-start(bf16[768,768]{1,0:T(8,128)(2,1)} %param.39), channel_id=1, source_target_pairs={{0,1},{1,0},{2,3},{3,2},{4,5},{5,4},{6,7},{7,6},{8,9},{9,8},{10,11... | collective-permute-start | bytes 3538952 | tf_op jit(solution)/shard_map/ppermute | solution.py:27
  19.1 27.7 %collective-permute-start.10 = (bf16[384,768]{1,0:T(8,128)(2,1)}, bf16[384,768]{1,0:T(8,128)(2,1)}, u32[]{:S(2)}, u32[]{:S(2)}) collective-permute-start(bf16[384,768]{1,0:T(8,128)(2,1)} %constant_dynamic-slice_fusion.6), channel_id=1, source_target_pairs={{0,2},{1,3},{2,0},{3,1},{4,6},{5,7},{6,4},{7,5},{8,10},{9,11},{10,... | collective-permute-start | bytes 1769480 | tf_op jit(solution)/shard_map/ppermute | solution.py:27
  22.1 15.6 %collective-permute-start.2 = (bf16[4,768]{1,0:T(4,128)(2,1)S(1)}, bf16[4,768]{1,0:T(4,128)(2,1)S(1)}, u32[]{:S(2)}, u32[]{:S(2)}) collective-permute-start(bf16[4,768]{1,0:T(4,128)(2,1)S(1)} %copy-done.39), channel_id=1, source_target_pairs={{0,4},{4,0},{1,5},{5,1},{2,6},{6,2},{3,7},{7,3},{8,12},{12,8},{9,1... | collective-permute-start | bytes 18440 | tf_op jit(solution)/shard_map/ppermute | solution.py:27
  23.6 12.3 %collective-permute-start.6 = (f32[1,768]{1,0:T(1,128)S(1)}, f32[1,768]{1,0:T(1,128)S(1)}, u32[]{:S(2)}, u32[]{:S(2)}) collective-permute-start(f32[1,768]{1,0:T(1,128)S(1)} %broadcast_in_dim.49), channel_id=1, source_target_pairs={{0,2},{1,3},{2,0},{3,1},{4,6},{5,7},{6,4},{7,5},{8,10},{9,11},{10,... | collective-permute-start | bytes 9224 | tf_op jit(solution)/shard_map/ppermute | solution.py:27
  36.0 16.4 %collective-permute-start.9 = (bf16[768,384]{1,0:T(8,128)(2,1)}, bf16[768,384]{1,0:T(8,128)(2,1)S(1)}, u32[]{:S(2)}, u32[]{:S(2)}) collective-permute-start(bf16[768,384]{1,0:T(8,128)(2,1)} %constant_dynamic-slice_fusion.8), channel_id=1, source_target_pairs={{0,2},{1,3},{2,0},{3,1},{4,6},{5,7},{6,4},{7,5},{8,10},{9,11},{10,... | collective-permute-start | bytes 1769480 | tf_op jit(solution)/shard_map/ppermute | solution.py:27
  37.8 4.2 %collective-permute-start.7 = (f32[2,768]{1,0:T(2,128)S(1)}, f32[2,768]{1,0:T(2,128)S(1)}, u32[]{:S(2)}, u32[]{:S(2)}) collective-permute-start(f32[2,768]{1,0:T(2,128)S(1)} %pad_maximum_fusion.12), channel_id=1, source_target_pairs={{0,1},{1,0},{2,3},{3,2},{4,5},{5,4},{6,7},{7,6},{8,9},{9,8},{10,11... | collective-permute-start | bytes 18440 | tf_op jit(solution)/shard_map/ppermute | solution.py:27
  37.9 24.1 %copy-start.61 = (f32[768]{0:T(1024)S(1)}, f32[768]{0:T(1024)}, u32[]{:S(2)}) copy-start(f32[768]{0:T(1024)} %param.34) | copy-start | bytes 9220
  37.9 3.8 %collective-permute-start.3 = (bf16[8,768]{1,0:T(8,128)(2,1)S(1)}, bf16[8,768]{1,0:T(8,128)(2,1)S(1)}, u32[]{:S(2)}, u32[]{:S(2)}) collective-permute-start(bf16[8,768]{1,0:T(8,128)(2,1)S(1)} %pad_maximum_fusion.10), channel_id=1, source_target_pairs={{0,8},{8,0},{16,24},{24,16},{1,9},{9,1},{17,25},{25,17},{2,10},{10... | collective-permute-start | bytes 36872 | tf_op jit(solution)/shard_map/ppermute | solution.py:27
  41.7 17.6 %collective-permute-start.1 = (bf16[256,768]{1,0:T(8,128)(2,1)S(1)}, bf16[256,768]{1,0:T(8,128)(2,1)S(1)}, u32[]{:S(2)}, u32[]{:S(2)}) collective-permute-start(bf16[256,768]{1,0:T(8,128)(2,1)S(1)} %fusion.65), channel_id=1, source_target_pairs={{0,2},{1,3},{2,0},{3,1},{4,6},{5,7},{6,4},{7,5},{8,10},{9,11},{10,... | collective-permute-start | bytes 1179656 | tf_op jit(solution)/shard_map/ppermute | solution.py:27
  42.0 4.8 %collective-permute-start.4 = (bf16[16,768]{1,0:T(8,128)(2,1)S(1)}, bf16[16,768]{1,0:T(8,128)(2,1)S(1)}, u32[]{:S(2)}, u32[]{:S(2)}) collective-permute-start(bf16[16,768]{1,0:T(8,128)(2,1)S(1)} %pad_maximum_fusion.8), channel_id=1, source_target_pairs={{0,16},{8,24},{16,0},{24,8},{1,17},{9,25},{17,1},{25,9},{2,18},{10... | collective-permute-start | bytes 73736 | tf_op jit(solution)/shard_map/ppermute | solution.py:27
  46.8 28.7 %collective-permute-start.5 = (bf16[768,768]{1,0:T(8,128)(2,1)}, bf16[768,768]{1,0:T(8,128)(2,1)S(1)}, u32[]{:S(2)}, u32[]{:S(2)}) collective-permute-start(bf16[768,768]{1,0:T(8,128)(2,1)} %param.37), channel_id=1, source_target_pairs={{0,1},{1,0},{2,3},{3,2},{4,5},{5,4},{6,7},{7,6},{8,9},{9,8},{10,11... | collective-permute-start | bytes 3538952 | tf_op jit(solution)/shard_map/ppermute | solution.py:27
  46.8 19.4 %collective-permute-start.14 = (bf16[384,768]{1,0:T(8,128)(2,1)}, bf16[384,768]{1,0:T(8,128)(2,1)S(1)}, u32[]{:S(2)}, u32[]{:S(2)}) collective-permute-start(bf16[384,768]{1,0:T(8,128)(2,1)} %collective-permute-done.10), channel_id=1, source_target_pairs={{0,4},{4,0},{1,5},{5,1},{2,6},{6,2},{3,7},{7,3},{8,12},{12,8},{9,1... | collective-permute-start | bytes 1769480 | tf_op jit(solution)/shard_map/ppermute | solution.py:27
  52.4 13.8 %copy-start.24 = (bf16[768,384]{1,0:T(8,128)(2,1)}, bf16[768,384]{1,0:T(8,128)(2,1)S(1)}, u32[]{:S(2)}) copy-start(bf16[768,384]{1,0:T(8,128)(2,1)S(1)} %collective-permute-done.9) | copy-start | bytes 1769476
  52.4 29.2 %collective-permute-start.12 = (bf16[384,768]{1,0:T(8,128)(2,1)}, bf16[384,768]{1,0:T(8,128)(2,1)S(1)}, u32[]{:S(2)}, u32[]{:S(2)}) collective-permute-start(bf16[384,768]{1,0:T(8,128)(2,1)} %collective-permute-done.10), channel_id=1, source_target_pairs={{0,1},{1,0},{2,3},{3,2},{4,5},{5,4},{6,7},{7,6},{8,9},{9,8},{10,11... | collective-permute-start | bytes 1769480 | tf_op jit(solution)/shard_map/ppermute | solution.py:27
  59.3 16.2 %collective-permute-start.13 = (bf16[768,384]{1,0:T(8,128)(2,1)S(1)}, bf16[768,384]{1,0:T(8,128)(2,1)S(1)}, u32[]{:S(2)}, u32[]{:S(2)}) collective-permute-start(bf16[768,384]{1,0:T(8,128)(2,1)S(1)} %collective-permute-done.9), channel_id=1, source_target_pairs={{0,4},{4,0},{1,5},{5,1},{2,6},{6,2},{3,7},{7,3},{8,12},{12,8},{9,1... | collective-permute-start | bytes 1769480 | tf_op jit(solution)/shard_map/ppermute | solution.py:27
  63.2 32.8 %copy-start.2 = (f32[256,768]{1,0:T(8,128)}, f32[256,768]{1,0:T(8,128)S(1)}, u32[]{:S(2)}) copy-start(f32[256,768]{1,0:T(8,128)S(1)} %get-tuple-element.82) | copy-start | bytes 2359300
  63.2 32.8 %copy-start.42 = (f32[256]{0:T(256)}, f32[256]{0:T(256)S(1)}, u32[]{:S(2)}) copy-start(f32[256]{0:T(256)S(1)} %broadcast_multiply_fusion.5) | copy-start | bytes 3076
  63.5 32.5 %copy-start.49 = (f32[256]{0:T(256)}, f32[256]{0:T(256)S(1)}, u32[]{:S(2)}) copy-start(f32[256]{0:T(256)S(1)} %add_rsqrt_fusion.1) | copy-start | bytes 3076
  66.2 14.6 %copy-start.23 = (bf16[384,768]{1,0:T(8,128)(2,1)}, bf16[384,768]{1,0:T(8,128)(2,1)S(1)}, u32[]{:S(2)}) copy-start(bf16[384,768]{1,0:T(8,128)(2,1)S(1)} %collective-permute-done.14) | copy-start | bytes 1769476
  66.2 15.0 %collective-permute-start.11 = (bf16[768,384]{1,0:T(8,128)(2,1)S(1)}, bf16[768,384]{1,0:T(8,128)(2,1)S(1)}, u32[]{:S(2)}, u32[]{:S(2)}) collective-permute-start(bf16[768,384]{1,0:T(8,128)(2,1)S(1)} %collective-permute-done.9), channel_id=1, source_target_pairs={{0,1},{1,0},{2,3},{3,2},{4,5},{5,4},{6,7},{7,6},{8,9},{9,8},{10,11... | collective-permute-start | bytes 1769480 | tf_op jit(solution)/shard_map/ppermute | solution.py:27
  75.5 7.5 %collective-permute-start.16 = (bf16[384,768]{1,0:T(8,128)(2,1)S(1)}, bf16[384,768]{1,0:T(8,128)(2,1)S(1)}, u32[]{:S(2)}, u32[]{:S(2)}) collective-permute-start(bf16[384,768]{1,0:T(8,128)(2,1)S(1)} %collective-permute-done.14), channel_id=1, source_target_pairs={{0,1},{1,0},{2,3},{3,2},{4,5},{5,4},{6,7},{7,6},{8,9},{9,8},{10,11... | collective-permute-start | bytes 1769480 | tf_op jit(solution)/shard_map/ppermute | solution.py:27
  75.5 7.1 %collective-permute-start.15 = (bf16[768,384]{1,0:T(8,128)(2,1)S(1)}, bf16[768,384]{1,0:T(8,128)(2,1)S(1)}, u32[]{:S(2)}, u32[]{:S(2)}) collective-permute-start(bf16[768,384]{1,0:T(8,128)(2,1)S(1)} %collective-permute-done.13), channel_id=1, source_target_pairs={{0,1},{1,0},{2,3},{3,2},{4,5},{5,4},{6,7},{7,6},{8,9},{9,8},{10,11... | collective-permute-start | bytes 1769480 | tf_op jit(solution)/shard_map/ppermute | solution.py:27
  85.8 3.7 %collective-permute-start.17 = (bf16[1,768]{1,0:T(2,128)(2,1)S(1)}, bf16[1,768]{1,0:T(2,128)(2,1)S(1)}, u32[]{:S(2)}, u32[]{:S(2)}) collective-permute-start(bf16[1,768]{1,0:T(2,128)(2,1)S(1)} %convert_element_type.301), channel_id=1, source_target_pairs={{0,4},{4,0},{1,5},{5,1},{2,6},{6,2},{3,7},{7,3},{8,12},{12,8},{9,1... | collective-permute-start | bytes 4616 | tf_op jit(solution)/shard_map/ppermute | solution.py:27
  89.5 3.7 %collective-permute-start.18 = (bf16[2,768]{1,0:T(2,128)(2,1)S(1)}, bf16[2,768]{1,0:T(2,128)(2,1)S(1)}, u32[]{:S(2)}, u32[]{:S(2)}) collective-permute-start(bf16[2,768]{1,0:T(2,128)(2,1)S(1)} %pad_maximum_fusion.14), channel_id=1, source_target_pairs={{0,8},{8,0},{16,24},{24,16},{1,9},{9,1},{17,25},{25,17},{2,10},{10... | collective-permute-start | bytes 9224 | tf_op jit(solution)/shard_map/ppermute | solution.py:27
  91.3 15.4 %collective-permute-start.34 = (bf16[256,768]{1,0:T(8,128)(2,1)S(1)}, bf16[256,768]{1,0:T(8,128)(2,1)}, u32[]{:S(2)}, u32[]{:S(2)}) collective-permute-start(bf16[256,768]{1,0:T(8,128)(2,1)S(1)} %fusion.43), channel_id=1, source_target_pairs={{0,2},{1,3},{2,0},{3,1},{4,6},{5,7},{6,4},{7,5},{8,10},{9,11},{10,... | collective-permute-start | bytes 1179656 | tf_op jit(solution)/shard_map/ppermute | solution.py:27
  93.1 4.6 %collective-permute-start.19 = (bf16[4,768]{1,0:T(4,128)(2,1)S(1)}, bf16[4,768]{1,0:T(4,128)(2,1)S(1)}, u32[]{:S(2)}, u32[]{:S(2)}) collective-permute-start(bf16[4,768]{1,0:T(4,128)(2,1)S(1)} %pad_maximum_fusion.13), channel_id=1, source_target_pairs={{0,16},{8,24},{16,0},{24,8},{1,17},{9,25},{17,1},{25,9},{2,18},{10... | collective-permute-start | bytes 18440 | tf_op jit(solution)/shard_map/ppermute | solution.py:27
  99.6 19.1 %copy-start.5 = (f32[256,768]{1,0:T(8,128)S(1)}, f32[256,768]{1,0:T(8,128)}, u32[]{:S(2)}) copy-start(f32[256,768]{1,0:T(8,128)} %copy-done.4) | copy-start | bytes 2359300
  99.6 19.1 %copy-start.45 = (f32[256]{0:T(256)S(1)}, f32[256]{0:T(256)}, u32[]{:S(2)}) copy-start(f32[256]{0:T(256)} %copy-done.44) | copy-start | bytes 3076
  99.6 19.1 %copy-start.56 = (f32[256]{0:T(256)S(1)}, f32[256]{0:T(256)}, u32[]{:S(2)}) copy-start(f32[256]{0:T(256)} %copy-done.55) | copy-start | bytes 3076
  99.6 19.1 %copy-start.60 = (f32[256]{0:T(256)S(1)}, f32[256]{0:T(256)}, u32[]{:S(2)}) copy-start(f32[256]{0:T(256)} %compare_convert_fusion) | copy-start | bytes 3076
  99.6 19.4 %copy-start.54 = (f32[768]{0:T(1024)S(1)}, f32[768]{0:T(1024)}, u32[]{:S(2)}) copy-start(f32[768]{0:T(1024)} %param.42) | copy-start | bytes 9220
  99.8 4.7 %collective-permute-start.20 = (f32[4,1024]{1,0:T(4,128)S(1)}, f32[4,1024]{1,0:T(4,128)S(1)}, u32[]{:S(2)}, u32[]{:S(2)}) collective-permute-start(f32[4,1024]{1,0:T(4,128)S(1)} %slice.209), channel_id=1, source_target_pairs={{0,16},{8,24},{16,0},{24,8},{1,17},{9,25},{17,1},{25,9},{2,18},{10... | collective-permute-start | bytes 49160 | tf_op jit(solution)/shard_map/ppermute | solution.py:27
  104.8 4.0 %collective-permute-start.21 = (f32[2,1024]{1,0:T(2,128)S(1)}, f32[2,1024]{1,0:T(2,128)S(1)}, u32[]{:S(2)}, u32[]{:S(2)}) collective-permute-start(f32[2,1024]{1,0:T(2,128)S(1)} %slice.214), channel_id=1, source_target_pairs={{0,8},{8,0},{16,24},{24,16},{1,9},{9,1},{17,25},{25,17},{2,10},{10... | collective-permute-start | bytes 24584 | tf_op jit(solution)/shard_map/ppermute | solution.py:27
  108.8 51.7 %collective-permute-start.35 = (bf16[2,256,768]{2,1,0:T(8,128)(2,1)}, bf16[2,256,768]{2,1,0:T(8,128)(2,1)}, u32[]{:S(2)}, u32[]{:S(2)}) collective-permute-start(bf16[2,256,768]{2,1,0:T(8,128)(2,1)} %pad_maximum_fusion.4), channel_id=1, source_target_pairs={{0,1},{1,0},{2,3},{3,2},{4,5},{5,4},{6,7},{7,6},{8,9},{9,8},{10,11... | collective-permute-start | bytes 2359304 | tf_op jit(solution)/shard_map/ppermute | solution.py:27
  109.1 3.7 %collective-permute-start.22 = (f32[1,1024]{1,0:T(1,128)S(1)}, f32[1,1024]{1,0:T(1,128)S(1)}, u32[]{:S(2)}, u32[]{:S(2)}) collective-permute-start(f32[1,1024]{1,0:T(1,128)S(1)} %slice.219), channel_id=1, source_target_pairs={{0,4},{4,0},{1,5},{5,1},{2,6},{6,2},{3,7},{7,3},{8,12},{12,8},{9,1... | collective-permute-start | bytes 12296 | tf_op jit(solution)/shard_map/ppermute | solution.py:27
  139.0 12.1 %collective-permute-start.23 = (bf16[256,768]{1,0:T(8,128)(2,1)S(1)}, bf16[256,768]{1,0:T(8,128)(2,1)S(1)}, u32[]{:S(2)}, u32[]{:S(2)}) collective-permute-start(bf16[256,768]{1,0:T(8,128)(2,1)S(1)} %get-tuple-element.72), channel_id=1, source_target_pairs={{0,2},{1,3},{2,0},{3,1},{4,6},{5,7},{6,4},{7,5},{8,10},{9,11},{10,... | collective-permute-start | bytes 1179656 | tf_op jit(solution)/shard_map/ppermute | solution.py:27
  140.5 19.0 %collective-permute-start.36 = (bf16[256,768]{1,0:T(8,128)(2,1)S(1)}, bf16[256,768]{1,0:T(8,128)(2,1)S(1)}, u32[]{:S(2)}, u32[]{:S(2)}) collective-permute-start(bf16[256,768]{1,0:T(8,128)(2,1)S(1)} %get-tuple-element.75), channel_id=1, source_target_pairs={{0,2},{1,3},{2,0},{3,1},{4,6},{5,7},{6,4},{7,5},{8,10},{9,11},{10,... | collective-permute-start | bytes 1179656 | tf_op jit(solution)/shard_map/ppermute | solution.py:27
  152.0 13.1 %collective-permute-start.24 = (bf16[2,256,768]{2,1,0:T(8,128)(2,1)}, bf16[2,256,768]{2,1,0:T(8,128)(2,1)}, u32[]{:S(2)}, u32[]{:S(2)}) collective-permute-start(bf16[2,256,768]{2,1,0:T(8,128)(2,1)} %pad_maximum_fusion.3), channel_id=1, source_target_pairs={{0,1},{1,0},{2,3},{3,2},{4,5},{5,4},{6,7},{7,6},{8,9},{9,8},{10,11... | collective-permute-start | bytes 2359304 | tf_op jit(solution)/shard_map/ppermute | solution.py:27
  152.2 2.5 collective-permute-start.32
  154.7 4.3 %collective-permute-start.33 = (f32[7,768]{1,0:T(8,128)S(1)}, f32[7,768]{1,0:T(8,128)S(1)}, u32[]{:S(2)}, u32[]{:S(2)}) collective-permute-start(f32[7,768]{1,0:T(8,128)S(1)} %add.408), channel_id=1, source_target_pairs={{0,2},{1,3},{2,0},{3,1},{4,6},{5,7},{6,4},{7,5},{8,10},{9,11},{10,... | collective-permute-start | bytes 64520 | tf_op jit(solution)/shard_map/ppermute | solution.py:27
  160.5 21.9 %collective-permute-start.37 = (bf16[2,256,768]{2,1,0:T(8,128)(2,1)}, bf16[2,256,768]{2,1,0:T(8,128)(2,1)}, u32[]{:S(2)}, u32[]{:S(2)}) collective-permute-start(bf16[2,256,768]{2,1,0:T(8,128)(2,1)} %pad_maximum_fusion.5), channel_id=1, source_target_pairs={{0,1},{1,0},{2,3},{3,2},{4,5},{5,4},{6,7},{7,6},{8,9},{9,8},{10,11... | collective-permute-start | bytes 2359304 | tf_op jit(solution)/shard_map/ppermute | solution.py:27
  181.3 26.6 %collective-permute-start.27 = (bf16[384,768]{1,0:T(8,128)(2,1)S(1)}, bf16[384,768]{1,0:T(8,128)(2,1)S(1)}, u32[]{:S(2)}, u32[]{:S(2)}) collective-permute-start(bf16[384,768]{1,0:T(8,128)(2,1)S(1)} %constant_dynamic-slice_fusion.2), channel_id=1, source_target_pairs={{0,4},{4,0},{1,5},{5,1},{2,6},{6,2},{3,7},{7,3},{8,12},{12,8},{9,1... | collective-permute-start | bytes 1769480 | tf_op jit(solution)/shard_map/ppermute | solution.py:27
  187.6 11.0 %collective-permute-start.38 = (f32[9,768]{1,0:T(8,128)S(1)}, f32[9,768]{1,0:T(8,128)S(1)}, u32[]{:S(2)}, u32[]{:S(2)}) collective-permute-start(f32[9,768]{1,0:T(8,128)S(1)} %pad_maximum_fusion.6), channel_id=1, source_target_pairs={{0,4},{4,0},{1,5},{5,1},{2,6},{6,2},{3,7},{7,3},{8,12},{12,8},{9,1... | collective-permute-start | bytes 82952 | tf_op jit(solution)/shard_map/ppermute | solution.py:27
  190.1 21.2 %collective-permute-start.41 = (bf16[384,768]{1,0:T(8,128)(2,1)S(1)}, bf16[384,768]{1,0:T(8,128)(2,1)S(1)}, u32[]{:S(2)}, u32[]{:S(2)}) collective-permute-start(bf16[384,768]{1,0:T(8,128)(2,1)S(1)} %constant_dynamic-slice_fusion.1), channel_id=1, source_target_pairs={{0,4},{4,0},{1,5},{5,1},{2,6},{6,2},{3,7},{7,3},{8,12},{12,8},{9,1... | collective-permute-start | bytes 1769480 | tf_op jit(solution)/shard_map/ppermute | solution.py:27
  198.7 4.2 %collective-permute-start.39 = (f32[9,768]{1,0:T(8,128)S(1)}, f32[9,768]{1,0:T(8,128)S(1)}, u32[]{:S(2)}, u32[]{:S(2)}) collective-permute-start(f32[9,768]{1,0:T(8,128)S(1)} %fusion.132), channel_id=1, source_target_pairs={{0,8},{8,0},{16,24},{24,16},{1,9},{9,1},{17,25},{25,17},{2,10},{10... | collective-permute-start | bytes 82952 | tf_op jit(solution)/shard_map/ppermute | solution.py:27
  201.7 49.5 %collective-permute-start.25 = (bf16[2,256,768]{2,1,0:T(8,128)(2,1)S(1)}, bf16[2,256,768]{2,1,0:T(8,128)(2,1)S(1)}, u32[]{:S(2)}, u32[]{:S(2)}) collective-permute-start(bf16[2,256,768]{2,1,0:T(8,128)(2,1)S(1)} %slice.186), channel_id=1, source_target_pairs={{0,1},{1,0},{2,3},{3,2},{4,5},{5,4},{6,7},{7,6},{8,9},{9,8},{10,11... | collective-permute-start | bytes 2359304 | tf_op jit(solution)/shard_map/ppermute | solution.py:27
  202.8 5.0 %collective-permute-start.40 = (f32[9,768]{1,0:T(8,128)S(1)}, f32[9,768]{1,0:T(8,128)S(1)}, u32[]{:S(2)}, u32[]{:S(2)}) collective-permute-start(f32[9,768]{1,0:T(8,128)S(1)} %add.416), channel_id=1, source_target_pairs={{0,16},{8,24},{16,0},{24,8},{1,17},{9,25},{17,1},{25,9},{2,18},{10... | collective-permute-start | bytes 82952 | tf_op jit(solution)/shard_map/ppermute | solution.py:27
  205.6 17.6 %collective-permute-start.46 = (bf16[384,768]{1,0:T(8,128)(2,1)S(1)}, bf16[384,768]{1,0:T(8,128)(2,1)S(1)}, u32[]{:S(2)}, u32[]{:S(2)}) collective-permute-start(bf16[384,768]{1,0:T(8,128)(2,1)S(1)} %constant_dynamic-slice_fusion), channel_id=1, source_target_pairs={{0,4},{4,0},{1,5},{5,1},{2,6},{6,2},{3,7},{7,3},{8,12},{12,8},{9,1... | collective-permute-start | bytes 1769480 | tf_op jit(solution)/shard_map/ppermute | solution.py:27
  208.1 18.6 %collective-permute-start.28 = (bf16[384,768]{1,0:T(8,128)(2,1)S(1)}, bf16[384,768]{1,0:T(8,128)(2,1)S(1)}, u32[]{:S(2)}, u32[]{:S(2)}) collective-permute-start(bf16[384,768]{1,0:T(8,128)(2,1)S(1)} %fusion.22), channel_id=1, source_target_pairs={{0,8},{24,16},{1,9},{25,17},{2,10},{26,18},{3,11},{27,19},{4,12},{... | collective-permute-start | bytes 1769480 | tf_op jit(solution)/shard_map/ppermute | solution.py:55
  211.4 26.0 %collective-permute-start.42 = (bf16[384,768]{1,0:T(8,128)(2,1)S(1)}, bf16[384,768]{1,0:T(8,128)(2,1)S(1)}, u32[]{:S(2)}, u32[]{:S(2)}) collective-permute-start(bf16[384,768]{1,0:T(8,128)(2,1)S(1)} %fusion.23), channel_id=1, source_target_pairs={{0,8},{24,16},{1,9},{25,17},{2,10},{26,18},{3,11},{27,19},{4,12},{... | collective-permute-start | bytes 1769480 | tf_op jit(solution)/shard_map/ppermute | solution.py:55
  223.4 24.0 %collective-permute-start.47 = (bf16[384,768]{1,0:T(8,128)(2,1)S(1)}, bf16[384,768]{1,0:T(8,128)(2,1)S(1)}, u32[]{:S(2)}, u32[]{:S(2)}) collective-permute-start(bf16[384,768]{1,0:T(8,128)(2,1)S(1)} %fusion.24), channel_id=1, source_target_pairs={{0,8},{24,16},{1,9},{25,17},{2,10},{26,18},{3,11},{27,19},{4,12},{... | collective-permute-start | bytes 1769480 | tf_op jit(solution)/shard_map/ppermute | solution.py:55
  226.9 21.4 %collective-permute-start.29 = (bf16[384,768]{1,0:T(8,128)(2,1)S(1)}, bf16[384,768]{1,0:T(8,128)(2,1)S(1)}, u32[]{:S(2)}, u32[]{:S(2)}) collective-permute-start(bf16[384,768]{1,0:T(8,128)(2,1)S(1)} %add_convert_fusion.5), channel_id=1, source_target_pairs={{8,16},{16,8},{9,17},{17,9},{10,18},{18,10},{11,19},{19,11},{12,20... | collective-permute-start | bytes 1769480 | tf_op jit(solution)/shard_map/ppermute | solution.py:57
  237.7 12.1 %collective-permute-start.43 = (bf16[384,768]{1,0:T(8,128)(2,1)S(1)}, bf16[384,768]{1,0:T(8,128)(2,1)S(1)}, u32[]{:S(2)}, u32[]{:S(2)}) collective-permute-start(bf16[384,768]{1,0:T(8,128)(2,1)S(1)} %add_convert_fusion.3), channel_id=1, source_target_pairs={{8,16},{16,8},{9,17},{17,9},{10,18},{18,10},{11,19},{19,11},{12,20... | collective-permute-start | bytes 1769480 | tf_op jit(solution)/shard_map/ppermute | solution.py:57
  247.6 5.4 %collective-permute-start.48 = (bf16[384,768]{1,0:T(8,128)(2,1)S(1)}, bf16[384,768]{1,0:T(8,128)(2,1)S(1)}, u32[]{:S(2)}, u32[]{:S(2)}) collective-permute-start(bf16[384,768]{1,0:T(8,128)(2,1)S(1)} %add_convert_fusion.1), channel_id=1, source_target_pairs={{8,16},{16,8},{9,17},{17,9},{10,18},{18,10},{11,19},{19,11},{12,20... | collective-permute-start | bytes 1769480 | tf_op jit(solution)/shard_map/ppermute | solution.py:57
  248.5 21.3 %collective-permute-start.30 = (bf16[384,768]{1,0:T(8,128)(2,1)S(1)}, bf16[384,768]{1,0:T(8,128)(2,1)S(1)}, u32[]{:S(2)}, u32[]{:S(2)}) collective-permute-start(bf16[384,768]{1,0:T(8,128)(2,1)S(1)} %add_convert_fusion.4), channel_id=1, source_target_pairs={{8,0},{16,24},{9,1},{17,25},{10,2},{18,26},{11,3},{19,27},{12,4},{... | collective-permute-start | bytes 1769480 | tf_op jit(solution)/shard_map/ppermute | solution.py:59
  250.0 32.5 %collective-permute-start.44 = (bf16[384,768]{1,0:T(8,128)(2,1)S(1)}, bf16[384,768]{1,0:T(8,128)(2,1)S(1)}, u32[]{:S(2)}, u32[]{:S(2)}) collective-permute-start(bf16[384,768]{1,0:T(8,128)(2,1)S(1)} %add_convert_fusion.2), channel_id=1, source_target_pairs={{8,0},{16,24},{9,1},{17,25},{10,2},{18,26},{11,3},{19,27},{12,4},{... | collective-permute-start | bytes 1769480 | tf_op jit(solution)/shard_map/ppermute | solution.py:59
  251.4 32.7 %collective-permute-start.26 = (bf16[256,768]{1,0:T(8,128)(2,1)S(1)}, bf16[256,768]{1,0:T(8,128)(2,1)S(1)}, u32[]{:S(2)}, u32[]{:S(2)}) collective-permute-start(bf16[256,768]{1,0:T(8,128)(2,1)S(1)} %fusion.67), channel_id=1, source_target_pairs={{0,2},{1,3},{2,0},{3,1},{4,6},{5,7},{6,4},{7,5},{8,10},{9,11},{10,... | collective-permute-start | bytes 1179656 | tf_op jit(solution)/shard_map/ppermute | solution.py:27
  253.1 31.0 %copy-start.38 = (bf16[256,256]{1,0:T(8,128)(2,1)S(1)}, bf16[256,256]{1,0:T(8,128)(2,1)}, u32[]{:S(2)}) copy-start(bf16[256,256]{1,0:T(8,128)(2,1)} %get-tuple-element.36) | copy-start | bytes 393220
  253.1 38.4 %collective-permute-start.49 = (bf16[384,768]{1,0:T(8,128)(2,1)S(1)}, bf16[384,768]{1,0:T(8,128)(2,1)S(1)}, u32[]{:S(2)}, u32[]{:S(2)}) collective-permute-start(bf16[384,768]{1,0:T(8,128)(2,1)S(1)} %add_convert_fusion), channel_id=1, source_target_pairs={{8,0},{16,24},{9,1},{17,25},{10,2},{18,26},{11,3},{19,27},{12,4},{... | collective-permute-start | bytes 1769480 | tf_op jit(solution)/shard_map/ppermute | solution.py:59
  269.9 23.7 %collective-permute-start.31 = (bf16[384,768]{1,0:T(8,128)(2,1)S(1)}, bf16[384,768]{1,0:T(8,128)(2,1)S(1)}, u32[]{:S(2)}, u32[]{:S(2)}) collective-permute-start(bf16[384,768]{1,0:T(8,128)(2,1)S(1)} %broadcast_select_fusion.2), channel_id=1, source_target_pairs={{0,4},{4,0},{1,5},{5,1},{2,6},{6,2},{3,7},{7,3},{8,12},{12,8},{9,1... | collective-permute-start | bytes 1769480 | tf_op jit(solution)/shard_map/ppermute | solution.py:27
  282.6 11.2 %collective-permute-start.45 = (bf16[384,768]{1,0:T(8,128)(2,1)S(1)}, bf16[384,768]{1,0:T(8,128)(2,1)S(1)}, u32[]{:S(2)}, u32[]{:S(2)}) collective-permute-start(bf16[384,768]{1,0:T(8,128)(2,1)S(1)} %broadcast_select_fusion.1), channel_id=1, source_target_pairs={{0,4},{4,0},{1,5},{5,1},{2,6},{6,2},{3,7},{7,3},{8,12},{12,8},{9,1... | collective-permute-start | bytes 1769480 | tf_op jit(solution)/shard_map/ppermute | solution.py:27
  291.7 13.5 %collective-permute-start.50 = (bf16[384,768]{1,0:T(8,128)(2,1)S(1)}, bf16[384,768]{1,0:T(8,128)(2,1)S(1)}, u32[]{:S(2)}, u32[]{:S(2)}) collective-permute-start(bf16[384,768]{1,0:T(8,128)(2,1)S(1)} %broadcast_select_fusion), channel_id=1, source_target_pairs={{0,4},{4,0},{1,5},{5,1},{2,6},{6,2},{3,7},{7,3},{8,12},{12,8},{9,1... | collective-permute-start | bytes 1769480 | tf_op jit(solution)/shard_map/ppermute | solution.py:27
  (56 other events, 268.5 us)

commit v3 on v1

v3 whole, which is shorter than its diff:
```python
import math

import jax
import jax.numpy as jnp
from jax import lax
from jax.experimental import pallas as pl
from jax.experimental.pallas import tpu as pltpu
from jax.sharding import PartitionSpec as P

HEAD = 64
eps = 1e-12
inv_temp = 20.0
loss_scale = 256.0
low = jnp.bfloat16
full = jnp.float32
LANES = 128


def dot(a, b, dims=((1,), (0,))):
    return lax.dot_general(a, b, (dims, ((), ())), preferred_element_type=full)


def swap(array, axis, stride):
    size = lax.axis_size(axis)
    return lax.ppermute(array, axis, [(i, i ^ stride) for i in range(size)])


def strides(axis):
    size = lax.axis_size(axis)
    assert size & (size - 1) == 0
    return [1 << k for k in range(size.bit_length() - 1)]


def plus(part, other):
    return (part.astype(full) + other.astype(full)).astype(low)


def carried(rows):
    high = lax.reduce_precision(rows, 8, 7)
    return jnp.concatenate([high, rows - high]).astype(low)


def plus_carried(part, other, rows):
    ends = [a[rows:].astype(full) for a in (part, other)]
    count = ends[0].shape[0] // 2
    total = sum(e[:count] + e[count:] for e in ends)
    return jnp.concatenate([plus(part[:rows], other[:rows]), carried(total)])


def inward(part):
    return lax.ppermute(part, "dp", [(0, 1), (3, 2)])


def across(part):
    return lax.ppermute(part, "dp", [(1, 2), (2, 1)])


def outward(part):
    z = lax.axis_index("dp")
    outer = lax.ppermute(part, "dp", [(1, 0), (2, 3)])
    return jnp.where((z == 0) | (z == 3), outer, part)


def ordered(total, other, f):
    return (jnp.where(f == 0, total, other), jnp.where(f == 0, other, total))


def norm_parts(resid):
    center = resid - jnp.mean(resid, axis=-1, keepdims=True)
    rstd = lax.rsqrt(jnp.mean(center * center, axis=-1, keepdims=True) + eps)
    return (center * rstd, rstd)


def norm_backward(scaled, normed, rstd):
    inner = jnp.mean(scaled, axis=-1, keepdims=True)
    along = jnp.mean(scaled * normed, axis=-1, keepdims=True)
    return rstd * (scaled - inner - normed * along)


def gelu_parts(pre):
    cdf = 0.5 * (1.0 + lax.erf(pre * math.sqrt(0.5)))
    slope = cdf + pre * (jnp.exp(-0.5 * pre * pre) * (1.0 / math.sqrt(2.0 * math.pi)))
    return (pre * cdf, slope)


def relative(b):
    return ((b & 1) << 1) | (b >> 1)


def attend_kernel(
    place_in, lens, mask, tokens, wq, wk, wv, wo, bq, bv, compact_out, q_out, k_out, v_out, p_out, ctx_out, near_out, away_out, table_out, count_out
):
    b = pl.program_id(0)
    crop = place_in[0] ^ relative(b)
    length = mask.shape[-1]
    crop_len = lens[crop]
    lane = lax.broadcasted_iota(jnp.int32, (1, length), 1)
    kept = jnp.where(((mask[pl.ds(crop, 1), :] == 1) | (lane == 0)) & (lane < crop_len), 1.0, 0.0)
    rows = lax.broadcasted_iota(jnp.int32, (length, length), 0)
    cols = lax.broadcasted_iota(jnp.int32, (length, length), 1)
    upto = jnp.where(rows <= cols, 1.0, 0.0).astype(low)
    rank = dot(jnp.broadcast_to(kept, (8, length)).astype(low), upto)[0:1]
    place = jnp.where(kept > 0.0, rank - 1.0, -1.0)
    table = jnp.where(place == rows.astype(full), 1.0, 0.0).astype(low)
    count = jnp.sum(kept)

    @pl.when(b == 0)
    def _():
        table_out[...] = table
        count_out[...] = jnp.full(count_out.shape, count, full)

    compact = dot(table, tokens[0]).astype(low)
    compact_out[0] = compact
    query = (dot(compact, wq[...], ((1,), (1,))) + bq[...]).astype(low)
    keys = dot(compact, wk[...], ((1,), (1,))).astype(low)
    values = (dot(compact, wv[...], ((1,), (1,))) + bv[...]).astype(low)
    q_out[0], k_out[0], v_out[0] = query, keys, values
    live = lane.astype(full) < count
    contexts = []
    for h in range(query.shape[1] // HEAD):
        span = slice(h * HEAD, (h + 1) * HEAD)
        scores = dot(query[:, span], keys[:, span], ((1,), (1,))) * (1.0 / math.sqrt(HEAD))
        scores = jnp.where(live, scores, -1e30)
        expo = jnp.exp(scores - jnp.max(scores, axis=1, keepdims=True))
        probs = (expo / jnp.sum(expo, axis=1, keepdims=True)).astype(low)
        p_out[0, h] = probs
        contexts.append(dot(probs, values[:, span]).astype(low))
    context = jnp.concatenate(contexts, axis=1)
    ctx_out[0] = context
    part = dot(context, wo[...]).astype(low)

    @pl.when(b < 2)
    def _():
        near_out[0] = part

    @pl.when(b >= 2)
    def _():
        away_out[0] = part


def attend(tokens, keep_mask, crop_len, place, wq, wk, wv, wo, bq, bv):
    seqs, length, width = tokens.shape
    mine = wq.shape[0]
    heads = mine // HEAD

    def const(*shape):
        return pl.BlockSpec(shape, lambda b, *_: (0,) * len(shape))

    def per(*shape):
        return pl.BlockSpec((1, *shape), lambda b, *_: (b,) + (0,) * len(shape))

    S = jax.ShapeDtypeStruct
    return pl.pallas_call(
        attend_kernel,
        grid_spec=pltpu.PrefetchScalarGridSpec(
            num_scalar_prefetch=2,
            grid=(seqs,),
            in_specs=[
                const(seqs, length),
                pl.BlockSpec((1, length, width), lambda b, place, lens: (place[0] ^ relative(b), 0, 0)),
                const(mine, width),
                const(mine, width),
                const(mine, width),
                const(mine, width),
                const(1, mine),
                const(1, mine),
            ],
            out_specs=[
                per(length, width),
                per(length, mine),
                per(length, mine),
                per(length, mine),
                per(heads, length, length),
                per(length, mine),
                pl.BlockSpec((1, length, width), lambda b, *_: (jnp.minimum(b, 1), 0, 0)),
                pl.BlockSpec((1, length, width), lambda b, *_: (jnp.maximum(b - 2, 0), 0, 0)),
                const(length, length),
                const(8, LANES),
            ],
        ),
        out_shape=[
            S((seqs, length, width), low),
            S((seqs, length, mine), low),
            S((seqs, length, mine), low),
            S((seqs, length, mine), low),
            S((seqs, heads, length, length), low),
            S((seqs, length, mine), low),
            S((2, length, width), low),
            S((2, length, width), low),
            S((length, length), low),
            S((8, LANES), full),
        ],
        name="attend",
    )(place, crop_len, keep_mask, tokens, wq, wk, wv, wo, bq[None], bv[None])


def attend_back_kernel(
    place, g0, g1, g2, g3, compact, q_in, k_in, v_in, p_in, ctx_in, wq, wk, wv, wo, near_out, away_out, *refs
):
    b = pl.program_id(0)
    qk_kept, qk_sent, vo_kept, vo_sent, qb_out, vb_out, grad_s, weights, qb, vb = refs

    @pl.when(b == 0)
    def _():
        weights[...] = jnp.zeros_like(weights)
        qb[...] = jnp.zeros_like(qb)
        vb[...] = jnp.zeros_like(vb)

    for i, g in enumerate((g0, g1, g2, g3)):

        @pl.when(b == i)
        def _(g=g):
            grad_s[...] = g[...]

    scale = 1.0 / math.sqrt(HEAD)
    grad = grad_s[...]
    mine = wq.shape[0]
    query, keys, values = q_in[0], k_in[0], v_in[0]
    context_grad = dot(grad, wo[...], ((1,), (1,))).astype(low)
    query_grads, keys_grads, values_grads = [], [], []
    for h in range(mine // HEAD):
        span = slice(h * HEAD, (h + 1) * HEAD)
        probs = p_in[0, h]
        wide = probs.astype(full)
        probs_grad = dot(context_grad[:, span], values[:, span], ((1,), (1,)))
        inner = jnp.sum(wide * probs_grad, axis=1, keepdims=True)
        score_grad = (wide * (probs_grad - inner)).astype(low)
        query_grads.append((dot(score_grad, keys[:, span]) * scale).astype(low))
        keys_grads.append((dot(score_grad, query[:, span], ((0,), (0,))) * scale).astype(low))
        values_grads.append(dot(probs, context_grad[:, span], ((0,), (0,))).astype(low))
    query_grad = jnp.concatenate(query_grads, axis=1)
    keys_grad = jnp.concatenate(keys_grads, axis=1)
    values_grad = jnp.concatenate(values_grads, axis=1)
    every = jnp.concatenate([query_grad, keys_grad, values_grad], axis=1)
    weights[: 3 * mine] += dot(every, compact[0], ((0,), (0,)))
    weights[3 * mine :] += dot(ctx_in[0], grad, ((0,), (0,)))
    qb[...] += jnp.sum(query_grad.astype(full), axis=0, keepdims=True)
    vb[...] += jnp.sum(values_grad.astype(full), axis=0, keepdims=True)
    back = dot(query_grad, wq[...])
    back += dot(keys_grad, wk[...])
    back += dot(values_grad, wv[...])

    @pl.when(b < 2)
    def _():
        near_out[0] = back.astype(low)

    @pl.when(b >= 2)
    def _():
        away_out[0] = back.astype(low)

    @pl.when(b == pl.num_programs(0) - 1)
    def _():
        f = place[1] >> 1
        for target, block in ((qk_kept, f), (qk_sent, 1 - f), (vo_kept, 2 + f), (vo_sent, 3 - f)):
            target[...] = weights[pl.ds(pl.multiple_of(block * mine, mine), mine), :].astype(low)
        qb_out[...] = qb[...]
        vb_out[...] = vb[...]


def attend_back(place, grads, compact, query, keys, values, probs, context, wq, wk, wv, wo):
    seqs, length, width = compact.shape
    mine = wq.shape[0]
    heads = mine // HEAD

    def const(*shape):
        return pl.BlockSpec(shape, lambda b, *_: (0,) * len(shape))

    def per(*shape):
        return pl.BlockSpec((1, *shape), lambda b, *_: (b,) + (0,) * len(shape))

    S = jax.ShapeDtypeStruct
    return pl.pallas_call(
        attend_back_kernel,
        grid_spec=pltpu.PrefetchScalarGridSpec(
            num_scalar_prefetch=1,
            grid=(seqs,),
            in_specs=[const(length, width)] * 4
            + [
                per(length, width),
                per(length, mine),
                per(length, mine),
                per(length, mine),
                per(heads, length, length),
                per(length, mine),
                const(mine, width),
                const(mine, width),
                const(mine, width),
                const(mine, width),
            ],
            out_specs=[
                pl.BlockSpec((1, length, width), lambda b, *_: (jnp.minimum(b, 1), 0, 0)),
                pl.BlockSpec((1, length, width), lambda b, *_: (jnp.maximum(b - 2, 0), 0, 0)),
                const(mine, width),
                const(mine, width),
                const(mine, width),
                const(mine, width),
                const(1, mine),
                const(1, mine),
            ],
            scratch_shapes=[
                pltpu.VMEM((length, width), low),
                pltpu.VMEM((4 * mine, width), full),
                pltpu.VMEM((1, mine), full),
                pltpu.VMEM((1, mine), full),
            ],
        ),
        out_shape=[S((2, length, width), low)] * 2 + [S((mine, width), low)] * 4 + [S((1, mine), full)] * 2,
        name="attend_back",
    )(place, *grads, compact, query, keys, values, probs, context, wq, wk, wv, wo)


WHOLE, QUARTERS = 4, 8


def weight_copies(place, wholes, quarters, up, down, sems):
    rows = quarters[0].shape[0] // 2
    shards = []
    for s in range(2):
        shards.append([(wholes[2 * s], up.at[s]), (wholes[2 * s + 1], down.at[s])])
    for s in range(2):
        copies = []
        for i, flip in enumerate((0, 2, 1, 3)):
            spot = pl.ds(pl.multiple_of((place[1] ^ flip) * rows, rows), rows)
            piece = quarters[4 * s + i]
            copies.append((piece.at[pl.ds(0, rows)], up.at[2 + s, spot]))
            copies.append((piece.at[pl.ds(rows, rows)], down.at[2 + s, spot]))
        shards.append(copies)
    number, made = 0, []
    for copies in shards:
        row = []
        for source, target in copies:
            row.append(pltpu.make_async_copy(source, target, sems.at[number]))
            number += 1
        made.append(row)
    return made


def ffn_kernel(place, *refs):
    wholes, quarters = refs[:WHOLE], refs[WHOLE : WHOLE + QUARTERS]
    middle, biases, down_bias, gain, shift, counts = refs[12:18]
    slopes_out, normed_out, rows_out, output_out, sums_out, pooled_out = refs[18:24]
    up, down, sems = refs[24:]
    shards = weight_copies(place, wholes, quarters, up, down, sems)
    for copies in shards:
        for copy in copies:
            copy.start()
    length, width = middle.shape
    mid = middle[...]
    mid_low = mid.astype(low)
    total = mid + down_bias[...]
    for s, copies in enumerate(shards):
        for copy in copies:
            copy.wait()
        hidden, slope = gelu_parts(dot(mid_low, up[s]) + biases[s : s + 1])
        slopes_out[s] = slope.astype(low)
        total += dot(hidden.astype(low), down[s])
    normed, rstd = norm_parts(total)
    normed_out[...] = normed
    output_out[0] = (normed * gain[...] + shift[...]).astype(low)
    count = counts[0:1, 0:1]
    live = jnp.where(lax.broadcasted_iota(jnp.int32, (length, 1), 0).astype(full) < count, 1.0, 0.0)
    factor = rstd * live
    rows_out[:, :width] = normed.astype(low)
    lane = lax.broadcasted_iota(jnp.int32, (length, LANES), 1)
    first = factor.astype(low).astype(full)
    rows_out[:, width:] = jnp.where(lane == 0, first, jnp.where(lane == 1, factor - first, 0.0)).astype(low)
    live_sum = jnp.sum(normed * live, axis=0, keepdims=True)
    sums_out[...] = live_sum
    pooled_out[:, :width] = (live_sum / count * gain[...] + shift[...]).astype(low)
    pooled_out[:, width:] = jnp.broadcast_to(count, (1, LANES)).astype(low)


def ffn_back_kernel(place, *refs):
    wholes, quarters = refs[:WHOLE], refs[WHOLE : WHOLE + QUARTERS]
    slopes, vector, normed_two, rows, normed_one, rstd_one, gain = refs[12:19]
    attn_out, one_out, sums_out = refs[19:22]
    up, down, sems = refs[22:]
    shards = weight_copies(place, wholes, quarters, up, down, sems)
    for copies in shards:
        for copy in copies:
            copy.start()
    length, width = normed_two.shape
    factor = rows[:, width : width + 1].astype(full) + rows[:, width + 1 : width + 2].astype(full)
    two_grad = norm_backward(jnp.broadcast_to(vector[...], (length, width)), normed_two[...], factor)
    ffn_grad = two_grad.astype(low)
    total = two_grad
    for s, copies in enumerate(shards):
        for copy in copies:
            copy.wait()
        grad = (slopes[s].astype(full) * dot(ffn_grad, down[s], ((1,), (1,)))).astype(low)
        total += dot(grad, up[s], ((1,), (1,)))
    normed = normed_one[...]
    one_grad = norm_backward(total * gain[...], normed, rstd_one[:, 0:1])
    one_out[...] = one_grad
    attn_grad = one_grad.astype(low)
    attn_out[...] = attn_grad
    sums_out[0:1] = jnp.sum(total * normed, axis=0, keepdims=True)
    sums_out[1:2] = jnp.sum(total, axis=0, keepdims=True)
    sums_out[2:3] = jnp.sum(ffn_grad.astype(full), axis=0, keepdims=True)
    sums_out[3:4] = jnp.sum(attn_grad.astype(full), axis=0, keepdims=True)
    sums_out[4:8] = jnp.zeros((4, width), full)


def with_weights(kernel, name, place, wholes, quarters, operands, outs):
    width, hidden = wholes[0].shape
    everywhere = pl.BlockSpec(memory_space=pl.ANY)
    return pl.pallas_call(
        kernel,
        grid_spec=pltpu.PrefetchScalarGridSpec(
            num_scalar_prefetch=1,
            grid=(1,),
            in_specs=[everywhere] * (WHOLE + QUARTERS)
            + [pl.BlockSpec(a.shape, lambda b, *_, rank=a.ndim: (0,) * rank) for a in operands],
            out_specs=[pl.BlockSpec(o.shape, lambda b, *_, rank=len(o.shape): (0,) * rank) for o in outs],
            scratch_shapes=[
                pltpu.VMEM((4, width, hidden), low),
                pltpu.VMEM((4, hidden, width), low),
                pltpu.SemaphoreType.DMA((20,)),
            ],
        ),
        out_shape=outs,
        name=name,
    )(place, *wholes, *quarters, *operands)


def ffn_weights_kernel(*refs):
    middles, rows = refs[:8], refs[8:16]
    vectors, up, bias, down = refs[16:20]
    down_out, up_out, bias_out = refs[20:]
    width = middles[0].shape[1]
    down_sum = up_sum = bias_sum = None
    for i in range(8):
        middle = middles[i][...]
        hidden, slope = gelu_parts(dot(middle, up[...]) + bias[...])
        normed = rows[i][:, :width].astype(full)
        factor = rows[i][:, width : width + 1].astype(full) + rows[i][:, width + 1 : width + 2].astype(full)
        vector = vectors[i : i + 1]
        along = jnp.mean(normed * vector, axis=1, keepdims=True)
        ffn_grad = (factor * ((vector - jnp.mean(vector, axis=1, keepdims=True)) - normed * along)).astype(low)
        pre_grad = (slope * dot(ffn_grad, down[...], ((1,), (1,)))).astype(low)
        one = dot(hidden.astype(low), ffn_grad, ((0,), (0,)))
        two = dot(middle, pre_grad, ((0,), (0,)))
        three = jnp.sum(pre_grad.astype(full), axis=0, keepdims=True)
        down_sum, up_sum, bias_sum = (one, two, three) if i == 0 else (down_sum + one, up_sum + two, bias_sum + three)
    down_out[...] = down_sum.astype(low)
    up_out[...] = up_sum.astype(low)
    bias_out[...] = bias_sum


def ffn_weights(middles, rows, vectors, up, bias, down):
    half, width = down.shape
    S = jax.ShapeDtypeStruct
    return pl.pallas_call(
        ffn_weights_kernel,
        out_shape=[S((half, width), low), S((width, half), low), S((1, half), full)],
        name="ffn_weights",
    )(*middles, *rows, vectors, up, bias, down)


def contrast(pooled, key_queue, gathered, returned):
    width = key_queue.shape[1]
    queries = jnp.concatenate([pooled, swap(pooled, "fsdp", 1)])
    both = queries
    queries = gathered(queries)
    for stride in strides("dp"):
        queries = jnp.concatenate([queries, swap(queries, "dp", stride)])
    logits = dot(queries[:, :width], key_queue, ((1,), (1,))) * inv_temp
    top = jnp.max(logits, axis=1, keepdims=True)
    expo = jnp.exp(logits - top)
    total = jnp.sum(expo, axis=1, keepdims=True)
    rows = dot(expo.astype(low), key_queue)
    state = jnp.concatenate([rows, jnp.broadcast_to(top, (top.shape[0], LANES)), jnp.broadcast_to(total, (top.shape[0], LANES))], axis=1)
    for axis, stride in [("dp", s) for s in reversed(strides("dp"))] + [("fsdp", 1)]:
        half = state.shape[0] // 2
        if axis == "fsdp":
            kept, other = state, swap(jnp.concatenate([state[1:2], state[0:1]]), axis, stride)
        else:
            if stride == 1:
                state = returned(state)
            kept, other = state[:half], swap(state[half:], axis, stride)
        top = jnp.maximum(kept[:, width : width + 1], other[:, width : width + 1])
        summed = kept * jnp.exp(kept[:, width : width + 1] - top) + other * jnp.exp(other[:, width : width + 1] - top)
        state = jnp.concatenate([summed[:, :width], jnp.broadcast_to(top, (top.shape[0], LANES)), summed[:, width + LANES :]], axis=1)
    return (state[:, width : width + 1], state[:, width + LANES : width + LANES + 1], state[:, :width], both)


def per_device(
    tokens,
    keep_mask,
    crop_len,
    pos_index,
    pos_keys,
    key_queue,
    query_weight,
    query_bias,
    key_weight,
    value_weight,
    value_bias,
    out_weight,
    out_bias,
    norm_gain,
    norm_shift,
    up_weight,
    up_bias,
    down_weight,
    down_bias,
    final_gain,
    final_shift,
):
    seqs, length, width = tokens.shape
    hidden = up_weight.shape[1]
    assert seqs == 4 and lax.axis_size("tensor") == 4 and lax.axis_size("fsdp") == 2 and hidden == width
    member = lax.axis_index("tensor")
    f = lax.axis_index("fsdp")
    z = lax.axis_index("dp")
    group = lax.axis_index(("dp", "fsdp"))
    devices = seqs * lax.axis_size("dp") * lax.axis_size("fsdp")
    mine = query_weight.shape[1]
    tie = lax.optimization_barrier
    kind = f * 2 + (z & 1)
    place = jnp.stack([member, kind]).astype(jnp.int32)
    quarter, half = hidden // 4, hidden // 2

    def quarter_of(which):
        return jnp.concatenate([lax.dynamic_slice_in_dim(w, which * quarter, quarter, 0) for w in (up_weight, down_weight)])

    piece_y = swap(quarter_of(kind), "tensor", 2)
    piece_d = swap(quarter_of(kind ^ 3), "tensor", 2)
    bias_pair = jnp.concatenate([up_bias[None], swap(up_bias[None], "tensor", 1)])
    biases = jnp.concatenate([bias_pair, swap(bias_pair, "tensor", 2)])
    wholes = [up_weight, down_weight, swap(up_weight, "tensor", 1), swap(down_weight, "tensor", 1)]
    up_half = lax.dynamic_slice_in_dim(up_weight, f * half, half, 1)
    down_half = lax.dynamic_slice_in_dim(down_weight, f * half, half, 0)
    bias_half = lax.dynamic_slice_in_dim(up_bias[None], f * half, half, 1)

    known = jnp.concatenate([pos_keys, swap(pos_keys, "fsdp", 1)])
    compact, query, keys, values, probs, context, near, away, table, counts = attend(
        tokens, keep_mask, crop_len, place, query_weight.T, key_weight.T, value_weight.T, out_weight, query_bias, value_bias
    )
    near, away, piece_y, known = tie((near, away, piece_y, known))
    other = swap(away, "tensor", 1)
    piece_x = swap(piece_y, "fsdp", 1)
    piece_z = swap(piece_y, "dp", 1)
    share = pos_keys.shape[0]
    spot = jnp.arange(devices, dtype=jnp.int32)[None]
    mates = jnp.stack([group, group ^ 1]) * share + member
    wanted = jnp.sum(jnp.where(spot == mates[:, None], pos_index[None], 0), axis=1, keepdims=True)
    chosen = jnp.where(((spot // share) ^ group) * share + spot % share == wanted, 1.0, 0.0).astype(low)
    sent, piece_d, biases, chosen = tie((plus(near[1], other[1]), piece_d, biases, chosen))
    hops = strides("dp")
    for stride in hops[:-1]:
        known = jnp.concatenate([known, swap(known, "dp", stride)])
    attn_out = near[0].astype(full) + other[0].astype(full) + swap(sent, "tensor", 2).astype(full)
    attn_out, piece_x, piece_z, known = tie((attn_out, piece_x, piece_z, known))

    normed_one, rstd_one = norm_parts(compact[0].astype(full) + attn_out + out_bias)
    rstd_one = jnp.broadcast_to(rstd_one, (length, LANES))
    middle = normed_one * norm_gain + norm_shift
    middle_low = middle.astype(low)
    quarters = [piece_y, piece_x, piece_z, piece_d]
    quarters = quarters + [swap(p, "tensor", 1) for p in quarters]
    S = jax.ShapeDtypeStruct
    slopes, normed_two, rows, output, live_sum, pooled = with_weights(
        ffn_kernel,
        "ffn",
        place,
        wholes,
        quarters,
        [middle, biases, down_bias[None], final_gain[None], final_shift[None], counts],
        [
            S((4, length, hidden), low),
            S((length, width), full),
            S((length, width + LANES), low),
            S((1, length, width), low),
            S((1, width), full),
            S((1, width + LANES), low),
        ],
    )

    middle_x, middle_y = swap(middle_low, "fsdp", 1), swap(middle_low, "tensor", 2)
    known = jnp.concatenate([known, swap(known, "dp", hops[-1])])
    pooled, middle_x, middle_y, known, rstd_one = tie((pooled, middle_x, middle_y, known, rstd_one))
    pairs = {}

    def gathered(queries):
        queries, row_own, mid = tie((queries, rows, middle_x))
        pairs["x"], pairs["y"] = swap(row_own, "fsdp", 1), swap(row_own, "tensor", 2)
        pairs["mid"] = swap(mid, "tensor", 2)
        return queries

    def returned(state):
        state, pairs["x"], pairs["y"], pairs["mid"] = tie((state, pairs["x"], pairs["y"], pairs["mid"]))
        return state

    positive = dot(chosen, known)
    top, total, key_sum, pooled_pair = contrast(pooled, key_queue, gathered, returned)
    count_pair = pooled_pair[:, width : width + 1].astype(full)
    middle_pair = [middle_low, middle_x, middle_y, pairs["mid"]]
    rows_pair = [rows, pairs["x"], pairs["y"], swap(pairs["x"], "tensor", 2)]
    middles = middle_pair + [swap(p, "tensor", 1) for p in middle_pair]
    rows_all = rows_pair + [swap(p, "tensor", 1) for p in rows_pair]

    pos_logit = jnp.sum(pooled_pair[:, :width].astype(full) * positive, axis=1, keepdims=True) * inv_temp
    top_final = jnp.maximum(top, pos_logit)
    lse = top_final + jnp.log(total * jnp.exp(top - top_final) + jnp.exp(pos_logit - top_final))
    loss_part = (lse - pos_logit)[0:1]
    step = loss_scale * inv_temp
    pooled_grad = key_sum * (step * jnp.exp(top - lse)) + step * (jnp.exp(pos_logit - lse) - 1.0) * positive
    result_row = pooled_grad / count_pair
    vector_pair = result_row * final_gain
    final_gain_part = result_row[0:1] * live_sum

    vectors_far = jnp.concatenate([vector_pair, swap(vector_pair, "tensor", 2)])
    vectors_all = jnp.concatenate([vectors_far, swap(vectors_far, "tensor", 1)])

    attn_grad, one_grad, sums = with_weights(
        ffn_back_kernel,
        "ffn_back",
        place,
        wholes,
        quarters,
        [slopes, vector_pair[0:1], normed_two, rows, normed_one, rstd_one, norm_gain[None]],
        [S((length, width), low), S((length, width), full), S((8, width), full)],
    )
    vectors_all, attn_grad, rows_all, middles = tie((vectors_all, attn_grad, rows_all, middles))
    down_part, up_part, up_bias_half = ffn_weights(middles, rows_all, vectors_all, up_half, bias_half, down_half)
    attn_far, attn_core, down_part, up_part = tie((swap(attn_grad, "tensor", 2), swap(attn_grad, "tensor", 1), down_part, up_part))
    attn_grads = [attn_grad, attn_far, attn_core, swap(attn_far, "tensor", 1)]

    near_in, away_in, qk_kept, qk_sent, vo_kept, vo_sent, query_bias_part, value_bias_part = attend_back(
        place, attn_grads, compact, query, keys, values, probs, context, query_weight.T, key_weight.T, value_weight.T, out_weight
    )
    line = lax.axis_size("dp") == 4
    down_next = inward(down_part) if line else down_part
    qk_sent, vo_sent, near_in, away_in, down_next = tie((qk_sent, vo_sent, near_in, away_in, down_next))
    qk_sum = plus(qk_kept, swap(qk_sent, "fsdp", 1))
    vectors = jnp.concatenate([final_gain_part, pooled_grad[0:1], sums[0:4], jnp.broadcast_to(loss_part / devices, (1, width))])
    vectors, _ = tie((vectors, qk_sent))
    for stride in (2, 1):
        vectors = vectors + swap(vectors, "tensor", stride)
    pad = jnp.zeros((1, width - 2 * mine), full)
    narrow = jnp.concatenate([query_bias_part, value_bias_part, pad], axis=1)
    blank = jnp.zeros_like(up_bias_half)
    up_bias_part = jnp.concatenate([jnp.where(f == 0, up_bias_half, blank), jnp.where(f == 0, blank, up_bias_half)], axis=1)
    vectors = jnp.concatenate([vectors, narrow, up_bias_part, jnp.zeros((7, width), full)])
    extra = carried(vectors)
    vo_sum = plus_carried(jnp.concatenate([vo_kept, extra]), swap(jnp.concatenate([vo_sent, extra]), "fsdp", 1), mine)
    if line:
        down_sum = plus(down_part, down_next)
        up_sum = plus(up_part, inward(up_part))
        qk_sum, up_sum = tie((qk_sum, up_sum))
        down_sum = plus(down_sum, across(down_sum))
        qk_sum = plus(qk_sum, inward(qk_sum))
        down_sum, vo_sum, qk_sum = tie((down_sum, vo_sum, qk_sum))
        up_sum = plus(up_sum, across(up_sum))
        vo_sum = plus_carried(vo_sum, inward(vo_sum), mine)
        up_sum, vo_sum = tie((up_sum, vo_sum))
        qk_sum = plus(qk_sum, across(qk_sum))
        down_sum = outward(down_sum)
        down_sum, qk_sum = tie((down_sum, qk_sum))
        vo_sum = plus_carried(vo_sum, across(vo_sum), mine)
        down_other = swap(down_sum, "fsdp", 1)
        up_sum = outward(up_sum)
        qk_sum = outward(qk_sum)
        up_sum, vo_sum = tie((up_sum, vo_sum))
        vo_sum = outward(vo_sum)
    else:
        down_sum, up_sum, qk_sum, vo_sum = [lax.psum(a.astype(full), "dp").astype(low) for a in (down_part, up_part, qk_sum, vo_sum)]
        down_other = swap(down_sum, "fsdp", 1)
    if line:
        extra = vo_sum[mine:].astype(full)
        vectors = extra[:16] + extra[16:]
    else:
        vectors = lax.psum(vectors + swap(vectors, "fsdp", 1), "dp")
    vo_sum = vo_sum[:mine]
    down_weight_grad = jnp.concatenate(ordered(down_sum, down_other, f)).astype(full)
    up_weight_grad = jnp.concatenate(ordered(up_sum, swap(up_sum, "fsdp", 1), f), axis=1).astype(full)
    query_grad, key_grad = ordered(qk_sum, swap(qk_sum, "fsdp", 1), f)
    value_grad, out_grad = ordered(vo_sum, swap(vo_sum, "fsdp", 1), f)

    other_in = swap(away_in, "tensor", 1)
    far_in = swap(plus(near_in[1], other_in[1]), "tensor", 2)
    back = near_in[0].astype(full) + other_in[0].astype(full) + far_in.astype(full)
    compact_grad = (one_grad + back).astype(low)
    input_grad = dot(table, compact_grad, ((0,), (0,))).astype(low)
    return (
        output,
        input_grad[None],
        query_grad.T.astype(full),
        vectors[7, :mine],
        key_grad.T.astype(full),
        value_grad.T.astype(full),
        vectors[7, mine : 2 * mine],
        out_grad.astype(full),
        vectors[5],
        vectors[2],
        vectors[3],
        up_weight_grad,
        vectors[8],
        down_weight_grad,
        vectors[4],
        vectors[0],
        vectors[1],
        vectors[6, 0],
    )


def solution(mesh):
    placed = (
        P(("dp", "fsdp"), None, None),
        P(("dp", "fsdp"), None),
        P(("dp", "fsdp")),
        P(),
        P(("dp", "fsdp"), None),
        P(("dp", "fsdp"), None),
        P(None, "tensor"),
        P("tensor"),
        P(None, "tensor"),
        P(None, "tensor"),
        P("tensor"),
        P("tensor", None),
        P(),
        P(),
        P(),
        P(None, "tensor"),
        P("tensor"),
        P("tensor", None),
        P(),
        P(),
        P(),
    )
    return jax.shard_map(
        per_device,
        mesh=mesh,
        in_specs=placed,
        out_specs=(
            P(("dp", "fsdp", "tensor"), None, None),
            P(("dp", "fsdp", "tensor"), None, None),
            P(None, "tensor"),
            P("tensor"),
            P(None, "tensor"),
            P(None, "tensor"),
            P("tensor"),
            P("tensor", None),
            P(),
            P(),
            P(),
            P(None, "tensor"),
            P("tensor"),
            P("tensor", None),
            P(),
            P(),
            P(),
            P(),
        ),
        check_vma=False,
    )
```

time: 265 us -> 265 us (level)
  Pallas kernels: 24.7 us -> 56.1 us
  starting transfers between devices: 51.3 us -> 68.7 us
  waiting for transfers between devices: 111 us -> 97.5 us
  matrix products: 16.7 us -> 3.79 us
  local copies, waits for them, and re-layouts: 26.7 us -> 15.1 us
  between operations: 8.38 us -> 2.6 us
  other arithmetic: 25.5 us -> 20.5 us
    pallas_call x1 -> x4, Pallas kernels: 13.4 us -> 43.9 us  [the longest x2 18.8 us: with_weights(): pl.pallas_call(kernel, grid_spec=pltpu.PrefetchScalarGridSpec(num_scalar_...]
    ppermute x34 -> x52, waiting for transfers between devices: 97.7 us -> 70.9 us  [swap(): return lax.ppermute(array, axis, [(i, i ^ stride) for i in range(size)])]
    ppermute x9 -> x12, waiting for transfers between devices: 13.6 us -> 26.6 us  [the longest x4 18.2 us: outward(): outer = lax.ppermute(part, 'dp', [(1, 0), (2, 3)])]
    dot_general x9 -> x4, matrix products: 16.7 us -> 3.79 us  [dot(): return lax.dot_general(a, b, (dims, ((), ())), preferred_element_type=full)]
    ppermute x34 -> x52, starting transfers between devices: 34.6 us -> 45.2 us  [swap(): return lax.ppermute(array, axis, [(i, i ^ stride) for i in range(size)])]
    unnamed x81 -> x90, local copies, waits for them, and re-layouts: 13.3 us -> 4.76 us
    ppermute x9 -> x12, starting transfers between devices: 16.6 us -> 23.5 us  [the longest x4 15 us: inward(): return lax.ppermute(part, 'dp', [(0, 1), (3, 2)])]
    reduce_sum x6 -> x1, other arithmetic: 5.62 us -> 0.18 us  [per_device(): jnp.sum(jnp.where(spot == mates[:, None], pos_index[None], 0), axis=1, ke...]
  transfers between devices with their start and end apart: 43 -> 64, of which waited for: 28 -> 22; matrix products, arithmetic and copies ran while one was open for 12% -> 11% of each run, Pallas kernels for 5% -> 21%
where the time goes in v3:
time: 265 us; the launch traced here: 264 us
  waiting for transfers between devices  97.5 us (37%)
  starting transfers between devices  68.7 us (26%)
  Pallas kernels  56.1 us (21%)
  other arithmetic  20.5 us (8%)
  local copies, waits for them, and re-layouts  15.1 us (6%)
  matrix products  3.79 us (1%)
    ppermute x52, waiting for transfers between devices, swap(): return lax.ppermute(array, axis, [(i, i ^ stride) for i in range(size)])  70.9 us
    ppermute x52, starting transfers between devices, swap(): return lax.ppermute(array, axis, [(i, i ^ stride) for i in range(size)])  45.2 us
    pallas_call x2, Pallas kernels, with_weights(): pl.pallas_call(kernel, grid_spec=pltpu.PrefetchScalarGridSpec(num_scalar_...  18.8 us
    ppermute x4, waiting for transfers between devices, outward(): outer = lax.ppermute(part, 'dp', [(1, 0), (2, 3)])  18.2 us
    ppermute x4, starting transfers between devices, inward(): return lax.ppermute(part, 'dp', [(0, 1), (3, 2)])  15 us
    pallas_call x1, Pallas kernels, attend_back(): pl.pallas_call(attend_back_kernel, grid_spec=pltpu.PrefetchScalarGridSpec...  13.9 us
    pallas_call x1, Pallas kernels, attend(): pl.pallas_call(attend_kernel, grid_spec=pltpu.PrefetchScalarGridSpec(num_...  12.2 us
    pallas_call x1, Pallas kernels, ffn_weights(): pl.pallas_call(ffn_weights_kernel, out_shape=[S((half, width), low), S((w...  11.2 us
  transfers between devices with their start and end apart: 64, of which 22 were waited for; matrix products, arithmetic and copies ran while one was open for 11% of the time, Pallas kernels for 21%

profile of v3, /device:TPU:0, one launch (start us, length us, event | category | flops | bytes accessed | tf_op | source)
XLA Modules:
  0.0 264.2 jit_solution(7424036144105343478)
XLA Ops:
  0.7 1.3 constant_dynamic-slice_fusion.2
  3.2 3.0 %collective-permute-start.2 = (bf16[384,768]{1,0:T(8,128)(2,1)}, bf16[384,768]{1,0:T(8,128)(2,1)}, u32[]{:S(2)}, u32[]{:S(2)}) collective-permute-start(bf16[384,768]{1,0:T(8,128)(2,1)} %pad_maximum_fusion), channel_id=1, source_target_pairs={{0,2},{1,3},{2,0},{3,1},{4,6},{5,7},{6,4},{7,5},{8,10},{9,11},{10,... | collective-permute-start | bytes 1769480 | tf_op jit(solution)/shard_map/ppermute | solution.py:25
  6.2 1.5 collective-permute-start.3
  9.7 12.2 %attend.1 = (bf16[4,256,768]{2,1,0:T(8,128)(2,1)}, bf16[4,256,192]{2,1,0:T(8,128)(2,1)}, bf16[4,256,192]{2,1,0:T(8,128)(2,1)}, bf16[4,256,192]{2,1,0:T(8,128)(2,...) custom-call(s32[2]{0:T(128)} %pad_add_fusion.place_in.place, ...), custom_call_target="tpu_custom_call" | custom-call | tf_op jit(solution)/shard_map/attend/pallas_call | solution.py:153
  22.8 1.6 collective-permute-start.7
  24.9 7.6 %collective-permute-done.7 = f32[2,768]{1,0:T(2,128)S(1)} collective-permute-done((f32[2,768]{1,0:T(2,128)S(1)}, f32[2,768]{1,0:T(2,128)S(1)}, u32[]{:S(2)}, u32[]{:S(2)}) %collective-permute-start.7) | collective-permute-done | bytes 6176 | tf_op jit(solution)/shard_map/ppermute | solution.py:25
  33.2 1.1 fusion.4
  34.3 1.8 collective-permute-start.8
  36.1 1.5 collective-permute-start.9
  37.6 1.6 collective-permute-start.10
  39.6 12.2 %collective-permute-done.11 = bf16[8,768]{1,0:T(8,128)(2,1)S(1)} collective-permute-done((bf16[8,768]{1,0:T(8,128)(2,1)S(1)}, bf16[8,768]{1,0:T(8,128)(2,1)S(1)}, u32[]{:S(2)}, u32[]{:S(2)}) %collective-permute-start.11) | collective-permute-done | bytes 12320 | tf_op jit(solution)/shard_map/ppermute | solution.py:25
  52.3 1.2 bitcast_add_fusion.1
  54.6 1.0 copy-done.7
  55.9 2.6 collective-permute-start.18
  58.5 1.4 fusion.44
  64.8 9.4 %ffn.1 = (bf16[4,256,768]{2,1,0:T(8,128)(2,1)}, f32[256,768]{1,0:T(8,128)}, bf16[256,896]{1,0:T(8,128)(2,1)}, bf16[1,256,768]{2,1,0:T(8,128)(2,1)}, f32[1,768]{1,0:T(1,128)}, /*index=5*/bf16[1,896]{1,0:T(2,128)(2,1)}) custom-call(s32[2]{0:T(128)} %pad_add_fusion.place_in.place, bf16[768,768]{1,0:T(8,128)(2,1)} %refs_0_.3, bf16[768,768]{1,0:T(8,128)(2,1)} %refs_1_.3, ...), custom_call_target="tpu_custom_call" | custom-call | tf_op jit(solution)/shard_map/ffn/pallas_call | solution.py:407
  75.0 1.4 collective-permute-start.19
  76.4 2.4 collective-permute-done.19
  79.5 1.6 collective-permute-start.20
  81.1 2.0 collective-permute-done.20
  83.2 2.7 %collective-permute-start.21 = (bf16[4,896]{1,0:T(4,128)(2,1)S(1)}, bf16[4,896]{1,0:T(4,128)(2,1)S(1)}, u32[]{:S(2)}, u32[]{:S(2)}) collective-permute-start(bf16[4,896]{1,0:T(4,128)(2,1)S(1)} %pad_maximum_fusion.20), channel_id=1, source_target_pairs={{0,16},{8,24},{16,0},{24,8},{1,17},{9,25},{17,1},{25,9},{2,18},{10... | collective-permute-start | bytes 21512 | tf_op jit(solution)/shard_map/ppermute | solution.py:25
  86.9 1.5 collective-permute-start.24
  88.4 1.0 fusion.47
  90.4 2.0 collective-permute-start.22
  92.5 2.6 collective-permute-done.22
  95.1 0.9 collective-permute-start.25
  96.3 11.5 %collective-permute-done.25.refs_3_ = bf16[256,768]{1,0:T(8,128)(2,1)} collective-permute-done((bf16[256,768]{1,0:T(8,128)(2,1)}, bf16[256,768]{1,0:T(8,128)(2,1)}, u32[]{:S(2)}, u32[]{:S(2)}) %collective-permute-start.25) | collective-permute-done | bytes 393248 | tf_op jit(solution)/shard_map/ppermute | solution.py:25
  107.8 1.8 collective-permute-start.26
  109.6 1.1 multiply_reduce_fusion.1
  110.6 0.9 collective-permute-done.26
  111.9 1.6 collective-permute-start.27
  113.6 1.6 collective-permute-start.30
  116.1 1.6 collective-permute-start.28
  118.2 7.3 %collective-permute-done.28 = f32[2,768]{1,0:T(2,128)S(1)} collective-permute-done((f32[2,768]{1,0:T(2,128)S(1)}, f32[2,768]{1,0:T(2,128)S(1)}, u32[]{:S(2)}, u32[]{:S(2)}) %collective-permute-start.28) | collective-permute-done | bytes 6176 | tf_op jit(solution)/shard_map/ppermute | solution.py:25
  126.2 2.1 collective-permute-done.29
  129.7 9.4 %ffn_back.1 = (bf16[256,768]{1,0:T(8,128)(2,1)}, f32[256,768]{1,0:T(8,128)}, f32[8,768]{1,0:T(8,128)}) custom-call(s32[2]{0:T(128)} %pad_add_fusion.place_in.place, bf16[768,768]{1,0:T(8,128)(2,1)} %refs_0_.3, bf16[768,768]{1,0:T(8,128)(2,1)} %refs_1_.3, bf16[768,768]{1,0:T(8,128)(2,1)} %copy-done.7, bf16[768,768]{1,0:T(8,128)(2,1)} %copy-done.8, ...), custom_call_target="tpu_custom_call" | custom-call | tf_op jit(solution)/shard_map/ffn_back/pallas_call | solution.py:407
  140.5 1.5 collective-permute-start.39
  142.8 0.9 constant_dynamic-slice_fusion.1.refs_17_
  145.8 11.2 %ffn_weights.1 = (bf16[384,768]{1,0:T(8,128)(2,1)}, bf16[768,384]{1,0:T(8,128)(2,1)}, f32[1,384]{1,0:T(1,128)}) custom-call(bf16[256,768]{1,0:T(8,128)(2,1)} %copy-done.15, bf16[256,768]{1,0:T(8,128)(2,1)} %collective-permute-done.16.refs_1_, bf16[256,768]{1,0:T(8,128)(2,1)} %collective-permute-done.17.refs_2_, ...), custom_call_target="tpu_custom_call" | custom-call | tf_op jit(solution)/shard_map/ffn_weights/pallas_call | solution.py:453
  157.8 3.7 %collective-permute-start.42 = (bf16[384,768]{1,0:T(8,128)(2,1)}, bf16[384,768]{1,0:T(8,128)(2,1)S(1)}, u32[]{:S(2)}, u32[]{:S(2)}) collective-permute-start(bf16[384,768]{1,0:T(8,128)(2,1)} %get-tuple-element.178), channel_id=1, source_target_pairs={{0,8},{24,16},{1,9},{25,17},{2,10},{26,18},{3,11},{27,19},{4,12},{... | collective-permute-start | bytes 1769480 | tf_op jit(solution)/shard_map/ppermute | solution.py:51
  161.7 1.6 collective-permute-start.50
  165.4 13.9 %attend_back.1 = (bf16[2,256,768]{2,1,0:T(8,128)(2,1)}, bf16[2,256,768]{2,1,0:T(8,128)(2,1)}, bf16[192,768]{1,0:T(8,128)(2,1)}, bf16[192,768]{1,0:T(8,128)(2,1)}...) custom-call(s32[2]{0:T(128)} %pad_add_fusion.place_in.place, ...), custom_call_target="tpu_custom_call" | custom-call | tf_op jit(solution)/shard_map/attend_back/pallas_call | solution.py:272
  181.5 2.5 collective-permute-done.46
  184.8 2.8 %collective-permute-done.50 = bf16[768,384]{1,0:T(8,128)(2,1)S(1)} collective-permute-done((bf16[768,384]{1,0:T(8,128)(2,1)}, bf16[768,384]{1,0:T(8,128)(2,1)S(1)}, u32[]{:S(2)}, u32[]{:S(2)}) %collective-permute-start.50) | collective-permute-done | bytes 589856 | tf_op jit(solution)/shard_map/ppermute | solution.py:51
  189.1 3.8 %collective-permute-start.51 = (bf16[192,768]{1,0:T(8,128)(2,1)S(1)}, bf16[192,768]{1,0:T(8,128)(2,1)S(1)}, u32[]{:S(2)}, u32[]{:S(2)}) collective-permute-start(bf16[192,768]{1,0:T(8,128)(2,1)S(1)} %add_convert_fusion.10), channel_id=1, source_target_pairs={{0,8},{24,16},{1,9},{25,17},{2,10},{26,18},{3,11},{27,19},{4,12},{... | collective-permute-start | bytes 884744 | tf_op jit(solution)/shard_map/ppermute | solution.py:51
  193.6 3.8 %collective-permute-done.48 = bf16[224,768]{1,0:T(8,128)(2,1)S(1)} collective-permute-done((bf16[224,768]{1,0:T(8,128)(2,1)S(1)}, bf16[224,768]{1,0:T(8,128)(2,1)S(1)}, u32[]{:S(2)}, u32[]{:S(2)}) %collective-permute-start.48) | collective-permute-done | bytes 344096 | tf_op jit(solution)/shard_map/ppermute | solution.py:25
  198.7 1.6 collective-permute-start.52
  201.0 5.9 %collective-permute-start.57 = (bf16[224,768]{1,0:T(8,128)(2,1)S(1)}, bf16[224,768]{1,0:T(8,128)(2,1)S(1)}, u32[]{:S(2)}, u32[]{:S(2)}) collective-permute-start(bf16[224,768]{1,0:T(8,128)(2,1)S(1)} %pad_maximum_fusion.3), channel_id=1, source_target_pairs={{0,8},{24,16},{1,9},{25,17},{2,10},{26,18},{3,11},{27,19},{4,12},{... | collective-permute-start | bytes 1032200 | tf_op jit(solution)/shard_map/ppermute | solution.py:51
  207.8 4.8 %collective-permute-done.57 = bf16[224,768]{1,0:T(8,128)(2,1)S(1)} collective-permute-done((bf16[224,768]{1,0:T(8,128)(2,1)S(1)}, bf16[224,768]{1,0:T(8,128)(2,1)S(1)}, u32[]{:S(2)}, u32[]{:S(2)}) %collective-permute-start.57) | collective-permute-done | bytes 344096 | tf_op jit(solution)/shard_map/ppermute | solution.py:51
  212.7 1.4 collective-permute-start.58
  215.0 1.3 collective-permute-start.54
  216.3 1.4 collective-permute-start.63
  217.6 1.1 fusion
  219.0 17.7 %collective-permute-done.54 = bf16[192,768]{1,0:T(8,128)(2,1)S(1)} collective-permute-done((bf16[192,768]{1,0:T(8,128)(2,1)S(1)}, bf16[192,768]{1,0:T(8,128)(2,1)S(1)}, u32[]{:S(2)}, u32[]{:S(2)}) %collective-permute-start.54) | collective-permute-done | bytes 294944 | tf_op jit(solution)/shard_map/ppermute | solution.py:60
  236.7 1.5 collective-permute-start.55
  238.2 1.3 collective-permute-start.60
  240.3 1.6 maximum_convert_fusion.1
  241.9 4.7 %collective-permute-done.55 = bf16[192,768]{1,0:T(8,128)(2,1)S(1)} collective-permute-done((bf16[192,768]{1,0:T(8,128)(2,1)S(1)}, bf16[192,768]{1,0:T(8,128)(2,1)S(1)}, u32[]{:S(2)}, u32[]{:S(2)}) %collective-permute-start.55) | collective-permute-done | bytes 294944 | tf_op jit(solution)/shard_map/ppermute | solution.py:25
  246.6 1.1 convert_bitcast_fusion.1
  248.3 1.0 collective-permute-start.61
  251.1 8.2 %collective-permute-done.62 = bf16[768,384]{1,0:T(8,128)(2,1)S(1)} collective-permute-done((bf16[768,384]{1,0:T(8,128)(2,1)S(1)}, bf16[768,384]{1,0:T(8,128)(2,1)S(1)}, u32[]{:S(2)}, u32[]{:S(2)}) %collective-permute-start.62) | collective-permute-done | bytes 589856 | tf_op jit(solution)/shard_map/ppermute | solution.py:25
  259.4 1.6 maximum_convert_fusion
  261.0 2.2 collective-permute-done.61
  263.1 1.1 select_convert_fusion
  (285 shorter events, 38.8 us)
Async XLA Ops:
  3.2 18.7 %collective-permute-start.2 = (bf16[384,768]{1,0:T(8,128)(2,1)}, bf16[384,768]{1,0:T(8,128)(2,1)}, u32[]{:S(2)}, u32[]{:S(2)}) collective-permute-start(bf16[384,768]{1,0:T(8,128)(2,1)} %pad_maximum_fusion), channel_id=1, source_target_pairs={{0,2},{1,3},{2,0},{3,1},{4,6},{5,7},{6,4},{7,5},{8,10},{9,11},{10,... | collective-permute-start | bytes 1769480 | tf_op jit(solution)/shard_map/ppermute | solution.py:25
  6.2 15.7 %collective-permute-start.3 = (bf16[4,768]{1,0:T(4,128)(2,1)S(1)}, bf16[4,768]{1,0:T(4,128)(2,1)S(1)}, u32[]{:S(2)}, u32[]{:S(2)}) collective-permute-start(bf16[4,768]{1,0:T(4,128)(2,1)S(1)} %copy-done.37), channel_id=1, source_target_pairs={{0,4},{4,0},{1,5},{5,1},{2,6},{6,2},{3,7},{7,3},{8,12},{12,8},{9,1... | collective-permute-start | bytes 18440 | tf_op jit(solution)/shard_map/ppermute | solution.py:25
  8.5 25.7 %collective-permute-start.5 = (bf16[384,768]{1,0:T(8,128)(2,1)}, bf16[384,768]{1,0:T(8,128)(2,1)}, u32[]{:S(2)}, u32[]{:S(2)}) collective-permute-start(bf16[384,768]{1,0:T(8,128)(2,1)} %pad_maximum_fusion.1), channel_id=1, source_target_pairs={{0,2},{1,3},{2,0},{3,1},{4,6},{5,7},{6,4},{7,5},{8,10},{9,11},{10,... | collective-permute-start | bytes 1769480 | tf_op jit(solution)/shard_map/ppermute | solution.py:25
  9.1 13.7 %collective-permute-start.6 = (f32[1,768]{1,0:T(1,128)S(1)}, f32[1,768]{1,0:T(1,128)S(1)}, u32[]{:S(2)}, u32[]{:S(2)}) collective-permute-start(f32[1,768]{1,0:T(1,128)S(1)} %broadcast_in_dim.105), channel_id=1, source_target_pairs={{0,1},{1,0},{2,3},{3,2},{4,5},{5,4},{6,7},{7,6},{8,9},{9,8},{10,11... | collective-permute-start | bytes 9224 | tf_op jit(solution)/shard_map/ppermute | solution.py:25
  21.9 11.2 %collective-permute-start.4 = (bf16[2,256,768]{2,1,0:T(8,128)(2,1)}, bf16[2,256,768]{2,1,0:T(8,128)(2,1)S(1)}, u32[]{:S(2)}, u32[]{:S(2)}) collective-permute-start(bf16[2,256,768]{2,1,0:T(8,128)(2,1)} %get-tuple-element.115), channel_id=1, source_target_pairs={{0,1},{1,0},{2,3},{3,2},{4,5},{5,4},{6,7},{7,6},{8,9},{9,8},{10,11... | collective-permute-start | bytes 2359304 | tf_op jit(solution)/shard_map/ppermute | solution.py:25
  22.8 9.8 %collective-permute-start.7 = (f32[2,768]{1,0:T(2,128)S(1)}, f32[2,768]{1,0:T(2,128)S(1)}, u32[]{:S(2)}, u32[]{:S(2)}) collective-permute-start(f32[2,768]{1,0:T(2,128)S(1)} %pad_maximum_fusion.21), channel_id=1, source_target_pairs={{0,2},{1,3},{2,0},{3,1},{4,6},{5,7},{6,4},{7,5},{8,10},{9,11},{10,... | collective-permute-start | bytes 18440 | tf_op jit(solution)/shard_map/ppermute | solution.py:25
  34.3 17.5 %collective-permute-start.8 = (bf16[256,768]{1,0:T(8,128)(2,1)S(1)}, bf16[256,768]{1,0:T(8,128)(2,1)S(1)}, u32[]{:S(2)}, u32[]{:S(2)}) collective-permute-start(bf16[256,768]{1,0:T(8,128)(2,1)S(1)} %fusion.4), channel_id=1, source_target_pairs={{0,2},{1,3},{2,0},{3,1},{4,6},{5,7},{6,4},{7,5},{8,10},{9,11},{10,... | collective-permute-start | bytes 1179656 | tf_op jit(solution)/shard_map/ppermute | solution.py:25
  36.1 17.4 %collective-permute-start.9 = (bf16[384,768]{1,0:T(8,128)(2,1)}, bf16[384,768]{1,0:T(8,128)(2,1)S(1)}, u32[]{:S(2)}, u32[]{:S(2)}) collective-permute-start(bf16[384,768]{1,0:T(8,128)(2,1)} %collective-permute-done.2.refs_4_), channel_id=1, source_target_pairs={{0,4},{4,0},{1,5},{5,1},{2,6},{6,2},{3,7},{7,3},{8,12},{12,8},{9,1... | collective-permute-start | bytes 1769480 | tf_op jit(solution)/shard_map/ppermute | solution.py:25
  37.6 16.0 %collective-permute-start.10 = (bf16[384,768]{1,0:T(8,128)(2,1)}, bf16[384,768]{1,0:T(8,128)(2,1)S(1)}, u32[]{:S(2)}, u32[]{:S(2)}) collective-permute-start(bf16[384,768]{1,0:T(8,128)(2,1)} %collective-permute-done.2.refs_4_), channel_id=1, source_target_pairs={{0,8},{8,0},{16,24},{24,16},{1,9},{9,1},{17,25},{25,17},{2,10},{10... | collective-permute-start | bytes 1769480 | tf_op jit(solution)/shard_map/ppermute | solution.py:25
  39.2 12.6 %collective-permute-start.11 = (bf16[8,768]{1,0:T(8,128)(2,1)S(1)}, bf16[8,768]{1,0:T(8,128)(2,1)S(1)}, u32[]{:S(2)}, u32[]{:S(2)}) collective-permute-start(bf16[8,768]{1,0:T(8,128)(2,1)S(1)} %pad_maximum_fusion.15), channel_id=1, source_target_pairs={{0,8},{8,0},{16,24},{24,16},{1,9},{9,1},{17,25},{25,17},{2,10},{10... | collective-permute-start | bytes 36872 | tf_op jit(solution)/shard_map/ppermute | solution.py:25
  39.6 15.0 %collective-permute-start = (bf16[768,768]{1,0:T(8,128)(2,1)S(1)}, bf16[768,768]{1,0:T(8,128)(2,1)S(1)}, u32[]{:S(2)}, u32[]{:S(2)}) collective-permute-start(bf16[768,768]{1,0:T(8,128)(2,1)S(1)} %copy-done.3), channel_id=1, source_target_pairs={{0,1},{1,0},{2,3},{3,2},{4,5},{5,4},{6,7},{7,6},{8,9},{9,8},{10,11... | collective-permute-start | bytes 3538952 | tf_op jit(solution)/shard_map/ppermute | solution.py:25
  51.8 4.1 %collective-permute-start.1 = (bf16[768,768]{1,0:T(8,128)(2,1)}, bf16[768,768]{1,0:T(8,128)(2,1)S(1)}, u32[]{:S(2)}, u32[]{:S(2)}) collective-permute-start(bf16[768,768]{1,0:T(8,128)(2,1)} %refs_1_.3), channel_id=1, source_target_pairs={{0,1},{1,0},{2,3},{3,2},{4,5},{5,4},{6,7},{7,6},{8,9},{9,8},{10,11... | collective-permute-start | bytes 3538952 | tf_op jit(solution)/shard_map/ppermute | solution.py:25
  51.8 8.2 %collective-permute-start.12 = (bf16[384,768]{1,0:T(8,128)(2,1)}, bf16[384,768]{1,0:T(8,128)(2,1)S(1)}, u32[]{:S(2)}, u32[]{:S(2)}) collective-permute-start(bf16[384,768]{1,0:T(8,128)(2,1)} %collective-permute-done.2.refs_4_), channel_id=1, source_target_pairs={{0,1},{1,0},{2,3},{3,2},{4,5},{5,4},{6,7},{7,6},{8,9},{9,8},{10,11... | collective-permute-start | bytes 1769480 | tf_op jit(solution)/shard_map/ppermute | solution.py:25
  53.5 10.1 %collective-permute-start.15 = (bf16[384,768]{1,0:T(8,128)(2,1)}, bf16[384,768]{1,0:T(8,128)(2,1)S(1)}, u32[]{:S(2)}, u32[]{:S(2)}) collective-permute-start(bf16[384,768]{1,0:T(8,128)(2,1)} %collective-permute-done.5.refs_7_), channel_id=1, source_target_pairs={{0,1},{1,0},{2,3},{3,2},{4,5},{5,4},{6,7},{7,6},{8,9},{9,8},{10,11... | collective-permute-start | bytes 1769480 | tf_op jit(solution)/shard_map/ppermute | solution.py:25
  53.6 9.9 %collective-permute-start.13 = (bf16[384,768]{1,0:T(8,128)(2,1)S(1)}, bf16[384,768]{1,0:T(8,128)(2,1)S(1)}, u32[]{:S(2)}, u32[]{:S(2)}) collective-permute-start(bf16[384,768]{1,0:T(8,128)(2,1)S(1)} %collective-permute-done.9.refs_5_), channel_id=1, source_target_pairs={{0,1},{1,0},{2,3},{3,2},{4,5},{5,4},{6,7},{7,6},{8,9},{9,8},{10,11... | collective-permute-start | bytes 1769480 | tf_op jit(solution)/shard_map/ppermute | solution.py:25
  55.6 7.9 %collective-permute-start.14 = (bf16[384,768]{1,0:T(8,128)(2,1)S(1)}, bf16[384,768]{1,0:T(8,128)(2,1)S(1)}, u32[]{:S(2)}, u32[]{:S(2)}) collective-permute-start(bf16[384,768]{1,0:T(8,128)(2,1)S(1)} %collective-permute-done.10.refs_6_), channel_id=1, source_target_pairs={{0,1},{1,0},{2,3},{3,2},{4,5},{5,4},{6,7},{7,6},{8,9},{9,8},{10,11... | collective-permute-start | bytes 1769480 | tf_op jit(solution)/shard_map/ppermute | solution.py:25
  55.9 4.7 %collective-permute-start.18 = (bf16[16,768]{1,0:T(8,128)(2,1)S(1)}, bf16[16,768]{1,0:T(8,128)(2,1)S(1)}, u32[]{:S(2)}, u32[]{:S(2)}) collective-permute-start(bf16[16,768]{1,0:T(8,128)(2,1)S(1)} %pad_maximum_fusion.8), channel_id=1, source_target_pairs={{0,16},{8,24},{16,0},{24,8},{1,17},{9,25},{17,1},{25,9},{2,18},{10... | collective-permute-start | bytes 73736 | tf_op jit(solution)/shard_map/ppermute | solution.py:25
  60.0 14.2 %collective-permute-start.16 = (bf16[256,768]{1,0:T(8,128)(2,1)S(1)}, bf16[256,768]{1,0:T(8,128)(2,1)}, u32[]{:S(2)}, u32[]{:S(2)}) collective-permute-start(bf16[256,768]{1,0:T(8,128)(2,1)S(1)} %get-tuple-element.148.refs_0_), channel_id=1, source_target_pairs={{0,4},{4,0},{1,5},{5,1},{2,6},{6,2},{3,7},{7,3},{8,12},{12,8},{9,1... | collective-permute-start | bytes 1179656 | tf_op jit(solution)/shard_map/ppermute | solution.py:25
  60.7 13.6 %collective-permute-start.17 = (bf16[256,768]{1,0:T(8,128)(2,1)S(1)}, bf16[256,768]{1,0:T(8,128)(2,1)}, u32[]{:S(2)}, u32[]{:S(2)}) collective-permute-start(bf16[256,768]{1,0:T(8,128)(2,1)S(1)} %get-tuple-element.148.refs_0_), channel_id=1, source_target_pairs={{0,2},{1,3},{2,0},{3,1},{4,6},{5,7},{6,4},{7,5},{8,10},{9,11},{10,... | collective-permute-start | bytes 1179656 | tf_op jit(solution)/shard_map/ppermute | solution.py:25
  75.0 3.8 %collective-permute-start.19 = (bf16[1,896]{1,0:T(2,128)(2,1)}, bf16[1,896]{1,0:T(2,128)(2,1)S(1)}, u32[]{:S(2)}, u32[]{:S(2)}) collective-permute-start(bf16[1,896]{1,0:T(2,128)(2,1)} %get-tuple-element.130), channel_id=1, source_target_pairs={{0,4},{4,0},{1,5},{5,1},{2,6},{6,2},{3,7},{7,3},{8,12},{12,8},{9,1... | collective-permute-start | bytes 5384 | tf_op jit(solution)/shard_map/ppermute | solution.py:25
  79.5 3.7 %collective-permute-start.20 = (bf16[2,896]{1,0:T(2,128)(2,1)S(1)}, bf16[2,896]{1,0:T(2,128)(2,1)S(1)}, u32[]{:S(2)}, u32[]{:S(2)}) collective-permute-start(bf16[2,896]{1,0:T(2,128)(2,1)S(1)} %pad_maximum_fusion.22), channel_id=1, source_target_pairs={{0,8},{8,0},{16,24},{24,16},{1,9},{9,1},{17,25},{25,17},{2,10},{10... | collective-permute-start | bytes 10760 | tf_op jit(solution)/shard_map/ppermute | solution.py:25
  83.2 5.2 %collective-permute-start.21 = (bf16[4,896]{1,0:T(4,128)(2,1)S(1)}, bf16[4,896]{1,0:T(4,128)(2,1)S(1)}, u32[]{:S(2)}, u32[]{:S(2)}) collective-permute-start(bf16[4,896]{1,0:T(4,128)(2,1)S(1)} %pad_maximum_fusion.20), channel_id=1, source_target_pairs={{0,16},{8,24},{16,0},{24,8},{1,17},{9,25},{17,1},{25,9},{2,18},{10... | collective-permute-start | bytes 21512 | tf_op jit(solution)/shard_map/ppermute | solution.py:25
  85.8 31.9 %collective-permute-start.35 = (bf16[256,768]{1,0:T(8,128)(2,1)S(1)}, bf16[256,768]{1,0:T(8,128)(2,1)}, u32[]{:S(2)}, u32[]{:S(2)}) collective-permute-start(bf16[256,768]{1,0:T(8,128)(2,1)S(1)} %get-tuple-element.148.refs_0_), channel_id=1, source_target_pairs={{0,1},{1,0},{2,3},{3,2},{4,5},{5,4},{6,7},{7,6},{8,9},{9,8},{10,11... | collective-permute-start | bytes 1179656 | tf_op jit(solution)/shard_map/ppermute | solution.py:25
  85.8 31.9 %collective-permute-start.36 = (bf16[256,768]{1,0:T(8,128)(2,1)}, bf16[256,768]{1,0:T(8,128)(2,1)}, u32[]{:S(2)}, u32[]{:S(2)}) collective-permute-start(bf16[256,768]{1,0:T(8,128)(2,1)} %collective-permute-done.16.refs_1_), channel_id=1, source_target_pairs={{0,1},{1,0},{2,3},{3,2},{4,5},{5,4},{6,7},{7,6},{8,9},{9,8},{10,11... | collective-permute-start | bytes 1179656 | tf_op jit(solution)/shard_map/ppermute | solution.py:25
  86.3 21.4 %collective-permute-start.23 = (bf16[256,896]{1,0:T(8,128)(2,1)}, bf16[256,896]{1,0:T(8,128)(2,1)}, u32[]{:S(2)}, u32[]{:S(2)}) collective-permute-start(bf16[256,896]{1,0:T(8,128)(2,1)} %get-tuple-element.156.refs_15_.refs_8_), channel_id=1, source_target_pairs={{0,4},{4,0},{1,5},{5,1},{2,6},{6,2},{3,7},{7,3},{8,12},{12,8},{9,1... | collective-permute-start | bytes 1376264 | tf_op jit(solution)/shard_map/ppermute | solution.py:25
  86.9 20.9 %collective-permute-start.24 = (bf16[256,896]{1,0:T(8,128)(2,1)}, bf16[256,896]{1,0:T(8,128)(2,1)}, u32[]{:S(2)}, u32[]{:S(2)}) collective-permute-start(bf16[256,896]{1,0:T(8,128)(2,1)} %get-tuple-element.156.refs_15_.refs_8_), channel_id=1, source_target_pairs={{0,2},{1,3},{2,0},{3,1},{4,6},{5,7},{6,4},{7,5},{8,10},{9,11},{10,... | collective-permute-start | bytes 1376264 | tf_op jit(solution)/shard_map/ppermute | solution.py:25
  90.4 4.7 %collective-permute-start.22 = (f32[4,1024]{1,0:T(4,128)S(1)}, f32[4,1024]{1,0:T(4,128)S(1)}, u32[]{:S(2)}, u32[]{:S(2)}) collective-permute-start(f32[4,1024]{1,0:T(4,128)S(1)} %slice.297), channel_id=1, source_target_pairs={{0,16},{8,24},{16,0},{24,8},{1,17},{9,25},{17,1},{25,9},{2,18},{10... | collective-permute-start | bytes 49160 | tf_op jit(solution)/shard_map/ppermute | solution.py:25
  95.1 12.7 %collective-permute-start.25 = (bf16[256,768]{1,0:T(8,128)(2,1)}, bf16[256,768]{1,0:T(8,128)(2,1)}, u32[]{:S(2)}, u32[]{:S(2)}) collective-permute-start(bf16[256,768]{1,0:T(8,128)(2,1)} %collective-permute-done.16.refs_1_), channel_id=1, source_target_pairs={{0,2},{1,3},{2,0},{3,1},{4,6},{5,7},{6,4},{7,5},{8,10},{9,11},{10,... | collective-permute-start | bytes 1179656 | tf_op jit(solution)/shard_map/ppermute | solution.py:25
  107.8 18.3 %collective-permute-start.37 = (bf16[256,768]{1,0:T(8,128)(2,1)}, bf16[256,768]{1,0:T(8,128)(2,1)S(1)}, u32[]{:S(2)}, u32[]{:S(2)}) collective-permute-start(bf16[256,768]{1,0:T(8,128)(2,1)} %collective-permute-done.17.refs_2_), channel_id=1, source_target_pairs={{0,1},{1,0},{2,3},{3,2},{4,5},{5,4},{6,7},{7,6},{8,9},{9,8},{10,11... | collective-permute-start | bytes 1179656 | tf_op jit(solution)/shard_map/ppermute | solution.py:25
  107.8 3.7 %collective-permute-start.26 = (f32[2,1024]{1,0:T(2,128)S(1)}, f32[2,1024]{1,0:T(2,128)S(1)}, u32[]{:S(2)}, u32[]{:S(2)}) collective-permute-start(f32[2,1024]{1,0:T(2,128)S(1)} %slice.238), channel_id=1, source_target_pairs={{0,8},{8,0},{16,24},{24,16},{1,9},{9,1},{17,25},{25,17},{2,10},{10... | collective-permute-start | bytes 24584 | tf_op jit(solution)/shard_map/ppermute | solution.py:25
  111.9 3.7 %collective-permute-start.27 = (f32[2,1024]{1,0:T(2,128)S(1)}, f32[2,1024]{1,0:T(2,128)S(1)}, u32[]{:S(2)}, u32[]{:S(2)}) collective-permute-start(f32[2,1024]{1,0:T(2,128)S(1)} %pad_maximum_fusion.19), channel_id=1, source_target_pairs={{0,4},{4,0},{1,5},{5,1},{2,6},{6,2},{3,7},{7,3},{8,12},{12,8},{9,1... | collective-permute-start | bytes 24584 | tf_op jit(solution)/shard_map/ppermute | solution.py:25
  113.6 11.9 %collective-permute-start.30 = (bf16[256,896]{1,0:T(8,128)(2,1)}, bf16[256,896]{1,0:T(8,128)(2,1)S(1)}, u32[]{:S(2)}, u32[]{:S(2)}) collective-permute-start(bf16[256,896]{1,0:T(8,128)(2,1)} %collective-permute-done.23.refs_9_), channel_id=1, source_target_pairs={{0,2},{1,3},{2,0},{3,1},{4,6},{5,7},{6,4},{7,5},{8,10},{9,11},{10,... | collective-permute-start | bytes 1376264 | tf_op jit(solution)/shard_map/ppermute | solution.py:25
  116.1 9.4 %collective-permute-start.28 = (f32[2,768]{1,0:T(2,128)S(1)}, f32[2,768]{1,0:T(2,128)S(1)}, u32[]{:S(2)}, u32[]{:S(2)}) collective-permute-start(f32[2,768]{1,0:T(2,128)S(1)} %get-tuple-element.229), channel_id=1, source_target_pairs={{0,2},{1,3},{2,0},{3,1},{4,6},{5,7},{6,4},{7,5},{8,10},{9,11},{10,... | collective-permute-start | bytes 18440 | tf_op jit(solution)/shard_map/ppermute | solution.py:25
  117.7 22.0 %collective-permute-start.31 = (bf16[256,896]{1,0:T(8,128)(2,1)}, bf16[256,896]{1,0:T(8,128)(2,1)}, u32[]{:S(2)}, u32[]{:S(2)}) collective-permute-start(bf16[256,896]{1,0:T(8,128)(2,1)} %get-tuple-element.156.refs_15_.refs_8_), channel_id=1, source_target_pairs={{0,1},{1,0},{2,3},{3,2},{4,5},{5,4},{6,7},{7,6},{8,9},{9,8},{10,11... | collective-permute-start | bytes 1376264 | tf_op jit(solution)/shard_map/ppermute | solution.py:25
  117.7 22.0 %collective-permute-start.32 = (bf16[256,896]{1,0:T(8,128)(2,1)}, bf16[256,896]{1,0:T(8,128)(2,1)}, u32[]{:S(2)}, u32[]{:S(2)}) collective-permute-start(bf16[256,896]{1,0:T(8,128)(2,1)} %collective-permute-done.23.refs_9_), channel_id=1, source_target_pairs={{0,1},{1,0},{2,3},{3,2},{4,5},{5,4},{6,7},{7,6},{8,9},{9,8},{10,11... | collective-permute-start | bytes 1376264 | tf_op jit(solution)/shard_map/ppermute | solution.py:25
  125.5 14.2 %collective-permute-start.33 = (bf16[256,896]{1,0:T(8,128)(2,1)}, bf16[256,896]{1,0:T(8,128)(2,1)}, u32[]{:S(2)}, u32[]{:S(2)}) collective-permute-start(bf16[256,896]{1,0:T(8,128)(2,1)} %collective-permute-done.24.refs_10_), channel_id=1, source_target_pairs={{0,1},{1,0},{2,3},{3,2},{4,5},{5,4},{6,7},{7,6},{8,9},{9,8},{10,11... | collective-permute-start | bytes 1376264 | tf_op jit(solution)/shard_map/ppermute | solution.py:25
  125.5 14.4 %collective-permute-start.34 = (bf16[256,896]{1,0:T(8,128)(2,1)S(1)}, bf16[256,896]{1,0:T(8,128)(2,1)}, u32[]{:S(2)}, u32[]{:S(2)}) collective-permute-start(bf16[256,896]{1,0:T(8,128)(2,1)S(1)} %collective-permute-done.30.refs_11_), channel_id=1, source_target_pairs={{0,1},{1,0},{2,3},{3,2},{4,5},{5,4},{6,7},{7,6},{8,9},{9,8},{10,11... | collective-permute-start | bytes 1376264 | tf_op jit(solution)/shard_map/ppermute | solution.py:25
  126.1 2.3 collective-permute-start.29
  128.3 11.4 %collective-permute-start.38 = (bf16[256,768]{1,0:T(8,128)(2,1)}, bf16[256,768]{1,0:T(8,128)(2,1)S(1)}, u32[]{:S(2)}, u32[]{:S(2)}) collective-permute-start(bf16[256,768]{1,0:T(8,128)(2,1)} %collective-permute-done.25.refs_3_), channel_id=1, source_target_pairs={{0,1},{1,0},{2,3},{3,2},{4,5},{5,4},{6,7},{7,6},{8,9},{9,8},{10,11... | collective-permute-start | bytes 1179656 | tf_op jit(solution)/shard_map/ppermute | solution.py:25
  140.5 16.5 %collective-permute-start.39 = (bf16[256,768]{1,0:T(8,128)(2,1)}, bf16[256,768]{1,0:T(8,128)(2,1)S(1)}, u32[]{:S(2)}, u32[]{:S(2)}) collective-permute-start(bf16[256,768]{1,0:T(8,128)(2,1)} %get-tuple-element.147.g0), channel_id=1, source_target_pairs={{0,2},{1,3},{2,0},{3,1},{4,6},{5,7},{6,4},{7,5},{8,10},{9,11},{10,... | collective-permute-start | bytes 1179656 | tf_op jit(solution)/shard_map/ppermute | solution.py:25
  142.0 15.0 %collective-permute-start.40 = (bf16[256,768]{1,0:T(8,128)(2,1)}, bf16[256,768]{1,0:T(8,128)(2,1)S(1)}, u32[]{:S(2)}, u32[]{:S(2)}) collective-permute-start(bf16[256,768]{1,0:T(8,128)(2,1)} %get-tuple-element.147.g0), channel_id=1, source_target_pairs={{0,1},{1,0},{2,3},{3,2},{4,5},{5,4},{6,7},{7,6},{8,9},{9,8},{10,11... | collective-permute-start | bytes 1179656 | tf_op jit(solution)/shard_map/ppermute | solution.py:25
  157.8 21.5 %collective-permute-start.42 = (bf16[384,768]{1,0:T(8,128)(2,1)}, bf16[384,768]{1,0:T(8,128)(2,1)S(1)}, u32[]{:S(2)}, u32[]{:S(2)}) collective-permute-start(bf16[384,768]{1,0:T(8,128)(2,1)} %get-tuple-element.178), channel_id=1, source_target_pairs={{0,8},{24,16},{1,9},{25,17},{2,10},{26,18},{3,11},{27,19},{4,12},{... | collective-permute-start | bytes 1769480 | tf_op jit(solution)/shard_map/ppermute | solution.py:51
  161.5 3.1 %collective-permute-start.41 = (bf16[256,768]{1,0:T(8,128)(2,1)S(1)}, bf16[256,768]{1,0:T(8,128)(2,1)S(1)}, u32[]{:S(2)}, u32[]{:S(2)}) collective-permute-start(bf16[256,768]{1,0:T(8,128)(2,1)S(1)} %collective-permute-done.39.g1), channel_id=1, source_target_pairs={{0,1},{1,0},{2,3},{3,2},{4,5},{5,4},{6,7},{7,6},{8,9},{9,8},{10,11... | collective-permute-start | bytes 1179656 | tf_op jit(solution)/shard_map/ppermute | solution.py:25
  161.7 25.8 %collective-permute-start.50 = (bf16[768,384]{1,0:T(8,128)(2,1)}, bf16[768,384]{1,0:T(8,128)(2,1)S(1)}, u32[]{:S(2)}, u32[]{:S(2)}) collective-permute-start(bf16[768,384]{1,0:T(8,128)(2,1)} %get-tuple-element.192), channel_id=1, source_target_pairs={{0,8},{24,16},{1,9},{25,17},{2,10},{26,18},{3,11},{27,19},{4,12},{... | collective-permute-start | bytes 1769480 | tf_op jit(solution)/shard_map/ppermute | solution.py:51
  179.3 27.6 %collective-permute-start.43 = (bf16[2,256,768]{2,1,0:T(8,128)(2,1)}, bf16[2,256,768]{2,1,0:T(8,128)(2,1)S(1)}, u32[]{:S(2)}, u32[]{:S(2)}) collective-permute-start(bf16[2,256,768]{2,1,0:T(8,128)(2,1)} %get-tuple-element.180), channel_id=1, source_target_pairs={{0,1},{1,0},{2,3},{3,2},{4,5},{5,4},{6,7},{7,6},{8,9},{9,8},{10,11... | collective-permute-start | bytes 2359304 | tf_op jit(solution)/shard_map/ppermute | solution.py:25
  179.5 9.5 %collective-permute-start.49 = (bf16[192,768]{1,0:T(8,128)(2,1)}, bf16[192,768]{1,0:T(8,128)(2,1)S(1)}, u32[]{:S(2)}, u32[]{:S(2)}) collective-permute-start(bf16[192,768]{1,0:T(8,128)(2,1)} %get-tuple-element.186), channel_id=1, source_target_pairs={{0,4},{4,0},{1,5},{5,1},{2,6},{6,2},{3,7},{7,3},{8,12},{12,8},{9,1... | collective-permute-start | bytes 884744 | tf_op jit(solution)/shard_map/ppermute | solution.py:25
  180.0 4.0 %collective-permute-start.46 = (f32[7,768]{1,0:T(8,128)}, f32[7,768]{1,0:T(8,128)S(1)}, u32[]{:S(2)}, u32[]{:S(2)}) collective-permute-start(f32[7,768]{1,0:T(8,128)} %maximum_maximum_fusion.1), channel_id=1, source_target_pairs={{0,2},{1,3},{2,0},{3,1},{4,6},{5,7},{6,4},{7,5},{8,10},{9,11},{10,... | collective-permute-start | bytes 64520 | tf_op jit(solution)/shard_map/ppermute | solution.py:25
  180.7 16.9 %collective-permute-start.45 = (bf16[384,768]{1,0:T(8,128)(2,1)S(1)}, bf16[384,768]{1,0:T(8,128)(2,1)S(1)}, u32[]{:S(2)}, u32[]{:S(2)}) collective-permute-start(bf16[384,768]{1,0:T(8,128)(2,1)S(1)} %add_convert_fusion.3), channel_id=1, source_target_pairs={{8,16},{16,8},{9,17},{17,9},{10,18},{18,10},{11,19},{19,11},{12,20... | collective-permute-start | bytes 1769480 | tf_op jit(solution)/shard_map/ppermute | solution.py:55
  184.8 2.9 %collective-permute-start.47 = (f32[7,768]{1,0:T(8,128)S(1)}, f32[7,768]{1,0:T(8,128)S(1)}, u32[]{:S(2)}, u32[]{:S(2)}) collective-permute-start(f32[7,768]{1,0:T(8,128)S(1)} %add.231), channel_id=1, source_target_pairs={{0,1},{1,0},{2,3},{3,2},{4,5},{5,4},{6,7},{7,6},{8,9},{9,8},{10,11... | collective-permute-start | bytes 64520 | tf_op jit(solution)/shard_map/ppermute | solution.py:25
  187.9 9.6 %collective-permute-start.48 = (bf16[224,768]{1,0:T(8,128)(2,1)S(1)}, bf16[224,768]{1,0:T(8,128)(2,1)S(1)}, u32[]{:S(2)}, u32[]{:S(2)}) collective-permute-start(bf16[224,768]{1,0:T(8,128)(2,1)S(1)} %pad_maximum_fusion.2), channel_id=1, source_target_pairs={{0,4},{4,0},{1,5},{5,1},{2,6},{6,2},{3,7},{7,3},{8,12},{12,8},{9,1... | collective-permute-start | bytes 1032200 | tf_op jit(solution)/shard_map/ppermute | solution.py:25
  189.1 9.6 %collective-permute-start.51 = (bf16[192,768]{1,0:T(8,128)(2,1)S(1)}, bf16[192,768]{1,0:T(8,128)(2,1)S(1)}, u32[]{:S(2)}, u32[]{:S(2)}) collective-permute-start(bf16[192,768]{1,0:T(8,128)(2,1)S(1)} %add_convert_fusion.10), channel_id=1, source_target_pairs={{0,8},{24,16},{1,9},{25,17},{2,10},{26,18},{3,11},{27,19},{4,12},{... | collective-permute-start | bytes 884744 | tf_op jit(solution)/shard_map/ppermute | solution.py:51
  192.9 14.6 %collective-permute-start.56 = (bf16[768,384]{1,0:T(8,128)(2,1)S(1)}, bf16[768,384]{1,0:T(8,128)(2,1)S(1)}, u32[]{:S(2)}, u32[]{:S(2)}) collective-permute-start(bf16[768,384]{1,0:T(8,128)(2,1)S(1)} %add_convert_fusion.1), channel_id=1, source_target_pairs={{8,16},{16,8},{9,17},{17,9},{10,18},{18,10},{11,19},{19,11},{12,20... | collective-permute-start | bytes 1769480 | tf_op jit(solution)/shard_map/ppermute | solution.py:55
  198.7 16.2 %collective-permute-start.52 = (bf16[384,768]{1,0:T(8,128)(2,1)S(1)}, bf16[384,768]{1,0:T(8,128)(2,1)S(1)}, u32[]{:S(2)}, u32[]{:S(2)}) collective-permute-start(bf16[384,768]{1,0:T(8,128)(2,1)S(1)} %add_convert_fusion.2), channel_id=1, source_target_pairs={{8,0},{16,24},{9,1},{17,25},{10,2},{18,26},{11,3},{19,27},{12,4},{... | collective-permute-start | bytes 1769480 | tf_op jit(solution)/shard_map/ppermute | solution.py:60
  200.3 7.4 %collective-permute-start.53 = (bf16[192,768]{1,0:T(8,128)(2,1)S(1)}, bf16[192,768]{1,0:T(8,128)(2,1)S(1)}, u32[]{:S(2)}, u32[]{:S(2)}) collective-permute-start(bf16[192,768]{1,0:T(8,128)(2,1)S(1)} %add_convert_fusion.9), channel_id=1, source_target_pairs={{8,16},{16,8},{9,17},{17,9},{10,18},{18,10},{11,19},{19,11},{12,20... | collective-permute-start | bytes 884744 | tf_op jit(solution)/shard_map/ppermute | solution.py:55
  201.0 11.6 %collective-permute-start.57 = (bf16[224,768]{1,0:T(8,128)(2,1)S(1)}, bf16[224,768]{1,0:T(8,128)(2,1)S(1)}, u32[]{:S(2)}, u32[]{:S(2)}) collective-permute-start(bf16[224,768]{1,0:T(8,128)(2,1)S(1)} %pad_maximum_fusion.3), channel_id=1, source_target_pairs={{0,8},{24,16},{1,9},{25,17},{2,10},{26,18},{3,11},{27,19},{4,12},{... | collective-permute-start | bytes 1032200 | tf_op jit(solution)/shard_map/ppermute | solution.py:51
  207.0 10.7 %collective-permute-start.44 = (bf16[256,768]{1,0:T(8,128)(2,1)S(1)}, bf16[256,768]{1,0:T(8,128)(2,1)S(1)}, u32[]{:S(2)}, u32[]{:S(2)}) collective-permute-start(bf16[256,768]{1,0:T(8,128)(2,1)S(1)} %fusion.5), channel_id=1, source_target_pairs={{0,2},{1,3},{2,0},{3,1},{4,6},{5,7},{6,4},{7,5},{8,10},{9,11},{10,... | collective-permute-start | bytes 1179656 | tf_op jit(solution)/shard_map/ppermute | solution.py:25
  212.7 25.4 %collective-permute-start.58 = (bf16[768,384]{1,0:T(8,128)(2,1)S(1)}, bf16[768,384]{1,0:T(8,128)(2,1)S(1)}, u32[]{:S(2)}, u32[]{:S(2)}) collective-permute-start(bf16[768,384]{1,0:T(8,128)(2,1)S(1)} %add_convert_fusion), channel_id=1, source_target_pairs={{8,0},{16,24},{9,1},{17,25},{10,2},{18,26},{11,3},{19,27},{12,4},{... | collective-permute-start | bytes 1769480 | tf_op jit(solution)/shard_map/ppermute | solution.py:60
  214.2 4.6 %collective-permute-start.59 = (bf16[224,768]{1,0:T(8,128)(2,1)S(1)}, bf16[224,768]{1,0:T(8,128)(2,1)S(1)}, u32[]{:S(2)}, u32[]{:S(2)}) collective-permute-start(bf16[224,768]{1,0:T(8,128)(2,1)S(1)} %pad_maximum_fusion.4), channel_id=1, source_target_pairs={{8,16},{16,8},{9,17},{17,9},{10,18},{18,10},{11,19},{19,11},{12,20... | collective-permute-start | bytes 1032200 | tf_op jit(solution)/shard_map/ppermute | solution.py:55
  215.0 21.7 %collective-permute-start.54 = (bf16[192,768]{1,0:T(8,128)(2,1)S(1)}, bf16[192,768]{1,0:T(8,128)(2,1)S(1)}, u32[]{:S(2)}, u32[]{:S(2)}) collective-permute-start(bf16[192,768]{1,0:T(8,128)(2,1)S(1)} %add_convert_fusion.8), channel_id=1, source_target_pairs={{8,0},{16,24},{9,1},{17,25},{10,2},{18,26},{11,3},{19,27},{12,4},{... | collective-permute-start | bytes 884744 | tf_op jit(solution)/shard_map/ppermute | solution.py:60
  216.3 24.0 %collective-permute-start.63 = (bf16[384,768]{1,0:T(8,128)(2,1)S(1)}, bf16[384,768]{1,0:T(8,128)(2,1)S(1)}, u32[]{:S(2)}, u32[]{:S(2)}) collective-permute-start(bf16[384,768]{1,0:T(8,128)(2,1)S(1)} %broadcast_select_fusion.5), channel_id=1, source_target_pairs={{0,4},{4,0},{1,5},{5,1},{2,6},{6,2},{3,7},{7,3},{8,12},{12,8},{9,1... | collective-permute-start | bytes 1769480 | tf_op jit(solution)/shard_map/ppermute | solution.py:25
  236.7 9.9 %collective-permute-start.55 = (bf16[192,768]{1,0:T(8,128)(2,1)S(1)}, bf16[192,768]{1,0:T(8,128)(2,1)S(1)}, u32[]{:S(2)}, u32[]{:S(2)}) collective-permute-start(bf16[192,768]{1,0:T(8,128)(2,1)S(1)} %broadcast_select_fusion.7), channel_id=1, source_target_pairs={{0,4},{4,0},{1,5},{5,1},{2,6},{6,2},{3,7},{7,3},{8,12},{12,8},{9,1... | collective-permute-start | bytes 884744 | tf_op jit(solution)/shard_map/ppermute | solution.py:25
  238.2 10.0 %collective-permute-start.60 = (bf16[224,768]{1,0:T(8,128)(2,1)S(1)}, bf16[224,768]{1,0:T(8,128)(2,1)S(1)}, u32[]{:S(2)}, u32[]{:S(2)}) collective-permute-start(bf16[224,768]{1,0:T(8,128)(2,1)S(1)} %pad_maximum_fusion.5), channel_id=1, source_target_pairs={{8,0},{16,24},{9,1},{17,25},{10,2},{18,26},{11,3},{19,27},{12,4},{... | collective-permute-start | bytes 1032200 | tf_op jit(solution)/shard_map/ppermute | solution.py:60
  239.5 19.7 %collective-permute-start.62 = (bf16[768,384]{1,0:T(8,128)(2,1)S(1)}, bf16[768,384]{1,0:T(8,128)(2,1)S(1)}, u32[]{:S(2)}, u32[]{:S(2)}) collective-permute-start(bf16[768,384]{1,0:T(8,128)(2,1)S(1)} %broadcast_select_fusion.4), channel_id=1, source_target_pairs={{0,4},{4,0},{1,5},{5,1},{2,6},{6,2},{3,7},{7,3},{8,12},{12,8},{9,1... | collective-permute-start | bytes 1769480 | tf_op jit(solution)/shard_map/ppermute | solution.py:25
  248.3 14.8 %collective-permute-start.61 = (bf16[192,768]{1,0:T(8,128)(2,1)S(1)}, bf16[192,768]{1,0:T(8,128)(2,1)S(1)}, u32[]{:S(2)}, u32[]{:S(2)}) collective-permute-start(bf16[192,768]{1,0:T(8,128)(2,1)S(1)} %slice.340), channel_id=1, source_target_pairs={{0,4},{4,0},{1,5},{5,1},{2,6},{6,2},{3,7},{7,3},{8,12},{12,8},{9,1... | collective-permute-start | bytes 884744 | tf_op jit(solution)/shard_map/ppermute | solution.py:25
  (45 other events, 417.6 us)

commit v4 on v3

--- a/solution.py
+++ b/solution.py
@@ -309,21 +309,21 @@
     )(place, *grads, compact, query, keys, values, probs, context, wq, wk, wv, wo)
 
 
-WHOLE, QUARTERS = 4, 8
+WHOLE, QUARTERS = 4, 6
 
 
 def weight_copies(place, wholes, quarters, up, down, sems):
-    rows = quarters[0].shape[0] // 2
+    rows = quarters[0].shape[0] // 4
     shards = []
     for s in range(2):
         shards.append([(wholes[2 * s], up.at[s]), (wholes[2 * s + 1], down.at[s])])
     for s in range(2):
         copies = []
-        for i, flip in enumerate((0, 2, 1, 3)):
+        for i, flip, start in ((0, 0, 0), (1, 2, 0), (2, 1, 0), (0, 3, 2)):
             spot = pl.ds(pl.multiple_of((place[1] ^ flip) * rows, rows), rows)
-            piece = quarters[4 * s + i]
-            copies.append((piece.at[pl.ds(0, rows)], up.at[2 + s, spot]))
-            copies.append((piece.at[pl.ds(rows, rows)], down.at[2 + s, spot]))
+            piece = quarters[3 * s + i]
+            copies.append((piece.at[pl.ds(start * rows, rows)], up.at[2 + s, spot]))
+            copies.append((piece.at[pl.ds((start + 1) * rows, rows)], down.at[2 + s, spot]))
         shards.append(copies)
     number, made = 0, []
     for copies in shards:
@@ -337,26 +337,29 @@
 
 def ffn_kernel(place, *refs):
     wholes, quarters = refs[:WHOLE], refs[WHOLE : WHOLE + QUARTERS]
-    middle, biases, down_bias, gain, shift, counts = refs[12:18]
-    slopes_out, normed_out, rows_out, output_out, sums_out, pooled_out = refs[18:24]
-    up, down, sems = refs[24:]
+    middle, biases, affine, counts = refs[10:14]
+    slopes_out, normed_out, rows_out, output_out, sums_out, pooled_out = refs[14:20]
+    up, down, sems = refs[20:]
+    down_bias, gain, shift = affine[0:1], affine[1:2], affine[2:3]
     shards = weight_copies(place, wholes, quarters, up, down, sems)
-    for copies in shards:
+    for copies in shards[:2]:
         for copy in copies:
             copy.start()
     length, width = middle.shape
     mid = middle[...]
     mid_low = mid.astype(low)
-    total = mid + down_bias[...]
+    total = mid + down_bias
     for s, copies in enumerate(shards):
         for copy in copies:
             copy.wait()
+        for copy in shards[s + 2] if s < 2 else []:
+            copy.start()
         hidden, slope = gelu_parts(dot(mid_low, up[s]) + biases[s : s + 1])
         slopes_out[s] = slope.astype(low)
         total += dot(hidden.astype(low), down[s])
     normed, rstd = norm_parts(total)
     normed_out[...] = normed
-    output_out[0] = (normed * gain[...] + shift[...]).astype(low)
+    output_out[0] = (normed * gain + shift).astype(low)
     count = counts[0:1, 0:1]
     live = jnp.where(lax.broadcasted_iota(jnp.int32, (length, 1), 0).astype(full) < count, 1.0, 0.0)
     factor = rstd * live
@@ -366,17 +369,17 @@
     rows_out[:, width:] = jnp.where(lane == 0, first, jnp.where(lane == 1, factor - first, 0.0)).astype(low)
     live_sum = jnp.sum(normed * live, axis=0, keepdims=True)
     sums_out[...] = live_sum
-    pooled_out[:, :width] = (live_sum / count * gain[...] + shift[...]).astype(low)
+    pooled_out[:, :width] = (live_sum / count * gain + shift).astype(low)
     pooled_out[:, width:] = jnp.broadcast_to(count, (1, LANES)).astype(low)
 
 
 def ffn_back_kernel(place, *refs):
     wholes, quarters = refs[:WHOLE], refs[WHOLE : WHOLE + QUARTERS]
-    slopes, vector, normed_two, rows, normed_one, rstd_one, gain = refs[12:19]
-    attn_out, one_out, sums_out = refs[19:22]
-    up, down, sems = refs[22:]
+    slopes, vector, normed_two, rows, summed, affine = refs[10:16]
+    attn_out, one_out, sums_out = refs[16:19]
+    up, down, sems = refs[19:]
     shards = weight_copies(place, wholes, quarters, up, down, sems)
-    for copies in shards:
+    for copies in shards[:2]:
         for copy in copies:
             copy.start()
     length, width = normed_two.shape
@@ -387,10 +390,12 @@
     for s, copies in enumerate(shards):
         for copy in copies:
             copy.wait()
+        for copy in shards[s + 2] if s < 2 else []:
+            copy.start()
         grad = (slopes[s].astype(full) * dot(ffn_grad, down[s], ((1,), (1,)))).astype(low)
         total += dot(grad, up[s], ((1,), (1,)))
-    normed = normed_one[...]
-    one_grad = norm_backward(total * gain[...], normed, rstd_one[:, 0:1])
+    normed, rstd = norm_parts(summed[...])
+    one_grad = norm_backward(total * affine[3:4], normed, rstd)
     one_out[...] = one_grad
     attn_grad = one_grad.astype(low)
     attn_out[...] = attn_grad
@@ -457,13 +462,14 @@
     )(*middles, *rows, vectors, up, bias, down)
 
 
-def contrast(pooled, key_queue, gathered, returned):
+def contrast(pooled, key_queue, gathered, halfway, returned):
     width = key_queue.shape[1]
     queries = jnp.concatenate([pooled, swap(pooled, "fsdp", 1)])
     both = queries
     queries = gathered(queries)
     for stride in strides("dp"):
         queries = jnp.concatenate([queries, swap(queries, "dp", stride)])
+    queries = halfway(queries)
     logits = dot(queries[:, :width], key_queue, ((1,), (1,))) * inv_temp
     top = jnp.max(logits, axis=1, keepdims=True)
     expo = jnp.exp(logits - top)
@@ -473,10 +479,9 @@
     for axis, stride in [("dp", s) for s in reversed(strides("dp"))] + [("fsdp", 1)]:
         half = state.shape[0] // 2
         if axis == "fsdp":
+            state = returned(state)
             kept, other = state, swap(jnp.concatenate([state[1:2], state[0:1]]), axis, stride)
         else:
-            if stride == 1:
-                state = returned(state)
             kept, other = state[:half], swap(state[half:], axis, stride)
         top = jnp.maximum(kept[:, width : width + 1], other[:, width : width + 1])
         summed = kept * jnp.exp(kept[:, width : width + 1] - top) + other * jnp.exp(other[:, width : width + 1] - top)
@@ -522,12 +527,9 @@
     quarter, half = hidden // 4, hidden // 2
 
     def quarter_of(which):
-        return jnp.concatenate([lax.dynamic_slice_in_dim(w, which * quarter, quarter, 0) for w in (up_weight, down_weight)])
-
-    piece_y = swap(quarter_of(kind), "tensor", 2)
-    piece_d = swap(quarter_of(kind ^ 3), "tensor", 2)
-    bias_pair = jnp.concatenate([up_bias[None], swap(up_bias[None], "tensor", 1)])
-    biases = jnp.concatenate([bias_pair, swap(bias_pair, "tensor", 2)])
+        return [lax.dynamic_slice_in_dim(w, which * quarter, quarter, 0) for w in (up_weight, down_weight)]
+
+    piece_y = swap(jnp.concatenate(quarter_of(kind) + quarter_of(kind ^ 3)), "tensor", 2)
     wholes = [up_weight, down_weight, swap(up_weight, "tensor", 1), swap(down_weight, "tensor", 1)]
     up_half = lax.dynamic_slice_in_dim(up_weight, f * half, half, 1)
     down_half = lax.dynamic_slice_in_dim(down_weight, f * half, half, 0)
@@ -537,28 +539,34 @@
     compact, query, keys, values, probs, context, near, away, table, counts = attend(
         tokens, keep_mask, crop_len, place, query_weight.T, key_weight.T, value_weight.T, out_weight, query_bias, value_bias
     )
-    near, away, piece_y, known = tie((near, away, piece_y, known))
+    affine = jnp.stack([down_bias, final_gain, final_shift, norm_gain])
+    for stride in strides("dp"):
+        known = jnp.concatenate([known, swap(known, "dp", stride)])
+    compact, piece_y, known, wholes, affine, up_half, down_half, bias_half = tie(
+        (compact, piece_y, known, wholes, affine, up_half, down_half, bias_half)
+    )
     other = swap(away, "tensor", 1)
-    piece_x = swap(piece_y, "fsdp", 1)
-    piece_z = swap(piece_y, "dp", 1)
     share = pos_keys.shape[0]
     spot = jnp.arange(devices, dtype=jnp.int32)[None]
     mates = jnp.stack([group, group ^ 1]) * share + member
     wanted = jnp.sum(jnp.where(spot == mates[:, None], pos_index[None], 0), axis=1, keepdims=True)
     chosen = jnp.where(((spot // share) ^ group) * share + spot % share == wanted, 1.0, 0.0).astype(low)
-    sent, piece_d, biases, chosen = tie((plus(near[1], other[1]), piece_d, biases, chosen))
-    hops = strides("dp")
-    for stride in hops[:-1]:
-        known = jnp.concatenate([known, swap(known, "dp", stride)])
+    sent, piece_y, bias_own = tie((plus(near[1], other[1]), piece_y, up_bias))
+    bias_far = swap(bias_own[None], "tensor", 2)
+    first = piece_y[: 2 * quarter]
+    piece_x = swap(first, "fsdp", 1)
+    piece_z = swap(first, "dp", 1)
+    bias_pair = jnp.concatenate([up_bias[None], bias_far])
+    bias_pair = jnp.concatenate([bias_pair, swap(bias_pair, "tensor", 1)])
+    biases = jnp.stack([bias_pair[0], bias_pair[2], bias_pair[1], bias_pair[3]])
     attn_out = near[0].astype(full) + other[0].astype(full) + swap(sent, "tensor", 2).astype(full)
-    attn_out, piece_x, piece_z, known = tie((attn_out, piece_x, piece_z, known))
-
-    normed_one, rstd_one = norm_parts(compact[0].astype(full) + attn_out + out_bias)
-    rstd_one = jnp.broadcast_to(rstd_one, (length, LANES))
-    middle = normed_one * norm_gain + norm_shift
+    quarters = [piece_y, piece_x, piece_z]
+    quarters = quarters + [swap(p, "tensor", 1) for p in quarters]
+
+    summed = compact[0].astype(full) + attn_out + out_bias
+    middle = norm_parts(summed)[0] * norm_gain + norm_shift
     middle_low = middle.astype(low)
-    quarters = [piece_y, piece_x, piece_z, piece_d]
-    quarters = quarters + [swap(p, "tensor", 1) for p in quarters]
+    quarters, biases, chosen, middle, middle_low = tie((quarters, biases, chosen, middle, middle_low))
     S = jax.ShapeDtypeStruct
     slopes, normed_two, rows, output, live_sum, pooled = with_weights(
         ffn_kernel,
@@ -566,7 +574,7 @@
         place,
         wholes,
         quarters,
-        [middle, biases, down_bias[None], final_gain[None], final_shift[None], counts],
+        [middle, biases, affine, counts],
         [
             S((4, length, hidden), low),
             S((length, width), full),
@@ -578,8 +586,7 @@
     )
 
     middle_x, middle_y = swap(middle_low, "fsdp", 1), swap(middle_low, "tensor", 2)
-    known = jnp.concatenate([known, swap(known, "dp", hops[-1])])
-    pooled, middle_x, middle_y, known, rstd_one = tie((pooled, middle_x, middle_y, known, rstd_one))
+    pooled, middle_x, middle_y = tie((pooled, middle_x, middle_y))
     pairs = {}
 
     def gathered(queries):
@@ -588,17 +595,21 @@
         pairs["mid"] = swap(mid, "tensor", 2)
         return queries
 
+    def halfway(queries):
+        queries, pairs["mid"] = tie((queries, pairs["mid"]))
+        return queries
+
     def returned(state):
-        state, pairs["x"], pairs["y"], pairs["mid"] = tie((state, pairs["x"], pairs["y"], pairs["mid"]))
+        state, pairs["x"], pairs["y"] = tie((state, pairs["x"], pairs["y"]))
         return state
 
     positive = dot(chosen, known)
-    top, total, key_sum, pooled_pair = contrast(pooled, key_queue, gathered, returned)
+    top, total, key_sum, pooled_pair = contrast(pooled, key_queue, gathered, halfway, returned)
     count_pair = pooled_pair[:, width : width + 1].astype(full)
     middle_pair = [middle_low, middle_x, middle_y, pairs["mid"]]
-    rows_pair = [rows, pairs["x"], pairs["y"], swap(pairs["x"], "tensor", 2)]
+    rows_pair = [rows, pairs["x"], pairs["y"]]
     middles = middle_pair + [swap(p, "tensor", 1) for p in middle_pair]
-    rows_all = rows_pair + [swap(p, "tensor", 1) for p in rows_pair]
+    rows_core = [swap(p, "tensor", 1) for p in rows_pair]
 
     pos_logit = jnp.sum(pooled_pair[:, :width].astype(full) * positive, axis=1, keepdims=True) * inv_temp
     top_final = jnp.maximum(top, pos_logit)
@@ -610,73 +621,72 @@
     vector_pair = result_row * final_gain
     final_gain_part = result_row[0:1] * live_sum
 
-    vectors_far = jnp.concatenate([vector_pair, swap(vector_pair, "tensor", 2)])
-    vectors_all = jnp.concatenate([vectors_far, swap(vectors_far, "tensor", 1)])
-
+    vector_pair, rows_core = tie((vector_pair, rows_core))
     attn_grad, one_grad, sums = with_weights(
         ffn_back_kernel,
         "ffn_back",
         place,
         wholes,
         quarters,
-        [slopes, vector_pair[0:1], normed_two, rows, normed_one, rstd_one, norm_gain[None]],
+        [slopes, vector_pair[0:1], normed_two, rows, summed, affine],
         [S((length, width), low), S((length, width), full), S((8, width), full)],
     )
-    vectors_all, attn_grad, rows_all, middles = tie((vectors_all, attn_grad, rows_all, middles))
-    down_part, up_part, up_bias_half = ffn_weights(middles, rows_all, vectors_all, up_half, bias_half, down_half)
-    attn_far, attn_core, down_part, up_part = tie((swap(attn_grad, "tensor", 2), swap(attn_grad, "tensor", 1), down_part, up_part))
+    vectors_far, rows_far, attn_grad, middles, sums = tie((swap(vector_pair, "tensor", 2), swap(pairs["x"], "tensor", 2), attn_grad, middles, sums))
+    vectors_far = jnp.concatenate([vector_pair, vectors_far])
+    vectors_all = jnp.concatenate([vectors_far, swap(vectors_far, "tensor", 1)])
+    rows_all = rows_pair + [rows_far] + rows_core + [swap(rows_far, "tensor", 1)]
+    vectors = jnp.concatenate([final_gain_part, pooled_grad[0:1], sums[0:4], jnp.broadcast_to(loss_part / devices, (1, width))])
+    down, up, up_bias_half = ffn_weights(middles, rows_all, vectors_all, up_half, bias_half, down_half)
+    vectors = vectors + swap(vectors, "tensor", 1)
+    attn_far, attn_core, down, up, vectors = tie((swap(attn_grad, "tensor", 2), swap(attn_grad, "tensor", 1), down, up, vectors))
     attn_grads = [attn_grad, attn_far, attn_core, swap(attn_far, "tensor", 1)]
 
     near_in, away_in, qk_kept, qk_sent, vo_kept, vo_sent, query_bias_part, value_bias_part = attend_back(
         place, attn_grads, compact, query, keys, values, probs, context, query_weight.T, key_weight.T, value_weight.T, out_weight
     )
     line = lax.axis_size("dp") == 4
-    down_next = inward(down_part) if line else down_part
-    qk_sent, vo_sent, near_in, away_in, down_next = tie((qk_sent, vo_sent, near_in, away_in, down_next))
-    qk_sum = plus(qk_kept, swap(qk_sent, "fsdp", 1))
-    vectors = jnp.concatenate([final_gain_part, pooled_grad[0:1], sums[0:4], jnp.broadcast_to(loss_part / devices, (1, width))])
-    vectors, _ = tie((vectors, qk_sent))
-    for stride in (2, 1):
-        vectors = vectors + swap(vectors, "tensor", stride)
+    moved = inward(down) if line else down
+    qk_sent, vo_sent, near_in, away_in, moved, vectors = tie((qk_sent, vo_sent, near_in, away_in, moved, vectors))
+    vectors = vectors + swap(vectors, "tensor", 2)
     pad = jnp.zeros((1, width - 2 * mine), full)
     narrow = jnp.concatenate([query_bias_part, value_bias_part, pad], axis=1)
     blank = jnp.zeros_like(up_bias_half)
     up_bias_part = jnp.concatenate([jnp.where(f == 0, up_bias_half, blank), jnp.where(f == 0, blank, up_bias_half)], axis=1)
     vectors = jnp.concatenate([vectors, narrow, up_bias_part, jnp.zeros((7, width), full)])
     extra = carried(vectors)
-    vo_sum = plus_carried(jnp.concatenate([vo_kept, extra]), swap(jnp.concatenate([vo_sent, extra]), "fsdp", 1), mine)
     if line:
-        down_sum = plus(down_part, down_next)
-        up_sum = plus(up_part, inward(up_part))
-        qk_sum, up_sum = tie((qk_sum, up_sum))
-        down_sum = plus(down_sum, across(down_sum))
-        qk_sum = plus(qk_sum, inward(qk_sum))
-        down_sum, vo_sum, qk_sum = tie((down_sum, vo_sum, qk_sum))
-        up_sum = plus(up_sum, across(up_sum))
-        vo_sum = plus_carried(vo_sum, inward(vo_sum), mine)
-        up_sum, vo_sum = tie((up_sum, vo_sum))
-        qk_sum = plus(qk_sum, across(qk_sum))
-        down_sum = outward(down_sum)
-        down_sum, qk_sum = tie((down_sum, qk_sum))
-        vo_sum = plus_carried(vo_sum, across(vo_sum), mine)
-        down_other = swap(down_sum, "fsdp", 1)
-        up_sum = outward(up_sum)
-        qk_sum = outward(qk_sum)
-        up_sum, vo_sum = tie((up_sum, vo_sum))
-        vo_sum = outward(vo_sum)
-    else:
-        down_sum, up_sum, qk_sum, vo_sum = [lax.psum(a.astype(full), "dp").astype(low) for a in (down_part, up_part, qk_sum, vo_sum)]
-        down_other = swap(down_sum, "fsdp", 1)
-    if line:
-        extra = vo_sum[mine:].astype(full)
+        up_in = inward(up)
+        qk = plus(qk_kept, swap(qk_sent, "fsdp", 1))
+        vo = plus_carried(jnp.concatenate([vo_kept, extra]), swap(jnp.concatenate([vo_sent, extra]), "fsdp", 1), mine)
+        down = plus(down, moved)
+        down = plus(down, across(down))
+        qk, up_in = tie((qk, up_in))
+        up = plus(up, up_in)
+        vo, down = tie((vo, down))
+        qk = plus(qk, inward(qk))
+        vo = plus_carried(vo, inward(vo), mine)
+        up = plus(up, across(up))
+        up, vo = tie((up, vo))
+        qk = plus(qk, across(qk))
+        down = outward(down)
+        qk, down = tie((qk, down))
+        vo = plus_carried(vo, across(vo), mine)
+        up = outward(up)
+        qk = outward(qk)
+        vo = outward(vo)
+        extra, vo = vo[mine:].astype(full), vo[:mine]
         vectors = extra[:16] + extra[16:]
     else:
+        down, up, qk, vo = [
+            lax.psum(a.astype(full), "dp").astype(low)
+            for a in (down, up, plus(qk_kept, swap(qk_sent, "fsdp", 1)), plus(vo_kept, swap(vo_sent, "fsdp", 1)))
+        ]
         vectors = lax.psum(vectors + swap(vectors, "fsdp", 1), "dp")
-    vo_sum = vo_sum[:mine]
-    down_weight_grad = jnp.concatenate(ordered(down_sum, down_other, f)).astype(full)
-    up_weight_grad = jnp.concatenate(ordered(up_sum, swap(up_sum, "fsdp", 1), f), axis=1).astype(full)
-    query_grad, key_grad = ordered(qk_sum, swap(qk_sum, "fsdp", 1), f)
-    value_grad, out_grad = ordered(vo_sum, swap(vo_sum, "fsdp", 1), f)
+    down_other, up_other, qk_other, vo_other = [swap(a, "fsdp", 1) for a in (down, up, qk, vo)]
+    down_weight_grad = jnp.concatenate(ordered(down, down_other, f)).astype(full)
+    up_weight_grad = jnp.concatenate(ordered(up, up_other, f), axis=1).astype(full)
+    query_grad, key_grad = ordered(qk, qk_other, f)
+    value_grad, out_grad = ordered(vo, vo_other, f)
 
     other_in = swap(away_in, "tensor", 1)
     far_in = swap(plus(near_in[1], other_in[1]), "tensor", 2)

time: 265 us -> 242 us (0.913)
  waiting for transfers between devices: 97.5 us -> 78.5 us
    ppermute x52 -> x50, waiting for transfers between devices: 70.9 us -> 50.6 us  [swap(): return lax.ppermute(array, axis, [(i, i ^ stride) for i in range(size)])]
    ppermute x4, waiting for transfers between devices: 18.2 us -> 25.6 us  [outward(): outer = lax.ppermute(part, 'dp', [(1, 0), (2, 3)])]
    ppermute x4, waiting for transfers between devices: 8.37 us -> 2.27 us  [inward(): return lax.ppermute(part, 'dp', [(0, 1), (3, 2)])]
    broadcast_in_dim x6 -> x2, local copies, waits for them, and re-layouts: 3.07 us -> 0.01 us  [the longest x1 0.01 us: per_device(): bias_far = swap(bias_own[None], 'tensor', 2)]
    ppermute x52 -> x50, starting transfers between devices: 45.2 us -> 45.8 us  [swap(): return lax.ppermute(array, axis, [(i, i ^ stride) for i in range(size)])]
  transfers between devices with their start and end apart: 64 -> 62, of which waited for: 22 -> 25; matrix products, arithmetic and copies ran while one was open for 11% -> 13% of each run, Pallas kernels for 21% -> 23%
where the time goes in v4:
time: 242 us; the launch traced here: 241 us
  waiting for transfers between devices  78.5 us (32%)
  starting transfers between devices  67 us (28%)
  Pallas kernels  55.7 us (23%)
  other arithmetic  19 us (8%)
  local copies, waits for them, and re-layouts  14.5 us (6%)
  matrix products  3.81 us (2%)
  between operations  2.49 us (1%)
    ppermute x50, waiting for transfers between devices, swap(): return lax.ppermute(array, axis, [(i, i ^ stride) for i in range(size)])  50.6 us
    ppermute x50, starting transfers between devices, swap(): return lax.ppermute(array, axis, [(i, i ^ stride) for i in range(size)])  45.8 us
    ppermute x4, waiting for transfers between devices, outward(): outer = lax.ppermute(part, 'dp', [(1, 0), (2, 3)])  25.6 us
    pallas_call x2, Pallas kernels, with_weights(): pl.pallas_call(kernel, grid_spec=pltpu.PrefetchScalarGridSpec(num_scalar_...  18.7 us
    pallas_call x1, Pallas kernels, attend_back(): pl.pallas_call(attend_back_kernel, grid_spec=pltpu.PrefetchScalarGridSpec...  13.9 us
    ppermute x4, starting transfers between devices, inward(): return lax.ppermute(part, 'dp', [(0, 1), (3, 2)])  12.9 us
    pallas_call x1, Pallas kernels, attend(): pl.pallas_call(attend_kernel, grid_spec=pltpu.PrefetchScalarGridSpec(num_...  11.9 us
    pallas_call x1, Pallas kernels, ffn_weights(): pl.pallas_call(ffn_weights_kernel, out_shape=[S((half, width), low), S((w...  11.2 us
  transfers between devices with their start and end apart: 62, of which 25 were waited for; matrix products, arithmetic and copies ran while one was open for 13% of the time, Pallas kernels for 23%

profile of v4, /device:TPU:0, one launch (start us, length us, event | category | flops | bytes accessed | tf_op | source)
XLA Modules:
  0.0 241.0 jit_solution(10642988704891475069)
XLA Ops:
  1.3 1.4 constant_dynamic-slice_fusion.5
  3.1 1.2 pad_maximum_fusion
  4.3 2.9 %collective-permute-start = (bf16[768,768]{1,0:T(8,128)(2,1)}, bf16[768,768]{1,0:T(8,128)(2,1)}, u32[]{:S(2)}, u32[]{:S(2)}) collective-permute-start(bf16[768,768]{1,0:T(8,128)(2,1)} %pad_maximum_fusion), channel_id=1, source_target_pairs={{0,2},{1,3},{2,0},{3,1},{4,6},{5,7},{6,4},{7,5},{8,10},{9,11},{10,... | collective-permute-start | bytes 3538952 | tf_op jit(solution)/shard_map/ppermute | solution.py:25
  7.2 1.5 collective-permute-start.1
  9.3 11.9 %attend.1 = (bf16[4,256,768]{2,1,0:T(8,128)(2,1)}, bf16[4,256,192]{2,1,0:T(8,128)(2,1)}, bf16[4,256,192]{2,1,0:T(8,128)(2,1)}, bf16[4,256,192]{2,1,0:T(8,128)(2,...) custom-call(s32[2]{0:T(128)} %get-tuple-element.278.place_in.place, ...), custom_call_target="tpu_custom_call" | custom-call | tf_op jit(solution)/shard_map/attend/pallas_call | solution.py:153
  21.4 2.1 constant_dynamic-slice_fusion.refs_19_
  24.3 1.6 collective-permute-start.2
  26.2 1.9 collective-permute-done.2
  28.1 2.7 %collective-permute-start.3 = (bf16[16,768]{1,0:T(8,128)(2,1)S(1)}, bf16[16,768]{1,0:T(8,128)(2,1)S(1)}, u32[]{:S(2)}, u32[]{:S(2)}) collective-permute-start(bf16[16,768]{1,0:T(8,128)(2,1)S(1)} %pad_maximum_fusion.7), channel_id=1, source_target_pairs={{0,16},{8,24},{16,0},{24,8},{1,17},{9,25},{17,1},{25,9},{2,18},{10... | collective-permute-start | bytes 73736 | tf_op jit(solution)/shard_map/ppermute | solution.py:25
  33.5 1.1 fusion.4
  35.4 1.5 collective-permute-start.14
  36.9 1.5 collective-permute-done.12
  39.1 1.1 slice.240
  40.8 1.6 collective-permute-start.8
  43.0 2.2 collective-permute-done.14
  45.3 1.4 fusion.45
  46.7 9.2 %collective-permute-done.7.refs_5_ = bf16[384,768]{1,0:T(8,128)(2,1)S(1)} collective-permute-done((bf16[384,768]{1,0:T(8,128)(2,1)S(1)}, bf16[384,768]{1,0:T(8,128)(2,1)S(1)}, u32[]{:S(2)}, u32[]{:S(2)}) %collective-permute-start.7) | collective-permute-done | bytes 589856 | tf_op jit(solution)/shard_map/ppermute | solution.py:25
  56.7 1.1 fusion.44
  59.6 1.1 collective-permute-start.15
  61.8 9.4 %ffn.1 = (bf16[4,256,768]{2,1,0:T(8,128)(2,1)}, f32[256,768]{1,0:T(8,128)}, bf16[256,896]{1,0:T(8,128)(2,1)}, bf16[1,256,768]{2,1,0:T(8,128)(2,1)}, f32[1,768]{1,0:T(1,128)}, /*index=5*/bf16[1,896]{1,0:T(2,128)(2,1)}) custom-call(s32[2]{0:T(128)} %get-tuple-element.278.place_in.place, bf16[768,768]{1,0:T(8,128)(2,1)} %refs_0_.1, bf16[768,768]{1,0:T(8,128)(2,1)} %refs_1_.1, ...), custom_call_target="tpu_custom_call" | custom-call | tf_op jit(solution)/shard_map/ffn/pallas_call | solution.py:412
  72.7 3.2 %collective-permute-done.17 = bf16[1,896]{1,0:T(2,128)(2,1)S(1)} collective-permute-done((bf16[1,896]{1,0:T(2,128)(2,1)}, bf16[1,896]{1,0:T(2,128)(2,1)S(1)}, u32[]{:S(2)}, u32[]{:S(2)}) %collective-permute-start.17) | collective-permute-done | bytes 1824 | tf_op jit(solution)/shard_map/ppermute | solution.py:25
  77.3 1.6 collective-permute-start.18
  78.9 2.0 collective-permute-done.18
  80.9 2.7 %collective-permute-start.19 = (bf16[4,896]{1,0:T(4,128)(2,1)S(1)}, bf16[4,896]{1,0:T(4,128)(2,1)S(1)}, u32[]{:S(2)}, u32[]{:S(2)}) collective-permute-start(bf16[4,896]{1,0:T(4,128)(2,1)S(1)} %pad_maximum_fusion.17), channel_id=1, source_target_pairs={{0,16},{8,24},{16,0},{24,8},{1,17},{9,25},{17,1},{25,9},{2,18},{10... | collective-permute-start | bytes 21512 | tf_op jit(solution)/shard_map/ppermute | solution.py:25
  84.1 1.5 collective-permute-start.23
  85.6 1.3 collective-permute-start.24
  87.0 1.0 fusion.50
  89.0 2.6 %collective-permute-start.21 = (f32[4,1024]{1,0:T(4,128)S(1)}, f32[4,1024]{1,0:T(4,128)S(1)}, u32[]{:S(2)}, u32[]{:S(2)}) collective-permute-start(f32[4,1024]{1,0:T(4,128)S(1)} %slice.317), channel_id=1, source_target_pairs={{0,16},{8,24},{16,0},{24,8},{1,17},{9,25},{17,1},{25,9},{2,18},{10... | collective-permute-start | bytes 49160 | tf_op jit(solution)/shard_map/ppermute | solution.py:25
  91.7 2.0 collective-permute-done.21
  94.0 1.6 collective-permute-start.22
  95.6 1.1 multiply_reduce_fusion.1
  96.7 1.0 collective-permute-done.22
  99.0 1.6 collective-permute-start.30
  100.6 1.2 collective-permute-done.25
  106.7 9.3 %ffn_back.1 = (bf16[256,768]{1,0:T(8,128)(2,1)}, f32[256,768]{1,0:T(8,128)}, f32[8,768]{1,0:T(8,128)}) custom-call(s32[2]{0:T(128)} %get-tuple-element.278.place_in.place, bf16[768,768]{1,0:T(8,128)(2,1)} %refs_0_.1, bf16[768,768]{1,0:T(8,128)(2,1)} %refs_1_.1, bf16[768,768]{1,0:T(8,128)(2,1)} %collective-permute-done.4.refs_2_, ...), custom_call_target="tpu_custom_call" | custom-call | tf_op jit(solution)/shard_map/ffn_back/pallas_call | solution.py:412
  116.1 1.6 collective-permute-start.35
  121.8 11.2 %ffn_weights.1 = (bf16[384,768]{1,0:T(8,128)(2,1)}, bf16[768,384]{1,0:T(8,128)(2,1)}, f32[1,384]{1,0:T(1,128)}) custom-call(bf16[256,768]{1,0:T(8,128)(2,1)} %copy-done.9, bf16[256,768]{1,0:T(8,128)(2,1)} %collective-permute-done.15.refs_1_, bf16[256,768]{1,0:T(8,128)(2,1)} %collective-permute-done.16.refs_2_, ...), custom_call_target="tpu_custom_call" | custom-call | tf_op jit(solution)/shard_map/ffn_weights/pallas_call | solution.py:458
  133.0 3.5 %collective-permute-start.41 = (bf16[384,768]{1,0:T(8,128)(2,1)}, bf16[384,768]{1,0:T(8,128)(2,1)S(1)}, u32[]{:S(2)}, u32[]{:S(2)}) collective-permute-start(bf16[384,768]{1,0:T(8,128)(2,1)} %get-tuple-element.196), channel_id=1, source_target_pairs={{0,8},{24,16},{1,9},{25,17},{2,10},{26,18},{3,11},{27,19},{4,12},{... | collective-permute-start | bytes 1769480 | tf_op jit(solution)/shard_map/ppermute | solution.py:51
  136.7 1.4 collective-permute-start.45
  139.5 13.9 %attend_back.1 = (bf16[2,256,768]{2,1,0:T(8,128)(2,1)}, bf16[2,256,768]{2,1,0:T(8,128)(2,1)}, bf16[192,768]{1,0:T(8,128)(2,1)}, bf16[192,768]{1,0:T(8,128)(2,1)}...) custom-call(s32[2]{0:T(128)} %get-tuple-element.278.place_in.place, ...), custom_call_target="tpu_custom_call" | custom-call | tf_op jit(solution)/shard_map/attend_back/pallas_call | solution.py:272
  155.2 1.5 collective-permute-start.44
  158.4 6.8 %collective-permute-done.44 = bf16[192,768]{1,0:T(8,128)(2,1)S(1)} collective-permute-done((bf16[192,768]{1,0:T(8,128)(2,1)S(1)}, bf16[192,768]{1,0:T(8,128)(2,1)S(1)}, u32[]{:S(2)}, u32[]{:S(2)}) %collective-permute-start.44) | collective-permute-done | bytes 294944 | tf_op jit(solution)/shard_map/ppermute | solution.py:25
  165.3 4.2 %collective-permute-start.46 = (bf16[192,768]{1,0:T(8,128)(2,1)S(1)}, bf16[192,768]{1,0:T(8,128)(2,1)S(1)}, u32[]{:S(2)}, u32[]{:S(2)}) collective-permute-start(bf16[192,768]{1,0:T(8,128)(2,1)S(1)} %add_convert_fusion.11), channel_id=1, source_target_pairs={{0,8},{24,16},{1,9},{25,17},{2,10},{26,18},{3,11},{27,19},{4,12},{... | collective-permute-start | bytes 884744 | tf_op jit(solution)/shard_map/ppermute | solution.py:51
  170.3 1.4 collective-permute-done.49
  172.1 3.9 %collective-permute-start.55 = (bf16[224,768]{1,0:T(8,128)(2,1)S(1)}, bf16[224,768]{1,0:T(8,128)(2,1)S(1)}, u32[]{:S(2)}, u32[]{:S(2)}) collective-permute-start(bf16[224,768]{1,0:T(8,128)(2,1)S(1)} %pad_maximum_fusion.2), channel_id=1, source_target_pairs={{0,8},{24,16},{1,9},{25,17},{2,10},{26,18},{3,11},{27,19},{4,12},{... | collective-permute-start | bytes 1032200 | tf_op jit(solution)/shard_map/ppermute | solution.py:51
  175.9 1.5 collective-permute-start.51
  178.4 1.5 collective-permute-start.43
  180.1 2.3 collective-permute-done.55
  182.5 1.4 collective-permute-start.59
  184.6 7.7 %collective-permute-done.51 = bf16[384,768]{1,0:T(8,128)(2,1)S(1)} collective-permute-done((bf16[384,768]{1,0:T(8,128)(2,1)S(1)}, bf16[384,768]{1,0:T(8,128)(2,1)S(1)}, u32[]{:S(2)}, u32[]{:S(2)}) %collective-permute-start.51) | collective-permute-done | bytes 589856 | tf_op jit(solution)/shard_map/ppermute | solution.py:60
  192.4 1.5 collective-permute-start.61
  194.0 1.3 collective-permute-start.52
  195.3 1.2 fusion
  196.6 1.3 collective-permute-start.57
  197.9 14.5 %collective-permute-done.52 = bf16[192,768]{1,0:T(8,128)(2,1)S(1)} collective-permute-done((bf16[192,768]{1,0:T(8,128)(2,1)S(1)}, bf16[192,768]{1,0:T(8,128)(2,1)S(1)}, u32[]{:S(2)}, u32[]{:S(2)}) %collective-permute-start.52) | collective-permute-done | bytes 294944 | tf_op jit(solution)/shard_map/ppermute | solution.py:60
  212.4 1.5 collective-permute-start.53
  214.7 3.4 %collective-permute-done.57 = bf16[224,768]{1,0:T(8,128)(2,1)S(1)} collective-permute-done((bf16[224,768]{1,0:T(8,128)(2,1)S(1)}, bf16[224,768]{1,0:T(8,128)(2,1)S(1)}, u32[]{:S(2)}, u32[]{:S(2)}) %collective-permute-start.57) | collective-permute-done | bytes 344096 | tf_op jit(solution)/shard_map/ppermute | solution.py:60
  218.2 1.5 collective-permute-start.58
  221.6 1.6 maximum_convert_fusion.1
  223.2 1.1 convert_bitcast_fusion.1
  224.3 12.8 %collective-permute-done.58 = bf16[192,768]{1,0:T(8,128)(2,1)S(1)} collective-permute-done((bf16[192,768]{1,0:T(8,128)(2,1)S(1)}, bf16[192,768]{1,0:T(8,128)(2,1)S(1)}, u32[]{:S(2)}, u32[]{:S(2)}) %collective-permute-start.58) | collective-permute-done | bytes 294944 | tf_op jit(solution)/shard_map/ppermute | solution.py:25
  237.1 1.1 select_convert_fusion
  238.3 1.6 maximum_convert_fusion
  239.9 1.2 copy-done.1
  (280 shorter events, 37.4 us)
Async XLA Ops:
  0.7 86.3 %copy-start = (bf16[2048,768]{1,0:T(8,128)(2,1)S(1)}, bf16[2048,768]{1,0:T(8,128)(2,1)}, u32[]{:S(2)}) copy-start(bf16[2048,768]{1,0:T(8,128)(2,1)} %param.26) | copy-start | bytes 9437188
  0.7 34.0 %collective-permute-start.4 = (bf16[768,768]{1,0:T(8,128)(2,1)}, bf16[768,768]{1,0:T(8,128)(2,1)}, u32[]{:S(2)}, u32[]{:S(2)}) collective-permute-start(bf16[768,768]{1,0:T(8,128)(2,1)} %refs_0_.1), channel_id=1, source_target_pairs={{0,1},{1,0},{2,3},{3,2},{4,5},{5,4},{6,7},{7,6},{8,9},{9,8},{10,11... | collective-permute-start | bytes 3538952 | tf_op jit(solution)/shard_map/ppermute | solution.py:25
  1.2 33.4 %collective-permute-start.5 = (bf16[768,768]{1,0:T(8,128)(2,1)}, bf16[768,768]{1,0:T(8,128)(2,1)}, u32[]{:S(2)}, u32[]{:S(2)}) collective-permute-start(bf16[768,768]{1,0:T(8,128)(2,1)} %refs_1_.1), channel_id=1, source_target_pairs={{0,1},{1,0},{2,3},{3,2},{4,5},{5,4},{6,7},{7,6},{8,9},{9,8},{10,11... | collective-permute-start | bytes 3538952 | tf_op jit(solution)/shard_map/ppermute | solution.py:25
  4.3 30.4 %collective-permute-start = (bf16[768,768]{1,0:T(8,128)(2,1)}, bf16[768,768]{1,0:T(8,128)(2,1)}, u32[]{:S(2)}, u32[]{:S(2)}) collective-permute-start(bf16[768,768]{1,0:T(8,128)(2,1)} %pad_maximum_fusion), channel_id=1, source_target_pairs={{0,2},{1,3},{2,0},{3,1},{4,6},{5,7},{6,4},{7,5},{8,10},{9,11},{10,... | collective-permute-start | bytes 3538952 | tf_op jit(solution)/shard_map/ppermute | solution.py:25
  7.2 17.1 %collective-permute-start.1 = (bf16[4,768]{1,0:T(4,128)(2,1)S(1)}, bf16[4,768]{1,0:T(4,128)(2,1)S(1)}, u32[]{:S(2)}, u32[]{:S(2)}) collective-permute-start(bf16[4,768]{1,0:T(4,128)(2,1)S(1)} %copy-done.29), channel_id=1, source_target_pairs={{0,4},{4,0},{1,5},{5,1},{2,6},{6,2},{3,7},{7,3},{8,12},{12,8},{9,1... | collective-permute-start | bytes 18440 | tf_op jit(solution)/shard_map/ppermute | solution.py:25
  21.2 12.4 %collective-permute-start.6 = (bf16[2,256,768]{2,1,0:T(8,128)(2,1)}, bf16[2,256,768]{2,1,0:T(8,128)(2,1)}, u32[]{:S(2)}, u32[]{:S(2)}) collective-permute-start(bf16[2,256,768]{2,1,0:T(8,128)(2,1)} %get-tuple-element.124), channel_id=1, source_target_pairs={{0,1},{1,0},{2,3},{3,2},{4,5},{5,4},{6,7},{7,6},{8,9},{9,8},{10,11... | collective-permute-start | bytes 2359304 | tf_op jit(solution)/shard_map/ppermute | solution.py:25
  24.3 3.8 %collective-permute-start.2 = (bf16[8,768]{1,0:T(8,128)(2,1)S(1)}, bf16[8,768]{1,0:T(8,128)(2,1)S(1)}, u32[]{:S(2)}, u32[]{:S(2)}) collective-permute-start(bf16[8,768]{1,0:T(8,128)(2,1)S(1)} %pad_maximum_fusion.11), channel_id=1, source_target_pairs={{0,8},{8,0},{16,24},{24,16},{1,9},{9,1},{17,25},{25,17},{2,10},{10... | collective-permute-start | bytes 36872 | tf_op jit(solution)/shard_map/ppermute | solution.py:25
  28.1 4.8 %collective-permute-start.3 = (bf16[16,768]{1,0:T(8,128)(2,1)S(1)}, bf16[16,768]{1,0:T(8,128)(2,1)S(1)}, u32[]{:S(2)}, u32[]{:S(2)}) collective-permute-start(bf16[16,768]{1,0:T(8,128)(2,1)S(1)} %pad_maximum_fusion.7), channel_id=1, source_target_pairs={{0,16},{8,24},{16,0},{24,8},{1,17},{9,25},{17,1},{25,9},{2,18},{10... | collective-permute-start | bytes 73736 | tf_op jit(solution)/shard_map/ppermute | solution.py:25
  34.7 3.7 %collective-permute-start.12 = (f32[1,768]{1,0:T(1,128)S(1)}, f32[1,768]{1,0:T(1,128)S(1)}, u32[]{:S(2)}, u32[]{:S(2)}) collective-permute-start(f32[1,768]{1,0:T(1,128)S(1)} %broadcast_in_dim.91), channel_id=1, source_target_pairs={{0,2},{1,3},{2,0},{3,1},{4,6},{5,7},{6,4},{7,5},{8,10},{9,11},{10,... | collective-permute-start | bytes 9224 | tf_op jit(solution)/shard_map/ppermute | solution.py:25
  35.4 9.9 %collective-permute-start.14 = (bf16[256,768]{1,0:T(8,128)(2,1)S(1)}, bf16[256,768]{1,0:T(8,128)(2,1)S(1)}, u32[]{:S(2)}, u32[]{:S(2)}) collective-permute-start(bf16[256,768]{1,0:T(8,128)(2,1)S(1)} %fusion.4), channel_id=1, source_target_pairs={{0,2},{1,3},{2,0},{3,1},{4,6},{5,7},{6,4},{7,5},{8,10},{9,11},{10,... | collective-permute-start | bytes 1179656 | tf_op jit(solution)/shard_map/ppermute | solution.py:25
  38.4 4.0 %collective-permute-start.13 = (f32[2,768]{1,0:T(2,128)S(1)}, f32[2,768]{1,0:T(2,128)S(1)}, u32[]{:S(2)}, u32[]{:S(2)}) collective-permute-start(f32[2,768]{1,0:T(2,128)S(1)} %pad_maximum_fusion.18), channel_id=1, source_target_pairs={{0,1},{1,0},{2,3},{3,2},{4,5},{5,4},{6,7},{7,6},{8,9},{9,8},{10,11... | collective-permute-start | bytes 18440 | tf_op jit(solution)/shard_map/ppermute | solution.py:25
  40.2 15.8 %collective-permute-start.7 = (bf16[384,768]{1,0:T(8,128)(2,1)S(1)}, bf16[384,768]{1,0:T(8,128)(2,1)S(1)}, u32[]{:S(2)}, u32[]{:S(2)}) collective-permute-start(bf16[384,768]{1,0:T(8,128)(2,1)S(1)} %slice.240), channel_id=1, source_target_pairs={{0,4},{4,0},{1,5},{5,1},{2,6},{6,2},{3,7},{7,3},{8,12},{12,8},{9,1... | collective-permute-start | bytes 1769480 | tf_op jit(solution)/shard_map/ppermute | solution.py:25
  40.8 15.4 %collective-permute-start.8 = (bf16[384,768]{1,0:T(8,128)(2,1)S(1)}, bf16[384,768]{1,0:T(8,128)(2,1)S(1)}, u32[]{:S(2)}, u32[]{:S(2)}) collective-permute-start(bf16[384,768]{1,0:T(8,128)(2,1)S(1)} %slice.240), channel_id=1, source_target_pairs={{0,8},{8,0},{16,24},{24,16},{1,9},{9,1},{17,25},{25,17},{2,10},{10... | collective-permute-start | bytes 1769480 | tf_op jit(solution)/shard_map/ppermute | solution.py:25
  42.4 16.4 %collective-permute-start.9 = (bf16[768,768]{1,0:T(8,128)(2,1)}, bf16[768,768]{1,0:T(8,128)(2,1)}, u32[]{:S(2)}, u32[]{:S(2)}) collective-permute-start(bf16[768,768]{1,0:T(8,128)(2,1)} %collective-permute-done.refs_4_), channel_id=1, source_target_pairs={{0,1},{1,0},{2,3},{3,2},{4,5},{5,4},{6,7},{7,6},{8,9},{9,8},{10,11... | collective-permute-start | bytes 3538952 | tf_op jit(solution)/shard_map/ppermute | solution.py:25
  56.0 2.0 collective-permute-start.10
  56.3 2.5 %collective-permute-start.11 = (bf16[384,768]{1,0:T(8,128)(2,1)S(1)}, bf16[384,768]{1,0:T(8,128)(2,1)S(1)}, u32[]{:S(2)}, u32[]{:S(2)}) collective-permute-start(bf16[384,768]{1,0:T(8,128)(2,1)S(1)} %collective-permute-done.8.refs_6_), channel_id=1, source_target_pairs={{0,1},{1,0},{2,3},{3,2},{4,5},{5,4},{6,7},{7,6},{8,9},{9,8},{10,11... | collective-permute-start | bytes 1769480 | tf_op jit(solution)/shard_map/ppermute | solution.py:25
  57.8 25.8 %copy-start.9 = (bf16[256,768]{1,0:T(8,128)(2,1)}, bf16[256,768]{1,0:T(8,128)(2,1)S(1)}, u32[]{:S(2)}) copy-start(bf16[256,768]{1,0:T(8,128)(2,1)S(1)} %get-tuple-element.165.refs_0_) | copy-start | bytes 1179652
  59.6 11.5 %collective-permute-start.15 = (bf16[256,768]{1,0:T(8,128)(2,1)S(1)}, bf16[256,768]{1,0:T(8,128)(2,1)}, u32[]{:S(2)}, u32[]{:S(2)}) collective-permute-start(bf16[256,768]{1,0:T(8,128)(2,1)S(1)} %get-tuple-element.165.refs_0_), channel_id=1, source_target_pairs={{0,4},{4,0},{1,5},{5,1},{2,6},{6,2},{3,7},{7,3},{8,12},{12,8},{9,1... | collective-permute-start | bytes 1179656 | tf_op jit(solution)/shard_map/ppermute | solution.py:25
  60.8 11.4 %collective-permute-start.16 = (bf16[256,768]{1,0:T(8,128)(2,1)S(1)}, bf16[256,768]{1,0:T(8,128)(2,1)}, u32[]{:S(2)}, u32[]{:S(2)}) collective-permute-start(bf16[256,768]{1,0:T(8,128)(2,1)S(1)} %get-tuple-element.165.refs_0_), channel_id=1, source_target_pairs={{0,2},{1,3},{2,0},{3,1},{4,6},{5,7},{6,4},{7,5},{8,10},{9,11},{10,... | collective-permute-start | bytes 1179656 | tf_op jit(solution)/shard_map/ppermute | solution.py:25
  72.1 3.8 %collective-permute-start.17 = (bf16[1,896]{1,0:T(2,128)(2,1)}, bf16[1,896]{1,0:T(2,128)(2,1)S(1)}, u32[]{:S(2)}, u32[]{:S(2)}) collective-permute-start(bf16[1,896]{1,0:T(2,128)(2,1)} %get-tuple-element.145), channel_id=1, source_target_pairs={{0,4},{4,0},{1,5},{5,1},{2,6},{6,2},{3,7},{7,3},{8,12},{12,8},{9,1... | collective-permute-start | bytes 5384 | tf_op jit(solution)/shard_map/ppermute | solution.py:25
  76.6 10.3 %collective-permute-start.20 = (bf16[256,768]{1,0:T(8,128)(2,1)}, bf16[256,768]{1,0:T(8,128)(2,1)}, u32[]{:S(2)}, u32[]{:S(2)}) collective-permute-start(bf16[256,768]{1,0:T(8,128)(2,1)} %collective-permute-done.15.refs_1_), channel_id=1, source_target_pairs={{0,2},{1,3},{2,0},{3,1},{4,6},{5,7},{6,4},{7,5},{8,10},{9,11},{10,... | collective-permute-start | bytes 1179656 | tf_op jit(solution)/shard_map/ppermute | solution.py:25
  77.3 3.6 %collective-permute-start.18 = (bf16[2,896]{1,0:T(2,128)(2,1)S(1)}, bf16[2,896]{1,0:T(2,128)(2,1)S(1)}, u32[]{:S(2)}, u32[]{:S(2)}) collective-permute-start(bf16[2,896]{1,0:T(2,128)(2,1)S(1)} %pad_maximum_fusion.19), channel_id=1, source_target_pairs={{0,8},{8,0},{16,24},{24,16},{1,9},{9,1},{17,25},{25,17},{2,10},{10... | collective-permute-start | bytes 10760 | tf_op jit(solution)/shard_map/ppermute | solution.py:25
  80.9 4.7 %collective-permute-start.19 = (bf16[4,896]{1,0:T(4,128)(2,1)S(1)}, bf16[4,896]{1,0:T(4,128)(2,1)S(1)}, u32[]{:S(2)}, u32[]{:S(2)}) collective-permute-start(bf16[4,896]{1,0:T(4,128)(2,1)S(1)} %pad_maximum_fusion.17), channel_id=1, source_target_pairs={{0,16},{8,24},{16,0},{24,8},{1,17},{9,25},{17,1},{25,9},{2,18},{10... | collective-permute-start | bytes 21512 | tf_op jit(solution)/shard_map/ppermute | solution.py:25
  83.6 18.6 %collective-permute-start.26 = (bf16[256,896]{1,0:T(8,128)(2,1)}, bf16[256,896]{1,0:T(8,128)(2,1)}, u32[]{:S(2)}, u32[]{:S(2)}) collective-permute-start(bf16[256,896]{1,0:T(8,128)(2,1)} %get-tuple-element.151.refs_13_.refs_8_), channel_id=1, source_target_pairs={{0,1},{1,0},{2,3},{3,2},{4,5},{5,4},{6,7},{7,6},{8,9},{9,8},{10,11... | collective-permute-start | bytes 1376264 | tf_op jit(solution)/shard_map/ppermute | solution.py:25
  83.6 20.5 %collective-permute-start.31 = (bf16[256,768]{1,0:T(8,128)(2,1)S(1)}, bf16[256,768]{1,0:T(8,128)(2,1)}, u32[]{:S(2)}, u32[]{:S(2)}) collective-permute-start(bf16[256,768]{1,0:T(8,128)(2,1)S(1)} %get-tuple-element.165.refs_0_), channel_id=1, source_target_pairs={{0,1},{1,0},{2,3},{3,2},{4,5},{5,4},{6,7},{7,6},{8,9},{9,8},{10,11... | collective-permute-start | bytes 1179656 | tf_op jit(solution)/shard_map/ppermute | solution.py:25
  84.1 13.9 %collective-permute-start.23 = (bf16[256,896]{1,0:T(8,128)(2,1)}, bf16[256,896]{1,0:T(8,128)(2,1)}, u32[]{:S(2)}, u32[]{:S(2)}) collective-permute-start(bf16[256,896]{1,0:T(8,128)(2,1)} %get-tuple-element.151.refs_13_.refs_8_), channel_id=1, source_target_pairs={{0,4},{4,0},{1,5},{5,1},{2,6},{6,2},{3,7},{7,3},{8,12},{12,8},{9,1... | collective-permute-start | bytes 1376264 | tf_op jit(solution)/shard_map/ppermute | solution.py:25
  85.6 12.5 %collective-permute-start.24 = (bf16[256,896]{1,0:T(8,128)(2,1)}, bf16[256,896]{1,0:T(8,128)(2,1)}, u32[]{:S(2)}, u32[]{:S(2)}) collective-permute-start(bf16[256,896]{1,0:T(8,128)(2,1)} %get-tuple-element.151.refs_13_.refs_8_), channel_id=1, source_target_pairs={{0,2},{1,3},{2,0},{3,1},{4,6},{5,7},{6,4},{7,5},{8,10},{9,11},{10,... | collective-permute-start | bytes 1376264 | tf_op jit(solution)/shard_map/ppermute | solution.py:25
  89.0 4.7 %collective-permute-start.21 = (f32[4,1024]{1,0:T(4,128)S(1)}, f32[4,1024]{1,0:T(4,128)S(1)}, u32[]{:S(2)}, u32[]{:S(2)}) collective-permute-start(f32[4,1024]{1,0:T(4,128)S(1)} %slice.317), channel_id=1, source_target_pairs={{0,16},{8,24},{16,0},{24,8},{1,17},{9,25},{17,1},{25,9},{2,18},{10... | collective-permute-start | bytes 49160 | tf_op jit(solution)/shard_map/ppermute | solution.py:25
  94.0 3.7 %collective-permute-start.22 = (f32[2,1024]{1,0:T(2,128)S(1)}, f32[2,1024]{1,0:T(2,128)S(1)}, u32[]{:S(2)}, u32[]{:S(2)}) collective-permute-start(f32[2,1024]{1,0:T(2,128)S(1)} %slice.322), channel_id=1, source_target_pairs={{0,8},{8,0},{16,24},{24,16},{1,9},{9,1},{17,25},{25,17},{2,10},{10... | collective-permute-start | bytes 24584 | tf_op jit(solution)/shard_map/ppermute | solution.py:25
  98.1 3.7 %collective-permute-start.25 = (f32[2,1024]{1,0:T(2,128)S(1)}, f32[2,1024]{1,0:T(2,128)S(1)}, u32[]{:S(2)}, u32[]{:S(2)}) collective-permute-start(f32[2,1024]{1,0:T(2,128)S(1)} %pad_maximum_fusion.16), channel_id=1, source_target_pairs={{0,4},{4,0},{1,5},{5,1},{2,6},{6,2},{3,7},{7,3},{8,12},{12,8},{9,1... | collective-permute-start | bytes 24584 | tf_op jit(solution)/shard_map/ppermute | solution.py:25
  99.0 3.8 %collective-permute-start.27 = (bf16[256,896]{1,0:T(8,128)(2,1)}, bf16[256,896]{1,0:T(8,128)(2,1)S(1)}, u32[]{:S(2)}, u32[]{:S(2)}) collective-permute-start(bf16[256,896]{1,0:T(8,128)(2,1)} %collective-permute-done.23.refs_9_), channel_id=1, source_target_pairs={{0,1},{1,0},{2,3},{3,2},{4,5},{5,4},{6,7},{7,6},{8,9},{9,8},{10,11... | collective-permute-start | bytes 1376264 | tf_op jit(solution)/shard_map/ppermute | solution.py:25
  99.0 17.0 %collective-permute-start.30 = (bf16[256,896]{1,0:T(8,128)(2,1)}, bf16[256,896]{1,0:T(8,128)(2,1)S(1)}, u32[]{:S(2)}, u32[]{:S(2)}) collective-permute-start(bf16[256,896]{1,0:T(8,128)(2,1)} %collective-permute-done.23.refs_9_), channel_id=1, source_target_pairs={{0,2},{1,3},{2,0},{3,1},{4,6},{5,7},{6,4},{7,5},{8,10},{9,11},{10,... | collective-permute-start | bytes 1376264 | tf_op jit(solution)/shard_map/ppermute | solution.py:25
  101.8 2.0 collective-permute-start.28
  102.2 13.8 %collective-permute-start.32 = (bf16[256,768]{1,0:T(8,128)(2,1)}, bf16[256,768]{1,0:T(8,128)(2,1)S(1)}, u32[]{:S(2)}, u32[]{:S(2)}) collective-permute-start(bf16[256,768]{1,0:T(8,128)(2,1)} %collective-permute-done.15.refs_1_), channel_id=1, source_target_pairs={{0,1},{1,0},{2,3},{3,2},{4,5},{5,4},{6,7},{7,6},{8,9},{9,8},{10,11... | collective-permute-start | bytes 1179656 | tf_op jit(solution)/shard_map/ppermute | solution.py:25
  102.8 13.2 %collective-permute-start.33 = (bf16[256,768]{1,0:T(8,128)(2,1)}, bf16[256,768]{1,0:T(8,128)(2,1)S(1)}, u32[]{:S(2)}, u32[]{:S(2)}) collective-permute-start(bf16[256,768]{1,0:T(8,128)(2,1)} %collective-permute-done.16.refs_2_), channel_id=1, source_target_pairs={{0,1},{1,0},{2,3},{3,2},{4,5},{5,4},{6,7},{7,6},{8,9},{9,8},{10,11... | collective-permute-start | bytes 1179656 | tf_op jit(solution)/shard_map/ppermute | solution.py:25
  103.8 12.2 %collective-permute-start.34 = (bf16[256,768]{1,0:T(8,128)(2,1)}, bf16[256,768]{1,0:T(8,128)(2,1)S(1)}, u32[]{:S(2)}, u32[]{:S(2)}) collective-permute-start(bf16[256,768]{1,0:T(8,128)(2,1)} %collective-permute-done.20.refs_3_), channel_id=1, source_target_pairs={{0,1},{1,0},{2,3},{3,2},{4,5},{5,4},{6,7},{7,6},{8,9},{9,8},{10,11... | collective-permute-start | bytes 1179656 | tf_op jit(solution)/shard_map/ppermute | solution.py:25
  104.1 12.0 %collective-permute-start.29 = (f32[2,768]{1,0:T(2,128)S(1)}, f32[2,768]{1,0:T(2,128)S(1)}, u32[]{:S(2)}, u32[]{:S(2)}) collective-permute-start(f32[2,768]{1,0:T(2,128)S(1)} %get-tuple-element.157), channel_id=1, source_target_pairs={{0,2},{1,3},{2,0},{3,1},{4,6},{5,7},{6,4},{7,5},{8,10},{9,11},{10,... | collective-permute-start | bytes 18440 | tf_op jit(solution)/shard_map/ppermute | solution.py:25
  116.1 16.9 %collective-permute-start.35 = (bf16[256,768]{1,0:T(8,128)(2,1)}, bf16[256,768]{1,0:T(8,128)(2,1)S(1)}, u32[]{:S(2)}, u32[]{:S(2)}) collective-permute-start(bf16[256,768]{1,0:T(8,128)(2,1)} %get-tuple-element.164.g0), channel_id=1, source_target_pairs={{0,2},{1,3},{2,0},{3,1},{4,6},{5,7},{6,4},{7,5},{8,10},{9,11},{10,... | collective-permute-start | bytes 1179656 | tf_op jit(solution)/shard_map/ppermute | solution.py:25
  117.7 15.3 %collective-permute-start.36 = (bf16[256,768]{1,0:T(8,128)(2,1)}, bf16[256,768]{1,0:T(8,128)(2,1)S(1)}, u32[]{:S(2)}, u32[]{:S(2)}) collective-permute-start(bf16[256,768]{1,0:T(8,128)(2,1)} %get-tuple-element.164.g0), channel_id=1, source_target_pairs={{0,1},{1,0},{2,3},{3,2},{4,5},{5,4},{6,7},{7,6},{8,9},{9,8},{10,11... | collective-permute-start | bytes 1179656 | tf_op jit(solution)/shard_map/ppermute | solution.py:25
  118.5 1.4 collective-permute-start.38
  119.0 1.9 collective-permute-start.37
  119.2 1.7 collective-permute-start.39
  133.0 20.4 %collective-permute-start.41 = (bf16[384,768]{1,0:T(8,128)(2,1)}, bf16[384,768]{1,0:T(8,128)(2,1)S(1)}, u32[]{:S(2)}, u32[]{:S(2)}) collective-permute-start(bf16[384,768]{1,0:T(8,128)(2,1)} %get-tuple-element.196), channel_id=1, source_target_pairs={{0,8},{24,16},{1,9},{25,17},{2,10},{26,18},{3,11},{27,19},{4,12},{... | collective-permute-start | bytes 1769480 | tf_op jit(solution)/shard_map/ppermute | solution.py:51
  136.5 2.3 collective-permute-start.40
  136.7 28.6 %collective-permute-start.45 = (bf16[768,384]{1,0:T(8,128)(2,1)}, bf16[768,384]{1,0:T(8,128)(2,1)S(1)}, u32[]{:S(2)}, u32[]{:S(2)}) collective-permute-start(bf16[768,384]{1,0:T(8,128)(2,1)} %get-tuple-element.202), channel_id=1, source_target_pairs={{0,8},{24,16},{1,9},{25,17},{2,10},{26,18},{3,11},{27,19},{4,12},{... | collective-permute-start | bytes 1769480 | tf_op jit(solution)/shard_map/ppermute | solution.py:51
  153.5 3.9 %collective-permute-start.48 = (f32[7,768]{1,0:T(8,128)S(1)}, f32[7,768]{1,0:T(8,128)S(1)}, u32[]{:S(2)}, u32[]{:S(2)}) collective-permute-start(f32[7,768]{1,0:T(8,128)S(1)} %fusion.36), channel_id=1, source_target_pairs={{0,2},{1,3},{2,0},{3,1},{4,6},{5,7},{6,4},{7,5},{8,10},{9,11},{10,... | collective-permute-start | bytes 64520 | tf_op jit(solution)/shard_map/ppermute | solution.py:25
  154.4 17.5 %collective-permute-start.50 = (bf16[384,768]{1,0:T(8,128)(2,1)S(1)}, bf16[384,768]{1,0:T(8,128)(2,1)S(1)}, u32[]{:S(2)}, u32[]{:S(2)}) collective-permute-start(bf16[384,768]{1,0:T(8,128)(2,1)S(1)} %add_convert_fusion.3), channel_id=1, source_target_pairs={{8,16},{16,8},{9,17},{17,9},{10,18},{18,10},{11,19},{19,11},{12,20... | collective-permute-start | bytes 1769480 | tf_op jit(solution)/shard_map/ppermute | solution.py:55
  155.2 9.9 %collective-permute-start.44 = (bf16[192,768]{1,0:T(8,128)(2,1)S(1)}, bf16[192,768]{1,0:T(8,128)(2,1)S(1)}, u32[]{:S(2)}, u32[]{:S(2)}) collective-permute-start(bf16[192,768]{1,0:T(8,128)(2,1)S(1)} %copy-done.42), channel_id=1, source_target_pairs={{0,4},{4,0},{1,5},{5,1},{2,6},{6,2},{3,7},{7,3},{8,12},{12,8},{9,1... | collective-permute-start | bytes 884744 | tf_op jit(solution)/shard_map/ppermute | solution.py:25
  156.8 21.5 %collective-permute-start.42 = (bf16[2,256,768]{2,1,0:T(8,128)(2,1)S(1)}, bf16[2,256,768]{2,1,0:T(8,128)(2,1)S(1)}, u32[]{:S(2)}, u32[]{:S(2)}) collective-permute-start(bf16[2,256,768]{2,1,0:T(8,128)(2,1)S(1)} %copy-done.41), channel_id=1, source_target_pairs={{0,1},{1,0},{2,3},{3,2},{4,5},{5,4},{6,7},{7,6},{8,9},{9,8},{10,11... | collective-permute-start | bytes 2359304 | tf_op jit(solution)/shard_map/ppermute | solution.py:25
  157.5 14.2 %collective-permute-start.49 = (bf16[224,768]{1,0:T(8,128)(2,1)S(1)}, bf16[224,768]{1,0:T(8,128)(2,1)S(1)}, u32[]{:S(2)}, u32[]{:S(2)}) collective-permute-start(bf16[224,768]{1,0:T(8,128)(2,1)S(1)} %pad_maximum_fusion.1), channel_id=1, source_target_pairs={{0,4},{4,0},{1,5},{5,1},{2,6},{6,2},{3,7},{7,3},{8,12},{12,8},{9,1... | collective-permute-start | bytes 1032200 | tf_op jit(solution)/shard_map/ppermute | solution.py:25
  165.3 12.2 %collective-permute-start.46 = (bf16[192,768]{1,0:T(8,128)(2,1)S(1)}, bf16[192,768]{1,0:T(8,128)(2,1)S(1)}, u32[]{:S(2)}, u32[]{:S(2)}) collective-permute-start(bf16[192,768]{1,0:T(8,128)(2,1)S(1)} %add_convert_fusion.11), channel_id=1, source_target_pairs={{0,8},{24,16},{1,9},{25,17},{2,10},{26,18},{3,11},{27,19},{4,12},{... | collective-permute-start | bytes 884744 | tf_op jit(solution)/shard_map/ppermute | solution.py:51
  169.6 10.2 %collective-permute-start.54 = (bf16[768,384]{1,0:T(8,128)(2,1)S(1)}, bf16[768,384]{1,0:T(8,128)(2,1)S(1)}, u32[]{:S(2)}, u32[]{:S(2)}) collective-permute-start(bf16[768,384]{1,0:T(8,128)(2,1)S(1)} %add_convert_fusion.1), channel_id=1, source_target_pairs={{8,16},{16,8},{9,17},{17,9},{10,18},{18,10},{11,19},{19,11},{12,20... | collective-permute-start | bytes 1769480 | tf_op jit(solution)/shard_map/ppermute | solution.py:55
  172.1 10.3 %collective-permute-start.55 = (bf16[224,768]{1,0:T(8,128)(2,1)S(1)}, bf16[224,768]{1,0:T(8,128)(2,1)S(1)}, u32[]{:S(2)}, u32[]{:S(2)}) collective-permute-start(bf16[224,768]{1,0:T(8,128)(2,1)S(1)} %pad_maximum_fusion.2), channel_id=1, source_target_pairs={{0,8},{24,16},{1,9},{25,17},{2,10},{26,18},{3,11},{27,19},{4,12},{... | collective-permute-start | bytes 1032200 | tf_op jit(solution)/shard_map/ppermute | solution.py:51
  175.9 16.4 %collective-permute-start.51 = (bf16[384,768]{1,0:T(8,128)(2,1)S(1)}, bf16[384,768]{1,0:T(8,128)(2,1)S(1)}, u32[]{:S(2)}, u32[]{:S(2)}) collective-permute-start(bf16[384,768]{1,0:T(8,128)(2,1)S(1)} %add_convert_fusion.2), channel_id=1, source_target_pairs={{8,0},{16,24},{9,1},{17,25},{10,2},{18,26},{11,3},{19,27},{12,4},{... | collective-permute-start | bytes 1769480 | tf_op jit(solution)/shard_map/ppermute | solution.py:60
  177.5 2.4 %collective-permute-start.47 = (bf16[192,768]{1,0:T(8,128)(2,1)S(1)}, bf16[192,768]{1,0:T(8,128)(2,1)S(1)}, u32[]{:S(2)}, u32[]{:S(2)}) collective-permute-start(bf16[192,768]{1,0:T(8,128)(2,1)S(1)} %add_convert_fusion.10), channel_id=1, source_target_pairs={{8,16},{16,8},{9,17},{17,9},{10,18},{18,10},{11,19},{19,11},{12,20... | collective-permute-start | bytes 884744 | tf_op jit(solution)/shard_map/ppermute | solution.py:55
  178.4 16.9 %collective-permute-start.43 = (bf16[256,768]{1,0:T(8,128)(2,1)S(1)}, bf16[256,768]{1,0:T(8,128)(2,1)S(1)}, u32[]{:S(2)}, u32[]{:S(2)}) collective-permute-start(bf16[256,768]{1,0:T(8,128)(2,1)S(1)} %fusion.5), channel_id=1, source_target_pairs={{0,2},{1,3},{2,0},{3,1},{4,6},{5,7},{6,4},{7,5},{8,10},{9,11},{10,... | collective-permute-start | bytes 1179656 | tf_op jit(solution)/shard_map/ppermute | solution.py:25
  182.5 31.4 %collective-permute-start.59 = (bf16[768,384]{1,0:T(8,128)(2,1)S(1)}, bf16[768,384]{1,0:T(8,128)(2,1)S(1)}, u32[]{:S(2)}, u32[]{:S(2)}) collective-permute-start(bf16[768,384]{1,0:T(8,128)(2,1)S(1)} %add_convert_fusion), channel_id=1, source_target_pairs={{8,0},{16,24},{9,1},{17,25},{10,2},{18,26},{11,3},{19,27},{12,4},{... | collective-permute-start | bytes 1769480 | tf_op jit(solution)/shard_map/ppermute | solution.py:60
  183.9 12.5 %collective-permute-start.56 = (bf16[224,768]{1,0:T(8,128)(2,1)S(1)}, bf16[224,768]{1,0:T(8,128)(2,1)S(1)}, u32[]{:S(2)}, u32[]{:S(2)}) collective-permute-start(bf16[224,768]{1,0:T(8,128)(2,1)S(1)} %pad_maximum_fusion.3), channel_id=1, source_target_pairs={{8,16},{16,8},{9,17},{17,9},{10,18},{18,10},{11,19},{19,11},{12,20... | collective-permute-start | bytes 1032200 | tf_op jit(solution)/shard_map/ppermute | solution.py:55
  192.4 29.1 %collective-permute-start.61 = (bf16[384,768]{1,0:T(8,128)(2,1)S(1)}, bf16[384,768]{1,0:T(8,128)(2,1)S(1)}, u32[]{:S(2)}, u32[]{:S(2)}) collective-permute-start(bf16[384,768]{1,0:T(8,128)(2,1)S(1)} %broadcast_select_fusion.5), channel_id=1, source_target_pairs={{0,4},{4,0},{1,5},{5,1},{2,6},{6,2},{3,7},{7,3},{8,12},{12,8},{9,1... | collective-permute-start | bytes 1769480 | tf_op jit(solution)/shard_map/ppermute | solution.py:25
  194.0 18.4 %collective-permute-start.52 = (bf16[192,768]{1,0:T(8,128)(2,1)S(1)}, bf16[192,768]{1,0:T(8,128)(2,1)S(1)}, u32[]{:S(2)}, u32[]{:S(2)}) collective-permute-start(bf16[192,768]{1,0:T(8,128)(2,1)S(1)} %add_convert_fusion.9), channel_id=1, source_target_pairs={{8,0},{16,24},{9,1},{17,25},{10,2},{18,26},{11,3},{19,27},{12,4},{... | collective-permute-start | bytes 884744 | tf_op jit(solution)/shard_map/ppermute | solution.py:60
  196.6 21.5 %collective-permute-start.57 = (bf16[224,768]{1,0:T(8,128)(2,1)S(1)}, bf16[224,768]{1,0:T(8,128)(2,1)S(1)}, u32[]{:S(2)}, u32[]{:S(2)}) collective-permute-start(bf16[224,768]{1,0:T(8,128)(2,1)S(1)} %pad_maximum_fusion.4), channel_id=1, source_target_pairs={{8,0},{16,24},{9,1},{17,25},{10,2},{18,26},{11,3},{19,27},{12,4},{... | collective-permute-start | bytes 1032200 | tf_op jit(solution)/shard_map/ppermute | solution.py:60
  212.4 10.7 %collective-permute-start.53 = (bf16[192,768]{1,0:T(8,128)(2,1)S(1)}, bf16[192,768]{1,0:T(8,128)(2,1)S(1)}, u32[]{:S(2)}, u32[]{:S(2)}) collective-permute-start(bf16[192,768]{1,0:T(8,128)(2,1)S(1)} %broadcast_select_fusion.7), channel_id=1, source_target_pairs={{0,4},{4,0},{1,5},{5,1},{2,6},{6,2},{3,7},{7,3},{8,12},{12,8},{9,1... | collective-permute-start | bytes 884744 | tf_op jit(solution)/shard_map/ppermute | solution.py:25
  214.0 24.2 %collective-permute-start.60 = (bf16[768,384]{1,0:T(8,128)(2,1)S(1)}, bf16[768,384]{1,0:T(8,128)(2,1)S(1)}, u32[]{:S(2)}, u32[]{:S(2)}) collective-permute-start(bf16[768,384]{1,0:T(8,128)(2,1)S(1)} %broadcast_select_fusion.2), channel_id=1, source_target_pairs={{0,4},{4,0},{1,5},{5,1},{2,6},{6,2},{3,7},{7,3},{8,12},{12,8},{9,1... | collective-permute-start | bytes 1769480 | tf_op jit(solution)/shard_map/ppermute | solution.py:25
  218.2 18.9 %collective-permute-start.58 = (bf16[192,768]{1,0:T(8,128)(2,1)S(1)}, bf16[192,768]{1,0:T(8,128)(2,1)S(1)}, u32[]{:S(2)}, u32[]{:S(2)}) collective-permute-start(bf16[192,768]{1,0:T(8,128)(2,1)S(1)} %slice.359), channel_id=1, source_target_pairs={{0,4},{4,0},{1,5},{5,1},{2,6},{6,2},{3,7},{7,3},{8,12},{12,8},{9,1... | collective-permute-start | bytes 884744 | tf_op jit(solution)/shard_map/ppermute | solution.py:25
  (42 other events, 278.4 us)

commit v5 on v4

--- a/solution.py
+++ b/solution.py
@@ -312,53 +312,35 @@
 WHOLE, QUARTERS = 4, 6
 
 
-def weight_copies(place, wholes, quarters, up, down, sems):
-    rows = quarters[0].shape[0] // 4
-    shards = []
+def gathered_weights(place, wholes, quarters, up, down):
+    rows = quarters[1].shape[0] // 2
+    shards = [(wholes[0], wholes[1]), (wholes[2], wholes[3])]
     for s in range(2):
-        shards.append([(wholes[2 * s], up.at[s]), (wholes[2 * s + 1], down.at[s])])
-    for s in range(2):
-        copies = []
         for i, flip, start in ((0, 0, 0), (1, 2, 0), (2, 1, 0), (0, 3, 2)):
             spot = pl.ds(pl.multiple_of((place[1] ^ flip) * rows, rows), rows)
             piece = quarters[3 * s + i]
-            copies.append((piece.at[pl.ds(start * rows, rows)], up.at[2 + s, spot]))
-            copies.append((piece.at[pl.ds((start + 1) * rows, rows)], down.at[2 + s, spot]))
-        shards.append(copies)
-    number, made = 0, []
-    for copies in shards:
-        row = []
-        for source, target in copies:
-            row.append(pltpu.make_async_copy(source, target, sems.at[number]))
-            number += 1
-        made.append(row)
-    return made
+            up[s, spot, :] = piece[start * rows : (start + 1) * rows]
+            down[s, spot, :] = piece[(start + 1) * rows : (start + 2) * rows]
+        shards.append((up.at[s], down.at[s]))
+    return shards
 
 
 def ffn_kernel(place, *refs):
     wholes, quarters = refs[:WHOLE], refs[WHOLE : WHOLE + QUARTERS]
     middle, biases, affine, counts = refs[10:14]
-    slopes_out, normed_out, rows_out, output_out, sums_out, pooled_out = refs[14:20]
-    up, down, sems = refs[20:]
+    slopes_out, rows_out, output_out, sums_out, pooled_out = refs[14:19]
+    up, down = refs[19:]
+    shards = gathered_weights(place, wholes, quarters, up, down)
     down_bias, gain, shift = affine[0:1], affine[1:2], affine[2:3]
-    shards = weight_copies(place, wholes, quarters, up, down, sems)
-    for copies in shards[:2]:
-        for copy in copies:
-            copy.start()
     length, width = middle.shape
     mid = middle[...]
     mid_low = mid.astype(low)
     total = mid + down_bias
-    for s, copies in enumerate(shards):
-        for copy in copies:
-            copy.wait()
-        for copy in shards[s + 2] if s < 2 else []:
-            copy.start()
-        hidden, slope = gelu_parts(dot(mid_low, up[s]) + biases[s : s + 1])
+    for s, (up_shard, down_shard) in enumerate(shards):
+        hidden, slope = gelu_parts(dot(mid_low, up_shard[...]) + biases[s : s + 1])
         slopes_out[s] = slope.astype(low)
-        total += dot(hidden.astype(low), down[s])
+        total += dot(hidden.astype(low), down_shard[...])
     normed, rstd = norm_parts(total)
-    normed_out[...] = normed
     output_out[0] = (normed * gain + shift).astype(low)
     count = counts[0:1, 0:1]
     live = jnp.where(lax.broadcasted_iota(jnp.int32, (length, 1), 0).astype(full) < count, 1.0, 0.0)
@@ -375,25 +357,18 @@
 
 def ffn_back_kernel(place, *refs):
     wholes, quarters = refs[:WHOLE], refs[WHOLE : WHOLE + QUARTERS]
-    slopes, vector, normed_two, rows, summed, affine = refs[10:16]
-    attn_out, one_out, sums_out = refs[16:19]
-    up, down, sems = refs[19:]
-    shards = weight_copies(place, wholes, quarters, up, down, sems)
-    for copies in shards[:2]:
-        for copy in copies:
-            copy.start()
-    length, width = normed_two.shape
+    slopes, summed, vector, rows, affine = refs[10:15]
+    attn_out, one_out, sums_out = refs[15:18]
+    up, down = refs[18:]
+    shards = gathered_weights(place, wholes, quarters, up, down)
+    length, width = one_out.shape
     factor = rows[:, width : width + 1].astype(full) + rows[:, width + 1 : width + 2].astype(full)
-    two_grad = norm_backward(jnp.broadcast_to(vector[...], (length, width)), normed_two[...], factor)
+    two_grad = norm_backward(jnp.broadcast_to(vector[0:1], (length, width)), rows[:, :width].astype(full), factor)
     ffn_grad = two_grad.astype(low)
     total = two_grad
-    for s, copies in enumerate(shards):
-        for copy in copies:
-            copy.wait()
-        for copy in shards[s + 2] if s < 2 else []:
-            copy.start()
-        grad = (slopes[s].astype(full) * dot(ffn_grad, down[s], ((1,), (1,)))).astype(low)
-        total += dot(grad, up[s], ((1,), (1,)))
+    for s, (up_shard, down_shard) in enumerate(shards):
+        grad = (slopes[s].astype(full) * dot(ffn_grad, down_shard[...], ((1,), (1,)))).astype(low)
+        total += dot(grad, up_shard[...], ((1,), (1,)))
     normed, rstd = norm_parts(summed[...])
     one_grad = norm_backward(total * affine[3:4], normed, rstd)
     one_out[...] = one_grad
@@ -408,22 +383,13 @@
 
 def with_weights(kernel, name, place, wholes, quarters, operands, outs):
     width, hidden = wholes[0].shape
-    everywhere = pl.BlockSpec(memory_space=pl.ANY)
+    inside = pl.BlockSpec(memory_space=pltpu.VMEM)
     return pl.pallas_call(
         kernel,
-        grid_spec=pltpu.PrefetchScalarGridSpec(
-            num_scalar_prefetch=1,
-            grid=(1,),
-            in_specs=[everywhere] * (WHOLE + QUARTERS)
-            + [pl.BlockSpec(a.shape, lambda b, *_, rank=a.ndim: (0,) * rank) for a in operands],
-            out_specs=[pl.BlockSpec(o.shape, lambda b, *_, rank=len(o.shape): (0,) * rank) for o in outs],
-            scratch_shapes=[
-                pltpu.VMEM((4, width, hidden), low),
-                pltpu.VMEM((4, hidden, width), low),
-                pltpu.SemaphoreType.DMA((20,)),
-            ],
-        ),
+        in_specs=[pl.BlockSpec(memory_space=pltpu.SMEM)] + [inside] * (WHOLE + QUARTERS + len(operands)),
+        out_specs=[inside] * len(outs),
         out_shape=outs,
+        scratch_shapes=[pltpu.VMEM((2, width, hidden), low), pltpu.VMEM((2, hidden, width), low)],
         name=name,
     )(place, *wholes, *quarters, *operands)
 
@@ -551,15 +517,16 @@
     mates = jnp.stack([group, group ^ 1]) * share + member
     wanted = jnp.sum(jnp.where(spot == mates[:, None], pos_index[None], 0), axis=1, keepdims=True)
     chosen = jnp.where(((spot // share) ^ group) * share + spot % share == wanted, 1.0, 0.0).astype(low)
-    sent, piece_y, bias_own = tie((plus(near[1], other[1]), piece_y, up_bias))
-    bias_far = swap(bias_own[None], "tensor", 2)
+    sent, piece_y = tie((plus(near[1], other[1]), piece_y))
     first = piece_y[: 2 * quarter]
     piece_x = swap(first, "fsdp", 1)
     piece_z = swap(first, "dp", 1)
+    attn_out = near[0].astype(full) + other[0].astype(full) + swap(sent, "tensor", 2).astype(full)
+    attn_out, bias_own = tie((attn_out, up_bias))
+    bias_far = swap(bias_own[None], "tensor", 2)
     bias_pair = jnp.concatenate([up_bias[None], bias_far])
     bias_pair = jnp.concatenate([bias_pair, swap(bias_pair, "tensor", 1)])
     biases = jnp.stack([bias_pair[0], bias_pair[2], bias_pair[1], bias_pair[3]])
-    attn_out = near[0].astype(full) + other[0].astype(full) + swap(sent, "tensor", 2).astype(full)
     quarters = [piece_y, piece_x, piece_z]
     quarters = quarters + [swap(p, "tensor", 1) for p in quarters]
 
@@ -568,7 +535,7 @@
     middle_low = middle.astype(low)
     quarters, biases, chosen, middle, middle_low = tie((quarters, biases, chosen, middle, middle_low))
     S = jax.ShapeDtypeStruct
-    slopes, normed_two, rows, output, live_sum, pooled = with_weights(
+    slopes, rows, output, live_sum, pooled = with_weights(
         ffn_kernel,
         "ffn",
         place,
@@ -577,7 +544,6 @@
         [middle, biases, affine, counts],
         [
             S((4, length, hidden), low),
-            S((length, width), full),
             S((length, width + LANES), low),
             S((1, length, width), low),
             S((1, width), full),
@@ -614,7 +580,7 @@
     pos_logit = jnp.sum(pooled_pair[:, :width].astype(full) * positive, axis=1, keepdims=True) * inv_temp
     top_final = jnp.maximum(top, pos_logit)
     lse = top_final + jnp.log(total * jnp.exp(top - top_final) + jnp.exp(pos_logit - top_final))
-    loss_part = (lse - pos_logit)[0:1]
+    loss_part = jnp.broadcast_to((lse - pos_logit) / devices, (2, width))
     step = loss_scale * inv_temp
     pooled_grad = key_sum * (step * jnp.exp(top - lse)) + step * (jnp.exp(pos_logit - lse) - 1.0) * positive
     result_row = pooled_grad / count_pair
@@ -628,14 +594,14 @@
         place,
         wholes,
         quarters,
-        [slopes, vector_pair[0:1], normed_two, rows, summed, affine],
+        [slopes, summed, vector_pair, rows, affine],
         [S((length, width), low), S((length, width), full), S((8, width), full)],
     )
     vectors_far, rows_far, attn_grad, middles, sums = tie((swap(vector_pair, "tensor", 2), swap(pairs["x"], "tensor", 2), attn_grad, middles, sums))
     vectors_far = jnp.concatenate([vector_pair, vectors_far])
     vectors_all = jnp.concatenate([vectors_far, swap(vectors_far, "tensor", 1)])
     rows_all = rows_pair + [rows_far] + rows_core + [swap(rows_far, "tensor", 1)]
-    vectors = jnp.concatenate([final_gain_part, pooled_grad[0:1], sums[0:4], jnp.broadcast_to(loss_part / devices, (1, width))])
+    vectors = jnp.concatenate([final_gain_part, pooled_grad[0:1], sums[0:4], loss_part[0:1]])
     down, up, up_bias_half = ffn_weights(middles, rows_all, vectors_all, up_half, bias_half, down_half)
     vectors = vectors + swap(vectors, "tensor", 1)
     attn_far, attn_core, down, up, vectors = tie((swap(attn_grad, "tensor", 2), swap(attn_grad, "tensor", 1), down, up, vectors))
@@ -669,7 +635,6 @@
         up, vo = tie((up, vo))
         qk = plus(qk, across(qk))
         down = outward(down)
-        qk, down = tie((qk, down))
         vo = plus_carried(vo, across(vo), mine)
         up = outward(up)
         qk = outward(qk)

time: 242 us -> 232 us (0.959)
  waiting for transfers between devices: 78.5 us -> 63.2 us
    ppermute x4, waiting for transfers between devices: 25.6 us -> 14.1 us  [outward(): outer = lax.ppermute(part, 'dp', [(1, 0), (2, 3)])]
    ppermute x50, waiting for transfers between devices: 50.6 us -> 45.2 us  [swap(): return lax.ppermute(array, axis, [(i, i ^ stride) for i in range(size)])]
  transfers between devices with their start and end apart: 62 -> 62, of which waited for: 25 -> 27; matrix products, arithmetic and copies ran while one was open for 13% -> 14% of each run, Pallas kernels for 23% -> 24%
where the time goes in v5:
time: 232 us; the launch traced here: 231 us
  starting transfers between devices  69 us (30%)
  waiting for transfers between devices  63.2 us (27%)
  Pallas kernels  54.9 us (24%)
  other arithmetic  21.3 us (9%)
  local copies, waits for them, and re-layouts  16.9 us (7%)
  matrix products  3.78 us (2%)
    ppermute x50, starting transfers between devices, swap(): return lax.ppermute(array, axis, [(i, i ^ stride) for i in range(size)])  46.8 us
    ppermute x50, waiting for transfers between devices, swap(): return lax.ppermute(array, axis, [(i, i ^ stride) for i in range(size)])  45.2 us
    pallas_call x2, Pallas kernels, with_weights(): pl.pallas_call(kernel, in_specs=[pl.BlockSpec(memory_space=pltpu.SMEM)] +...  17.7 us
    ppermute x4, waiting for transfers between devices, outward(): outer = lax.ppermute(part, 'dp', [(1, 0), (2, 3)])  14.1 us
    ppermute x4, starting transfers between devices, inward(): return lax.ppermute(part, 'dp', [(0, 1), (3, 2)])  14 us
    pallas_call x1, Pallas kernels, attend_back(): pl.pallas_call(attend_back_kernel, grid_spec=pltpu.PrefetchScalarGridSpec...  13.9 us
    pallas_call x1, Pallas kernels, attend(): pl.pallas_call(attend_kernel, grid_spec=pltpu.PrefetchScalarGridSpec(num_...  12 us
    pallas_call x1, Pallas kernels, ffn_weights(): pl.pallas_call(ffn_weights_kernel, out_shape=[S((half, width), low), S((w...  11.2 us
  transfers between devices with their start and end apart: 62, of which 27 were waited for; matrix products, arithmetic and copies ran while one was open for 14% of the time, Pallas kernels for 24%

profile of v5, /device:TPU:0, one launch (start us, length us, event | category | flops | bytes accessed | tf_op | source)
XLA Modules:
  0.0 231.0 jit_solution(2589211185219892798)
XLA Ops:
  0.7 1.2 constant_dynamic-slice_fusion.5
  3.0 1.1 pad_maximum_fusion
  4.2 3.0 %collective-permute-start = (bf16[768,768]{1,0:T(8,128)(2,1)}, bf16[768,768]{1,0:T(8,128)(2,1)}, u32[]{:S(2)}, u32[]{:S(2)}) collective-permute-start(bf16[768,768]{1,0:T(8,128)(2,1)} %pad_maximum_fusion), channel_id=1, source_target_pairs={{0,2},{1,3},{2,0},{3,1},{4,6},{5,7},{6,4},{7,5},{8,10},{9,11},{10,... | collective-permute-start | bytes 3538952 | tf_op jit(solution)/shard_map/ppermute | solution.py:25
  8.3 12.0 %attend.1 = (bf16[4,256,768]{2,1,0:T(8,128)(2,1)}, bf16[4,256,192]{2,1,0:T(8,128)(2,1)}, bf16[4,256,192]{2,1,0:T(8,128)(2,1)}, bf16[4,256,192]{2,1,0:T(8,128)(2,...) custom-call(s32[2]{0:T(128)} %get-tuple-element.274.place_in.place, ...), custom_call_target="tpu_custom_call" | custom-call | tf_op jit(solution)/shard_map/attend/pallas_call | solution.py:153
  20.4 1.6 collective-permute-start.1
  22.0 2.0 constant_dynamic-slice_fusion.refs_19_
  24.1 1.6 collective-permute-start.2
  25.8 2.0 constant_dynamic-slice_fusion.1.refs_17_
  27.9 2.7 %collective-permute-start.3 = (bf16[16,768]{1,0:T(8,128)(2,1)S(1)}, bf16[16,768]{1,0:T(8,128)(2,1)S(1)}, u32[]{:S(2)}, u32[]{:S(2)}) collective-permute-start(bf16[16,768]{1,0:T(8,128)(2,1)S(1)} %pad_maximum_fusion.7), channel_id=1, source_target_pairs={{0,16},{8,24},{16,0},{24,8},{1,17},{9,25},{17,1},{25,9},{2,18},{10... | collective-permute-start | bytes 73736 | tf_op jit(solution)/shard_map/ppermute | solution.py:25
  36.0 1.1 slice.241
  37.1 1.6 collective-permute-start.7
  38.7 1.6 collective-permute-start.8
  40.3 3.9 %collective-permute-done.12 = bf16[256,768]{1,0:T(8,128)(2,1)S(1)} collective-permute-done((bf16[256,768]{1,0:T(8,128)(2,1)S(1)}, bf16[256,768]{1,0:T(8,128)(2,1)S(1)}, u32[]{:S(2)}, u32[]{:S(2)}) %collective-permute-start.12) | collective-permute-done | bytes 393248 | tf_op jit(solution)/shard_map/ppermute | solution.py:25
  44.1 1.1 bitcast_add_fusion.1
  45.3 1.2 fusion.44
  46.5 1.1 collective-permute-start.13
  47.9 2.3 collective-permute-done.13
  51.1 1.2 collective-permute-done.8.refs_6_
  52.3 1.1 fusion.43
  57.3 8.6 %ffn.1 = (bf16[4,256,768]{2,1,0:T(8,128)(2,1)}, bf16[256,896]{1,0:T(8,128)(2,1)}, bf16[1,256,768]{2,1,0:T(8,128)(2,1)}, f32[1,768]{1,0:T(1,128)}, bf16[1,896]{1,0:T(2,128)(2,1)}) custom-call(s32[2]{0:T(128)} %get-tuple-element.274.place_in.place, bf16[768,768]{1,0:T(8,128)(2,1)} %refs_0_.1, bf16[768,768]{1,0:T(8,128)(2,1)} %refs_1_.1, ...), custom_call_target="tpu_custom_call" | custom-call | tf_op jit(solution)/shard_map/ffn/pallas_call | solution.py:387
  65.9 1.6 collective-permute-done.15.refs_1_
  67.7 1.5 collective-permute-start.17
  69.2 2.3 %collective-permute-done.17 = bf16[1,896]{1,0:T(2,128)(2,1)S(1)} collective-permute-done((bf16[1,896]{1,0:T(2,128)(2,1)}, bf16[1,896]{1,0:T(2,128)(2,1)S(1)}, u32[]{:S(2)}, u32[]{:S(2)}) %collective-permute-start.17) | collective-permute-done | bytes 1824 | tf_op jit(solution)/shard_map/ppermute | solution.py:25
  73.2 1.2 collective-permute-start.18
  74.4 2.4 %collective-permute-done.18 = bf16[2,896]{1,0:T(2,128)(2,1)S(1)} collective-permute-done((bf16[2,896]{1,0:T(2,128)(2,1)S(1)}, bf16[2,896]{1,0:T(2,128)(2,1)S(1)}, u32[]{:S(2)}, u32[]{:S(2)}) %collective-permute-start.18) | collective-permute-done | bytes 3616 | tf_op jit(solution)/shard_map/ppermute | solution.py:25
  76.8 2.7 %collective-permute-start.19 = (bf16[4,896]{1,0:T(4,128)(2,1)S(1)}, bf16[4,896]{1,0:T(4,128)(2,1)S(1)}, u32[]{:S(2)}, u32[]{:S(2)}) collective-permute-start(bf16[4,896]{1,0:T(4,128)(2,1)S(1)} %pad_maximum_fusion.17), channel_id=1, source_target_pairs={{0,16},{8,24},{16,0},{24,8},{1,17},{9,25},{17,1},{25,9},{2,18},{10... | collective-permute-start | bytes 21512 | tf_op jit(solution)/shard_map/ppermute | solution.py:25
  80.0 1.1 collective-permute-start.23
  81.4 1.1 collective-permute-start.24
  84.6 2.6 %collective-permute-start.21 = (f32[4,1024]{1,0:T(4,128)S(1)}, f32[4,1024]{1,0:T(4,128)S(1)}, u32[]{:S(2)}, u32[]{:S(2)}) collective-permute-start(f32[4,1024]{1,0:T(4,128)S(1)} %slice.318), channel_id=1, source_target_pairs={{0,16},{8,24},{16,0},{24,8},{1,17},{9,25},{17,1},{25,9},{2,18},{10... | collective-permute-start | bytes 49160 | tf_op jit(solution)/shard_map/ppermute | solution.py:25
  87.3 2.0 collective-permute-done.21
  89.6 1.6 collective-permute-start.22
  93.7 1.5 collective-permute-start.25
  96.2 1.3 collective-permute-done.25
  99.7 1.4 collective-permute-start.29
  102.4 9.2 %ffn_back.1 = (bf16[256,768]{1,0:T(8,128)(2,1)}, f32[256,768]{1,0:T(8,128)}, f32[8,768]{1,0:T(8,128)}) custom-call(s32[2]{0:T(128)} %get-tuple-element.274.place_in.place, bf16[768,768]{1,0:T(8,128)(2,1)} %refs_0_.1, bf16[768,768]{1,0:T(8,128)(2,1)} %refs_1_.1, bf16[768,768]{1,0:T(8,128)(2,1)} %collective-permute-done.4.refs_2_, ...), custom_call_target="tpu_custom_call" | custom-call | tf_op jit(solution)/shard_map/ffn_back/pallas_call | solution.py:387
  115.4 1.3 pad_maximum_fusion.8.refs_16_
  117.6 11.2 %ffn_weights.1 = (bf16[384,768]{1,0:T(8,128)(2,1)}, bf16[768,384]{1,0:T(8,128)(2,1)}, f32[1,384]{1,0:T(1,128)}) custom-call(bf16[256,768]{1,0:T(8,128)(2,1)} %copy-done.7, bf16[256,768]{1,0:T(8,128)(2,1)} %collective-permute-done.15.refs_1_, bf16[256,768]{1,0:T(8,128)(2,1)} %collective-permute-done.16.refs_2_, ...), custom_call_target="tpu_custom_call" | custom-call | tf_op jit(solution)/shard_map/ffn_weights/pallas_call | solution.py:424
  128.9 3.5 %collective-permute-start.41 = (bf16[384,768]{1,0:T(8,128)(2,1)}, bf16[384,768]{1,0:T(8,128)(2,1)S(1)}, u32[]{:S(2)}, u32[]{:S(2)}) collective-permute-start(bf16[384,768]{1,0:T(8,128)(2,1)} %get-tuple-element.194), channel_id=1, source_target_pairs={{0,8},{24,16},{1,9},{25,17},{2,10},{26,18},{3,11},{27,19},{4,12},{... | collective-permute-start | bytes 1769480 | tf_op jit(solution)/shard_map/ppermute | solution.py:51
  132.6 1.6 collective-permute-start.45
  135.6 13.9 %attend_back.1 = (bf16[2,256,768]{2,1,0:T(8,128)(2,1)}, bf16[2,256,768]{2,1,0:T(8,128)(2,1)}, bf16[192,768]{1,0:T(8,128)(2,1)}, bf16[192,768]{1,0:T(8,128)(2,1)}...) custom-call(s32[2]{0:T(128)} %get-tuple-element.274.place_in.place, ...), custom_call_target="tpu_custom_call" | custom-call | tf_op jit(solution)/shard_map/attend_back/pallas_call | solution.py:272
  149.7 1.4 collective-permute-start.51
  153.7 1.7 collective-permute-start.52
  155.5 6.5 %collective-permute-done.44 = bf16[192,768]{1,0:T(8,128)(2,1)S(1)} collective-permute-done((bf16[192,768]{1,0:T(8,128)(2,1)S(1)}, bf16[192,768]{1,0:T(8,128)(2,1)S(1)}, u32[]{:S(2)}, u32[]{:S(2)}) %collective-permute-start.44) | collective-permute-done | bytes 294944 | tf_op jit(solution)/shard_map/ppermute | solution.py:25
  163.0 5.7 %collective-permute-start.46 = (bf16[192,768]{1,0:T(8,128)(2,1)S(1)}, bf16[192,768]{1,0:T(8,128)(2,1)S(1)}, u32[]{:S(2)}, u32[]{:S(2)}) collective-permute-start(bf16[192,768]{1,0:T(8,128)(2,1)S(1)} %add_convert_fusion.11), channel_id=1, source_target_pairs={{0,8},{24,16},{1,9},{25,17},{2,10},{26,18},{3,11},{27,19},{4,12},{... | collective-permute-start | bytes 884744 | tf_op jit(solution)/shard_map/ppermute | solution.py:51
  169.1 3.2 %collective-permute-start.54 = (bf16[224,768]{1,0:T(8,128)(2,1)S(1)}, bf16[224,768]{1,0:T(8,128)(2,1)S(1)}, u32[]{:S(2)}, u32[]{:S(2)}) collective-permute-start(bf16[224,768]{1,0:T(8,128)(2,1)S(1)} %pad_maximum_fusion.2), channel_id=1, source_target_pairs={{0,8},{24,16},{1,9},{25,17},{2,10},{26,18},{3,11},{27,19},{4,12},{... | collective-permute-start | bytes 1032200 | tf_op jit(solution)/shard_map/ppermute | solution.py:51
  172.3 1.3 collective-permute-start.60
  173.6 1.3 collective-permute-done.46
  176.3 1.3 collective-permute-start.48
  177.6 2.7 %collective-permute-done.54 = bf16[224,768]{1,0:T(8,128)(2,1)S(1)} collective-permute-done((bf16[224,768]{1,0:T(8,128)(2,1)S(1)}, bf16[224,768]{1,0:T(8,128)(2,1)S(1)}, u32[]{:S(2)}, u32[]{:S(2)}) %collective-permute-start.54) | collective-permute-done | bytes 344096 | tf_op jit(solution)/shard_map/ppermute | solution.py:51
  180.5 1.4 collective-permute-start.58
  182.6 6.8 %collective-permute-done.60 = bf16[384,768]{1,0:T(8,128)(2,1)S(1)} collective-permute-done((bf16[384,768]{1,0:T(8,128)(2,1)S(1)}, bf16[384,768]{1,0:T(8,128)(2,1)S(1)}, u32[]{:S(2)}, u32[]{:S(2)}) %collective-permute-start.60) | collective-permute-done | bytes 589856 | tf_op jit(solution)/shard_map/ppermute | solution.py:60
  189.5 2.0 collective-permute-start.61
  191.5 1.1 fusion
  192.6 3.2 %collective-permute-done.48 = bf16[192,768]{1,0:T(8,128)(2,1)S(1)} collective-permute-done((bf16[192,768]{1,0:T(8,128)(2,1)S(1)}, bf16[192,768]{1,0:T(8,128)(2,1)S(1)}, u32[]{:S(2)}, u32[]{:S(2)}) %collective-permute-start.48) | collective-permute-done | bytes 294944 | tf_op jit(solution)/shard_map/ppermute | solution.py:60
  195.9 1.9 collective-permute-start.49
  197.9 1.3 collective-permute-start.56
  199.2 8.0 %collective-permute-done.49 = bf16[192,768]{1,0:T(8,128)(2,1)S(1)} collective-permute-done((bf16[192,768]{1,0:T(8,128)(2,1)S(1)}, bf16[192,768]{1,0:T(8,128)(2,1)S(1)}, u32[]{:S(2)}, u32[]{:S(2)}) %collective-permute-start.49) | collective-permute-done | bytes 294944 | tf_op jit(solution)/shard_map/ppermute | solution.py:25
  208.6 1.9 collective-permute-start.59
  210.5 3.8 %collective-permute-done.56 = bf16[224,768]{1,0:T(8,128)(2,1)S(1)} collective-permute-done((bf16[224,768]{1,0:T(8,128)(2,1)S(1)}, bf16[224,768]{1,0:T(8,128)(2,1)S(1)}, u32[]{:S(2)}, u32[]{:S(2)}) %collective-permute-start.56) | collective-permute-done | bytes 344096 | tf_op jit(solution)/shard_map/ppermute | solution.py:60
  214.4 1.2 collective-permute-start.57
  217.5 1.6 maximum_convert_fusion.1
  219.1 8.0 %collective-permute-done.57 = bf16[192,768]{1,0:T(8,128)(2,1)S(1)} collective-permute-done((bf16[192,768]{1,0:T(8,128)(2,1)S(1)}, bf16[192,768]{1,0:T(8,128)(2,1)S(1)}, u32[]{:S(2)}, u32[]{:S(2)}) %collective-permute-start.57) | collective-permute-done | bytes 294944 | tf_op jit(solution)/shard_map/ppermute | solution.py:25
  228.3 1.6 maximum_convert_fusion
  229.9 1.2 copy-done.1
  (278 shorter events, 41.9 us)
Async XLA Ops:
  0.7 82.0 %copy-start = (bf16[2048,768]{1,0:T(8,128)(2,1)S(1)}, bf16[2048,768]{1,0:T(8,128)(2,1)}, u32[]{:S(2)}) copy-start(bf16[2048,768]{1,0:T(8,128)(2,1)} %param.26) | copy-start | bytes 9437188
  4.2 30.2 %collective-permute-start = (bf16[768,768]{1,0:T(8,128)(2,1)}, bf16[768,768]{1,0:T(8,128)(2,1)}, u32[]{:S(2)}, u32[]{:S(2)}) collective-permute-start(bf16[768,768]{1,0:T(8,128)(2,1)} %pad_maximum_fusion), channel_id=1, source_target_pairs={{0,2},{1,3},{2,0},{3,1},{4,6},{5,7},{6,4},{7,5},{8,10},{9,11},{10,... | collective-permute-start | bytes 3538952 | tf_op jit(solution)/shard_map/ppermute | solution.py:25
  7.2 27.3 %collective-permute-start.4 = (bf16[768,768]{1,0:T(8,128)(2,1)}, bf16[768,768]{1,0:T(8,128)(2,1)}, u32[]{:S(2)}, u32[]{:S(2)}) collective-permute-start(bf16[768,768]{1,0:T(8,128)(2,1)} %refs_0_.1), channel_id=1, source_target_pairs={{0,1},{1,0},{2,3},{3,2},{4,5},{5,4},{6,7},{7,6},{8,9},{9,8},{10,11... | collective-permute-start | bytes 3538952 | tf_op jit(solution)/shard_map/ppermute | solution.py:25
  7.2 27.3 %collective-permute-start.5 = (bf16[768,768]{1,0:T(8,128)(2,1)}, bf16[768,768]{1,0:T(8,128)(2,1)}, u32[]{:S(2)}, u32[]{:S(2)}) collective-permute-start(bf16[768,768]{1,0:T(8,128)(2,1)} %refs_1_.1), channel_id=1, source_target_pairs={{0,1},{1,0},{2,3},{3,2},{4,5},{5,4},{6,7},{7,6},{8,9},{9,8},{10,11... | collective-permute-start | bytes 3538952 | tf_op jit(solution)/shard_map/ppermute | solution.py:25
  20.3 13.0 %collective-permute-start.6 = (bf16[2,256,768]{2,1,0:T(8,128)(2,1)}, bf16[2,256,768]{2,1,0:T(8,128)(2,1)}, u32[]{:S(2)}, u32[]{:S(2)}) collective-permute-start(bf16[2,256,768]{2,1,0:T(8,128)(2,1)} %get-tuple-element.122), channel_id=1, source_target_pairs={{0,1},{1,0},{2,3},{3,2},{4,5},{5,4},{6,7},{7,6},{8,9},{9,8},{10,11... | collective-permute-start | bytes 2359304 | tf_op jit(solution)/shard_map/ppermute | solution.py:25
  20.4 3.7 %collective-permute-start.1 = (bf16[4,768]{1,0:T(4,128)(2,1)S(1)}, bf16[4,768]{1,0:T(4,128)(2,1)S(1)}, u32[]{:S(2)}, u32[]{:S(2)}) collective-permute-start(bf16[4,768]{1,0:T(4,128)(2,1)S(1)} %copy-done.28), channel_id=1, source_target_pairs={{0,4},{4,0},{1,5},{5,1},{2,6},{6,2},{3,7},{7,3},{8,12},{12,8},{9,1... | collective-permute-start | bytes 18440 | tf_op jit(solution)/shard_map/ppermute | solution.py:25
  24.1 3.8 %collective-permute-start.2 = (bf16[8,768]{1,0:T(8,128)(2,1)S(1)}, bf16[8,768]{1,0:T(8,128)(2,1)S(1)}, u32[]{:S(2)}, u32[]{:S(2)}) collective-permute-start(bf16[8,768]{1,0:T(8,128)(2,1)S(1)} %pad_maximum_fusion.11), channel_id=1, source_target_pairs={{0,8},{8,0},{16,24},{24,16},{1,9},{9,1},{17,25},{25,17},{2,10},{10... | collective-permute-start | bytes 36872 | tf_op jit(solution)/shard_map/ppermute | solution.py:25
  27.9 4.8 %collective-permute-start.3 = (bf16[16,768]{1,0:T(8,128)(2,1)S(1)}, bf16[16,768]{1,0:T(8,128)(2,1)S(1)}, u32[]{:S(2)}, u32[]{:S(2)}) collective-permute-start(bf16[16,768]{1,0:T(8,128)(2,1)S(1)} %pad_maximum_fusion.7), channel_id=1, source_target_pairs={{0,16},{8,24},{16,0},{24,8},{1,17},{9,25},{17,1},{25,9},{2,18},{10... | collective-permute-start | bytes 73736 | tf_op jit(solution)/shard_map/ppermute | solution.py:25
  34.5 9.7 %collective-permute-start.12 = (bf16[256,768]{1,0:T(8,128)(2,1)S(1)}, bf16[256,768]{1,0:T(8,128)(2,1)S(1)}, u32[]{:S(2)}, u32[]{:S(2)}) collective-permute-start(bf16[256,768]{1,0:T(8,128)(2,1)S(1)} %fusion.4), channel_id=1, source_target_pairs={{0,2},{1,3},{2,0},{3,1},{4,6},{5,7},{6,4},{7,5},{8,10},{9,11},{10,... | collective-permute-start | bytes 1179656 | tf_op jit(solution)/shard_map/ppermute | solution.py:25
  37.1 14.0 %collective-permute-start.7 = (bf16[384,768]{1,0:T(8,128)(2,1)S(1)}, bf16[384,768]{1,0:T(8,128)(2,1)S(1)}, u32[]{:S(2)}, u32[]{:S(2)}) collective-permute-start(bf16[384,768]{1,0:T(8,128)(2,1)S(1)} %slice.241), channel_id=1, source_target_pairs={{0,4},{4,0},{1,5},{5,1},{2,6},{6,2},{3,7},{7,3},{8,12},{12,8},{9,1... | collective-permute-start | bytes 1769480 | tf_op jit(solution)/shard_map/ppermute | solution.py:25
  38.7 13.7 %collective-permute-start.8 = (bf16[384,768]{1,0:T(8,128)(2,1)S(1)}, bf16[384,768]{1,0:T(8,128)(2,1)S(1)}, u32[]{:S(2)}, u32[]{:S(2)}) collective-permute-start(bf16[384,768]{1,0:T(8,128)(2,1)S(1)} %slice.241), channel_id=1, source_target_pairs={{0,8},{8,0},{16,24},{24,16},{1,9},{9,1},{17,25},{25,17},{2,10},{10... | collective-permute-start | bytes 1769480 | tf_op jit(solution)/shard_map/ppermute | solution.py:25
  40.3 14.7 %collective-permute-start.9 = (bf16[768,768]{1,0:T(8,128)(2,1)}, bf16[768,768]{1,0:T(8,128)(2,1)}, u32[]{:S(2)}, u32[]{:S(2)}) collective-permute-start(bf16[768,768]{1,0:T(8,128)(2,1)} %collective-permute-done.refs_4_), channel_id=1, source_target_pairs={{0,1},{1,0},{2,3},{3,2},{4,5},{5,4},{6,7},{7,6},{8,9},{9,8},{10,11... | collective-permute-start | bytes 3538952 | tf_op jit(solution)/shard_map/ppermute | solution.py:25
  46.5 3.7 %collective-permute-start.13 = (f32[1,768]{1,0:T(1,128)S(1)}, f32[1,768]{1,0:T(1,128)S(1)}, u32[]{:S(2)}, u32[]{:S(2)}) collective-permute-start(f32[1,768]{1,0:T(1,128)S(1)} %broadcast_in_dim.89), channel_id=1, source_target_pairs={{0,2},{1,3},{2,0},{3,1},{4,6},{5,7},{6,4},{7,5},{8,10},{9,11},{10,... | collective-permute-start | bytes 9224 | tf_op jit(solution)/shard_map/ppermute | solution.py:25
  50.2 3.3 %collective-permute-start.14 = (f32[2,768]{1,0:T(2,128)S(1)}, f32[2,768]{1,0:T(2,128)S(1)}, u32[]{:S(2)}, u32[]{:S(2)}) collective-permute-start(f32[2,768]{1,0:T(2,128)S(1)} %pad_maximum_fusion.18), channel_id=1, source_target_pairs={{0,1},{1,0},{2,3},{3,2},{4,5},{5,4},{6,7},{7,6},{8,9},{9,8},{10,11... | collective-permute-start | bytes 18440 | tf_op jit(solution)/shard_map/ppermute | solution.py:25
  51.1 3.1 %collective-permute-start.10 = (bf16[384,768]{1,0:T(8,128)(2,1)S(1)}, bf16[384,768]{1,0:T(8,128)(2,1)S(1)}, u32[]{:S(2)}, u32[]{:S(2)}) collective-permute-start(bf16[384,768]{1,0:T(8,128)(2,1)S(1)} %collective-permute-done.7.refs_5_), channel_id=1, source_target_pairs={{0,1},{1,0},{2,3},{3,2},{4,5},{5,4},{6,7},{7,6},{8,9},{9,8},{10,11... | collective-permute-start | bytes 1769480 | tf_op jit(solution)/shard_map/ppermute | solution.py:25
  52.3 2.0 collective-permute-start.11
  53.4 26.1 %copy-start.7 = (bf16[256,768]{1,0:T(8,128)(2,1)}, bf16[256,768]{1,0:T(8,128)(2,1)S(1)}, u32[]{:S(2)}) copy-start(bf16[256,768]{1,0:T(8,128)(2,1)S(1)} %get-tuple-element.163.refs_0_) | copy-start | bytes 1179652
  55.8 11.6 %collective-permute-start.15 = (bf16[256,768]{1,0:T(8,128)(2,1)S(1)}, bf16[256,768]{1,0:T(8,128)(2,1)}, u32[]{:S(2)}, u32[]{:S(2)}) collective-permute-start(bf16[256,768]{1,0:T(8,128)(2,1)S(1)} %get-tuple-element.163.refs_0_), channel_id=1, source_target_pairs={{0,4},{4,0},{1,5},{5,1},{2,6},{6,2},{3,7},{7,3},{8,12},{12,8},{9,1... | collective-permute-start | bytes 1179656 | tf_op jit(solution)/shard_map/ppermute | solution.py:25
  56.6 11.1 %collective-permute-start.16 = (bf16[256,768]{1,0:T(8,128)(2,1)S(1)}, bf16[256,768]{1,0:T(8,128)(2,1)}, u32[]{:S(2)}, u32[]{:S(2)}) collective-permute-start(bf16[256,768]{1,0:T(8,128)(2,1)S(1)} %get-tuple-element.163.refs_0_), channel_id=1, source_target_pairs={{0,2},{1,3},{2,0},{3,1},{4,6},{5,7},{6,4},{7,5},{8,10},{9,11},{10,... | collective-permute-start | bytes 1179656 | tf_op jit(solution)/shard_map/ppermute | solution.py:25
  67.7 3.8 %collective-permute-start.17 = (bf16[1,896]{1,0:T(2,128)(2,1)}, bf16[1,896]{1,0:T(2,128)(2,1)S(1)}, u32[]{:S(2)}, u32[]{:S(2)}) collective-permute-start(bf16[1,896]{1,0:T(2,128)(2,1)} %get-tuple-element.144), channel_id=1, source_target_pairs={{0,4},{4,0},{1,5},{5,1},{2,6},{6,2},{3,7},{7,3},{8,12},{12,8},{9,1... | collective-permute-start | bytes 5384 | tf_op jit(solution)/shard_map/ppermute | solution.py:25
  72.2 10.4 %collective-permute-start.20 = (bf16[256,768]{1,0:T(8,128)(2,1)}, bf16[256,768]{1,0:T(8,128)(2,1)}, u32[]{:S(2)}, u32[]{:S(2)}) collective-permute-start(bf16[256,768]{1,0:T(8,128)(2,1)} %collective-permute-done.15.refs_1_), channel_id=1, source_target_pairs={{0,2},{1,3},{2,0},{3,1},{4,6},{5,7},{6,4},{7,5},{8,10},{9,11},{10,... | collective-permute-start | bytes 1179656 | tf_op jit(solution)/shard_map/ppermute | solution.py:25
  73.2 3.6 %collective-permute-start.18 = (bf16[2,896]{1,0:T(2,128)(2,1)S(1)}, bf16[2,896]{1,0:T(2,128)(2,1)S(1)}, u32[]{:S(2)}, u32[]{:S(2)}) collective-permute-start(bf16[2,896]{1,0:T(2,128)(2,1)S(1)} %pad_maximum_fusion.19), channel_id=1, source_target_pairs={{0,8},{8,0},{16,24},{24,16},{1,9},{9,1},{17,25},{25,17},{2,10},{10... | collective-permute-start | bytes 10760 | tf_op jit(solution)/shard_map/ppermute | solution.py:25
  76.8 4.6 %collective-permute-start.19 = (bf16[4,896]{1,0:T(4,128)(2,1)S(1)}, bf16[4,896]{1,0:T(4,128)(2,1)S(1)}, u32[]{:S(2)}, u32[]{:S(2)}) collective-permute-start(bf16[4,896]{1,0:T(4,128)(2,1)S(1)} %pad_maximum_fusion.17), channel_id=1, source_target_pairs={{0,16},{8,24},{16,0},{24,8},{1,17},{9,25},{17,1},{25,9},{2,18},{10... | collective-permute-start | bytes 21512 | tf_op jit(solution)/shard_map/ppermute | solution.py:25
  79.5 18.4 %collective-permute-start.26 = (bf16[256,896]{1,0:T(8,128)(2,1)}, bf16[256,896]{1,0:T(8,128)(2,1)}, u32[]{:S(2)}, u32[]{:S(2)}) collective-permute-start(bf16[256,896]{1,0:T(8,128)(2,1)} %get-tuple-element.150.refs_13_.refs_8_), channel_id=1, source_target_pairs={{0,1},{1,0},{2,3},{3,2},{4,5},{5,4},{6,7},{7,6},{8,9},{9,8},{10,11... | collective-permute-start | bytes 1376264 | tf_op jit(solution)/shard_map/ppermute | solution.py:25
  79.5 20.2 %collective-permute-start.31 = (bf16[256,768]{1,0:T(8,128)(2,1)S(1)}, bf16[256,768]{1,0:T(8,128)(2,1)}, u32[]{:S(2)}, u32[]{:S(2)}) collective-permute-start(bf16[256,768]{1,0:T(8,128)(2,1)S(1)} %get-tuple-element.163.refs_0_), channel_id=1, source_target_pairs={{0,1},{1,0},{2,3},{3,2},{4,5},{5,4},{6,7},{7,6},{8,9},{9,8},{10,11... | collective-permute-start | bytes 1179656 | tf_op jit(solution)/shard_map/ppermute | solution.py:25
  80.0 13.7 %collective-permute-start.23 = (bf16[256,896]{1,0:T(8,128)(2,1)}, bf16[256,896]{1,0:T(8,128)(2,1)}, u32[]{:S(2)}, u32[]{:S(2)}) collective-permute-start(bf16[256,896]{1,0:T(8,128)(2,1)} %get-tuple-element.150.refs_13_.refs_8_), channel_id=1, source_target_pairs={{0,4},{4,0},{1,5},{5,1},{2,6},{6,2},{3,7},{7,3},{8,12},{12,8},{9,1... | collective-permute-start | bytes 1376264 | tf_op jit(solution)/shard_map/ppermute | solution.py:25
  81.4 12.2 %collective-permute-start.24 = (bf16[256,896]{1,0:T(8,128)(2,1)}, bf16[256,896]{1,0:T(8,128)(2,1)}, u32[]{:S(2)}, u32[]{:S(2)}) collective-permute-start(bf16[256,896]{1,0:T(8,128)(2,1)} %get-tuple-element.150.refs_13_.refs_8_), channel_id=1, source_target_pairs={{0,2},{1,3},{2,0},{3,1},{4,6},{5,7},{6,4},{7,5},{8,10},{9,11},{10,... | collective-permute-start | bytes 1376264 | tf_op jit(solution)/shard_map/ppermute | solution.py:25
  84.6 4.7 %collective-permute-start.21 = (f32[4,1024]{1,0:T(4,128)S(1)}, f32[4,1024]{1,0:T(4,128)S(1)}, u32[]{:S(2)}, u32[]{:S(2)}) collective-permute-start(f32[4,1024]{1,0:T(4,128)S(1)} %slice.318), channel_id=1, source_target_pairs={{0,16},{8,24},{16,0},{24,8},{1,17},{9,25},{17,1},{25,9},{2,18},{10... | collective-permute-start | bytes 49160 | tf_op jit(solution)/shard_map/ppermute | solution.py:25
  89.6 3.7 %collective-permute-start.22 = (f32[2,1024]{1,0:T(2,128)S(1)}, f32[2,1024]{1,0:T(2,128)S(1)}, u32[]{:S(2)}, u32[]{:S(2)}) collective-permute-start(f32[2,1024]{1,0:T(2,128)S(1)} %slice.323), channel_id=1, source_target_pairs={{0,8},{8,0},{16,24},{24,16},{1,9},{9,1},{17,25},{25,17},{2,10},{10... | collective-permute-start | bytes 24584 | tf_op jit(solution)/shard_map/ppermute | solution.py:25
  93.7 3.7 %collective-permute-start.25 = (f32[2,1024]{1,0:T(2,128)S(1)}, f32[2,1024]{1,0:T(2,128)S(1)}, u32[]{:S(2)}, u32[]{:S(2)}) collective-permute-start(f32[2,1024]{1,0:T(2,128)S(1)} %pad_maximum_fusion.16), channel_id=1, source_target_pairs={{0,4},{4,0},{1,5},{5,1},{2,6},{6,2},{3,7},{7,3},{8,12},{12,8},{9,1... | collective-permute-start | bytes 24584 | tf_op jit(solution)/shard_map/ppermute | solution.py:25
  95.4 3.0 %collective-permute-start.27 = (bf16[256,896]{1,0:T(8,128)(2,1)}, bf16[256,896]{1,0:T(8,128)(2,1)S(1)}, u32[]{:S(2)}, u32[]{:S(2)}) collective-permute-start(bf16[256,896]{1,0:T(8,128)(2,1)} %collective-permute-done.23.refs_9_), channel_id=1, source_target_pairs={{0,1},{1,0},{2,3},{3,2},{4,5},{5,4},{6,7},{7,6},{8,9},{9,8},{10,11... | collective-permute-start | bytes 1376264 | tf_op jit(solution)/shard_map/ppermute | solution.py:25
  95.5 16.3 %collective-permute-start.30 = (bf16[256,896]{1,0:T(8,128)(2,1)}, bf16[256,896]{1,0:T(8,128)(2,1)S(1)}, u32[]{:S(2)}, u32[]{:S(2)}) collective-permute-start(bf16[256,896]{1,0:T(8,128)(2,1)} %collective-permute-done.23.refs_9_), channel_id=1, source_target_pairs={{0,2},{1,3},{2,0},{3,1},{4,6},{5,7},{6,4},{7,5},{8,10},{9,11},{10,... | collective-permute-start | bytes 1376264 | tf_op jit(solution)/shard_map/ppermute | solution.py:25
  97.4 2.0 collective-permute-start.28
  97.9 13.7 %collective-permute-start.32 = (bf16[256,768]{1,0:T(8,128)(2,1)}, bf16[256,768]{1,0:T(8,128)(2,1)S(1)}, u32[]{:S(2)}, u32[]{:S(2)}) collective-permute-start(bf16[256,768]{1,0:T(8,128)(2,1)} %collective-permute-done.15.refs_1_), channel_id=1, source_target_pairs={{0,1},{1,0},{2,3},{3,2},{4,5},{5,4},{6,7},{7,6},{8,9},{9,8},{10,11... | collective-permute-start | bytes 1179656 | tf_op jit(solution)/shard_map/ppermute | solution.py:25
  98.5 13.1 %collective-permute-start.33 = (bf16[256,768]{1,0:T(8,128)(2,1)}, bf16[256,768]{1,0:T(8,128)(2,1)S(1)}, u32[]{:S(2)}, u32[]{:S(2)}) collective-permute-start(bf16[256,768]{1,0:T(8,128)(2,1)} %collective-permute-done.16.refs_2_), channel_id=1, source_target_pairs={{0,1},{1,0},{2,3},{3,2},{4,5},{5,4},{6,7},{7,6},{8,9},{9,8},{10,11... | collective-permute-start | bytes 1179656 | tf_op jit(solution)/shard_map/ppermute | solution.py:25
  99.5 12.1 %collective-permute-start.34 = (bf16[256,768]{1,0:T(8,128)(2,1)}, bf16[256,768]{1,0:T(8,128)(2,1)S(1)}, u32[]{:S(2)}, u32[]{:S(2)}) collective-permute-start(bf16[256,768]{1,0:T(8,128)(2,1)} %collective-permute-done.20.refs_3_), channel_id=1, source_target_pairs={{0,1},{1,0},{2,3},{3,2},{4,5},{5,4},{6,7},{7,6},{8,9},{9,8},{10,11... | collective-permute-start | bytes 1179656 | tf_op jit(solution)/shard_map/ppermute | solution.py:25
  99.7 12.1 %collective-permute-start.29 = (f32[2,768]{1,0:T(2,128)S(1)}, f32[2,768]{1,0:T(2,128)S(1)}, u32[]{:S(2)}, u32[]{:S(2)}) collective-permute-start(f32[2,768]{1,0:T(2,128)S(1)} %get-tuple-element.156.refs_12_), channel_id=1, source_target_pairs={{0,2},{1,3},{2,0},{3,1},{4,6},{5,7},{6,4},{7,5},{8,10},{9,11},{10,... | collective-permute-start | bytes 18440 | tf_op jit(solution)/shard_map/ppermute | solution.py:25
  111.8 17.0 %collective-permute-start.35 = (bf16[256,768]{1,0:T(8,128)(2,1)}, bf16[256,768]{1,0:T(8,128)(2,1)S(1)}, u32[]{:S(2)}, u32[]{:S(2)}) collective-permute-start(bf16[256,768]{1,0:T(8,128)(2,1)} %get-tuple-element.162.g0), channel_id=1, source_target_pairs={{0,2},{1,3},{2,0},{3,1},{4,6},{5,7},{6,4},{7,5},{8,10},{9,11},{10,... | collective-permute-start | bytes 1179656 | tf_op jit(solution)/shard_map/ppermute | solution.py:25
  112.6 16.3 %collective-permute-start.36 = (bf16[256,768]{1,0:T(8,128)(2,1)}, bf16[256,768]{1,0:T(8,128)(2,1)S(1)}, u32[]{:S(2)}, u32[]{:S(2)}) collective-permute-start(bf16[256,768]{1,0:T(8,128)(2,1)} %get-tuple-element.162.g0), channel_id=1, source_target_pairs={{0,1},{1,0},{2,3},{3,2},{4,5},{5,4},{6,7},{7,6},{8,9},{9,8},{10,11... | collective-permute-start | bytes 1179656 | tf_op jit(solution)/shard_map/ppermute | solution.py:25
  114.0 1.4 collective-permute-start.38
  114.6 2.2 collective-permute-start.37
  114.7 2.0 collective-permute-start.39
  128.9 20.8 %collective-permute-start.41 = (bf16[384,768]{1,0:T(8,128)(2,1)}, bf16[384,768]{1,0:T(8,128)(2,1)S(1)}, u32[]{:S(2)}, u32[]{:S(2)}) collective-permute-start(bf16[384,768]{1,0:T(8,128)(2,1)} %get-tuple-element.194), channel_id=1, source_target_pairs={{0,8},{24,16},{1,9},{25,17},{2,10},{26,18},{3,11},{27,19},{4,12},{... | collective-permute-start | bytes 1769480 | tf_op jit(solution)/shard_map/ppermute | solution.py:51
  132.4 2.4 %collective-permute-start.40 = (bf16[256,768]{1,0:T(8,128)(2,1)S(1)}, bf16[256,768]{1,0:T(8,128)(2,1)S(1)}, u32[]{:S(2)}, u32[]{:S(2)}) collective-permute-start(bf16[256,768]{1,0:T(8,128)(2,1)S(1)} %collective-permute-done.35.g1), channel_id=1, source_target_pairs={{0,1},{1,0},{2,3},{3,2},{4,5},{5,4},{6,7},{7,6},{8,9},{9,8},{10,11... | collective-permute-start | bytes 1179656 | tf_op jit(solution)/shard_map/ppermute | solution.py:25
  132.6 29.5 %collective-permute-start.45 = (bf16[768,384]{1,0:T(8,128)(2,1)}, bf16[768,384]{1,0:T(8,128)(2,1)S(1)}, u32[]{:S(2)}, u32[]{:S(2)}) collective-permute-start(bf16[768,384]{1,0:T(8,128)(2,1)} %get-tuple-element.200), channel_id=1, source_target_pairs={{0,8},{24,16},{1,9},{25,17},{2,10},{26,18},{3,11},{27,19},{4,12},{... | collective-permute-start | bytes 1769480 | tf_op jit(solution)/shard_map/ppermute | solution.py:51
  149.7 3.9 %collective-permute-start.51 = (f32[7,768]{1,0:T(8,128)S(1)}, f32[7,768]{1,0:T(8,128)S(1)}, u32[]{:S(2)}, u32[]{:S(2)}) collective-permute-start(f32[7,768]{1,0:T(8,128)S(1)} %fusion.36), channel_id=1, source_target_pairs={{0,2},{1,3},{2,0},{3,1},{4,6},{5,7},{6,4},{7,5},{8,10},{9,11},{10,... | collective-permute-start | bytes 64520 | tf_op jit(solution)/shard_map/ppermute | solution.py:25
  151.2 17.7 %collective-permute-start.53 = (bf16[384,768]{1,0:T(8,128)(2,1)S(1)}, bf16[384,768]{1,0:T(8,128)(2,1)S(1)}, u32[]{:S(2)}, u32[]{:S(2)}) collective-permute-start(bf16[384,768]{1,0:T(8,128)(2,1)S(1)} %add_convert_fusion.1), channel_id=1, source_target_pairs={{8,16},{16,8},{9,17},{17,9},{10,18},{18,10},{11,19},{19,11},{12,20... | collective-permute-start | bytes 1769480 | tf_op jit(solution)/shard_map/ppermute | solution.py:55
  152.1 9.9 %collective-permute-start.44 = (bf16[192,768]{1,0:T(8,128)(2,1)S(1)}, bf16[192,768]{1,0:T(8,128)(2,1)S(1)}, u32[]{:S(2)}, u32[]{:S(2)}) collective-permute-start(bf16[192,768]{1,0:T(8,128)(2,1)S(1)} %copy-done.41), channel_id=1, source_target_pairs={{0,4},{4,0},{1,5},{5,1},{2,6},{6,2},{3,7},{7,3},{8,12},{12,8},{9,1... | collective-permute-start | bytes 884744 | tf_op jit(solution)/shard_map/ppermute | solution.py:25
  152.8 22.9 %collective-permute-start.42 = (bf16[2,256,768]{2,1,0:T(8,128)(2,1)S(1)}, bf16[2,256,768]{2,1,0:T(8,128)(2,1)S(1)}, u32[]{:S(2)}, u32[]{:S(2)}) collective-permute-start(bf16[2,256,768]{2,1,0:T(8,128)(2,1)S(1)} %copy-done.40), channel_id=1, source_target_pairs={{0,1},{1,0},{2,3},{3,2},{4,5},{5,4},{6,7},{7,6},{8,9},{9,8},{10,11... | collective-permute-start | bytes 2359304 | tf_op jit(solution)/shard_map/ppermute | solution.py:25
  153.7 15.0 %collective-permute-start.52 = (bf16[224,768]{1,0:T(8,128)(2,1)S(1)}, bf16[224,768]{1,0:T(8,128)(2,1)S(1)}, u32[]{:S(2)}, u32[]{:S(2)}) collective-permute-start(bf16[224,768]{1,0:T(8,128)(2,1)S(1)} %pad_maximum_fusion.1), channel_id=1, source_target_pairs={{0,4},{4,0},{1,5},{5,1},{2,6},{6,2},{3,7},{7,3},{8,12},{12,8},{9,1... | collective-permute-start | bytes 1032200 | tf_op jit(solution)/shard_map/ppermute | solution.py:25
  162.3 13.8 %collective-permute-start.50 = (bf16[768,384]{1,0:T(8,128)(2,1)S(1)}, bf16[768,384]{1,0:T(8,128)(2,1)S(1)}, u32[]{:S(2)}, u32[]{:S(2)}) collective-permute-start(bf16[768,384]{1,0:T(8,128)(2,1)S(1)} %add_convert_fusion.3), channel_id=1, source_target_pairs={{8,16},{16,8},{9,17},{17,9},{10,18},{18,10},{11,19},{19,11},{12,20... | collective-permute-start | bytes 1769480 | tf_op jit(solution)/shard_map/ppermute | solution.py:55
  163.0 11.9 %collective-permute-start.46 = (bf16[192,768]{1,0:T(8,128)(2,1)S(1)}, bf16[192,768]{1,0:T(8,128)(2,1)S(1)}, u32[]{:S(2)}, u32[]{:S(2)}) collective-permute-start(bf16[192,768]{1,0:T(8,128)(2,1)S(1)} %add_convert_fusion.11), channel_id=1, source_target_pairs={{0,8},{24,16},{1,9},{25,17},{2,10},{26,18},{3,11},{27,19},{4,12},{... | collective-permute-start | bytes 884744 | tf_op jit(solution)/shard_map/ppermute | solution.py:51
  169.1 11.2 %collective-permute-start.54 = (bf16[224,768]{1,0:T(8,128)(2,1)S(1)}, bf16[224,768]{1,0:T(8,128)(2,1)S(1)}, u32[]{:S(2)}, u32[]{:S(2)}) collective-permute-start(bf16[224,768]{1,0:T(8,128)(2,1)S(1)} %pad_maximum_fusion.2), channel_id=1, source_target_pairs={{0,8},{24,16},{1,9},{25,17},{2,10},{26,18},{3,11},{27,19},{4,12},{... | collective-permute-start | bytes 1032200 | tf_op jit(solution)/shard_map/ppermute | solution.py:51
  172.3 17.1 %collective-permute-start.60 = (bf16[384,768]{1,0:T(8,128)(2,1)S(1)}, bf16[384,768]{1,0:T(8,128)(2,1)S(1)}, u32[]{:S(2)}, u32[]{:S(2)}) collective-permute-start(bf16[384,768]{1,0:T(8,128)(2,1)S(1)} %add_convert_fusion), channel_id=1, source_target_pairs={{8,0},{16,24},{9,1},{17,25},{10,2},{18,26},{11,3},{19,27},{12,4},{... | collective-permute-start | bytes 1769480 | tf_op jit(solution)/shard_map/ppermute | solution.py:60
  175.0 1.3 collective-permute-start.47
  175.8 15.7 %collective-permute-start.43 = (bf16[256,768]{1,0:T(8,128)(2,1)S(1)}, bf16[256,768]{1,0:T(8,128)(2,1)S(1)}, u32[]{:S(2)}, u32[]{:S(2)}) collective-permute-start(bf16[256,768]{1,0:T(8,128)(2,1)S(1)} %fusion.5), channel_id=1, source_target_pairs={{0,2},{1,3},{2,0},{3,1},{4,6},{5,7},{6,4},{7,5},{8,10},{9,11},{10,... | collective-permute-start | bytes 1179656 | tf_op jit(solution)/shard_map/ppermute | solution.py:25
  176.3 19.5 %collective-permute-start.48 = (bf16[192,768]{1,0:T(8,128)(2,1)S(1)}, bf16[192,768]{1,0:T(8,128)(2,1)S(1)}, u32[]{:S(2)}, u32[]{:S(2)}) collective-permute-start(bf16[192,768]{1,0:T(8,128)(2,1)S(1)} %add_convert_fusion.9), channel_id=1, source_target_pairs={{8,0},{16,24},{9,1},{17,25},{10,2},{18,26},{11,3},{19,27},{12,4},{... | collective-permute-start | bytes 884744 | tf_op jit(solution)/shard_map/ppermute | solution.py:60
  180.5 28.0 %collective-permute-start.58 = (bf16[768,384]{1,0:T(8,128)(2,1)S(1)}, bf16[768,384]{1,0:T(8,128)(2,1)S(1)}, u32[]{:S(2)}, u32[]{:S(2)}) collective-permute-start(bf16[768,384]{1,0:T(8,128)(2,1)S(1)} %add_convert_fusion.2), channel_id=1, source_target_pairs={{8,0},{16,24},{9,1},{17,25},{10,2},{18,26},{11,3},{19,27},{12,4},{... | collective-permute-start | bytes 1769480 | tf_op jit(solution)/shard_map/ppermute | solution.py:60
  181.9 15.9 %collective-permute-start.55 = (bf16[224,768]{1,0:T(8,128)(2,1)S(1)}, bf16[224,768]{1,0:T(8,128)(2,1)S(1)}, u32[]{:S(2)}, u32[]{:S(2)}) collective-permute-start(bf16[224,768]{1,0:T(8,128)(2,1)S(1)} %pad_maximum_fusion.3), channel_id=1, source_target_pairs={{8,16},{16,8},{9,17},{17,9},{10,18},{18,10},{11,19},{19,11},{12,20... | collective-permute-start | bytes 1032200 | tf_op jit(solution)/shard_map/ppermute | solution.py:55
  189.5 27.9 %collective-permute-start.61 = (bf16[384,768]{1,0:T(8,128)(2,1)S(1)}, bf16[384,768]{1,0:T(8,128)(2,1)S(1)}, u32[]{:S(2)}, u32[]{:S(2)}) collective-permute-start(bf16[384,768]{1,0:T(8,128)(2,1)S(1)} %broadcast_select_fusion), channel_id=1, source_target_pairs={{0,4},{4,0},{1,5},{5,1},{2,6},{6,2},{3,7},{7,3},{8,12},{12,8},{9,1... | collective-permute-start | bytes 1769480 | tf_op jit(solution)/shard_map/ppermute | solution.py:25
  195.9 11.3 %collective-permute-start.49 = (bf16[192,768]{1,0:T(8,128)(2,1)S(1)}, bf16[192,768]{1,0:T(8,128)(2,1)S(1)}, u32[]{:S(2)}, u32[]{:S(2)}) collective-permute-start(bf16[192,768]{1,0:T(8,128)(2,1)S(1)} %broadcast_select_fusion.7), channel_id=1, source_target_pairs={{0,4},{4,0},{1,5},{5,1},{2,6},{6,2},{3,7},{7,3},{8,12},{12,8},{9,1... | collective-permute-start | bytes 884744 | tf_op jit(solution)/shard_map/ppermute | solution.py:25
  197.9 16.3 %collective-permute-start.56 = (bf16[224,768]{1,0:T(8,128)(2,1)S(1)}, bf16[224,768]{1,0:T(8,128)(2,1)S(1)}, u32[]{:S(2)}, u32[]{:S(2)}) collective-permute-start(bf16[224,768]{1,0:T(8,128)(2,1)S(1)} %pad_maximum_fusion.4), channel_id=1, source_target_pairs={{8,0},{16,24},{9,1},{17,25},{10,2},{18,26},{11,3},{19,27},{12,4},{... | collective-permute-start | bytes 1032200 | tf_op jit(solution)/shard_map/ppermute | solution.py:60
  208.6 19.6 %collective-permute-start.59 = (bf16[768,384]{1,0:T(8,128)(2,1)S(1)}, bf16[768,384]{1,0:T(8,128)(2,1)S(1)}, u32[]{:S(2)}, u32[]{:S(2)}) collective-permute-start(bf16[768,384]{1,0:T(8,128)(2,1)S(1)} %broadcast_select_fusion.3), channel_id=1, source_target_pairs={{0,4},{4,0},{1,5},{5,1},{2,6},{6,2},{3,7},{7,3},{8,12},{12,8},{9,1... | collective-permute-start | bytes 1769480 | tf_op jit(solution)/shard_map/ppermute | solution.py:25
  214.4 12.7 %collective-permute-start.57 = (bf16[192,768]{1,0:T(8,128)(2,1)S(1)}, bf16[192,768]{1,0:T(8,128)(2,1)S(1)}, u32[]{:S(2)}, u32[]{:S(2)}) collective-permute-start(bf16[192,768]{1,0:T(8,128)(2,1)S(1)} %slice.360), channel_id=1, source_target_pairs={{0,4},{4,0},{1,5},{5,1},{2,6},{6,2},{3,7},{7,3},{8,12},{12,8},{9,1... | collective-permute-start | bytes 884744 | tf_op jit(solution)/shard_map/ppermute | solution.py:25
  (41 other events, 276.9 us)

commit v6 on v5

--- a/solution.py
+++ b/solution.py
@@ -396,8 +396,8 @@
 
 def ffn_weights_kernel(*refs):
     middles, rows = refs[:8], refs[8:16]
-    vectors, up, bias, down = refs[16:20]
-    down_out, up_out, bias_out = refs[20:]
+    vectors, (up, bias, down) = refs[16:20], refs[20:23]
+    down_out, up_out, bias_out = refs[23:]
     width = middles[0].shape[1]
     down_sum = up_sum = bias_sum = None
     for i in range(8):
@@ -405,7 +405,7 @@
         hidden, slope = gelu_parts(dot(middle, up[...]) + bias[...])
         normed = rows[i][:, :width].astype(full)
         factor = rows[i][:, width : width + 1].astype(full) + rows[i][:, width + 1 : width + 2].astype(full)
-        vector = vectors[i : i + 1]
+        vector = vectors[i // 2][i % 2 : i % 2 + 1]
         along = jnp.mean(normed * vector, axis=1, keepdims=True)
         ffn_grad = (factor * ((vector - jnp.mean(vector, axis=1, keepdims=True)) - normed * along)).astype(low)
         pre_grad = (slope * dot(ffn_grad, down[...], ((1,), (1,)))).astype(low)
@@ -425,7 +425,7 @@
         ffn_weights_kernel,
         out_shape=[S((half, width), low), S((width, half), low), S((1, half), full)],
         name="ffn_weights",
-    )(*middles, *rows, vectors, up, bias, down)
+    )(*middles, *rows, *vectors, up, bias, down)
 
 
 def contrast(pooled, key_queue, gathered, halfway, returned):
@@ -585,8 +585,6 @@
     pooled_grad = key_sum * (step * jnp.exp(top - lse)) + step * (jnp.exp(pos_logit - lse) - 1.0) * positive
     result_row = pooled_grad / count_pair
     vector_pair = result_row * final_gain
-    final_gain_part = result_row[0:1] * live_sum
-
     vector_pair, rows_core = tie((vector_pair, rows_core))
     attn_grad, one_grad, sums = with_weights(
         ffn_back_kernel,
@@ -597,9 +595,21 @@
         [slopes, summed, vector_pair, rows, affine],
         [S((length, width), low), S((length, width), full), S((8, width), full)],
     )
-    vectors_far, rows_far, attn_grad, middles, sums = tie((swap(vector_pair, "tensor", 2), swap(pairs["x"], "tensor", 2), attn_grad, middles, sums))
-    vectors_far = jnp.concatenate([vector_pair, vectors_far])
-    vectors_all = jnp.concatenate([vectors_far, swap(vectors_far, "tensor", 1)])
+    vectors_far, vectors_core, rows_far, attn_grad, middles, sums, pooled_grad, loss_part, result_row = tie(
+        (
+            swap(vector_pair, "tensor", 2),
+            swap(vector_pair, "tensor", 1),
+            swap(pairs["x"], "tensor", 2),
+            attn_grad,
+            middles,
+            sums,
+            pooled_grad,
+            loss_part,
+            result_row,
+        )
+    )
+    final_gain_part = result_row[0:1] * live_sum
+    vectors_all = [vector_pair, vectors_far, vectors_core, swap(vectors_far, "tensor", 1)]
     rows_all = rows_pair + [rows_far] + rows_core + [swap(rows_far, "tensor", 1)]
     vectors = jnp.concatenate([final_gain_part, pooled_grad[0:1], sums[0:4], loss_part[0:1]])
     down, up, up_bias_half = ffn_weights(middles, rows_all, vectors_all, up_half, bias_half, down_half)

time: 232 us -> 231 us (level)
  starting transfers between devices: 69 us -> 73.3 us
  other arithmetic: 21.3 us -> 18.7 us
    ppermute x50 -> x51, starting transfers between devices: 46.8 us -> 50.7 us  [swap(): return lax.ppermute(array, axis, [(i, i ^ stride) for i in range(size)])]
    unnamed x86 -> x92, local copies, waits for them, and re-layouts: 4.37 us -> 4.94 us
    ppermute x50 -> x51, waiting for transfers between devices: 45.2 us -> 45.2 us  [swap(): return lax.ppermute(array, axis, [(i, i ^ stride) for i in range(size)])]
  transfers between devices with their start and end apart: 62 -> 63, of which waited for: 27 -> 28; matrix products, arithmetic and copies ran while one was open for 14% -> 12% of each run, Pallas kernels for 24% -> 24%
where the time goes in v6:
time: 231 us; the launch traced here: 230 us
  starting transfers between devices  73.3 us (32%)
  waiting for transfers between devices  61.1 us (26%)
  Pallas kernels  55 us (24%)
  other arithmetic  18.7 us (8%)
  local copies, waits for them, and re-layouts  16.3 us (7%)
  matrix products  3.77 us (2%)
    ppermute x51, starting transfers between devices, swap(): return lax.ppermute(array, axis, [(i, i ^ stride) for i in range(size)])  50.7 us
    ppermute x51, waiting for transfers between devices, swap(): return lax.ppermute(array, axis, [(i, i ^ stride) for i in range(size)])  45.2 us
    pallas_call x2, Pallas kernels, with_weights(): pl.pallas_call(kernel, in_specs=[pl.BlockSpec(memory_space=pltpu.SMEM)] +...  17.8 us
    ppermute x4, starting transfers between devices, inward(): return lax.ppermute(part, 'dp', [(0, 1), (3, 2)])  14.3 us
    pallas_call x1, Pallas kernels, attend_back(): pl.pallas_call(attend_back_kernel, grid_spec=pltpu.PrefetchScalarGridSpec...  13.9 us
    ppermute x4, waiting for transfers between devices, outward(): outer = lax.ppermute(part, 'dp', [(1, 0), (2, 3)])  13.7 us
    pallas_call x1, Pallas kernels, attend(): pl.pallas_call(attend_kernel, grid_spec=pltpu.PrefetchScalarGridSpec(num_...  12 us
    pallas_call x1, Pallas kernels, ffn_weights(): pl.pallas_call(ffn_weights_kernel, out_shape=[S((half, width), low), S((w...  11.2 us
  transfers between devices with their start and end apart: 63, of which 28 were waited for; matrix products, arithmetic and copies ran while one was open for 12% of the time, Pallas kernels for 24%

profile of v6, /device:TPU:0, one launch (start us, length us, event | category | flops | bytes accessed | tf_op | source)
XLA Modules:
  0.0 229.9 jit_solution(2347335777377174337)
XLA Ops:
  0.7 1.2 constant_dynamic-slice_fusion.5
  1.9 1.1 constant_dynamic-slice_fusion.4
  3.0 1.1 pad_maximum_fusion
  4.2 3.0 %collective-permute-start = (bf16[768,768]{1,0:T(8,128)(2,1)}, bf16[768,768]{1,0:T(8,128)(2,1)}, u32[]{:S(2)}, u32[]{:S(2)}) collective-permute-start(bf16[768,768]{1,0:T(8,128)(2,1)} %pad_maximum_fusion), channel_id=1, source_target_pairs={{0,2},{1,3},{2,0},{3,1},{4,6},{5,7},{6,4},{7,5},{8,10},{9,11},{10,... | collective-permute-start | bytes 3538952 | tf_op jit(solution)/shard_map/ppermute | solution.py:25
  8.3 12.0 %attend.1 = (bf16[4,256,768]{2,1,0:T(8,128)(2,1)}, bf16[4,256,192]{2,1,0:T(8,128)(2,1)}, bf16[4,256,192]{2,1,0:T(8,128)(2,1)}, bf16[4,256,192]{2,1,0:T(8,128)(2,...) custom-call(s32[2]{0:T(128)} %get-tuple-element.281.place_in.place, ...), custom_call_target="tpu_custom_call" | custom-call | tf_op jit(solution)/shard_map/attend/pallas_call | solution.py:153
  20.4 1.6 collective-permute-start.1
  22.0 2.0 constant_dynamic-slice_fusion.refs_22_
  24.1 1.6 collective-permute-start.2
  25.8 2.0 constant_dynamic-slice_fusion.1.refs_20_
  27.9 2.7 %collective-permute-start.3 = (bf16[16,768]{1,0:T(8,128)(2,1)S(1)}, bf16[16,768]{1,0:T(8,128)(2,1)S(1)}, u32[]{:S(2)}, u32[]{:S(2)}) collective-permute-start(bf16[16,768]{1,0:T(8,128)(2,1)S(1)} %pad_maximum_fusion.7), channel_id=1, source_target_pairs={{0,16},{8,24},{16,0},{24,8},{1,17},{9,25},{17,1},{25,9},{2,18},{10... | collective-permute-start | bytes 73736 | tf_op jit(solution)/shard_map/ppermute | solution.py:25
  35.5 1.1 slice.237
  36.6 1.6 collective-permute-start.7
  38.2 1.6 collective-permute-start.8
  39.7 4.4 %collective-permute-done.12 = bf16[256,768]{1,0:T(8,128)(2,1)S(1)} collective-permute-done((bf16[256,768]{1,0:T(8,128)(2,1)S(1)}, bf16[256,768]{1,0:T(8,128)(2,1)S(1)}, u32[]{:S(2)}, u32[]{:S(2)}) %collective-permute-start.12) | collective-permute-done | bytes 393248 | tf_op jit(solution)/shard_map/ppermute | solution.py:25
  44.1 1.1 bitcast_add_fusion.1
  45.3 1.2 fusion.43
  46.5 1.1 collective-permute-start.13
  47.9 2.3 collective-permute-done.13
  51.8 1.1 fusion.42
  56.9 8.6 %ffn.1 = (bf16[4,256,768]{2,1,0:T(8,128)(2,1)}, bf16[256,896]{1,0:T(8,128)(2,1)}, bf16[1,256,768]{2,1,0:T(8,128)(2,1)}, f32[1,768]{1,0:T(1,128)}, bf16[1,896]{1,0:T(2,128)(2,1)}) custom-call(s32[2]{0:T(128)} %get-tuple-element.281.place_in.place, bf16[768,768]{1,0:T(8,128)(2,1)} %refs_0_.1, bf16[768,768]{1,0:T(8,128)(2,1)} %refs_1_.1, ...), custom_call_target="tpu_custom_call" | custom-call | tf_op jit(solution)/shard_map/ffn/pallas_call | solution.py:387
  65.5 1.5 collective-permute-done.15.refs_1_
  67.2 1.5 collective-permute-start.17
  68.7 2.3 %collective-permute-done.17 = bf16[1,896]{1,0:T(2,128)(2,1)S(1)} collective-permute-done((bf16[1,896]{1,0:T(2,128)(2,1)}, bf16[1,896]{1,0:T(2,128)(2,1)S(1)}, u32[]{:S(2)}, u32[]{:S(2)}) %collective-permute-start.17) | collective-permute-done | bytes 1824 | tf_op jit(solution)/shard_map/ppermute | solution.py:25
  72.8 1.6 collective-permute-start.18
  74.3 2.0 collective-permute-done.18
  76.4 2.7 %collective-permute-start.19 = (bf16[4,896]{1,0:T(4,128)(2,1)S(1)}, bf16[4,896]{1,0:T(4,128)(2,1)S(1)}, u32[]{:S(2)}, u32[]{:S(2)}) collective-permute-start(bf16[4,896]{1,0:T(4,128)(2,1)S(1)} %pad_maximum_fusion.16), channel_id=1, source_target_pairs={{0,16},{8,24},{16,0},{24,8},{1,17},{9,25},{17,1},{25,9},{2,18},{10... | collective-permute-start | bytes 21512 | tf_op jit(solution)/shard_map/ppermute | solution.py:25
  79.5 1.1 collective-permute-start.23
  81.0 1.1 collective-permute-start.24
  84.1 2.6 %collective-permute-start.21 = (f32[4,1024]{1,0:T(4,128)S(1)}, f32[4,1024]{1,0:T(4,128)S(1)}, u32[]{:S(2)}, u32[]{:S(2)}) collective-permute-start(f32[4,1024]{1,0:T(4,128)S(1)} %slice.313), channel_id=1, source_target_pairs={{0,16},{8,24},{16,0},{24,8},{1,17},{9,25},{17,1},{25,9},{2,18},{10... | collective-permute-start | bytes 49160 | tf_op jit(solution)/shard_map/ppermute | solution.py:25
  86.8 2.0 collective-permute-done.21
  89.1 1.6 collective-permute-start.22
  93.8 1.5 collective-permute-start.25
  95.5 2.0 collective-permute-done.25
  98.3 1.3 collective-permute-start.31
  100.8 9.3 %ffn_back.1 = (bf16[256,768]{1,0:T(8,128)(2,1)}, f32[256,768]{1,0:T(8,128)}, f32[8,768]{1,0:T(8,128)}) custom-call(s32[2]{0:T(128)} %get-tuple-element.281.place_in.place, bf16[768,768]{1,0:T(8,128)(2,1)} %refs_0_.1, bf16[768,768]{1,0:T(8,128)(2,1)} %refs_1_.1, bf16[768,768]{1,0:T(8,128)(2,1)} %collective-permute-done.4.refs_2_, ...), custom_call_target="tpu_custom_call" | custom-call | tf_op jit(solution)/shard_map/ffn_back/pallas_call | solution.py:387
  110.2 1.3 collective-permute-done.31.refs_11_
  111.6 1.3 collective-permute-start.36
  117.0 11.2 %ffn_weights.1 = (bf16[384,768]{1,0:T(8,128)(2,1)}, bf16[768,384]{1,0:T(8,128)(2,1)}, f32[1,384]{1,0:T(1,128)}) custom-call(bf16[256,768]{1,0:T(8,128)(2,1)} %copy-done.7, bf16[256,768]{1,0:T(8,128)(2,1)} %collective-permute-done.15.refs_1_, bf16[256,768]{1,0:T(8,128)(2,1)} %collective-permute-done.16.refs_2_, ...), custom_call_target="tpu_custom_call" | custom-call | tf_op jit(solution)/shard_map/ffn_weights/pallas_call | solution.py:424
  128.2 3.5 %collective-permute-start.42 = (bf16[384,768]{1,0:T(8,128)(2,1)}, bf16[384,768]{1,0:T(8,128)(2,1)S(1)}, u32[]{:S(2)}, u32[]{:S(2)}) collective-permute-start(bf16[384,768]{1,0:T(8,128)(2,1)} %get-tuple-element.202), channel_id=1, source_target_pairs={{0,8},{24,16},{1,9},{25,17},{2,10},{26,18},{3,11},{27,19},{4,12},{... | collective-permute-start | bytes 1769480 | tf_op jit(solution)/shard_map/ppermute | solution.py:51
  131.9 1.6 collective-permute-start.46
  135.0 13.9 %attend_back.1 = (bf16[2,256,768]{2,1,0:T(8,128)(2,1)}, bf16[2,256,768]{2,1,0:T(8,128)(2,1)}, bf16[192,768]{1,0:T(8,128)(2,1)}, bf16[192,768]{1,0:T(8,128)(2,1)}...) custom-call(s32[2]{0:T(128)} %get-tuple-element.281.place_in.place, ...), custom_call_target="tpu_custom_call" | custom-call | tf_op jit(solution)/shard_map/attend_back/pallas_call | solution.py:272
  150.8 1.5 collective-permute-start.45
  153.8 7.0 %collective-permute-done.45 = bf16[192,768]{1,0:T(8,128)(2,1)S(1)} collective-permute-done((bf16[192,768]{1,0:T(8,128)(2,1)S(1)}, bf16[192,768]{1,0:T(8,128)(2,1)S(1)}, u32[]{:S(2)}, u32[]{:S(2)}) %collective-permute-start.45) | collective-permute-done | bytes 294944 | tf_op jit(solution)/shard_map/ppermute | solution.py:25
  161.7 5.7 %collective-permute-start.47 = (bf16[192,768]{1,0:T(8,128)(2,1)S(1)}, bf16[192,768]{1,0:T(8,128)(2,1)S(1)}, u32[]{:S(2)}, u32[]{:S(2)}) collective-permute-start(bf16[192,768]{1,0:T(8,128)(2,1)S(1)} %add_convert_fusion.11), channel_id=1, source_target_pairs={{0,8},{24,16},{1,9},{25,17},{2,10},{26,18},{3,11},{27,19},{4,12},{... | collective-permute-start | bytes 884744 | tf_op jit(solution)/shard_map/ppermute | solution.py:51
  167.8 3.5 %collective-permute-start.55 = (bf16[224,768]{1,0:T(8,128)(2,1)S(1)}, bf16[224,768]{1,0:T(8,128)(2,1)S(1)}, u32[]{:S(2)}, u32[]{:S(2)}) collective-permute-start(bf16[224,768]{1,0:T(8,128)(2,1)S(1)} %pad_maximum_fusion.2), channel_id=1, source_target_pairs={{0,8},{24,16},{1,9},{25,17},{2,10},{26,18},{3,11},{27,19},{4,12},{... | collective-permute-start | bytes 1032200 | tf_op jit(solution)/shard_map/ppermute | solution.py:51
  171.4 1.3 collective-permute-start.61
  174.0 1.7 collective-permute-start.44
  176.0 1.3 collective-permute-start.49
  177.3 1.8 collective-permute-done.55
  179.2 1.4 collective-permute-start.59
  181.4 7.4 %collective-permute-done.61 = bf16[384,768]{1,0:T(8,128)(2,1)S(1)} collective-permute-done((bf16[384,768]{1,0:T(8,128)(2,1)S(1)}, bf16[384,768]{1,0:T(8,128)(2,1)S(1)}, u32[]{:S(2)}, u32[]{:S(2)}) %collective-permute-start.61) | collective-permute-done | bytes 589856 | tf_op jit(solution)/shard_map/ppermute | solution.py:60
  188.8 2.3 %collective-permute-start.62 = (bf16[384,768]{1,0:T(8,128)(2,1)S(1)}, bf16[384,768]{1,0:T(8,128)(2,1)S(1)}, u32[]{:S(2)}, u32[]{:S(2)}) collective-permute-start(bf16[384,768]{1,0:T(8,128)(2,1)S(1)} %broadcast_select_fusion), channel_id=1, source_target_pairs={{0,4},{4,0},{1,5},{5,1},{2,6},{6,2},{3,7},{7,3},{8,12},{12,8},{9,1... | collective-permute-start | bytes 1769480 | tf_op jit(solution)/shard_map/ppermute | solution.py:25
  191.2 1.1 fusion
  192.3 2.8 %collective-permute-done.49 = bf16[192,768]{1,0:T(8,128)(2,1)S(1)} collective-permute-done((bf16[192,768]{1,0:T(8,128)(2,1)S(1)}, bf16[192,768]{1,0:T(8,128)(2,1)S(1)}, u32[]{:S(2)}, u32[]{:S(2)}) %collective-permute-start.49) | collective-permute-done | bytes 294944 | tf_op jit(solution)/shard_map/ppermute | solution.py:60
  195.1 2.3 %collective-permute-start.50 = (bf16[192,768]{1,0:T(8,128)(2,1)S(1)}, bf16[192,768]{1,0:T(8,128)(2,1)S(1)}, u32[]{:S(2)}, u32[]{:S(2)}) collective-permute-start(bf16[192,768]{1,0:T(8,128)(2,1)S(1)} %broadcast_select_fusion.7), channel_id=1, source_target_pairs={{0,4},{4,0},{1,5},{5,1},{2,6},{6,2},{3,7},{7,3},{8,12},{12,8},{9,1... | collective-permute-start | bytes 884744 | tf_op jit(solution)/shard_map/ppermute | solution.py:25
  197.6 1.3 collective-permute-start.57
  198.9 7.4 %collective-permute-done.50 = bf16[192,768]{1,0:T(8,128)(2,1)S(1)} collective-permute-done((bf16[192,768]{1,0:T(8,128)(2,1)S(1)}, bf16[192,768]{1,0:T(8,128)(2,1)S(1)}, u32[]{:S(2)}, u32[]{:S(2)}) %collective-permute-start.50) | collective-permute-done | bytes 294944 | tf_op jit(solution)/shard_map/ppermute | solution.py:25
  207.8 2.3 %collective-permute-start.60 = (bf16[768,384]{1,0:T(8,128)(2,1)S(1)}, bf16[768,384]{1,0:T(8,128)(2,1)S(1)}, u32[]{:S(2)}, u32[]{:S(2)}) collective-permute-start(bf16[768,384]{1,0:T(8,128)(2,1)S(1)} %broadcast_select_fusion.3), channel_id=1, source_target_pairs={{0,4},{4,0},{1,5},{5,1},{2,6},{6,2},{3,7},{7,3},{8,12},{12,8},{9,1... | collective-permute-start | bytes 1769480 | tf_op jit(solution)/shard_map/ppermute | solution.py:25
  210.1 3.2 %collective-permute-done.57 = bf16[224,768]{1,0:T(8,128)(2,1)S(1)} collective-permute-done((bf16[224,768]{1,0:T(8,128)(2,1)S(1)}, bf16[224,768]{1,0:T(8,128)(2,1)S(1)}, u32[]{:S(2)}, u32[]{:S(2)}) %collective-permute-start.57) | collective-permute-done | bytes 344096 | tf_op jit(solution)/shard_map/ppermute | solution.py:60
  213.4 1.7 collective-permute-start.58
  217.0 1.6 maximum_convert_fusion.1
  218.6 7.3 %collective-permute-done.58 = bf16[192,768]{1,0:T(8,128)(2,1)S(1)} collective-permute-done((bf16[192,768]{1,0:T(8,128)(2,1)S(1)}, bf16[192,768]{1,0:T(8,128)(2,1)S(1)}, u32[]{:S(2)}, u32[]{:S(2)}) %collective-permute-start.58) | collective-permute-done | bytes 294944 | tf_op jit(solution)/shard_map/ppermute | solution.py:25
  227.2 1.6 maximum_convert_fusion
  228.7 1.2 copy-done.1
  (283 shorter events, 40.2 us)
Async XLA Ops:
  0.7 81.5 %copy-start = (bf16[2048,768]{1,0:T(8,128)(2,1)S(1)}, bf16[2048,768]{1,0:T(8,128)(2,1)}, u32[]{:S(2)}) copy-start(bf16[2048,768]{1,0:T(8,128)(2,1)} %param.26) | copy-start | bytes 9437188
  4.2 30.3 %collective-permute-start = (bf16[768,768]{1,0:T(8,128)(2,1)}, bf16[768,768]{1,0:T(8,128)(2,1)}, u32[]{:S(2)}, u32[]{:S(2)}) collective-permute-start(bf16[768,768]{1,0:T(8,128)(2,1)} %pad_maximum_fusion), channel_id=1, source_target_pairs={{0,2},{1,3},{2,0},{3,1},{4,6},{5,7},{6,4},{7,5},{8,10},{9,11},{10,... | collective-permute-start | bytes 3538952 | tf_op jit(solution)/shard_map/ppermute | solution.py:25
  7.2 27.3 %collective-permute-start.4 = (bf16[768,768]{1,0:T(8,128)(2,1)}, bf16[768,768]{1,0:T(8,128)(2,1)}, u32[]{:S(2)}, u32[]{:S(2)}) collective-permute-start(bf16[768,768]{1,0:T(8,128)(2,1)} %refs_0_.1), channel_id=1, source_target_pairs={{0,1},{1,0},{2,3},{3,2},{4,5},{5,4},{6,7},{7,6},{8,9},{9,8},{10,11... | collective-permute-start | bytes 3538952 | tf_op jit(solution)/shard_map/ppermute | solution.py:25
  7.2 27.3 %collective-permute-start.5 = (bf16[768,768]{1,0:T(8,128)(2,1)}, bf16[768,768]{1,0:T(8,128)(2,1)}, u32[]{:S(2)}, u32[]{:S(2)}) collective-permute-start(bf16[768,768]{1,0:T(8,128)(2,1)} %refs_1_.1), channel_id=1, source_target_pairs={{0,1},{1,0},{2,3},{3,2},{4,5},{5,4},{6,7},{7,6},{8,9},{9,8},{10,11... | collective-permute-start | bytes 3538952 | tf_op jit(solution)/shard_map/ppermute | solution.py:25
  20.3 13.0 %collective-permute-start.6 = (bf16[2,256,768]{2,1,0:T(8,128)(2,1)}, bf16[2,256,768]{2,1,0:T(8,128)(2,1)}, u32[]{:S(2)}, u32[]{:S(2)}) collective-permute-start(bf16[2,256,768]{2,1,0:T(8,128)(2,1)} %get-tuple-element.126), channel_id=1, source_target_pairs={{0,1},{1,0},{2,3},{3,2},{4,5},{5,4},{6,7},{7,6},{8,9},{9,8},{10,11... | collective-permute-start | bytes 2359304 | tf_op jit(solution)/shard_map/ppermute | solution.py:25
  20.4 3.7 %collective-permute-start.1 = (bf16[4,768]{1,0:T(4,128)(2,1)S(1)}, bf16[4,768]{1,0:T(4,128)(2,1)S(1)}, u32[]{:S(2)}, u32[]{:S(2)}) collective-permute-start(bf16[4,768]{1,0:T(4,128)(2,1)S(1)} %copy-done.27), channel_id=1, source_target_pairs={{0,4},{4,0},{1,5},{5,1},{2,6},{6,2},{3,7},{7,3},{8,12},{12,8},{9,1... | collective-permute-start | bytes 18440 | tf_op jit(solution)/shard_map/ppermute | solution.py:25
  24.1 3.8 %collective-permute-start.2 = (bf16[8,768]{1,0:T(8,128)(2,1)S(1)}, bf16[8,768]{1,0:T(8,128)(2,1)S(1)}, u32[]{:S(2)}, u32[]{:S(2)}) collective-permute-start(bf16[8,768]{1,0:T(8,128)(2,1)S(1)} %pad_maximum_fusion.11), channel_id=1, source_target_pairs={{0,8},{8,0},{16,24},{24,16},{1,9},{9,1},{17,25},{25,17},{2,10},{10... | collective-permute-start | bytes 36872 | tf_op jit(solution)/shard_map/ppermute | solution.py:25
  27.9 4.8 %collective-permute-start.3 = (bf16[16,768]{1,0:T(8,128)(2,1)S(1)}, bf16[16,768]{1,0:T(8,128)(2,1)S(1)}, u32[]{:S(2)}, u32[]{:S(2)}) collective-permute-start(bf16[16,768]{1,0:T(8,128)(2,1)S(1)} %pad_maximum_fusion.7), channel_id=1, source_target_pairs={{0,16},{8,24},{16,0},{24,8},{1,17},{9,25},{17,1},{25,9},{2,18},{10... | collective-permute-start | bytes 73736 | tf_op jit(solution)/shard_map/ppermute | solution.py:25
  34.5 9.7 %collective-permute-start.12 = (bf16[256,768]{1,0:T(8,128)(2,1)S(1)}, bf16[256,768]{1,0:T(8,128)(2,1)S(1)}, u32[]{:S(2)}, u32[]{:S(2)}) collective-permute-start(bf16[256,768]{1,0:T(8,128)(2,1)S(1)} %fusion.4), channel_id=1, source_target_pairs={{0,2},{1,3},{2,0},{3,1},{4,6},{5,7},{6,4},{7,5},{8,10},{9,11},{10,... | collective-permute-start | bytes 1179656 | tf_op jit(solution)/shard_map/ppermute | solution.py:25
  36.6 14.0 %collective-permute-start.7 = (bf16[384,768]{1,0:T(8,128)(2,1)S(1)}, bf16[384,768]{1,0:T(8,128)(2,1)S(1)}, u32[]{:S(2)}, u32[]{:S(2)}) collective-permute-start(bf16[384,768]{1,0:T(8,128)(2,1)S(1)} %slice.237), channel_id=1, source_target_pairs={{0,4},{4,0},{1,5},{5,1},{2,6},{6,2},{3,7},{7,3},{8,12},{12,8},{9,1... | collective-permute-start | bytes 1769480 | tf_op jit(solution)/shard_map/ppermute | solution.py:25
  38.2 13.7 %collective-permute-start.8 = (bf16[384,768]{1,0:T(8,128)(2,1)S(1)}, bf16[384,768]{1,0:T(8,128)(2,1)S(1)}, u32[]{:S(2)}, u32[]{:S(2)}) collective-permute-start(bf16[384,768]{1,0:T(8,128)(2,1)S(1)} %slice.237), channel_id=1, source_target_pairs={{0,8},{8,0},{16,24},{24,16},{1,9},{9,1},{17,25},{25,17},{2,10},{10... | collective-permute-start | bytes 1769480 | tf_op jit(solution)/shard_map/ppermute | solution.py:25
  39.7 14.8 %collective-permute-start.9 = (bf16[768,768]{1,0:T(8,128)(2,1)}, bf16[768,768]{1,0:T(8,128)(2,1)}, u32[]{:S(2)}, u32[]{:S(2)}) collective-permute-start(bf16[768,768]{1,0:T(8,128)(2,1)} %collective-permute-done.refs_4_), channel_id=1, source_target_pairs={{0,1},{1,0},{2,3},{3,2},{4,5},{5,4},{6,7},{7,6},{8,9},{9,8},{10,11... | collective-permute-start | bytes 3538952 | tf_op jit(solution)/shard_map/ppermute | solution.py:25
  46.5 3.7 %collective-permute-start.13 = (f32[1,768]{1,0:T(1,128)S(1)}, f32[1,768]{1,0:T(1,128)S(1)}, u32[]{:S(2)}, u32[]{:S(2)}) collective-permute-start(f32[1,768]{1,0:T(1,128)S(1)} %broadcast_in_dim.91), channel_id=1, source_target_pairs={{0,2},{1,3},{2,0},{3,1},{4,6},{5,7},{6,4},{7,5},{8,10},{9,11},{10,... | collective-permute-start | bytes 9224 | tf_op jit(solution)/shard_map/ppermute | solution.py:25
  50.2 2.8 %collective-permute-start.14 = (f32[2,768]{1,0:T(2,128)S(1)}, f32[2,768]{1,0:T(2,128)S(1)}, u32[]{:S(2)}, u32[]{:S(2)}) collective-permute-start(f32[2,768]{1,0:T(2,128)S(1)} %pad_maximum_fusion.17), channel_id=1, source_target_pairs={{0,1},{1,0},{2,3},{3,2},{4,5},{5,4},{6,7},{7,6},{8,9},{9,8},{10,11... | collective-permute-start | bytes 18440 | tf_op jit(solution)/shard_map/ppermute | solution.py:25
  50.6 3.1 %collective-permute-start.10 = (bf16[384,768]{1,0:T(8,128)(2,1)S(1)}, bf16[384,768]{1,0:T(8,128)(2,1)S(1)}, u32[]{:S(2)}, u32[]{:S(2)}) collective-permute-start(bf16[384,768]{1,0:T(8,128)(2,1)S(1)} %collective-permute-done.7.refs_5_), channel_id=1, source_target_pairs={{0,1},{1,0},{2,3},{3,2},{4,5},{5,4},{6,7},{7,6},{8,9},{9,8},{10,11... | collective-permute-start | bytes 1769480 | tf_op jit(solution)/shard_map/ppermute | solution.py:25
  51.8 2.0 collective-permute-start.11
  55.3 11.6 %collective-permute-start.15 = (bf16[256,768]{1,0:T(8,128)(2,1)S(1)}, bf16[256,768]{1,0:T(8,128)(2,1)}, u32[]{:S(2)}, u32[]{:S(2)}) collective-permute-start(bf16[256,768]{1,0:T(8,128)(2,1)S(1)} %get-tuple-element.167.refs_0_), channel_id=1, source_target_pairs={{0,4},{4,0},{1,5},{5,1},{2,6},{6,2},{3,7},{7,3},{8,12},{12,8},{9,1... | collective-permute-start | bytes 1179656 | tf_op jit(solution)/shard_map/ppermute | solution.py:25
  56.1 11.1 %collective-permute-start.16 = (bf16[256,768]{1,0:T(8,128)(2,1)S(1)}, bf16[256,768]{1,0:T(8,128)(2,1)}, u32[]{:S(2)}, u32[]{:S(2)}) collective-permute-start(bf16[256,768]{1,0:T(8,128)(2,1)S(1)} %get-tuple-element.167.refs_0_), channel_id=1, source_target_pairs={{0,2},{1,3},{2,0},{3,1},{4,6},{5,7},{6,4},{7,5},{8,10},{9,11},{10,... | collective-permute-start | bytes 1179656 | tf_op jit(solution)/shard_map/ppermute | solution.py:25
  67.2 3.8 %collective-permute-start.17 = (bf16[1,896]{1,0:T(2,128)(2,1)}, bf16[1,896]{1,0:T(2,128)(2,1)S(1)}, u32[]{:S(2)}, u32[]{:S(2)}) collective-permute-start(bf16[1,896]{1,0:T(2,128)(2,1)} %get-tuple-element.148), channel_id=1, source_target_pairs={{0,4},{4,0},{1,5},{5,1},{2,6},{6,2},{3,7},{7,3},{8,12},{12,8},{9,1... | collective-permute-start | bytes 5384 | tf_op jit(solution)/shard_map/ppermute | solution.py:25
  71.7 10.4 %collective-permute-start.20 = (bf16[256,768]{1,0:T(8,128)(2,1)}, bf16[256,768]{1,0:T(8,128)(2,1)}, u32[]{:S(2)}, u32[]{:S(2)}) collective-permute-start(bf16[256,768]{1,0:T(8,128)(2,1)} %collective-permute-done.15.refs_1_), channel_id=1, source_target_pairs={{0,2},{1,3},{2,0},{3,1},{4,6},{5,7},{6,4},{7,5},{8,10},{9,11},{10,... | collective-permute-start | bytes 1179656 | tf_op jit(solution)/shard_map/ppermute | solution.py:25
  72.8 3.6 %collective-permute-start.18 = (bf16[2,896]{1,0:T(2,128)(2,1)S(1)}, bf16[2,896]{1,0:T(2,128)(2,1)S(1)}, u32[]{:S(2)}, u32[]{:S(2)}) collective-permute-start(bf16[2,896]{1,0:T(2,128)(2,1)S(1)} %pad_maximum_fusion.18), channel_id=1, source_target_pairs={{0,8},{8,0},{16,24},{24,16},{1,9},{9,1},{17,25},{25,17},{2,10},{10... | collective-permute-start | bytes 10760 | tf_op jit(solution)/shard_map/ppermute | solution.py:25
  76.4 4.6 %collective-permute-start.19 = (bf16[4,896]{1,0:T(4,128)(2,1)S(1)}, bf16[4,896]{1,0:T(4,128)(2,1)S(1)}, u32[]{:S(2)}, u32[]{:S(2)}) collective-permute-start(bf16[4,896]{1,0:T(4,128)(2,1)S(1)} %pad_maximum_fusion.16), channel_id=1, source_target_pairs={{0,16},{8,24},{16,0},{24,8},{1,17},{9,25},{17,1},{25,9},{2,18},{10... | collective-permute-start | bytes 21512 | tf_op jit(solution)/shard_map/ppermute | solution.py:25
  79.0 18.6 %collective-permute-start.26 = (bf16[256,896]{1,0:T(8,128)(2,1)}, bf16[256,896]{1,0:T(8,128)(2,1)}, u32[]{:S(2)}, u32[]{:S(2)}) collective-permute-start(bf16[256,896]{1,0:T(8,128)(2,1)} %get-tuple-element.154.refs_13_.refs_8_), channel_id=1, source_target_pairs={{0,1},{1,0},{2,3},{3,2},{4,5},{5,4},{6,7},{7,6},{8,9},{9,8},{10,11... | collective-permute-start | bytes 1376264 | tf_op jit(solution)/shard_map/ppermute | solution.py:25
  79.0 21.0 %collective-permute-start.32 = (bf16[256,768]{1,0:T(8,128)(2,1)S(1)}, bf16[256,768]{1,0:T(8,128)(2,1)}, u32[]{:S(2)}, u32[]{:S(2)}) collective-permute-start(bf16[256,768]{1,0:T(8,128)(2,1)S(1)} %get-tuple-element.167.refs_0_), channel_id=1, source_target_pairs={{0,1},{1,0},{2,3},{3,2},{4,5},{5,4},{6,7},{7,6},{8,9},{9,8},{10,11... | collective-permute-start | bytes 1179656 | tf_op jit(solution)/shard_map/ppermute | solution.py:25
  79.5 13.6 %collective-permute-start.23 = (bf16[256,896]{1,0:T(8,128)(2,1)}, bf16[256,896]{1,0:T(8,128)(2,1)}, u32[]{:S(2)}, u32[]{:S(2)}) collective-permute-start(bf16[256,896]{1,0:T(8,128)(2,1)} %get-tuple-element.154.refs_13_.refs_8_), channel_id=1, source_target_pairs={{0,4},{4,0},{1,5},{5,1},{2,6},{6,2},{3,7},{7,3},{8,12},{12,8},{9,1... | collective-permute-start | bytes 1376264 | tf_op jit(solution)/shard_map/ppermute | solution.py:25
  81.0 12.2 %collective-permute-start.24 = (bf16[256,896]{1,0:T(8,128)(2,1)}, bf16[256,896]{1,0:T(8,128)(2,1)}, u32[]{:S(2)}, u32[]{:S(2)}) collective-permute-start(bf16[256,896]{1,0:T(8,128)(2,1)} %get-tuple-element.154.refs_13_.refs_8_), channel_id=1, source_target_pairs={{0,2},{1,3},{2,0},{3,1},{4,6},{5,7},{6,4},{7,5},{8,10},{9,11},{10,... | collective-permute-start | bytes 1376264 | tf_op jit(solution)/shard_map/ppermute | solution.py:25
  84.1 4.7 %collective-permute-start.21 = (f32[4,1024]{1,0:T(4,128)S(1)}, f32[4,1024]{1,0:T(4,128)S(1)}, u32[]{:S(2)}, u32[]{:S(2)}) collective-permute-start(f32[4,1024]{1,0:T(4,128)S(1)} %slice.313), channel_id=1, source_target_pairs={{0,16},{8,24},{16,0},{24,8},{1,17},{9,25},{17,1},{25,9},{2,18},{10... | collective-permute-start | bytes 49160 | tf_op jit(solution)/shard_map/ppermute | solution.py:25
  89.1 3.7 %collective-permute-start.22 = (f32[2,1024]{1,0:T(2,128)S(1)}, f32[2,1024]{1,0:T(2,128)S(1)}, u32[]{:S(2)}, u32[]{:S(2)}) collective-permute-start(f32[2,1024]{1,0:T(2,128)S(1)} %slice.318), channel_id=1, source_target_pairs={{0,8},{8,0},{16,24},{24,16},{1,9},{9,1},{17,25},{25,17},{2,10},{10... | collective-permute-start | bytes 24584 | tf_op jit(solution)/shard_map/ppermute | solution.py:25
  93.2 5.1 %collective-permute-start.27 = (bf16[256,896]{1,0:T(8,128)(2,1)}, bf16[256,896]{1,0:T(8,128)(2,1)S(1)}, u32[]{:S(2)}, u32[]{:S(2)}) collective-permute-start(bf16[256,896]{1,0:T(8,128)(2,1)} %collective-permute-done.23.refs_9_), channel_id=1, source_target_pairs={{0,1},{1,0},{2,3},{3,2},{4,5},{5,4},{6,7},{7,6},{8,9},{9,8},{10,11... | collective-permute-start | bytes 1376264 | tf_op jit(solution)/shard_map/ppermute | solution.py:25
  93.3 5.1 %collective-permute-start.28 = (bf16[256,896]{1,0:T(8,128)(2,1)}, bf16[256,896]{1,0:T(8,128)(2,1)S(1)}, u32[]{:S(2)}, u32[]{:S(2)}) collective-permute-start(bf16[256,896]{1,0:T(8,128)(2,1)} %collective-permute-done.24.refs_10_), channel_id=1, source_target_pairs={{0,1},{1,0},{2,3},{3,2},{4,5},{5,4},{6,7},{7,6},{8,9},{9,8},{10,11... | collective-permute-start | bytes 1376264 | tf_op jit(solution)/shard_map/ppermute | solution.py:25
  93.8 3.7 %collective-permute-start.25 = (f32[2,1024]{1,0:T(2,128)S(1)}, f32[2,1024]{1,0:T(2,128)S(1)}, u32[]{:S(2)}, u32[]{:S(2)}) collective-permute-start(f32[2,1024]{1,0:T(2,128)S(1)} %pad_maximum_fusion.15), channel_id=1, source_target_pairs={{0,4},{4,0},{1,5},{5,1},{2,6},{6,2},{3,7},{7,3},{8,12},{12,8},{9,1... | collective-permute-start | bytes 24584 | tf_op jit(solution)/shard_map/ppermute | solution.py:25
  97.5 3.3 %collective-permute-start.33 = (bf16[256,768]{1,0:T(8,128)(2,1)}, bf16[256,768]{1,0:T(8,128)(2,1)S(1)}, u32[]{:S(2)}, u32[]{:S(2)}) collective-permute-start(bf16[256,768]{1,0:T(8,128)(2,1)} %collective-permute-done.15.refs_1_), channel_id=1, source_target_pairs={{0,1},{1,0},{2,3},{3,2},{4,5},{5,4},{6,7},{7,6},{8,9},{9,8},{10,11... | collective-permute-start | bytes 1179656 | tf_op jit(solution)/shard_map/ppermute | solution.py:25
  97.7 12.5 %collective-permute-start.34 = (bf16[256,768]{1,0:T(8,128)(2,1)}, bf16[256,768]{1,0:T(8,128)(2,1)S(1)}, u32[]{:S(2)}, u32[]{:S(2)}) collective-permute-start(bf16[256,768]{1,0:T(8,128)(2,1)} %collective-permute-done.16.refs_2_), channel_id=1, source_target_pairs={{0,1},{1,0},{2,3},{3,2},{4,5},{5,4},{6,7},{7,6},{8,9},{9,8},{10,11... | collective-permute-start | bytes 1179656 | tf_op jit(solution)/shard_map/ppermute | solution.py:25
  98.2 11.9 %collective-permute-start.35 = (bf16[256,768]{1,0:T(8,128)(2,1)}, bf16[256,768]{1,0:T(8,128)(2,1)S(1)}, u32[]{:S(2)}, u32[]{:S(2)}) collective-permute-start(bf16[256,768]{1,0:T(8,128)(2,1)} %collective-permute-done.20.refs_3_), channel_id=1, source_target_pairs={{0,1},{1,0},{2,3},{3,2},{4,5},{5,4},{6,7},{7,6},{8,9},{9,8},{10,11... | collective-permute-start | bytes 1179656 | tf_op jit(solution)/shard_map/ppermute | solution.py:25
  98.3 13.1 %collective-permute-start.31 = (bf16[256,896]{1,0:T(8,128)(2,1)}, bf16[256,896]{1,0:T(8,128)(2,1)S(1)}, u32[]{:S(2)}, u32[]{:S(2)}) collective-permute-start(bf16[256,896]{1,0:T(8,128)(2,1)} %collective-permute-done.23.refs_9_), channel_id=1, source_target_pairs={{0,2},{1,3},{2,0},{3,1},{4,6},{5,7},{6,4},{7,5},{8,10},{9,11},{10,... | collective-permute-start | bytes 1376264 | tf_op jit(solution)/shard_map/ppermute | solution.py:25
  100.0 11.5 %collective-permute-start.29 = (f32[2,768]{1,0:T(2,128)S(1)}, f32[2,768]{1,0:T(2,128)S(1)}, u32[]{:S(2)}, u32[]{:S(2)}) collective-permute-start(f32[2,768]{1,0:T(2,128)S(1)} %get-tuple-element.160.refs_12_.refs_16_), channel_id=1, source_target_pairs={{0,2},{1,3},{2,0},{3,1},{4,6},{5,7},{6,4},{7,5},{8,10},{9,11},{10,... | collective-permute-start | bytes 18440 | tf_op jit(solution)/shard_map/ppermute | solution.py:25
  100.8 10.7 %collective-permute-start.30 = (f32[2,768]{1,0:T(2,128)S(1)}, f32[2,768]{1,0:T(2,128)S(1)}, u32[]{:S(2)}, u32[]{:S(2)}) collective-permute-start(f32[2,768]{1,0:T(2,128)S(1)} %get-tuple-element.160.refs_12_.refs_16_), channel_id=1, source_target_pairs={{0,1},{1,0},{2,3},{3,2},{4,5},{5,4},{6,7},{7,6},{8,9},{9,8},{10,11... | collective-permute-start | bytes 18440 | tf_op jit(solution)/shard_map/ppermute | solution.py:25
  111.6 16.6 %collective-permute-start.36 = (bf16[256,768]{1,0:T(8,128)(2,1)}, bf16[256,768]{1,0:T(8,128)(2,1)S(1)}, u32[]{:S(2)}, u32[]{:S(2)}) collective-permute-start(bf16[256,768]{1,0:T(8,128)(2,1)} %get-tuple-element.166.g0), channel_id=1, source_target_pairs={{0,2},{1,3},{2,0},{3,1},{4,6},{5,7},{6,4},{7,5},{8,10},{9,11},{10,... | collective-permute-start | bytes 1179656 | tf_op jit(solution)/shard_map/ppermute | solution.py:25
  112.9 15.3 %collective-permute-start.37 = (bf16[256,768]{1,0:T(8,128)(2,1)}, bf16[256,768]{1,0:T(8,128)(2,1)S(1)}, u32[]{:S(2)}, u32[]{:S(2)}) collective-permute-start(bf16[256,768]{1,0:T(8,128)(2,1)} %get-tuple-element.166.g0), channel_id=1, source_target_pairs={{0,1},{1,0},{2,3},{3,2},{4,5},{5,4},{6,7},{7,6},{8,9},{9,8},{10,11... | collective-permute-start | bytes 1179656 | tf_op jit(solution)/shard_map/ppermute | solution.py:25
  112.9 2.7 %collective-permute-start.38 = (bf16[256,896]{1,0:T(8,128)(2,1)S(1)}, bf16[256,896]{1,0:T(8,128)(2,1)S(1)}, u32[]{:S(2)}, u32[]{:S(2)}) collective-permute-start(bf16[256,896]{1,0:T(8,128)(2,1)S(1)} %collective-permute-done.31.refs_11_), channel_id=1, source_target_pairs={{0,1},{1,0},{2,3},{3,2},{4,5},{5,4},{6,7},{7,6},{8,9},{9,8},{10,11... | collective-permute-start | bytes 1376264 | tf_op jit(solution)/shard_map/ppermute | solution.py:25
  114.2 1.3 collective-permute-start.40
  114.3 1.3 collective-permute-start.39
  128.2 20.8 %collective-permute-start.42 = (bf16[384,768]{1,0:T(8,128)(2,1)}, bf16[384,768]{1,0:T(8,128)(2,1)S(1)}, u32[]{:S(2)}, u32[]{:S(2)}) collective-permute-start(bf16[384,768]{1,0:T(8,128)(2,1)} %get-tuple-element.202), channel_id=1, source_target_pairs={{0,8},{24,16},{1,9},{25,17},{2,10},{26,18},{3,11},{27,19},{4,12},{... | collective-permute-start | bytes 1769480 | tf_op jit(solution)/shard_map/ppermute | solution.py:51
  131.7 2.5 %collective-permute-start.41 = (bf16[256,768]{1,0:T(8,128)(2,1)S(1)}, bf16[256,768]{1,0:T(8,128)(2,1)S(1)}, u32[]{:S(2)}, u32[]{:S(2)}) collective-permute-start(bf16[256,768]{1,0:T(8,128)(2,1)S(1)} %collective-permute-done.36.g1), channel_id=1, source_target_pairs={{0,1},{1,0},{2,3},{3,2},{4,5},{5,4},{6,7},{7,6},{8,9},{9,8},{10,11... | collective-permute-start | bytes 1179656 | tf_op jit(solution)/shard_map/ppermute | solution.py:25
  131.9 28.9 %collective-permute-start.46 = (bf16[768,384]{1,0:T(8,128)(2,1)}, bf16[768,384]{1,0:T(8,128)(2,1)S(1)}, u32[]{:S(2)}, u32[]{:S(2)}) collective-permute-start(bf16[768,384]{1,0:T(8,128)(2,1)} %get-tuple-element.208), channel_id=1, source_target_pairs={{0,8},{24,16},{1,9},{25,17},{2,10},{26,18},{3,11},{27,19},{4,12},{... | collective-permute-start | bytes 1769480 | tf_op jit(solution)/shard_map/ppermute | solution.py:51
  149.0 3.9 %collective-permute-start.52 = (f32[7,768]{1,0:T(8,128)S(1)}, f32[7,768]{1,0:T(8,128)S(1)}, u32[]{:S(2)}, u32[]{:S(2)}) collective-permute-start(f32[7,768]{1,0:T(8,128)S(1)} %fusion.36), channel_id=1, source_target_pairs={{0,2},{1,3},{2,0},{3,1},{4,6},{5,7},{6,4},{7,5},{8,10},{9,11},{10,... | collective-permute-start | bytes 64520 | tf_op jit(solution)/shard_map/ppermute | solution.py:25
  150.0 17.7 %collective-permute-start.54 = (bf16[384,768]{1,0:T(8,128)(2,1)S(1)}, bf16[384,768]{1,0:T(8,128)(2,1)S(1)}, u32[]{:S(2)}, u32[]{:S(2)}) collective-permute-start(bf16[384,768]{1,0:T(8,128)(2,1)S(1)} %add_convert_fusion.1), channel_id=1, source_target_pairs={{8,16},{16,8},{9,17},{17,9},{10,18},{18,10},{11,19},{19,11},{12,20... | collective-permute-start | bytes 1769480 | tf_op jit(solution)/shard_map/ppermute | solution.py:55
  150.8 9.9 %collective-permute-start.45 = (bf16[192,768]{1,0:T(8,128)(2,1)S(1)}, bf16[192,768]{1,0:T(8,128)(2,1)S(1)}, u32[]{:S(2)}, u32[]{:S(2)}) collective-permute-start(bf16[192,768]{1,0:T(8,128)(2,1)S(1)} %copy-done.44), channel_id=1, source_target_pairs={{0,4},{4,0},{1,5},{5,1},{2,6},{6,2},{3,7},{7,3},{8,12},{12,8},{9,1... | collective-permute-start | bytes 884744 | tf_op jit(solution)/shard_map/ppermute | solution.py:25
  152.3 21.6 %collective-permute-start.43 = (bf16[2,256,768]{2,1,0:T(8,128)(2,1)S(1)}, bf16[2,256,768]{2,1,0:T(8,128)(2,1)S(1)}, u32[]{:S(2)}, u32[]{:S(2)}) collective-permute-start(bf16[2,256,768]{2,1,0:T(8,128)(2,1)S(1)} %copy-done.43), channel_id=1, source_target_pairs={{0,1},{1,0},{2,3},{3,2},{4,5},{5,4},{6,7},{7,6},{8,9},{9,8},{10,11... | collective-permute-start | bytes 2359304 | tf_op jit(solution)/shard_map/ppermute | solution.py:25
  153.1 14.4 %collective-permute-start.53 = (bf16[224,768]{1,0:T(8,128)(2,1)S(1)}, bf16[224,768]{1,0:T(8,128)(2,1)S(1)}, u32[]{:S(2)}, u32[]{:S(2)}) collective-permute-start(bf16[224,768]{1,0:T(8,128)(2,1)S(1)} %pad_maximum_fusion.1), channel_id=1, source_target_pairs={{0,4},{4,0},{1,5},{5,1},{2,6},{6,2},{3,7},{7,3},{8,12},{12,8},{9,1... | collective-permute-start | bytes 1032200 | tf_op jit(solution)/shard_map/ppermute | solution.py:25
  161.0 14.7 %collective-permute-start.51 = (bf16[768,384]{1,0:T(8,128)(2,1)S(1)}, bf16[768,384]{1,0:T(8,128)(2,1)S(1)}, u32[]{:S(2)}, u32[]{:S(2)}) collective-permute-start(bf16[768,384]{1,0:T(8,128)(2,1)S(1)} %add_convert_fusion.3), channel_id=1, source_target_pairs={{8,16},{16,8},{9,17},{17,9},{10,18},{18,10},{11,19},{19,11},{12,20... | collective-permute-start | bytes 1769480 | tf_op jit(solution)/shard_map/ppermute | solution.py:55
  161.7 11.4 %collective-permute-start.47 = (bf16[192,768]{1,0:T(8,128)(2,1)S(1)}, bf16[192,768]{1,0:T(8,128)(2,1)S(1)}, u32[]{:S(2)}, u32[]{:S(2)}) collective-permute-start(bf16[192,768]{1,0:T(8,128)(2,1)S(1)} %add_convert_fusion.11), channel_id=1, source_target_pairs={{0,8},{24,16},{1,9},{25,17},{2,10},{26,18},{3,11},{27,19},{4,12},{... | collective-permute-start | bytes 884744 | tf_op jit(solution)/shard_map/ppermute | solution.py:51
  167.8 11.2 %collective-permute-start.55 = (bf16[224,768]{1,0:T(8,128)(2,1)S(1)}, bf16[224,768]{1,0:T(8,128)(2,1)S(1)}, u32[]{:S(2)}, u32[]{:S(2)}) collective-permute-start(bf16[224,768]{1,0:T(8,128)(2,1)S(1)} %pad_maximum_fusion.2), channel_id=1, source_target_pairs={{0,8},{24,16},{1,9},{25,17},{2,10},{26,18},{3,11},{27,19},{4,12},{... | collective-permute-start | bytes 1032200 | tf_op jit(solution)/shard_map/ppermute | solution.py:51
  171.4 17.4 %collective-permute-start.61 = (bf16[384,768]{1,0:T(8,128)(2,1)S(1)}, bf16[384,768]{1,0:T(8,128)(2,1)S(1)}, u32[]{:S(2)}, u32[]{:S(2)}) collective-permute-start(bf16[384,768]{1,0:T(8,128)(2,1)S(1)} %add_convert_fusion), channel_id=1, source_target_pairs={{8,0},{16,24},{9,1},{17,25},{10,2},{18,26},{11,3},{19,27},{12,4},{... | collective-permute-start | bytes 1769480 | tf_op jit(solution)/shard_map/ppermute | solution.py:60
  173.2 2.7 %collective-permute-start.48 = (bf16[192,768]{1,0:T(8,128)(2,1)S(1)}, bf16[192,768]{1,0:T(8,128)(2,1)S(1)}, u32[]{:S(2)}, u32[]{:S(2)}) collective-permute-start(bf16[192,768]{1,0:T(8,128)(2,1)S(1)} %add_convert_fusion.10), channel_id=1, source_target_pairs={{8,16},{16,8},{9,17},{17,9},{10,18},{18,10},{11,19},{19,11},{12,20... | collective-permute-start | bytes 884744 | tf_op jit(solution)/shard_map/ppermute | solution.py:55
  174.0 17.1 %collective-permute-start.44 = (bf16[256,768]{1,0:T(8,128)(2,1)S(1)}, bf16[256,768]{1,0:T(8,128)(2,1)S(1)}, u32[]{:S(2)}, u32[]{:S(2)}) collective-permute-start(bf16[256,768]{1,0:T(8,128)(2,1)S(1)} %fusion.5), channel_id=1, source_target_pairs={{0,2},{1,3},{2,0},{3,1},{4,6},{5,7},{6,4},{7,5},{8,10},{9,11},{10,... | collective-permute-start | bytes 1179656 | tf_op jit(solution)/shard_map/ppermute | solution.py:25
  176.0 19.1 %collective-permute-start.49 = (bf16[192,768]{1,0:T(8,128)(2,1)S(1)}, bf16[192,768]{1,0:T(8,128)(2,1)S(1)}, u32[]{:S(2)}, u32[]{:S(2)}) collective-permute-start(bf16[192,768]{1,0:T(8,128)(2,1)S(1)} %add_convert_fusion.9), channel_id=1, source_target_pairs={{8,0},{16,24},{9,1},{17,25},{10,2},{18,26},{11,3},{19,27},{12,4},{... | collective-permute-start | bytes 884744 | tf_op jit(solution)/shard_map/ppermute | solution.py:60
  179.2 28.5 %collective-permute-start.59 = (bf16[768,384]{1,0:T(8,128)(2,1)S(1)}, bf16[768,384]{1,0:T(8,128)(2,1)S(1)}, u32[]{:S(2)}, u32[]{:S(2)}) collective-permute-start(bf16[768,384]{1,0:T(8,128)(2,1)S(1)} %add_convert_fusion.2), channel_id=1, source_target_pairs={{8,0},{16,24},{9,1},{17,25},{10,2},{18,26},{11,3},{19,27},{12,4},{... | collective-permute-start | bytes 1769480 | tf_op jit(solution)/shard_map/ppermute | solution.py:60
  180.7 16.8 %collective-permute-start.56 = (bf16[224,768]{1,0:T(8,128)(2,1)S(1)}, bf16[224,768]{1,0:T(8,128)(2,1)S(1)}, u32[]{:S(2)}, u32[]{:S(2)}) collective-permute-start(bf16[224,768]{1,0:T(8,128)(2,1)S(1)} %pad_maximum_fusion.3), channel_id=1, source_target_pairs={{8,16},{16,8},{9,17},{17,9},{10,18},{18,10},{11,19},{19,11},{12,20... | collective-permute-start | bytes 1032200 | tf_op jit(solution)/shard_map/ppermute | solution.py:55
  188.8 28.1 %collective-permute-start.62 = (bf16[384,768]{1,0:T(8,128)(2,1)S(1)}, bf16[384,768]{1,0:T(8,128)(2,1)S(1)}, u32[]{:S(2)}, u32[]{:S(2)}) collective-permute-start(bf16[384,768]{1,0:T(8,128)(2,1)S(1)} %broadcast_select_fusion), channel_id=1, source_target_pairs={{0,4},{4,0},{1,5},{5,1},{2,6},{6,2},{3,7},{7,3},{8,12},{12,8},{9,1... | collective-permute-start | bytes 1769480 | tf_op jit(solution)/shard_map/ppermute | solution.py:25
  195.1 11.2 %collective-permute-start.50 = (bf16[192,768]{1,0:T(8,128)(2,1)S(1)}, bf16[192,768]{1,0:T(8,128)(2,1)S(1)}, u32[]{:S(2)}, u32[]{:S(2)}) collective-permute-start(bf16[192,768]{1,0:T(8,128)(2,1)S(1)} %broadcast_select_fusion.7), channel_id=1, source_target_pairs={{0,4},{4,0},{1,5},{5,1},{2,6},{6,2},{3,7},{7,3},{8,12},{12,8},{9,1... | collective-permute-start | bytes 884744 | tf_op jit(solution)/shard_map/ppermute | solution.py:25
  197.6 15.7 %collective-permute-start.57 = (bf16[224,768]{1,0:T(8,128)(2,1)S(1)}, bf16[224,768]{1,0:T(8,128)(2,1)S(1)}, u32[]{:S(2)}, u32[]{:S(2)}) collective-permute-start(bf16[224,768]{1,0:T(8,128)(2,1)S(1)} %pad_maximum_fusion.4), channel_id=1, source_target_pairs={{8,0},{16,24},{9,1},{17,25},{10,2},{18,26},{11,3},{19,27},{12,4},{... | collective-permute-start | bytes 1032200 | tf_op jit(solution)/shard_map/ppermute | solution.py:60
  207.8 19.3 %collective-permute-start.60 = (bf16[768,384]{1,0:T(8,128)(2,1)S(1)}, bf16[768,384]{1,0:T(8,128)(2,1)S(1)}, u32[]{:S(2)}, u32[]{:S(2)}) collective-permute-start(bf16[768,384]{1,0:T(8,128)(2,1)S(1)} %broadcast_select_fusion.3), channel_id=1, source_target_pairs={{0,4},{4,0},{1,5},{5,1},{2,6},{6,2},{3,7},{7,3},{8,12},{12,8},{9,1... | collective-permute-start | bytes 1769480 | tf_op jit(solution)/shard_map/ppermute | solution.py:25
  213.4 12.5 %collective-permute-start.58 = (bf16[192,768]{1,0:T(8,128)(2,1)S(1)}, bf16[192,768]{1,0:T(8,128)(2,1)S(1)}, u32[]{:S(2)}, u32[]{:S(2)}) collective-permute-start(bf16[192,768]{1,0:T(8,128)(2,1)S(1)} %slice.353), channel_id=1, source_target_pairs={{0,4},{4,0},{1,5},{5,1},{2,6},{6,2},{3,7},{7,3},{8,12},{12,8},{9,1... | collective-permute-start | bytes 884744 | tf_op jit(solution)/shard_map/ppermute | solution.py:25
  (45 other events, 306.6 us)
